TPU v7x, 32 devices: a whole 2x2x4 slice. The times are simulated.
32 devices in a mesh: dp: 2 (over x), fsdp: 16 (over z, y, core).
Axes of the slice: x: 2, y: 2, z: 4, core: 2. Of those that a mesh axis runs over, the one named last changes fastest.
Arguments:
- inputs: bfloat16 [16, 1024, 1024], P('fsdp', 'dp'), may hold values from -6 to 6
- segment_ids: int32 [16, 1024], P('fsdp', 'dp'), may hold values from 0 to 2, never falling along the last dimension, each value on 1 to 512 neighbouring positions
- key_mask: int32 [16, 1024], P('fsdp', 'dp'), may hold values 0 or 1
- lead_index: int32 [16, 2], P('fsdp'), may hold values from 0 to 7
- cotangent_first: bfloat16 [16, 1024, 1024], P('fsdp', 'dp'), may hold values from -6 to 6
- cotangent_second: bfloat16 [16, 1024, 1024], P('fsdp', 'dp'), may hold values from -6 to 6
- w_qkv: bfloat16 [1024, 3072], P(('dp', 'fsdp')), may hold values from -0.1875 to 0.1875
- w_out: bfloat16 [1024, 1024], P(('dp', 'fsdp')), may hold values from -3 to 3
- w_up: bfloat16 [1024, 4096], P(('dp', 'fsdp')), may hold values from -0.1875 to 0.1875
- w_down: bfloat16 [4096, 1024], P(('dp', 'fsdp')), may hold values from -0.09375 to 0.09375
- biases: bfloat16 [4, 1024], P(None, ('dp', 'fsdp')), may hold values from -3 to 3
- up_bias: bfloat16 [4096], P(('dp', 'fsdp')), may hold values from -3 to 3
- norm_gains: bfloat16 [2, 1024], P(None, ('dp', 'fsdp')), may hold values from 0.099609375 to 1.8984375
- norm_shifts: bfloat16 [2, 1024], P(None, ('dp', 'fsdp')), may hold values from -2 to 2
- lead_table: bfloat16 [8, 1024], P(None, ('dp', 'fsdp')), may hold values from -5 to 5
Outputs:
- first_out: bfloat16 [16, 1024, 1024], P('fsdp', 'dp')
- second_out: bfloat16 [16, 1024, 1024], P('fsdp', 'dp')
- input_grad: float32 [16, 1024, 1024], P('fsdp', 'dp')
- grad_qkv: float32 [1024, 3072], P(('dp', 'fsdp'))
- grad_out: float32 [1024, 1024], P(('dp', 'fsdp'))
- grad_up: float32 [1024, 4096], P(('dp', 'fsdp'))
- grad_down: float32 [4096, 1024], P(('dp', 'fsdp'))
- grad_biases: float32 [4, 1024], P(None, ('dp', 'fsdp'))
- grad_up_bias: float32 [4096], P(('dp', 'fsdp'))
- grad_gains: float32 [2, 1024], P(None, ('dp', 'fsdp'))
- grad_shifts: float32 [2, 1024], P(None, ('dp', 'fsdp'))
- grad_lead: float32 [8, 1024], P(None, ('dp', 'fsdp'))
Inputs may be any that keep to these rules, and one draw needn't show every extreme that they name: `segment_ids`: sample numbers never fall along a group; each sample has 1 to min(2048, 512) patches, and one of each group has exactly min(2048, 512).
All inputs are finite; a program needn't handle non-finite values. No bound on the sum of `key_mask` on one device may be relied on, other than what follows from the above.
Results may differ from a plain program's by a relative error of at most 0.013.
Values may be sent and summed in bfloat16 or wider, within the bound.
No kernel may reach another device: no remote copies, remote signals or barrier semaphores. Data moves between devices by JAX's collectives and lax.ppermute only.
A program may use at most 256 MiB of HBM per device.

v0:
```python
from functools import partial
import math

import jax
import jax.numpy as jnp
from jax import lax
from jax.sharding import PartitionSpec as P

HEAD = 64


SCALE = 0.125
EPSILON = 1e-06
NEGATIVE = -1e30
ACROSS = (((0,), (0,)), ((), ()))
WITHIN = (((1,), (1,)), ((), ()))


def layer_norm(tensor, gain_row, shift_row):
    average = jnp.mean(tensor, axis=-1, keepdims=True)
    centred = tensor - average
    variance = jnp.mean(centred * centred, axis=-1, keepdims=True)
    return centred * lax.rsqrt(variance + EPSILON) * gain_row + shift_row


def product(left_side, right_side):
    return jnp.dot(left_side, right_side, preferred_element_type=jnp.float32)


def outer_sum(left_side, right_side):
    return lax.dot_general(left_side, right_side, ACROSS, preferred_element_type=jnp.float32)


def back_product(left_side, right_side):
    return lax.dot_general(left_side, right_side, WITHIN, preferred_element_type=jnp.float32)


def by_heads(tensor):
    return tensor.reshape(tensor.shape[0], tensor.shape[1] // HEAD, HEAD)


def permitted(query_seg, query_pos, key_seg, key_open, key_pos):
    matching = query_seg[:, None] == key_seg[None, :]
    return matching & ((key_open[None, :] == 1) | (query_pos[:, None] == key_pos[None, :]))


def scores(query_heads, key_heads):
    return (
        jnp.einsum("bhd,khd->hbk", query_heads, key_heads, preferred_element_type=jnp.float32)
        * SCALE
    )


def sweep(length, visitor, initial):
    stride = math.gcd(length, 512)
    return lax.fori_loop(
        0,
        length // stride,
        lambda position, running: visitor(position * stride, stride, running),
        initial,
    )


def body(
    inputs,
    segment_ids,
    key_mask,
    lead_index,
    cotangent_first,
    cotangent_second,
    w_qkv,
    w_out,
    w_up,
    w_down,
    biases,
    up_bias,
    norm_gains,
    norm_shifts,
    lead_table,
):
    tokens = inputs.shape[1]
    model = inputs.shape[2]
    heads = model // HEAD
    own_seg = segment_ids[0]
    own_open = key_mask[0]
    own_pos = lax.axis_index("dp") * tokens + jnp.arange(tokens, dtype=jnp.int32)
    all_seg, all_open = (
        lax.all_gather(own_seg, "dp", axis=0, tiled=True),
        lax.all_gather(own_open, "dp", axis=0, tiled=True),
    )

    def collect():
        return (
            lax.all_gather(w_qkv, ("dp", "fsdp"), axis=0, tiled=True),
            lax.all_gather(w_out, ("dp", "fsdp"), axis=0, tiled=True),
            lax.all_gather(w_up, ("dp", "fsdp"), axis=0, tiled=True),
            lax.all_gather(w_down, ("dp", "fsdp"), axis=0, tiled=True),
            lax.all_gather(biases, ("dp", "fsdp"), axis=1, tiled=True),
            lax.all_gather(up_bias, ("dp", "fsdp"), axis=0, tiled=True),
            lax.all_gather(norm_gains, ("dp", "fsdp"), axis=1, tiled=True),
            lax.all_gather(norm_shifts, ("dp", "fsdp"), axis=1, tiled=True),
            lax.all_gather(lead_table, ("dp", "fsdp"), axis=1, tiled=True),
        )

    def key_labels(row_start, stride):
        key_seg = lax.dynamic_slice_in_dim(all_seg, row_start, stride, 0)
        key_open = lax.dynamic_slice_in_dim(all_open, row_start, stride, 0)
        key_pos = row_start + jnp.arange(stride, dtype=jnp.int32)
        return permitted(own_seg, own_pos, key_seg, key_open, key_pos)

    def forward(start_in, lead_id, params):
        (
            weight_qkv,
            weight_out,
            weight_up,
            weight_down,
            bias_rows,
            bias_up,
            gain_rows,
            shift_rows,
            lead_rows,
        ) = params
        bias_full = bias_rows.astype(jnp.float32)
        gains = gain_rows.astype(jnp.float32)
        shifts = shift_rows.astype(jnp.float32)
        chooser = (jnp.arange(lead_rows.shape[0], dtype=jnp.int32) == lead_id).astype(jnp.float32)
        lead_vec = jnp.sum(chooser[:, None] * lead_rows.astype(jnp.float32), axis=0)
        hidden = start_in + lead_vec[None, :]
        normed = layer_norm(hidden, gains[0], shifts[0]).astype(jnp.bfloat16)
        mixed = product(normed, weight_qkv)
        query = (mixed[:, :model] + bias_full[0]).astype(jnp.bfloat16)
        keys = mixed[:, model : 2 * model].astype(jnp.bfloat16)
        values = (mixed[:, 2 * model :] + bias_full[1]).astype(jnp.bfloat16)
        query_heads = by_heads(query)
        start_stats = (
            jnp.full((heads, tokens), NEGATIVE, jnp.float32),
            jnp.zeros((heads, tokens), jnp.float32),
        )
        shard_rows = lax.all_gather(keys, "dp", axis=0, tiled=True)

        def visitor(offset, stride, inner):
            highest, denominator = inner
            key_block = by_heads(lax.dynamic_slice_in_dim(shard_rows, offset, stride, 0))
            allowed = key_labels(offset, stride)
            masked = jnp.where(allowed[None], scores(query_heads, key_block), NEGATIVE)
            new_high = jnp.maximum(highest, jnp.max(masked, axis=-1))
            weights = jnp.where(allowed[None], jnp.exp(masked - new_high[..., None]), 0.0)
            return (new_high, denominator * jnp.exp(highest - new_high) + jnp.sum(weights, axis=-1))

        highest, denominator = sweep(shard_rows.shape[0], visitor, start_stats)
        log_total = highest + jnp.log(denominator)
        start_out = jnp.zeros((tokens, heads, HEAD), jnp.float32)
        key_part = lax.all_gather(keys, "dp", axis=0, tiled=True)
        value_part = lax.all_gather(values, "dp", axis=0, tiled=True)

        def visitor(offset, stride, inner):
            key_block = by_heads(lax.dynamic_slice_in_dim(key_part, offset, stride, 0))
            value_block = by_heads(lax.dynamic_slice_in_dim(value_part, offset, stride, 0))
            allowed = key_labels(offset, stride)
            masked = jnp.where(allowed[None], scores(query_heads, key_block), NEGATIVE)
            probs = jnp.exp(masked - log_total[..., None]).astype(jnp.bfloat16)
            return inner + jnp.einsum(
                "hbk,khd->bhd", probs, value_block, preferred_element_type=jnp.float32
            )

        attn = sweep(key_part.shape[0], visitor, start_out).reshape(tokens, model)
        attn_low = attn.astype(jnp.bfloat16)
        middle = hidden + product(attn_low, weight_out) + bias_full[2]
        normed_mid = layer_norm(middle, gains[1], shifts[1]).astype(jnp.bfloat16)
        gate_in = product(normed_mid, weight_up) + bias_up.astype(jnp.float32)
        activated = jax.nn.gelu(gate_in, approximate=False).astype(jnp.bfloat16)
        result = middle + product(activated, weight_down) + bias_full[3]
        saved = (
            hidden,
            normed,
            query,
            keys,
            values,
            log_total,
            attn,
            attn_low,
            middle,
            normed_mid,
            gate_in,
            activated,
            chooser,
        )
        return (result, saved)

    def backward(saved, grad_res, params):
        (
            weight_qkv,
            weight_out,
            weight_up,
            weight_down,
            bias_rows,
            bias_up,
            gain_rows,
            shift_rows,
            lead_rows,
        ) = params
        (
            hidden,
            normed,
            query,
            keys,
            values,
            log_total,
            attn,
            attn_low,
            middle,
            normed_mid,
            gate_in,
            activated,
            chooser,
        ) = saved
        gains = gain_rows.astype(jnp.float32)
        shifts = shift_rows.astype(jnp.float32)
        grad_low = grad_res.astype(jnp.bfloat16)
        term_down = outer_sum(activated, grad_low)
        bias_down = jnp.sum(grad_low.astype(jnp.float32), axis=0)
        gate_pull = jax.vjp(partial(jax.nn.gelu, approximate=False), gate_in)[1]
        grad_gate = gate_pull(back_product(grad_low, weight_down))[0].astype(jnp.bfloat16)
        term_up = outer_sum(normed_mid, grad_gate)
        bias_gate = jnp.sum(grad_gate.astype(jnp.float32), axis=0)
        mid_pull = jax.vjp(layer_norm, middle, gains[1], shifts[1])[1]
        grad_mid_part, gain_mid, shift_mid = mid_pull(back_product(grad_gate, weight_up))
        grad_mid = grad_res + grad_mid_part
        grad_branch = grad_mid.astype(jnp.bfloat16)
        term_out = outer_sum(attn_low, grad_branch)
        bias_attn = jnp.sum(grad_branch.astype(jnp.float32), axis=0)
        grad_attn = back_product(grad_branch, weight_out).astype(jnp.bfloat16)
        grad_attn_heads = by_heads(grad_attn)
        delta = jnp.sum(by_heads(grad_attn.astype(jnp.float32)) * by_heads(attn), axis=-1).T
        query_heads = by_heads(query)
        keys_heads = by_heads(keys)
        values_heads = by_heads(values)
        start_query = jnp.zeros((tokens, heads, HEAD), jnp.float32)
        key_part = lax.all_gather(keys, "dp", axis=0, tiled=True)
        value_part = lax.all_gather(values, "dp", axis=0, tiled=True)

        def visitor(offset, stride, inner):
            key_block = by_heads(lax.dynamic_slice_in_dim(key_part, offset, stride, 0))
            value_block = by_heads(lax.dynamic_slice_in_dim(value_part, offset, stride, 0))
            allowed = key_labels(offset, stride)
            masked = jnp.where(allowed[None], scores(query_heads, key_block), NEGATIVE)
            probs = jnp.exp(masked - log_total[..., None])
            grad_probs = jnp.einsum(
                "bhd,khd->hbk", grad_attn_heads, value_block, preferred_element_type=jnp.float32
            )
            grad_logits = (probs * (grad_probs - delta[..., None])).astype(jnp.bfloat16)
            return inner + jnp.einsum(
                "hbk,khd->bhd", grad_logits, key_block, preferred_element_type=jnp.float32
            )

        grad_query = sweep(key_part.shape[0], visitor, start_query)
        all_lse, all_delta = (
            lax.all_gather(log_total, "dp", axis=1, tiled=True),
            lax.all_gather(delta, "dp", axis=1, tiled=True),
        )
        start_keys = (
            jnp.zeros((tokens, heads, HEAD), jnp.float32),
            jnp.zeros((tokens, heads, HEAD), jnp.float32),
        )
        query_part = lax.all_gather(query, "dp", axis=0, tiled=True)
        grad_part = lax.all_gather(grad_attn, "dp", axis=0, tiled=True)

        def visitor(offset, stride, inner):
            grad_keys, grad_values = inner
            query_block = by_heads(lax.dynamic_slice_in_dim(query_part, offset, stride, 0))
            grad_block = by_heads(lax.dynamic_slice_in_dim(grad_part, offset, stride, 0))
            query_seg = lax.dynamic_slice_in_dim(all_seg, offset, stride, 0)
            query_pos = offset + jnp.arange(stride, dtype=jnp.int32)
            allowed = permitted(query_seg, query_pos, own_seg, own_open, own_pos)
            lse_block = lax.dynamic_slice_in_dim(all_lse, offset, stride, 1)
            delta_block = lax.dynamic_slice_in_dim(all_delta, offset, stride, 1)
            masked = jnp.where(allowed[None], scores(query_block, keys_heads), NEGATIVE)
            probs = jnp.exp(masked - lse_block[..., None])
            grad_probs = jnp.einsum(
                "bhd,khd->hbk", grad_block, values_heads, preferred_element_type=jnp.float32
            )
            grad_logits = (probs * (grad_probs - delta_block[..., None])).astype(jnp.bfloat16)
            grad_values = grad_values + jnp.einsum(
                "hbk,bhd->khd",
                probs.astype(jnp.bfloat16),
                grad_block,
                preferred_element_type=jnp.float32,
            )
            grad_keys = grad_keys + jnp.einsum(
                "hbk,bhd->khd", grad_logits, query_block, preferred_element_type=jnp.float32
            )
            return (grad_keys, grad_values)

        grad_keys, grad_values = sweep(query_part.shape[0], visitor, start_keys)
        query_low = (grad_query * SCALE).reshape(tokens, model).astype(jnp.bfloat16)
        keys_low = (grad_keys * SCALE).reshape(tokens, model).astype(jnp.bfloat16)
        values_low = grad_values.reshape(tokens, model).astype(jnp.bfloat16)
        grad_mixed = jnp.concatenate([query_low, keys_low, values_low], axis=1)
        term_qkv = outer_sum(normed, grad_mixed)
        bias_query = jnp.sum(query_low.astype(jnp.float32), axis=0)
        bias_value = jnp.sum(values_low.astype(jnp.float32), axis=0)
        in_pull = jax.vjp(layer_norm, hidden, gains[0], shifts[0])[1]
        grad_in_part, gain_in, shift_in = in_pull(back_product(grad_mixed, weight_qkv))
        grad_start = grad_mid + grad_in_part
        term_lead = chooser[:, None] * jnp.sum(grad_start, axis=0)[None, :]
        terms = (
            term_qkv,
            term_out,
            term_up,
            term_down,
            jnp.stack([bias_query, bias_value, bias_attn, bias_down]),
            bias_gate,
            jnp.stack([gain_in, gain_mid]),
            jnp.stack([shift_in, shift_mid]),
            term_lead,
        )
        return (grad_start, terms)

    def spread(terms):
        return (
            lax.psum_scatter(terms[0], ("dp", "fsdp"), scatter_dimension=0, tiled=True),
            lax.psum_scatter(terms[1], ("dp", "fsdp"), scatter_dimension=0, tiled=True),
            lax.psum_scatter(terms[2], ("dp", "fsdp"), scatter_dimension=0, tiled=True),
            lax.psum_scatter(terms[3], ("dp", "fsdp"), scatter_dimension=0, tiled=True),
            lax.psum_scatter(terms[4], ("dp", "fsdp"), scatter_dimension=1, tiled=True),
            lax.psum_scatter(terms[5], ("dp", "fsdp"), scatter_dimension=0, tiled=True),
            lax.psum_scatter(terms[6], ("dp", "fsdp"), scatter_dimension=1, tiled=True),
            lax.psum_scatter(terms[7], ("dp", "fsdp"), scatter_dimension=1, tiled=True),
            lax.psum_scatter(terms[8], ("dp", "fsdp"), scatter_dimension=1, tiled=True),
        )

    result_first, saved_first = forward(inputs[0].astype(jnp.float32), lead_index[0, 0], collect())
    first_low = result_first.astype(jnp.bfloat16)
    result_second, saved_second = forward(
        first_low.astype(jnp.float32), lead_index[0, 1], collect()
    )
    second_low = result_second.astype(jnp.bfloat16)
    grad_between, terms_second = backward(
        saved_second, cotangent_second[0].astype(jnp.float32), collect()
    )
    early = spread(terms_second)
    grad_first, terms_first = backward(
        saved_first, cotangent_first[0].astype(jnp.float32) + grad_between, collect()
    )
    shards = jax.tree.map(jnp.add, early, spread(terms_first))
    return (
        first_low[None],
        second_low[None],
        grad_first[None],
        shards[0],
        shards[1],
        shards[2],
        shards[3],
        shards[4],
        shards[5],
        shards[6],
        shards[7],
        shards[8],
    )


def solution(mesh):
    placed = (
        P("fsdp", "dp", None),
        P("fsdp", "dp"),
        P("fsdp", "dp"),
        P("fsdp", None),
        P("fsdp", "dp", None),
        P("fsdp", "dp", None),
        P(("dp", "fsdp"), None),
        P(("dp", "fsdp"), None),
        P(("dp", "fsdp"), None),
        P(("dp", "fsdp"), None),
        P(None, ("dp", "fsdp")),
        P(("dp", "fsdp")),
        P(None, ("dp", "fsdp")),
        P(None, ("dp", "fsdp")),
        P(None, ("dp", "fsdp")),
    )
    return jax.shard_map(
        body,
        mesh=mesh,
        in_specs=placed,
        out_specs=(
            P("fsdp", "dp", None),
            P("fsdp", "dp", None),
            P("fsdp", "dp", None),
            P(("dp", "fsdp"), None),
            P(("dp", "fsdp"), None),
            P(("dp", "fsdp"), None),
            P(("dp", "fsdp"), None),
            P(None, ("dp", "fsdp")),
            P(("dp", "fsdp")),
            P(None, ("dp", "fsdp")),
            P(None, ("dp", "fsdp")),
            P(None, ("dp", "fsdp")),
        ),
        check_vma=False,
    )
```

profile of v0, /device:TPU:0, one launch (start us, length us, event | category | flops | bytes accessed | tf_op | source)
XLA Modules:
  0.0 2176.4 jit_solution(3869051892882395)
XLA Ops:
  8.0 43.9 %all-gather.2 = bf16[32,32,8]{1,2,0:T(8,128)(2,1)S(1)} all-gather(bf16[1,32,8]{1,2,0:T(8,128)(2,1)} %bitcast.553), channel_id=1, replica_groups=mesh['dp'=2,'fsdp'=16] {'dp','fsdp'}, dimensions={0}, use_global_device_ids=true | all-gather | bytes 16896 | tf_op jit(solution)/shard_map/all_gather | solution.py:102
  52.0 36.9 %all-gather.3 = bf16[32,32,2]{1,2,0:T(2,128)(2,1)S(1)} all-gather(bf16[1,32,2]{1,2,0:T(2,128)(2,1)} %bitcast.555), channel_id=1, replica_groups=mesh['dp'=2,'fsdp'=16] {'dp','fsdp'}, dimensions={0}, use_global_device_ids=true | all-gather | bytes 4224 | tf_op jit(solution)/shard_map/all_gather | solution.py:100
  88.9 37.9 %all-gather.4 = bf16[32,32,2]{1,2,0:T(2,128)(2,1)S(1)} all-gather(bf16[1,32,2]{1,2,0:T(2,128)(2,1)} %bitcast.556), channel_id=1, replica_groups=mesh['dp'=2,'fsdp'=16] {'dp','fsdp'}, dimensions={0}, use_global_device_ids=true | all-gather | bytes 4224 | tf_op jit(solution)/shard_map/all_gather | solution.py:101
  143.5 36.7 %all-gather.5 = bf16[32,32,4]{1,2,0:T(4,128)(2,1)S(1)} all-gather(bf16[1,32,4]{1,2,0:T(4,128)(2,1)S(1)} %bitcast.554), channel_id=1, replica_groups=mesh['dp'=2,'fsdp'=16] {'dp','fsdp'}, dimensions={0}, use_global_device_ids=true | all-gather | bytes 8448 | tf_op jit(solution)/shard_map/all_gather | solution.py:98
  195.3 38.0 %all-gather.6 = bf16[32,1,128]{2,1,0:T(2,128)(2,1)S(1)} all-gather(bf16[1,1,128]{2,1,0:T(2,128)(2,1)S(1)} %bitcast.557), channel_id=1, replica_groups=mesh['dp'=2,'fsdp'=16] {'dp','fsdp'}, dimensions={0}, use_global_device_ids=true | all-gather | bytes 8448 | tf_op jit(solution)/shard_map/all_gather | solution.py:99
  240.8 31.9 %while.120 = (s32[]{:T(128)}, f32[16,512]{1,0:T(8,128)S(1)}, f32[16,512]{1,0:T(8,128)S(1)}, s32[1,512]{1,0:T(1,128)S(1)}, s32[1024]{0:T(1024)S(1)}, /*index=5*/s...) while((s32[]{:T(128)}, f32[16,512]{1,0:T(8,128)S(1)}, ...), condition=%wide.region_6.7_spmd.clone, body=%wide.region_3.6_spmd.clone.sunk | while | flops 571516416 | bytes 38980808 | solution.py:56
  272.7 23.8 %while.121 = (s32[]{:T(128)}, f32[512,16,64]{0,2,1:T(8,128)}, bf16[1024,1024]{0,1:T(8,128)(2,1)}, s32[1,512]{1,0:T(1,128)S(1)}, s32[1024]{0:T(1024)S(1)}, /*inde...) while((s32[]{:T(128)}, f32[512,16,64]{0,2,1:T(8,128)}, ...), condition=%wide.region_8.9_spmd.clone, body=%wide.region_7.8_spmd.clone.sunk | while | flops 1092617728 | bytes 12111057 | solution.py:56
  305.8 48.0 %all-gather.28.cloned.1.call-done = bf16[1024,4096]{1,0:T(8,128)(2,1)} async-done(((bf16[32,4096]{1,0:T(8,128)(2,1)}), bf16[1024,4096]{1,0:T(8,128)(2,1)}) %all-gather.28.cloned.1.call-update) | async-done | bytes 8388624 | tf_op jit(solution)/shard_map/all_gather | solution.py:96
  353.8 28.3 %multiply_convert_fusion.3 = (bf16[512,4096]{1,0:T(8,128)(2,1)}, f32[512,4096]{1,0:T(8,128)}, f32[512,4096]{1,0:T(8,128)}) fusion(f32[4096]{0:T(1024)S(1)} %bitcast.537, bf16[1024,4096]{1,0:T(8,128)(2,1)} %all-gather.28.cloned.1.call-done, f32[512,1024]{1,0:T(8,128)} %copy-done.6, f32[1024]{0:T(1024)S(1)} %bitcast.520, f32[1024]{0:T(1024)S(1)} %bitcast.509, ...), kind=kOutput, calls=%fused_computation.149 | convolution fusion | flops 4436000768 | bytes 31485952 | tf_op jit(solution)/shard_map/dot_general | solution.py:27
  382.1 50.6 %all-gather.30.cloned.1.call-done = bf16[4096,1024]{1,0:T(8,128)(2,1)} async-done(((bf16[128,1024]{1,0:T(8,128)(2,1)}), bf16[4096,1024]{1,0:T(8,128)(2,1)}) %all-gather.30.cloned.1.call-update) | async-done | bytes 8388624 | tf_op jit(solution)/shard_map/all_gather | solution.py:97
  457.8 26.8 %all-gather.34.cloned.1.call-done = bf16[1024,1024]{1,0:T(8,128)(2,1)} async-done(((bf16[512,1024]{1,0:T(8,128)(2,1)}), bf16[1024,1024]{1,0:T(8,128)(2,1)}) %all-gather.34.cloned.1.call-update) | async-done | bytes 2097168 | tf_op jit(solution)/shard_map/all_gather | solution.py:153
  487.5 32.4 %while.122 = (s32[]{:T(128)}, f32[16,512]{1,0:T(8,128)S(1)}, f32[16,512]{1,0:T(8,128)S(1)}, s32[1,512]{1,0:T(1,128)S(1)}, s32[1024]{0:T(1024)S(1)}, /*index=5*/s...) while((s32[]{:T(128)}, f32[16,512]{1,0:T(8,128)S(1)}, ...), condition=%wide.region_17.18_spmd.clone, body=%wide.region_14.17_spmd.clone.sunk | while | flops 571516416 | bytes 38980808 | solution.py:56
  523.9 24.1 %while.123 = (s32[]{:T(128)}, f32[512,16,64]{0,2,1:T(8,128)}, bf16[1024,1024]{0,1:T(8,128)(2,1)}, s32[1,512]{1,0:T(1,128)S(1)}, s32[1024]{0:T(1024)S(1)}, /*inde...) while((s32[]{:T(128)}, f32[512,16,64]{0,2,1:T(8,128)}, ...), condition=%wide.region_19.20_spmd.clone, body=%wide.region_18.19_spmd.clone.sunk | while | flops 1092617728 | bytes 12111057 | solution.py:56
  553.8 28.2 %multiply_convert_fusion.2 = (bf16[512,4096]{1,0:T(8,128)(2,1)}, f32[512,4096]{1,0:T(8,128)}, f32[512,4096]{1,0:T(8,128)}) fusion(f32[4096]{0:T(1024)S(1)} %bitcast.538, bf16[1024,4096]{1,0:T(8,128)(2,1)} %all-gather.28.cloned.1.call-done, f32[512,1024]{1,0:T(8,128)S(1)} %get-tuple-element.2441, f32[512]{0:T(512)S(1)} %fusion.117, ...), kind=kOutput, calls=%fused_computation.136 | convolution fusion | flops 4436000768 | bytes 31485952 | tf_op jit(solution)/shard_map/dot_general | solution.py:27
  582.0 14.0 convert_reduce_fusion.1
  644.5 46.6 %while.124 = (s32[]{:T(128)}, f32[512,16,64]{0,2,1:T(8,128)}, bf16[1024,1024]{0,1:T(8,128)(2,1)S(1)}, s32[1,512]{1,0:T(1,128)S(1)}, s32[1024]{0:T(1024)S(1)}, /*...) while((s32[]{:T(128)}, f32[512,16,64]{0,2,1:T(8,128)}, ...), condition=%wide.region_26.27_spmd.clone, body=%wide.region_25.26_spmd.clone.sunk | while | flops 1637877248 | bytes 51989756 | solution.py:56
  694.5 76.7 %while.125 = (s32[]{:T(128)}, f32[512,16,64]{0,2,1:T(8,128)}, f32[512,16,64]{0,2,1:T(8,128)}, bf16[1024,1024]{1,0:T(8,128)(2,1)}, s32[1024]{0:T(1024)S(1)}, /*in...) while((s32[]{:T(128)}, f32[512,16,64]{0,2,1:T(8,128)}, ...), condition=%wide.region_28.29_spmd.clone, body=%wide.region_27.28_spmd.clone.sunk | while | flops 2192573952 | bytes 78892320 | solution.py:56
  718.5 13.8 bitcast_add_fusion.19
  756.6 14.4 bitcast_add_fusion.19
  785.9 14.4 convert_reduce_fusion
  819.8 46.6 %while.126 = (s32[]{:T(128)}, f32[512,16,64]{0,2,1:T(8,128)}, bf16[1024,1024]{0,1:T(8,128)(2,1)S(1)}, s32[1,512]{1,0:T(1,128)S(1)}, s32[1024]{0:T(1024)S(1)}, /*...) while((s32[]{:T(128)}, f32[512,16,64]{0,2,1:T(8,128)}, ...), condition=%wide.region_35.36_spmd.clone, body=%wide.region_34.35_spmd.clone.sunk | while | flops 1637877248 | bytes 51989756 | solution.py:56
  874.6 76.7 %while.127 = (s32[]{:T(128)}, f32[512,16,64]{0,2,1:T(8,128)}, f32[512,16,64]{0,2,1:T(8,128)}, bf16[1024,1024]{1,0:T(8,128)(2,1)}, s32[1024]{0:T(1024)S(1)}, /*in...) while((s32[]{:T(128)}, f32[512,16,64]{0,2,1:T(8,128)}, ...), condition=%wide.region_37.38_spmd.clone, body=%wide.region_36.37_spmd.clone.sunk | while | flops 2192573952 | bytes 78630144 | solution.py:56
  898.5 13.9 bitcast_add_fusion.22
  936.6 14.5 bitcast_add_fusion.22
  1057.5 39.5 %all-reduce = f32[4096]{0:T(1024)S(1)} all-reduce(f32[4096]{0:T(1024)S(1)} %add.740), channel_id=18, replica_groups=mesh['dp'=2,'fsdp'=16] {'dp','fsdp'}, use_global_device_ids=true, to_apply=%region_59.60.clone | all-reduce | flops 4096 | bytes 32768
  1101.9 131.4 %reduce-scatter.27.cloned.1.call-done = f32[32,2]{1,0:T(8,128)} async-done(((f32[1024,2]{1,0:T(8,128)}), f32[32,2]{1,0:T(8,128)}) %reduce-scatter.27.cloned.1.call-update) | async-done | bytes 272
  1234.7 130.8 %reduce-scatter.25.cloned.1.call-done = f32[32,4]{1,0:T(8,128)} async-done(((f32[1024,4]{1,0:T(8,128)}), f32[32,4]{1,0:T(8,128)}) %reduce-scatter.25.cloned.1.call-update) | async-done | bytes 528
  1366.9 130.6 %reduce-scatter.31.cloned.1.call-done = f32[32,8]{1,0:T(8,128)} async-done(((f32[1024,8]{1,0:T(8,128)}), f32[32,8]{1,0:T(8,128)}) %reduce-scatter.31.cloned.1.call-update) | async-done | bytes 1040
  1498.9 139.3 %reduce-scatter.19.cloned.1.call-done = f32[32,1024]{1,0:T(8,128)} async-done(((f32[1024,1024]{1,0:T(8,128)}), f32[32,1024]{1,0:T(8,128)}) %reduce-scatter.19.cloned.1.call-update) | async-done | bytes 131088 | tf_op jit(solution)/shard_map/reduce_scatter | solution.py:322
  1638.2 157.7 %reduce-scatter.17.cloned.1.call-done = f32[32,3072]{1,0:T(8,128)} async-done(((f32[1024,3072]{1,0:T(8,128)}), f32[32,3072]{1,0:T(8,128)}) %reduce-scatter.17.cloned.1.call-update) | async-done | bytes 393232 | tf_op jit(solution)/shard_map/reduce_scatter | solution.py:321
  1795.9 185.8 %reduce-scatter.23.cloned.1.call-done = f32[128,1024]{1,0:T(8,128)} async-done(((f32[4096,1024]{1,0:T(8,128)}), f32[128,1024]{1,0:T(8,128)}) %reduce-scatter.23.cloned.1.call-update) | async-done | bytes 524304 | tf_op jit(solution)/shard_map/reduce_scatter | solution.py:324
  1981.7 187.4 %reduce-scatter.21.cloned.1.call-done = f32[32,4096]{1,0:T(8,128)} async-done(((f32[1024,4096]{1,0:T(8,128)}), f32[32,4096]{1,0:T(8,128)}) %reduce-scatter.21.cloned.1.call-update) | async-done | bytes 524304 | tf_op jit(solution)/shard_map/reduce_scatter | solution.py:323
  (593 shorter events, 595.4 us)
Async XLA Ops:
  7.2 126.4 %all-gather.20.cloned.1.call-start = ((), (), s32[]{:S(2)}) async-start(), calls=%async_computation.8 | async-start | bytes 6488064 | tf_op jit(solution)/shard_map/all_gather | solution.py:94
  7.9 226.0 %all-gather.24.cloned.1.call-start = ((), (), s32[]{:S(2)}) async-start(), calls=%async_computation.10 | async-start | bytes 3145728 | tf_op jit(solution)/shard_map/all_gather | solution.py:153
  130.2 170.2 %copy-start.52 = (f32[1024]{0:T(1024)}, f32[1024]{0:T(1024)S(1)}, u32[]{:S(2)}) copy-start(f32[1024]{0:T(1024)S(1)} %get-tuple-element.2180) | copy-start | bytes 12292
  133.5 472.3 %copy-start.70 = (f32[1,1024]{1,0:T(1,128)}, f32[1,1024]{1,0:T(1,128)S(1)}, u32[]{:S(2)}) copy-start(f32[1,1024]{1,0:T(1,128)S(1)} %get-tuple-element.2429) | copy-start | bytes 12292
  133.5 420.2 %copy-start.77 = (f32[1,1024]{1,0:T(1,128)}, f32[1,1024]{1,0:T(1,128)S(1)}, u32[]{:S(2)}) copy-start(f32[1,1024]{1,0:T(1,128)S(1)} %get-tuple-element.2431) | copy-start | bytes 12292
  143.5 93.3 %all-gather.22.cloned.1.call-start = ((), (), s32[]{:S(2)}) async-start(), calls=%async_computation.9 | async-start | bytes 3145728 | tf_op jit(solution)/shard_map/all_gather | solution.py:154
  181.0 119.5 %copy-start.60 = (f32[1,1024]{1,0:T(1,128)}, f32[1,1024]{1,0:T(1,128)S(1)}, u32[]{:S(2)}) copy-start(f32[1,1024]{1,0:T(1,128)S(1)} %get-tuple-element.2426) | copy-start | bytes 12292
  184.8 115.6 %all-gather.26.cloned.1.call-start = ((), (), s32[]{:S(2)}) async-start(), calls=%async_computation.11 | async-start | bytes 2162688 | tf_op jit(solution)/shard_map/all_gather | solution.py:95
  185.4 168.4 %all-gather.28.cloned.1.call-start = ((), (), s32[]{:S(2)}) async-start(), calls=%async_computation.12 | async-start | bytes 8650752 | tf_op jit(solution)/shard_map/all_gather | solution.py:96
  186.0 246.7 %all-gather.30.cloned.1.call-start = ((), (), s32[]{:S(2)}) async-start(), calls=%async_computation.13 | async-start | bytes 8650752 | tf_op jit(solution)/shard_map/all_gather | solution.py:97
  186.6 298.1 %all-gather.34.cloned.1.call-start = ((), (), s32[]{:S(2)}) async-start(), calls=%async_computation.15 | async-start | bytes 3145728 | tf_op jit(solution)/shard_map/all_gather | solution.py:153
  233.3 348.7 %copy-start.118 = (f32[32,1,128]{2,1,0:T(1,128)}, f32[32,1,128]{2,1,0:T(1,128)S(1)}, u32[]{:S(2)}) copy-start(f32[32,1,128]{2,1,0:T(1,128)S(1)} %convert_element_type.319) | copy-start | bytes 49156
  304.0 78.1 %copy-start.81 = (f32[512]{0:T(512)}, f32[512]{0:T(512)S(1)}, u32[]{:S(2)}) copy-start(f32[512]{0:T(512)S(1)} %broadcast_multiply_fusion.2) | copy-start | bytes 6148
  305.7 76.4 %copy-start.90 = (f32[512]{0:T(512)}, f32[512]{0:T(512)S(1)}, u32[]{:S(2)}) copy-start(f32[512]{0:T(512)S(1)} %fusion.115) | copy-start | bytes 6148
  353.8 78.9 %copy-start.7 = (f32[512,1024]{1,0:T(8,128)S(1)}, f32[512,1024]{1,0:T(8,128)}, u32[]{:S(2)}) copy-start(f32[512,1024]{1,0:T(8,128)} %copy-done.6) | copy-start | bytes 6291460
  353.8 78.9 %copy-start.62 = (f32[1024]{0:T(1024)S(1)}, f32[1024]{0:T(1024)}, u32[]{:S(2)}) copy-start(f32[1024]{0:T(1024)} %get-tuple-element.2179) | copy-start | bytes 12292
  353.8 78.9 %copy-start.131 = (f32[1,1024]{1,0:T(1,128)S(1)}, f32[1,1024]{1,0:T(1,128)}, u32[]{:S(2)}) copy-start(f32[1,1024]{1,0:T(1,128)} %get-tuple-element.2425) | copy-start | bytes 12292
  452.8 67.2 %all-gather.32.cloned.1.call-start = ((), (), s32[]{:S(2)}) async-start(), calls=%async_computation.14 | async-start | bytes 3145728 | tf_op jit(solution)/shard_map/all_gather | solution.py:154
  456.7 237.7 %all-gather.36.cloned.1.call-start = ((), (), s32[]{:S(2)}) async-start(), calls=%async_computation.16 | async-start | bytes 3145728 | tf_op jit(solution)/shard_map/all_gather | solution.py:265
  457.8 236.7 %all-gather.38.cloned.1.call-start = ((), (), s32[]{:S(2)}) async-start(), calls=%async_computation.17 | async-start | bytes 3145728 | tf_op jit(solution)/shard_map/all_gather | solution.py:266
  553.4 52.4 %copy-start.11 = (f32[512,1024]{1,0:T(8,128)}, f32[512,1024]{1,0:T(8,128)S(1)}, u32[]{:S(2)}) copy-start(f32[512,1024]{1,0:T(8,128)S(1)} %get-tuple-element.2441) | copy-start | bytes 6291460
  612.0 262.5 %all-gather.40.cloned.1.call-start = ((), (), s32[]{:S(2)}) async-start(), calls=%async_computation.18 | async-start | bytes 3145728 | tf_op jit(solution)/shard_map/all_gather | solution.py:265
  616.7 257.8 %all-gather.42.cloned.1.call-start = ((), (), s32[]{:S(2)}) async-start(), calls=%async_computation.19 | async-start | bytes 3145728 | tf_op jit(solution)/shard_map/all_gather | solution.py:266
  819.7 280.9 %reduce-scatter.29.cloned.1.call-start = ((), (), s32[]{:S(2)}) async-start(), calls=%async_computation.26 | async-start | bytes 540672
  819.8 54.8 %copy-start.54 = (f32[16,1024]{1,0:T(8,128)S(1)}, f32[16,1024]{1,0:T(8,128)}, u32[]{:S(2)}) copy-start(f32[16,1024]{1,0:T(8,128)} %all_gather.114) | copy-start | bytes 196612
  966.4 266.9 %reduce-scatter.27.cloned.1.call-start = ((), (), s32[]{:S(2)}) async-start(), calls=%async_computation.25 | async-start | bytes 540672
  970.9 394.6 %reduce-scatter.25.cloned.1.call-start = ((), (), s32[]{:S(2)}) async-start(), calls=%async_computation.24 | async-start | bytes 540672
  972.1 525.4 %reduce-scatter.31.cloned.1.call-start = ((), (), s32[]{:S(2)}) async-start(), calls=%async_computation.27 | async-start | bytes 540672
  973.3 664.9 %reduce-scatter.19.cloned.1.call-start = ((), (), s32[]{:S(2)}) async-start(), calls=%async_computation.21 | async-start | bytes 4325376 | tf_op jit(solution)/shard_map/reduce_scatter | solution.py:322
  979.2 816.7 %reduce-scatter.17.cloned.1.call-start = ((), (), s32[]{:S(2)}) async-start(), calls=%async_computation.20 | async-start | bytes 12976128 | tf_op jit(solution)/shard_map/reduce_scatter | solution.py:321
  996.2 985.5 %reduce-scatter.23.cloned.1.call-start = ((), (), s32[]{:S(2)}) async-start(), calls=%async_computation.23 | async-start | bytes 17301504 | tf_op jit(solution)/shard_map/reduce_scatter | solution.py:324
  1019.7 1149.4 %reduce-scatter.21.cloned.1.call-start = ((), (), s32[]{:S(2)}) async-start(), calls=%async_computation.22 | async-start | bytes 17301504 | tf_op jit(solution)/shard_map/reduce_scatter | solution.py:323
  (129 other events, 1188.7 us)
Sparse Core Ops, SparseCore 0:
  10.9 72.2 all-gather.19
  143.6 29.2 all-gather.23
  184.9 30.5 all-gather.21
  218.3 56.4 all-gather.25
  277.5 76.2 all-gather.27
  356.5 76.1 all-gather.29
  452.9 31.6 all-gather.33
  486.2 33.1 all-gather.31
  520.9 33.1 all-gather.35
  612.2 34.4 all-gather.37
  648.2 33.0 all-gather.39
  819.8 33.0 all-gather.41
  966.5 133.9 reduce-scatter.28
  1102.7 130.5 reduce-scatter.26
  1235.4 130.0 reduce-scatter.24
  1367.7 129.7 reduce-scatter.30
  1500.2 137.9 reduce-scatter.18
  1644.6 151.2 reduce-scatter.16
  1798.9 182.7 reduce-scatter.22
  1984.5 184.5 reduce-scatter.20
where the time goes:
time: 2180 us
  waiting for transfers between devices  1190 us (55%)
  matrix products  518 us (24%)
  blocking collectives  262 us (12%)
  local copies, waits for them, and re-layouts  98 us (4%)
  other arithmetic  85.3 us (4%)
    unnamed x24, waiting for transfers between devices  398 us
    reduce_scatter x1, waiting for transfers between devices, spread(): lax.psum_scatter(terms[2], ('dp', 'fsdp'), scatter_dimension=0, tiled=True)  187 us
    reduce_scatter x1, waiting for transfers between devices, spread(): lax.psum_scatter(terms[3], ('dp', 'fsdp'), scatter_dimension=0, tiled=True)  186 us
    reduce_scatter x1, waiting for transfers between devices, spread(): lax.psum_scatter(terms[0], ('dp', 'fsdp'), scatter_dimension=0, tiled=True)  158 us
    reduce_scatter x1, waiting for transfers between devices, spread(): lax.psum_scatter(terms[1], ('dp', 'fsdp'), scatter_dimension=0, tiled=True)  139 us
    dot_general x12, matrix products, scores(): jnp.einsum('bhd,khd->hbk', query_heads, key_heads, preferred_element_type...  102 us
    dot_general x8, matrix products, product(): return jnp.dot(left_side, right_side, preferred_element_type=jnp.float32)  94.9 us
    dot_general x8, matrix products, outer_sum(): lax.dot_general(left_side, right_side, ACROSS, preferred_element_type=jnp...  74.1 us
  transfers between devices with their start and end apart: 20, of which 11 were waited for; matrix products, arithmetic and copies ran while one was open for 26% of the time, Pallas kernels for 0%

commit v1 on v0

v1 whole, which is shorter than its diff:
```python
from functools import partial
import math

import jax
import jax.numpy as jnp
import numpy as np
from jax import lax
from jax.experimental import pallas as pl
from jax.experimental.pallas import tpu as pltpu
from jax.sharding import Mesh, PartitionSpec as P

HEAD = 64
SCALE = 0.125
EPSILON = 1e-06
NEGATIVE = -1e30
ACROSS = (((0,), (0,)), ((), ()))
WITHIN = (((1,), (1,)), ((), ()))
BF = jnp.bfloat16
F32 = jnp.float32


def layer_norm(tensor, gain_row, shift_row):
    average = jnp.mean(tensor, axis=-1, keepdims=True)
    centred = tensor - average
    variance = jnp.mean(centred * centred, axis=-1, keepdims=True)
    return centred * lax.rsqrt(variance + EPSILON) * gain_row + shift_row


def product(left_side, right_side):
    return jnp.dot(left_side, right_side, preferred_element_type=F32)


def outer_sum(left_side, right_side):
    return lax.dot_general(left_side, right_side, ACROSS, preferred_element_type=F32)


def back_product(left_side, right_side):
    return lax.dot_general(left_side, right_side, WITHIN, preferred_element_type=F32)


def by_heads(tensor):
    return tensor.reshape(tensor.shape[0], tensor.shape[1] // HEAD, HEAD)


def permitted(query_seg, query_pos, key_seg, key_open, key_pos):
    matching = query_seg[:, None] == key_seg[None, :]
    return matching & ((key_open[None, :] == 1) | (query_pos[:, None] == key_pos[None, :]))


def scores(query_heads, key_heads):
    return (
        jnp.einsum("bhd,khd->hbk", query_heads, key_heads, preferred_element_type=F32) * SCALE
    )


def sweep(length, visitor, initial):
    stride = math.gcd(length, 512)
    return lax.fori_loop(
        0,
        length // stride,
        lambda position, running: visitor(position * stride, stride, running),
        initial,
    )


class Grid:
    def __init__(self, sizes):
        self.size = dict(sizes)
        self.at = {name: lax.axis_index(name) for name in sizes}
        self.places = jnp.stack([self.at[name] for name in sizes]).astype(jnp.int32)
        self.shards = math.prod(sizes.values())
        index = 0
        for name in sizes:
            index = index * sizes[name] + self.at[name]
        self.shard = index

    def shift(self, tensor, axis, step):
        n = self.size[axis]
        return lax.ppermute(tensor, axis, [(i, (i + step) % n) for i in range(n)])

    def far_steps(self):
        return [(a, b) for a in range(self.size["h"]) for b in range(self.size["z"])]

    def far_shift(self, tensor, step):
        high, deep = self.size["h"], self.size["z"]
        pairs = [
            (a * deep + b, ((a + step[0]) % high) * deep + (b + step[1]) % deep)
            for a in range(high)
            for b in range(deep)
        ]
        return lax.ppermute(tensor, ("h", "z"), pairs)

    def swap(self, tensor):
        return lax.ppermute(tensor, ("x", "c"), [(0, 0), (1, 2), (2, 1), (3, 3)])

    def rows(self, tensor):
        if self.size["h"] > 1:
            tensor = lax.all_gather(tensor, "h", axis=0, tiled=False)
        else:
            tensor = tensor[None]
        other = self.shift(tensor, "c", 1)
        first = self.at["c"] == 0
        both = jnp.stack([jnp.where(first, tensor, other), jnp.where(first, other, tensor)], axis=1)
        return both.reshape((-1,) + tensor.shape[2:])


def place(places, pieces, out_shapes, moves):
    def kernel(at_ref, *refs):
        ins, outs, sems = refs[: len(pieces)], refs[len(pieces) : -1], refs[-1]
        copies = [
            pltpu.make_async_copy(source, target, sems.at[i])
            for i, (source, target) in enumerate(moves(at_ref, ins, outs))
        ]
        for copy in copies:
            copy.start()
        for copy in copies:
            copy.wait()

    count = 2 * len(pieces)
    moved = sum(math.prod(s.shape) * 2 for s in out_shapes)
    return pl.pallas_call(
        kernel,
        out_shape=out_shapes,
        in_specs=[pl.BlockSpec(memory_space=pltpu.SMEM)]
        + [pl.BlockSpec(memory_space=pl.ANY)] * len(pieces),
        out_specs=[pl.BlockSpec(memory_space=pl.ANY)] * len(out_shapes),
        scratch_shapes=[pltpu.SemaphoreType.DMA((count,))],
        cost_estimate=pl.CostEstimate(flops=0, transcendentals=0, bytes_accessed=2 * moved),
        name="place",
    )(places, *pieces)


def gather_weights(grid, shard, widths):
    high, wide, deep, tall = (grid.size[name] for name in "hxzy")
    rows, columns = shard.shape
    half = rows // 2
    steps = grid.far_steps()
    pieces = [shard if step == (0, 0) else grid.far_shift(shard, step) for step in steps]

    def far_moves(at, ins, outs):
        listed = []
        for step, ref in zip(steps, ins):
            a = lax.rem(at[0] - step[0] + high, high)
            b = lax.rem(at[2] - step[1] + deep, deep)
            for colour in range(2):
                listed.append((ref.at[pl.ds(colour * half, half)], outs[colour].at[a, b]))
        return listed

    lines = place(
        grid.places,
        pieces,
        [jax.ShapeDtypeStruct((high, deep, half, columns), shard.dtype)] * 2,
        far_moves,
    )
    tagged = []
    first_a = [grid.shift(lines[0], "x", k) for k in range(1, wide)]
    first_b = [grid.shift(lines[1], "y", k) for k in range(1, tall)]
    tagged.append((lines[0], 0, 0, 0))
    tagged.append((lines[1], 0, 0, 1))
    tagged += [(t, k + 1, 0, 0) for k, t in enumerate(first_a)]
    tagged += [(t, 0, k + 1, 1) for k, t in enumerate(first_b)]
    held_a = [(lines[0], 0)] + [(t, k + 1) for k, t in enumerate(first_a)]
    held_b = [(lines[1], 0)] + [(t, k + 1) for k, t in enumerate(first_b)]
    for (ta, ka), (tb, kb) in zip(held_a, held_b):
        tagged += [(grid.shift(ta, "y", k), ka, k, 0) for k in range(1, tall)]
        tagged += [(grid.shift(tb, "x", k), k, kb, 1) for k in range(1, wide)]
    if len(held_b) > len(held_a):
        for tb, kb in held_b[len(held_a) :]:
            tagged += [(grid.shift(tb, "x", k), k, kb, 1) for k in range(1, wide)]
    pairs = [t + (0,) for t in tagged] + [(grid.shift(t[0], "c", 1),) + t[1:] + (1,) for t in tagged]
    offsets = [sum(widths[:i]) for i in range(len(widths))]

    def last_moves(at, ins, outs):
        listed = []
        for ref, (_, kx, ky, colour, kc) in zip(ins, pairs):
            px = lax.rem(at[1] - kx + wide, wide)
            py = lax.rem(at[3] - ky + tall, tall)
            pc = lax.rem(at[4] - kc + 2, 2)
            for out, offset, width in zip(outs, offsets, widths):
                listed.append(
                    (
                        ref.at[:, :, :, pl.ds(offset, width)],
                        out.at[:, px, :, py, pc, pl.ds(colour * half, half)],
                    )
                )
        return listed

    full = place(
        grid.places,
        [t[0] for t in pairs],
        [
            jax.ShapeDtypeStruct((high, wide, deep, tall, 2, rows, width), shard.dtype)
            for width in widths
        ],
        last_moves,
    )
    return [t.reshape(-1, width) for t, width in zip(full, widths)]


def pick(tensor, index, axis):
    return lax.dynamic_index_in_dim(tensor, index, axis, keepdims=False)


def total(parts):
    result = parts[0].astype(F32)
    for part in parts[1:]:
        result = result + part.astype(F32)
    return result


def scatter_sum(grid, term):
    high, wide, deep, tall = (grid.size[name] for name in "hxzy")
    rows, columns = term.shape[0] // grid.shards, term.shape[1]
    half = rows // 2
    view = term.reshape(high, wide, deep, tall, 2, rows, columns)
    pair_at = grid.at["c"]
    sent = grid.shift(pick(view, 1 - pair_at, 4), "c", 1)
    kept = pick(view, pair_at, 4)
    parts = []
    for colour, order in enumerate(("xy", "yx")):
        held = [t[..., colour * half : (colour + 1) * half, :] for t in (kept, sent)]
        axes = ["h", "x", "z", "y"]
        for name in order:
            n, own, axis = grid.size[name], grid.at[name], axes.index(name)
            arrived = [
                grid.shift(
                    total([pick(t, lax.rem(own + k, n), axis) for t in held]).astype(BF), name, k
                )
                for k in range(1, n)
            ]
            held = [pick(t, own, axis) for t in held] + arrived
            axes.remove(name)
        parts.append(held)

    def at_far(step):
        a = lax.rem(grid.at["h"] + step[0], high)
        b = lax.rem(grid.at["z"] + step[1], deep)
        return jnp.concatenate(
            [total([pick(pick(t, a, 0), b, 0) for t in held]) for held in parts], axis=0
        )

    arrived = [
        grid.far_shift(at_far(step).astype(BF), step) for step in grid.far_steps() if step != (0, 0)
    ]
    return total([at_far((0, 0))] + arrived)


def everywhere(grid, tensor):
    for name in "cxy":
        tensor = total([tensor] + [grid.shift(tensor, name, k) for k in range(1, grid.size[name])]).astype(
            tensor.dtype
        )
    return total(
        [tensor] + [grid.far_shift(tensor, s) for s in grid.far_steps() if s != (0, 0)]
    ).astype(tensor.dtype)


def body(
    sizes,
    inputs,
    segment_ids,
    key_mask,
    lead_index,
    cotangent_first,
    cotangent_second,
    w_qkv,
    w_out,
    w_up,
    w_down,
    biases,
    up_bias,
    norm_gains,
    norm_shifts,
    lead_table,
):
    grid = Grid(sizes)
    tokens, model = inputs.shape[1], inputs.shape[2]
    heads = model // HEAD
    shards = grid.shards
    share = model // shards

    small = jnp.concatenate(
        [t.reshape(-1) for t in (biases, up_bias, norm_gains, norm_shifts, lead_table)]
    )
    mine = jnp.arange(shards, dtype=jnp.int32)[:, None] == grid.shard
    small = everywhere(grid, jnp.where(mine, small[None, :], jnp.zeros((), BF)))
    lengths = [t.shape[0] for t in (biases, norm_gains, norm_shifts, lead_table)]

    def unpack(start, count):
        block = small[:, start : start + count * share].reshape(shards, count, share)
        return block.transpose(1, 0, 2).reshape(count, model).astype(F32)

    own_up = up_bias.shape[0]
    bias_full = unpack(0, lengths[0])
    bias_up = small[:, lengths[0] * share : lengths[0] * share + own_up].reshape(-1).astype(F32)
    begin = lengths[0] * share + own_up
    gains = unpack(begin, lengths[1])
    shifts = unpack(begin + lengths[1] * share, lengths[2])
    lead_rows = unpack(begin + (lengths[1] + lengths[2]) * share, lengths[3])

    labels = grid.swap(
        jnp.concatenate([segment_ids, key_mask, jnp.broadcast_to(lead_index.reshape(2, 1), (2, tokens))])
    )
    own_seg, own_open = labels[0], labels[1]
    leads = (labels[2, 0], labels[3, 0])
    start_low = grid.swap(inputs[0])
    seed_first = grid.swap(cotangent_first[0])
    seed_second = grid.swap(cotangent_second[0])
    every = grid.rows(labels[:2].T)
    all_seg, all_open = every[:, 0], every[:, 1]
    own_pos = (grid.at["h"] * 2 + grid.at["c"]) * tokens + jnp.arange(tokens, dtype=jnp.int32)

    (weight_qkv,) = gather_weights(grid, w_qkv, [w_qkv.shape[1]])
    weight_up, weight_out = gather_weights(
        grid, jnp.concatenate([w_up, w_out], axis=1), [w_up.shape[1], w_out.shape[1]]
    )
    (weight_down,) = gather_weights(grid, w_down, [w_down.shape[1]])

    def key_labels(row_start, stride):
        key_seg = lax.dynamic_slice_in_dim(all_seg, row_start, stride, 0)
        key_open = lax.dynamic_slice_in_dim(all_open, row_start, stride, 0)
        key_pos = row_start + jnp.arange(stride, dtype=jnp.int32)
        return permitted(own_seg, own_pos, key_seg, key_open, key_pos)

    def forward(start_in, lead_id):
        chooser = (jnp.arange(lead_rows.shape[0], dtype=jnp.int32) == lead_id).astype(F32)
        lead_vec = jnp.sum(chooser[:, None] * lead_rows, axis=0)
        hidden = start_in + lead_vec[None, :]
        normed = layer_norm(hidden, gains[0], shifts[0]).astype(BF)
        mixed = product(normed, weight_qkv)
        query = (mixed[:, :model] + bias_full[0]).astype(BF)
        keys = mixed[:, model : 2 * model].astype(BF)
        values = (mixed[:, 2 * model :] + bias_full[1]).astype(BF)
        query_heads = by_heads(query)
        start_stats = (
            jnp.full((heads, tokens), NEGATIVE, F32),
            jnp.zeros((heads, tokens), F32),
        )
        both_part = grid.rows(jnp.concatenate([keys, values], axis=1))
        key_part, value_part = both_part[:, :model], both_part[:, model:]

        def visitor(offset, stride, inner):
            highest, denominator = inner
            key_block = by_heads(lax.dynamic_slice_in_dim(key_part, offset, stride, 0))
            allowed = key_labels(offset, stride)
            masked = jnp.where(allowed[None], scores(query_heads, key_block), NEGATIVE)
            new_high = jnp.maximum(highest, jnp.max(masked, axis=-1))
            weights = jnp.where(allowed[None], jnp.exp(masked - new_high[..., None]), 0.0)
            return (new_high, denominator * jnp.exp(highest - new_high) + jnp.sum(weights, axis=-1))

        highest, denominator = sweep(key_part.shape[0], visitor, start_stats)
        log_total = highest + jnp.log(denominator)
        start_out = jnp.zeros((tokens, heads, HEAD), F32)

        def visitor(offset, stride, inner):
            key_block = by_heads(lax.dynamic_slice_in_dim(key_part, offset, stride, 0))
            value_block = by_heads(lax.dynamic_slice_in_dim(value_part, offset, stride, 0))
            allowed = key_labels(offset, stride)
            masked = jnp.where(allowed[None], scores(query_heads, key_block), NEGATIVE)
            probs = jnp.exp(masked - log_total[..., None]).astype(BF)
            return inner + jnp.einsum(
                "hbk,khd->bhd", probs, value_block, preferred_element_type=F32
            )

        attn = sweep(key_part.shape[0], visitor, start_out).reshape(tokens, model)
        attn_low = attn.astype(BF)
        middle = hidden + product(attn_low, weight_out) + bias_full[2]
        normed_mid = layer_norm(middle, gains[1], shifts[1]).astype(BF)
        gate_in = product(normed_mid, weight_up) + bias_up
        activated = jax.nn.gelu(gate_in, approximate=False).astype(BF)
        result = middle + product(activated, weight_down) + bias_full[3]
        saved = (
            hidden,
            normed,
            query,
            keys,
            values,
            key_part,
            value_part,
            log_total,
            attn,
            attn_low,
            middle,
            normed_mid,
            gate_in,
            activated,
            chooser,
        )
        return (result, saved)

    def backward(saved, grad_res, earlier, close):
        (
            hidden,
            normed,
            query,
            keys,
            values,
            key_part,
            value_part,
            log_total,
            attn,
            attn_low,
            middle,
            normed_mid,
            gate_in,
            activated,
            chooser,
        ) = saved

        def join(name, left_side, right_side):
            term = outer_sum(left_side, right_side)
            if earlier is not None:
                term = earlier[name].astype(F32) + term
            return close(term.astype(BF))

        terms = {}
        grad_low = grad_res.astype(BF)
        terms["down"] = join("down", activated, grad_low)
        bias_down = jnp.sum(grad_low.astype(F32), axis=0)
        gate_pull = jax.vjp(partial(jax.nn.gelu, approximate=False), gate_in)[1]
        grad_gate = gate_pull(back_product(grad_low, weight_down))[0].astype(BF)
        terms["up"] = join("up", normed_mid, grad_gate)
        bias_gate = jnp.sum(grad_gate.astype(F32), axis=0)
        mid_pull = jax.vjp(layer_norm, middle, gains[1], shifts[1])[1]
        grad_mid_part, gain_mid, shift_mid = mid_pull(back_product(grad_gate, weight_up))
        grad_mid = grad_res + grad_mid_part
        grad_branch = grad_mid.astype(BF)
        terms["out"] = join("out", attn_low, grad_branch)
        bias_attn = jnp.sum(grad_branch.astype(F32), axis=0)
        grad_attn = back_product(grad_branch, weight_out).astype(BF)
        grad_attn_heads = by_heads(grad_attn)
        delta = jnp.sum(by_heads(grad_attn.astype(F32)) * by_heads(attn), axis=-1).T
        query_heads = by_heads(query)
        keys_heads = by_heads(keys)
        values_heads = by_heads(values)
        start_query = jnp.zeros((tokens, heads, HEAD), F32)

        def visitor(offset, stride, inner):
            key_block = by_heads(lax.dynamic_slice_in_dim(key_part, offset, stride, 0))
            value_block = by_heads(lax.dynamic_slice_in_dim(value_part, offset, stride, 0))
            allowed = key_labels(offset, stride)
            masked = jnp.where(allowed[None], scores(query_heads, key_block), NEGATIVE)
            probs = jnp.exp(masked - log_total[..., None])
            grad_probs = jnp.einsum(
                "bhd,khd->hbk", grad_attn_heads, value_block, preferred_element_type=F32
            )
            grad_logits = (probs * (grad_probs - delta[..., None])).astype(BF)
            return inner + jnp.einsum(
                "hbk,khd->bhd", grad_logits, key_block, preferred_element_type=F32
            )

        grad_query = sweep(key_part.shape[0], visitor, start_query)
        stats = grid.rows(jnp.concatenate([log_total, delta]).T).T
        all_lse, all_delta = stats[:heads], stats[heads:]
        start_keys = (
            jnp.zeros((tokens, heads, HEAD), F32),
            jnp.zeros((tokens, heads, HEAD), F32),
        )
        both_part = grid.rows(jnp.concatenate([query, grad_attn], axis=1))
        query_part, grad_part = both_part[:, :model], both_part[:, model:]

        def visitor(offset, stride, inner):
            grad_keys, grad_values = inner
            query_block = by_heads(lax.dynamic_slice_in_dim(query_part, offset, stride, 0))
            grad_block = by_heads(lax.dynamic_slice_in_dim(grad_part, offset, stride, 0))
            query_seg = lax.dynamic_slice_in_dim(all_seg, offset, stride, 0)
            query_pos = offset + jnp.arange(stride, dtype=jnp.int32)
            allowed = permitted(query_seg, query_pos, own_seg, own_open, own_pos)
            lse_block = lax.dynamic_slice_in_dim(all_lse, offset, stride, 1)
            delta_block = lax.dynamic_slice_in_dim(all_delta, offset, stride, 1)
            masked = jnp.where(allowed[None], scores(query_block, keys_heads), NEGATIVE)
            probs = jnp.exp(masked - lse_block[..., None])
            grad_probs = jnp.einsum(
                "bhd,khd->hbk", grad_block, values_heads, preferred_element_type=F32
            )
            grad_logits = (probs * (grad_probs - delta_block[..., None])).astype(BF)
            grad_values = grad_values + jnp.einsum(
                "hbk,bhd->khd", probs.astype(BF), grad_block, preferred_element_type=F32
            )
            grad_keys = grad_keys + jnp.einsum(
                "hbk,bhd->khd", grad_logits, query_block, preferred_element_type=F32
            )
            return (grad_keys, grad_values)

        grad_keys, grad_values = sweep(query_part.shape[0], visitor, start_keys)
        query_low = (grad_query * SCALE).reshape(tokens, model).astype(BF)
        keys_low = (grad_keys * SCALE).reshape(tokens, model).astype(BF)
        values_low = grad_values.reshape(tokens, model).astype(BF)
        grad_mixed = jnp.concatenate([query_low, keys_low, values_low], axis=1)
        terms["qkv"] = join("qkv", normed, grad_mixed)
        bias_query = jnp.sum(query_low.astype(F32), axis=0)
        bias_value = jnp.sum(values_low.astype(F32), axis=0)
        in_pull = jax.vjp(layer_norm, hidden, gains[0], shifts[0])[1]
        grad_in_part, gain_in, shift_in = in_pull(back_product(grad_mixed, weight_qkv))
        grad_start = grad_mid + grad_in_part
        lead_sum = jnp.sum(grad_start, axis=0)
        term_lead = chooser[:, None] * lead_sum[None, :]
        vectors = (
            jnp.stack([bias_query, bias_value, bias_attn, bias_down]),
            bias_gate,
            jnp.stack([gain_in, gain_mid]),
            jnp.stack([shift_in, shift_mid]),
            term_lead,
        )
        return (grad_start, terms, vectors)

    result_first, saved_first = forward(start_low.astype(F32), leads[0])
    first_low = result_first.astype(BF)
    result_second, saved_second = forward(first_low.astype(F32), leads[1])
    second_low = result_second.astype(BF)
    grad_between, terms_second, vectors_second = backward(
        saved_second, seed_second.astype(F32), None, lambda t: t
    )
    grad_first, shares, vectors_first = backward(
        saved_first, seed_first.astype(F32) + grad_between, terms_second, partial(scatter_sum, grid)
    )
    vectors = [a + b for a, b in zip(vectors_second, vectors_first)]

    def pack(block):
        return block.reshape(-1, shards, share).transpose(1, 0, 2).reshape(shards, -1)

    packed = jnp.concatenate(
        [
            pack(vectors[0]),
            vectors[1].reshape(shards, -1),
            pack(vectors[2]),
            pack(vectors[3]),
            pack(vectors[4]),
        ],
        axis=1,
    )
    own_row = pick(everywhere(grid, packed), grid.shard, 0)
    cuts = np.cumsum([lengths[0] * share, own_up, lengths[1] * share, lengths[2] * share])
    small_out = jnp.split(own_row, [int(cut) for cut in cuts])
    return (
        grid.swap(first_low)[None],
        grid.swap(second_low)[None],
        grid.swap(grad_first.astype(BF)).astype(F32)[None],
        shares["qkv"],
        shares["out"],
        shares["up"],
        shares["down"],
        small_out[0].reshape(lengths[0], share),
        small_out[1],
        small_out[2].reshape(lengths[1], share),
        small_out[3].reshape(lengths[2], share),
        small_out[4].reshape(lengths[3], share),
    )


def solution(mesh):
    dp, fsdp = mesh.shape["dp"], mesh.shape["fsdp"]
    tall = fsdp // 8
    sizes = {"h": dp // 2, "x": 2, "z": 4, "y": tall, "c": 2}
    fine = Mesh(np.asarray(mesh.devices).reshape(tuple(sizes.values())), tuple(sizes))
    one, two, every = ("z", "y", "c"), ("h", "x"), ("h", "x", "z", "y", "c")
    placed = (
        P(one, two, None),
        P(one, two),
        P(one, two),
        P(one, None),
        P(one, two, None),
        P(one, two, None),
        P(every, None),
        P(every, None),
        P(every, None),
        P(every, None),
        P(None, every),
        P(every),
        P(None, every),
        P(None, every),
        P(None, every),
    )
    return jax.shard_map(
        partial(body, sizes),
        mesh=fine,
        in_specs=placed,
        out_specs=(
            P(one, two, None),
            P(one, two, None),
            P(one, two, None),
            P(every, None),
            P(every, None),
            P(every, None),
            P(every, None),
            P(None, every),
            P(every),
            P(None, every),
            P(None, every),
            P(None, every),
        ),
        check_vma=False,
    )
```

time: 2180 us -> 1980 us (0.908)
  waiting for transfers between devices: 1190 us -> 187 us
  Pallas kernels: 0 us -> 870 us
  blocking collectives: 262 us -> 0 us
  starting transfers between devices: 1.28 us -> 137 us
  local copies, waits for them, and re-layouts: 98 us -> 154 us
  other arithmetic: 85.3 us -> 131 us
  matrix products: 518 us -> 485 us
    pallas_call x0 -> x6, Pallas kernels: none -> 870 us  [place(): pl.pallas_call(kernel, out_shape=out_shapes, in_specs=[pl.BlockSpec(memor...]
    reduce_scatter x4 -> x0, waiting for transfers between devices: 670 us -> none  [the longest x1 187 us: spread(): lax.psum_scatter(terms[2], ('dp', 'fsdp'), scatter_dimension=0, tiled=True)]
    unnamed x24 -> x0, waiting for transfers between devices: 398 us -> none
    all_gather x11 -> x0, blocking collectives: 222 us -> none  [the longest x1 43.9 us: collect(): lax.all_gather(lead_table, ('dp', 'fsdp'), axis=1, tiled=True)]
    ppermute x0 -> x109, waiting for transfers between devices: none -> 187 us  [the longest x75 151 us: shift(): return lax.ppermute(tensor, axis, [(i, (i + step) % n) for i in range(n)])]
    ppermute x0 -> x109, starting transfers between devices: none -> 137 us  [the longest x27 52.3 us: far_shift(): return lax.ppermute(tensor, ('h', 'z'), pairs)]
    all_gather x12 -> x0, waiting for transfers between devices: 125 us -> none  [the longest x1 50.6 us: collect(): lax.all_gather(w_down, ('dp', 'fsdp'), axis=0, tiled=True)]
    unnamed x1 -> x0, blocking collectives: 39.5 us -> none
  transfers between devices with their start and end apart: 20 -> 109, of which waited for: 11 -> 31; matrix products, arithmetic and copies ran while one was open for 26% -> 28% of each run, Pallas kernels for 0% -> 44%
where the time goes in v1:
time: 1980 us; the launch traced here: 1970 us
  Pallas kernels  870 us (44%)
  matrix products  485 us (24%)
  waiting for transfers between devices  187 us (9%)
  local copies, waits for them, and re-layouts  154 us (8%)
  starting transfers between devices  137 us (7%)
  other arithmetic  131 us (7%)
    pallas_call x6, Pallas kernels, place(): pl.pallas_call(kernel, out_shape=out_shapes, in_specs=[pl.BlockSpec(memor...  870 us
    ppermute x75, waiting for transfers between devices, shift(): return lax.ppermute(tensor, axis, [(i, (i + step) % n) for i in range(n)])  151 us
    dot_general x12, matrix products, scores(): jnp.einsum('bhd,khd->hbk', query_heads, key_heads, preferred_element_type...  99 us
    dot_general x8, matrix products, product(): return jnp.dot(left_side, right_side, preferred_element_type=F32)  87.5 us
    dot_general x8, matrix products, back_product(): lax.dot_general(left_side, right_side, WITHIN, preferred_element_type=F32)  63 us
    dot_general x4, matrix products, visitor(): jnp.einsum('hbk,bhd->khd', grad_logits, query_block, preferred_element_ty...  56.7 us
    dot_general x8, matrix products, outer_sum(): lax.dot_general(left_side, right_side, ACROSS, preferred_element_type=F32)  55.7 us
    ppermute x27, starting transfers between devices, far_shift(): return lax.ppermute(tensor, ('h', 'z'), pairs)  52.3 us
  transfers between devices with their start and end apart: 109, of which 31 were waited for; matrix products, arithmetic and copies ran while one was open for 28% of the time, Pallas kernels for 44%

profile of v1, /device:TPU:0, one launch (start us, length us, event | category | flops | bytes accessed | tf_op | source)
XLA Modules:
  0.0 1969.4 jit_solution(10559189987749139821)
XLA Ops:
  46.1 25.7 %place.6 = (bf16[1,4,16,3072]{3,2,1,0:T(8,128)(2,1)}, bf16[1,4,16,3072]{3,2,1,0:T(8,128)(2,1)}) custom-call(s32[5]{0:T(128)} %stack.149.at_ref, bf16[32,3072]{1,0:T(8,128)(2,1)} %refs_0_.2, bf16[32,3072]{1,0:T(8,128)(2,1)} %copy-done.119, bf16[32,3072]{1,0:T(8,128)(2,1)} %copy-done.120, bf16[32,3072]{1,0:T(8,128)(2,1)} %copy-done.118), custom_call_target="tpu_custom_call" | custom-call | bytes 1572864 | tf_op jit(solution)/shard_map/place/pallas_call | solution.py:121
  85.5 33.6 %place.10 = (bf16[1,4,64,1024]{3,2,1,0:T(8,128)(2,1)}, bf16[1,4,64,1024]{3,2,1,0:T(8,128)(2,1)}) custom-call(s32[5]{0:T(128)} %stack.149.at_ref, bf16[128,1024]{1,0:T(8,128)(2,1)} %refs_0_.3, bf16[128,1024]{1,0:T(8,128)(2,1)} %copy-done.111, bf16[128,1024]{1,0:T(8,128)(2,1)} %copy-done.112, bf16[128,1024]{1,0:T(8,128)(2,1)} %copy-done.113), custom_call_target="tpu_custom_call" | custom-call | bytes 2097152 | tf_op jit(solution)/shard_map/place/pallas_call | solution.py:121
  127.0 19.0 collective-permute-done.47.refs_2_
  159.4 41.5 %place.8 = (bf16[1,4,16,5120]{3,2,1,0:T(8,128)(2,1)}, bf16[1,4,16,5120]{3,2,1,0:T(8,128)(2,1)}) custom-call(s32[5]{0:T(128)} %stack.149.at_ref, bf16[32,5120]{1,0:T(8,128)(2,1)} %copy-done.62, bf16[32,5120]{1,0:T(8,128)(2,1)} %collective-permute-done.27.refs_1_, bf16[32,5120]{1,0:T(8,128)(2,1)} %copy-done.102, bf16[32,5120]{1,0:T(8,128)(2,1)} %copy-done.103), custom_call_target="tpu_custom_call" | custom-call | bytes 2621440 | tf_op jit(solution)/shard_map/place/pallas_call | solution.py:121
  205.1 192.8 %place.7 = bf16[1,2,4,2,2,32,3072]{6,5,4,3,2,1,0:T(8,128)(2,1)} custom-call(s32[5]{0:T(128)} %stack.149.at_ref, bf16[1,4,16,3072]{3,2,1,0:T(8,128)(2,1)} %get-tuple-element.1496.refs_0_, bf16[1,4,16,3072]{3,2,1,0:T(8,128)(2,1)} %get-tuple-element.1497.refs_1_, bf16[1,4,16,3072]{3,2,1,0:T(8,128)(2,1)} %copy-done.96, bf16[1,4,16,3072]{3,2,1,0:T(8,128)(2,1)} %copy-done.97, ...), custom_call_target="tpu_custom_call" | custom-call | bytes 12582912 | tf_op jit(solution)/shard_map/place/pallas_call | solution.py:121
  407.4 21.4 %collective-permute-done.31.refs_3_ = bf16[1,4,16,5120]{3,2,1,0:T(8,128)(2,1)} collective-permute-done((bf16[1,4,16,5120]{3,2,1,0:T(8,128)(2,1)S(1)}, bf16[1,4,16,5120]{3,2,1,0:T(8,128)(2,1)}, u32[]{:S(2)}, u32[]{:S(2)}) %collective-permute-start.31) | collective-permute-done | bytes 655392 | tf_op jit(solution)/shard_map/ppermute | solution.py:79
  447.0 15.0 collective-permute-done.34.refs_6_
  470.6 256.2 %place.11 = bf16[1,2,4,2,2,128,1024]{6,5,4,3,2,1,0:T(8,128)(2,1)} custom-call(s32[5]{0:T(128)} %stack.149.at_ref, bf16[1,4,64,1024]{3,2,1,0:T(8,128)(2,1)} %get-tuple-element.1505.refs_0_, bf16[1,4,64,1024]{3,2,1,0:T(8,128)(2,1)} %get-tuple-element.1506.refs_1_, bf16[1,4,64,1024]{3,2,1,0:T(8,128)(2,1)} %copy-done.89, bf16[1,4,64,1024]{3,2,1,0:T(8,128)(2,1)} %copy-done.91, ...), custom_call_target="tpu_custom_call" | custom-call | bytes 16777216 | tf_op jit(solution)/shard_map/place/pallas_call | solution.py:121
  726.8 319.9 %place.9 = (bf16[1,2,4,2,2,32,4096]{6,5,4,3,2,1,0:T(8,128)(2,1)}, bf16[1,2,4,2,2,32,1024]{6,5,4,3,2,1,0:T(8,128)(2,1)}) custom-call(s32[5]{0:T(128)} %stack.149.at_ref, bf16[1,4,16,5120]{3,2,1,0:T(8,128)(2,1)} %get-tuple-element.1501.refs_0_, bf16[1,4,16,5120]{3,2,1,0:T(8,128)(2,1)} %get-tuple-element.1502.refs_1_, bf16[1,4,16,5120]{3,2,1,0:T(8,128)(2,1)} %copy-done.83, ...), custom_call_target="tpu_custom_call" | custom-call | bytes 20971520 | tf_op jit(solution)/shard_map/place/pallas_call | solution.py:121
  1055.1 31.7 %while.120 = (s32[]{:T(128)}, f32[16,512]{1,0:T(8,128)S(1)}, f32[16,512]{1,0:T(8,128)S(1)}, s32[1,512]{1,0:T(1,128)S(1)}, s32[1024]{0:T(1024)S(1)}, /*index=5*/s...) while((s32[]{:T(128)}, f32[16,512]{1,0:T(8,128)S(1)}, ...), condition=%wide.region_6.7_spmd.clone, body=%wide.region_3.6_spmd.clone.sunk | while | flops 571516416 | bytes 38980808 | solution.py:58
  1090.8 23.9 %while.121 = (s32[]{:T(128)}, f32[512,16,64]{0,2,1:T(8,128)}, bf16[1024,1024]{0,1:T(8,128)(2,1)}, s32[1,512]{1,0:T(1,128)S(1)}, s32[1024]{0:T(1024)S(1)}, /*inde...) while((s32[]{:T(128)}, f32[512,16,64]{0,2,1:T(8,128)}, ...), condition=%wide.region_8.9_spmd.clone, body=%wide.region_7.8_spmd.clone.sunk | while | flops 1092617728 | bytes 12111057 | solution.py:58
  1122.1 27.8 %multiply_convert_fusion.3 = (bf16[512,4096]{1,0:T(8,128)(2,1)S(1)}, f32[512,4096]{1,0:T(8,128)}, f32[512,4096]{1,0:T(8,128)}) fusion(f32[4096]{0:T(1024)S(1)} %copy-done.155, bf16[1024,4096]{1,0:T(8,128)(2,1)} %bitcast.964, f32[512,1024]{1,0:T(8,128)S(1)} %get-tuple-element.2352, f32[1024]{0:T(1024)S(1)} %copy-done.169, f32[1024]{0:T(1024)S(1)} %mul.577, ...), kind=kOutput, calls=%fused_computation.160 | convolution fusion | flops 4436000768 | bytes 31485952 | tf_op jit(solution)/shard_map/dot_general | solution.py:30
  1211.1 31.7 %while.122 = (s32[]{:T(128)}, f32[16,512]{1,0:T(8,128)S(1)}, f32[16,512]{1,0:T(8,128)S(1)}, s32[1,512]{1,0:T(1,128)S(1)}, s32[1024]{0:T(1024)S(1)}, /*index=5*/s...) while((s32[]{:T(128)}, f32[16,512]{1,0:T(8,128)S(1)}, ...), condition=%wide.region_17.18_spmd.clone, body=%wide.region_14.17_spmd.clone.sunk | while | flops 571516416 | bytes 38980808 | solution.py:58
  1246.8 24.0 %while.123 = (s32[]{:T(128)}, f32[512,16,64]{0,2,1:T(8,128)}, bf16[1024,1024]{0,1:T(8,128)(2,1)}, s32[1,512]{1,0:T(1,128)S(1)}, s32[1024]{0:T(1024)S(1)}, /*inde...) while((s32[]{:T(128)}, f32[512,16,64]{0,2,1:T(8,128)}, ...), condition=%wide.region_19.20_spmd.clone, body=%wide.region_18.19_spmd.clone.sunk | while | flops 1092617728 | bytes 12111057 | solution.py:58
  1276.6 28.3 %multiply_convert_fusion.2 = (bf16[512,4096]{1,0:T(8,128)(2,1)}, f32[512,4096]{1,0:T(8,128)}, f32[512,4096]{1,0:T(8,128)}) fusion(f32[4096]{0:T(1024)S(1)} %copy-done.156, bf16[1024,4096]{1,0:T(8,128)(2,1)} %bitcast.965, f32[512,1024]{1,0:T(8,128)S(1)} %get-tuple-element.2357, f32[512]{0:T(512)S(1)} %fusion.176, f32[512]{0:T(512)S(1)} %broadcast_multiply_fusion, ...), kind=kOutput, calls=%fused_computation.147 | convolution fusion | flops 4436000768 | bytes 31485952 | tf_op jit(solution)/shard_map/dot_general | solution.py:30
  1304.8 13.2 convert_reduce_fusion.1
  1339.9 45.8 %while.124 = (s32[]{:T(128)}, f32[512,16,64]{0,2,1:T(8,128)}, bf16[1024,1024]{0,1:T(8,128)(2,1)S(1)}, s32[1,512]{1,0:T(1,128)S(1)}, s32[1024]{0:T(1024)S(1)}, /*...) while((s32[]{:T(128)}, f32[512,16,64]{0,2,1:T(8,128)}, ...), condition=%wide.region_26.27_spmd.clone, body=%wide.region_25.26_spmd.clone.sunk | while | flops 1637877248 | bytes 51989756 | solution.py:58
  1351.0 11.7 bitcast_add_fusion.18
  1373.8 12.0 bitcast_add_fusion.18
  1428.4 76.6 %while.125 = (s32[]{:T(128)}, f32[512,16,64]{0,2,1:T(8,128)}, f32[512,16,64]{0,2,1:T(8,128)}, bf16[1024,1024]{1,0:T(8,128)(2,1)}, s32[1024]{0:T(1024)S(1)}, /*in...) while((s32[]{:T(128)}, f32[512,16,64]{0,2,1:T(8,128)}, ...), condition=%wide.region_28.29_spmd.clone, body=%wide.region_27.28_spmd.clone.sunk | while | flops 2192573952 | bytes 78630144 | solution.py:58
  1452.3 13.9 bitcast_add_fusion.19
  1490.3 14.5 bitcast_add_fusion.19
  1524.0 13.2 convert_reduce_fusion
  1558.0 45.6 %while.126 = (s32[]{:T(128)}, f32[512,16,64]{0,2,1:T(8,128)}, bf16[1024,1024]{0,1:T(8,128)(2,1)S(1)}, s32[1,512]{1,0:T(1,128)S(1)}, s32[1024]{0:T(1024)S(1)}, /*...) while((s32[]{:T(128)}, f32[512,16,64]{0,2,1:T(8,128)}, ...), condition=%wide.region_35.36_spmd.clone, body=%wide.region_34.35_spmd.clone.sunk | while | flops 1637877248 | bytes 51989756 | solution.py:58
  1568.9 11.6 bitcast_add_fusion.21
  1591.6 12.0 bitcast_add_fusion.21
  1690.5 76.7 %while.127 = (s32[]{:T(128)}, f32[512,16,64]{0,2,1:T(8,128)}, f32[512,16,64]{0,2,1:T(8,128)}, bf16[1024,1024]{1,0:T(8,128)(2,1)}, s32[1024]{0:T(1024)S(1)}, /*in...) while((s32[]{:T(128)}, f32[512,16,64]{0,2,1:T(8,128)}, ...), condition=%wide.region_37.38_spmd.clone, body=%wide.region_36.37_spmd.clone.sunk | while | flops 2192573952 | bytes 78630144 | solution.py:58
  1714.5 13.9 bitcast_add_fusion.22
  1752.5 14.5 bitcast_add_fusion.22
  1838.7 17.6 collective-permute-done.96
  1860.4 18.4 collective-permute-done.88
  1900.4 13.0 collective-permute-done.72
  (986 shorter events, 803.4 us)
Async XLA Ops:
  28.8 49.7 %collective-permute-start.27 = (bf16[32,5120]{1,0:T(8,128)(2,1)S(1)}, bf16[32,5120]{1,0:T(8,128)(2,1)}, u32[]{:S(2)}, u32[]{:S(2)}) collective-permute-start(bf16[32,5120]{1,0:T(8,128)(2,1)S(1)} %constant_dynamic-update-slice_fusion.refs_0_), channel_id=1, source_target_pairs={{0,4},{4,8},{8,12},{12,0},{1,5},{5,9},{9,13},{13,1},{2,6},{6,10},{... | collective-permute-start | bytes 983048 | tf_op jit(solution)/shard_map/ppermute | solution.py:91
  71.8 49.9 %collective-permute-start.11 = (bf16[1,4,16,3072]{3,2,1,0:T(8,128)(2,1)}, bf16[1,4,16,3072]{3,2,1,0:T(8,128)(2,1)S(1)}, u32[]{:S(2)}, u32[]{:S(2)}) collective-permute-start(bf16[1,4,16,3072]{3,2,1,0:T(8,128)(2,1)} %get-tuple-element.1496.refs_0_), channel_id=1, source_target_pairs={{0,16},{16,0},{1,17},{17,1},{2,18},{18,2},{3,19},{19,3},{4,20},{20... | collective-permute-start | bytes 1179656 | tf_op jit(solution)/shard_map/ppermute | solution.py:79
  76.5 45.4 %collective-permute-start.12 = (bf16[1,4,16,3072]{3,2,1,0:T(8,128)(2,1)}, bf16[1,4,16,3072]{3,2,1,0:T(8,128)(2,1)S(1)}, u32[]{:S(2)}, u32[]{:S(2)}) collective-permute-start(bf16[1,4,16,3072]{3,2,1,0:T(8,128)(2,1)} %get-tuple-element.1497.refs_1_), channel_id=1, source_target_pairs={{0,2},{2,0},{1,3},{3,1},{4,6},{6,4},{5,7},{7,5},{8,10},{10,8},{9,1... | collective-permute-start | bytes 1179656 | tf_op jit(solution)/shard_map/ppermute | solution.py:79
  119.8 81.1 %collective-permute-start = (bf16[512,1024]{1,0:T(8,128)(2,1)}, bf16[512,1024]{1,0:T(8,128)(2,1)S(1)}, u32[]{:S(2)}, u32[]{:S(2)}) collective-permute-start(bf16[512,1024]{1,0:T(8,128)(2,1)} %bitcast.968), channel_id=1, source_target_pairs={{0,0},{1,16},{16,1},{17,17},{2,2},{3,18},{18,3},{19,19},{4,4},{5,2... | collective-permute-start | bytes 3145736 | tf_op jit(solution)/shard_map/ppermute | solution.py:94
  148.2 53.9 %collective-permute-start.21 = (bf16[1,4,16,3072]{3,2,1,0:T(8,128)(2,1)}, bf16[1,4,16,3072]{3,2,1,0:T(8,128)(2,1)}, u32[]{:S(2)}, u32[]{:S(2)}) collective-permute-start(bf16[1,4,16,3072]{3,2,1,0:T(8,128)(2,1)} %copy-done.98), channel_id=1, source_target_pairs={{0,1},{1,0},{2,3},{3,2},{4,5},{5,4},{6,7},{7,6},{8,9},{9,8},{10,11... | collective-permute-start | bytes 1179656 | tf_op jit(solution)/shard_map/ppermute | solution.py:79
  157.0 45.8 %collective-permute-start.22 = (bf16[1,4,16,3072]{3,2,1,0:T(8,128)(2,1)}, bf16[1,4,16,3072]{3,2,1,0:T(8,128)(2,1)}, u32[]{:S(2)}, u32[]{:S(2)}) collective-permute-start(bf16[1,4,16,3072]{3,2,1,0:T(8,128)(2,1)} %copy-done.99), channel_id=1, source_target_pairs={{0,1},{1,0},{2,3},{3,2},{4,5},{5,4},{6,7},{7,6},{8,9},{9,8},{10,11... | collective-permute-start | bytes 1179656 | tf_op jit(solution)/shard_map/ppermute | solution.py:79
  157.0 47.1 %collective-permute-start.23 = (bf16[1,4,16,3072]{3,2,1,0:T(8,128)(2,1)}, bf16[1,4,16,3072]{3,2,1,0:T(8,128)(2,1)}, u32[]{:S(2)}, u32[]{:S(2)}) collective-permute-start(bf16[1,4,16,3072]{3,2,1,0:T(8,128)(2,1)} %collective-permute-done.15.refs_6_), channel_id=1, source_target_pairs={{0,1},{1,0},{2,3},{3,2},{4,5},{5,4},{6,7},{7,6},{8,9},{9,8},{10,11... | collective-permute-start | bytes 1179656 | tf_op jit(solution)/shard_map/ppermute | solution.py:79
  157.5 46.5 %collective-permute-start.24 = (bf16[1,4,16,3072]{3,2,1,0:T(8,128)(2,1)}, bf16[1,4,16,3072]{3,2,1,0:T(8,128)(2,1)}, u32[]{:S(2)}, u32[]{:S(2)}) collective-permute-start(bf16[1,4,16,3072]{3,2,1,0:T(8,128)(2,1)} %collective-permute-done.16.refs_7_), channel_id=1, source_target_pairs={{0,1},{1,0},{2,3},{3,2},{4,5},{5,4},{6,7},{7,6},{8,9},{9,8},{10,11... | collective-permute-start | bytes 1179656 | tf_op jit(solution)/shard_map/ppermute | solution.py:79
  201.0 199.8 %collective-permute-start.30 = (bf16[1,4,16,5120]{3,2,1,0:T(8,128)(2,1)}, bf16[1,4,16,5120]{3,2,1,0:T(8,128)(2,1)S(1)}, u32[]{:S(2)}, u32[]{:S(2)}) collective-permute-start(bf16[1,4,16,5120]{3,2,1,0:T(8,128)(2,1)} %get-tuple-element.1501.refs_0_), channel_id=1, source_target_pairs={{0,16},{16,0},{1,17},{17,1},{2,18},{18,2},{3,19},{19,3},{4,20},{20... | collective-permute-start | bytes 1966088 | tf_op jit(solution)/shard_map/ppermute | solution.py:79
  202.1 195.7 %collective-permute-start.49 = (bf16[1,4,64,1024]{3,2,1,0:T(8,128)(2,1)}, bf16[1,4,64,1024]{3,2,1,0:T(8,128)(2,1)}, u32[]{:S(2)}, u32[]{:S(2)}) collective-permute-start(bf16[1,4,64,1024]{3,2,1,0:T(8,128)(2,1)} %get-tuple-element.1505.refs_0_), channel_id=1, source_target_pairs={{0,2},{2,0},{1,3},{3,1},{4,6},{6,4},{5,7},{7,5},{8,10},{10,8},{9,1... | collective-permute-start | bytes 1572872 | tf_op jit(solution)/shard_map/ppermute | solution.py:79
  202.8 196.6 %collective-permute-start.50 = (bf16[1,4,64,1024]{3,2,1,0:T(8,128)(2,1)}, bf16[1,4,64,1024]{3,2,1,0:T(8,128)(2,1)}, u32[]{:S(2)}, u32[]{:S(2)}) collective-permute-start(bf16[1,4,64,1024]{3,2,1,0:T(8,128)(2,1)} %get-tuple-element.1506.refs_1_), channel_id=1, source_target_pairs={{0,16},{16,0},{1,17},{17,1},{2,18},{18,2},{3,19},{19,3},{4,20},{20... | collective-permute-start | bytes 1572872 | tf_op jit(solution)/shard_map/ppermute | solution.py:79
  204.1 196.0 %collective-permute-start.53 = (bf16[1,4,64,1024]{3,2,1,0:T(8,128)(2,1)}, bf16[1,4,64,1024]{3,2,1,0:T(8,128)(2,1)}, u32[]{:S(2)}, u32[]{:S(2)}) collective-permute-start(bf16[1,4,64,1024]{3,2,1,0:T(8,128)(2,1)} %get-tuple-element.1505.refs_0_), channel_id=1, source_target_pairs={{0,1},{1,0},{2,3},{3,2},{4,5},{5,4},{6,7},{7,6},{8,9},{9,8},{10,11... | collective-permute-start | bytes 1572872 | tf_op jit(solution)/shard_map/ppermute | solution.py:79
  204.1 196.8 %collective-permute-start.54 = (bf16[1,4,64,1024]{3,2,1,0:T(8,128)(2,1)}, bf16[1,4,64,1024]{3,2,1,0:T(8,128)(2,1)}, u32[]{:S(2)}, u32[]{:S(2)}) collective-permute-start(bf16[1,4,64,1024]{3,2,1,0:T(8,128)(2,1)} %get-tuple-element.1506.refs_1_), channel_id=1, source_target_pairs={{0,1},{1,0},{2,3},{3,2},{4,5},{5,4},{6,7},{7,6},{8,9},{9,8},{10,11... | collective-permute-start | bytes 1572872 | tf_op jit(solution)/shard_map/ppermute | solution.py:79
  434.1 612.6 %collective-permute-start.25 = (bf16[1,512,2048]{2,1,0:T(8,128)(2,1)}, bf16[1,512,2048]{2,1,0:T(8,128)(2,1)}, u32[]{:S(2)}, u32[]{:S(2)}) collective-permute-start(bf16[1,512,2048]{2,1,0:T(8,128)(2,1)} %maximum_bitcast_fusion), channel_id=1, source_target_pairs={{0,1},{1,0},{2,3},{3,2},{4,5},{5,4},{6,7},{7,6},{8,9},{9,8},{10,11... | collective-permute-start | bytes 6291464 | tf_op jit(solution)/shard_map/ppermute | solution.py:79
  462.6 264.1 %collective-permute-start.40 = (bf16[1,4,16,5120]{3,2,1,0:T(8,128)(2,1)}, bf16[1,4,16,5120]{3,2,1,0:T(8,128)(2,1)}, u32[]{:S(2)}, u32[]{:S(2)}) collective-permute-start(bf16[1,4,16,5120]{3,2,1,0:T(8,128)(2,1)} %copy-done.84), channel_id=1, source_target_pairs={{0,1},{1,0},{2,3},{3,2},{4,5},{5,4},{6,7},{7,6},{8,9},{9,8},{10,11... | collective-permute-start | bytes 1966088 | tf_op jit(solution)/shard_map/ppermute | solution.py:79
  463.2 263.6 %collective-permute-start.41 = (bf16[1,4,16,5120]{3,2,1,0:T(8,128)(2,1)}, bf16[1,4,16,5120]{3,2,1,0:T(8,128)(2,1)}, u32[]{:S(2)}, u32[]{:S(2)}) collective-permute-start(bf16[1,4,16,5120]{3,2,1,0:T(8,128)(2,1)} %copy-done.85), channel_id=1, source_target_pairs={{0,1},{1,0},{2,3},{3,2},{4,5},{5,4},{6,7},{7,6},{8,9},{9,8},{10,11... | collective-permute-start | bytes 1966088 | tf_op jit(solution)/shard_map/ppermute | solution.py:79
  464.3 262.5 %collective-permute-start.42 = (bf16[1,4,16,5120]{3,2,1,0:T(8,128)(2,1)}, bf16[1,4,16,5120]{3,2,1,0:T(8,128)(2,1)}, u32[]{:S(2)}, u32[]{:S(2)}) collective-permute-start(bf16[1,4,16,5120]{3,2,1,0:T(8,128)(2,1)} %collective-permute-done.34.refs_6_), channel_id=1, source_target_pairs={{0,1},{1,0},{2,3},{3,2},{4,5},{5,4},{6,7},{7,6},{8,9},{9,8},{10,11... | collective-permute-start | bytes 1966088 | tf_op jit(solution)/shard_map/ppermute | solution.py:79
  465.0 261.8 %collective-permute-start.43 = (bf16[1,4,16,5120]{3,2,1,0:T(8,128)(2,1)}, bf16[1,4,16,5120]{3,2,1,0:T(8,128)(2,1)}, u32[]{:S(2)}, u32[]{:S(2)}) collective-permute-start(bf16[1,4,16,5120]{3,2,1,0:T(8,128)(2,1)} %collective-permute-done.35.refs_7_), channel_id=1, source_target_pairs={{0,1},{1,0},{2,3},{3,2},{4,5},{5,4},{6,7},{7,6},{8,9},{9,8},{10,11... | collective-permute-start | bytes 1966088 | tf_op jit(solution)/shard_map/ppermute | solution.py:79
  1175.8 129.0 %collective-permute-start.65 = (bf16[512,1024]{1,0:T(8,128)(2,1)}, bf16[512,1024]{1,0:T(8,128)(2,1)}, u32[]{:S(2)}, u32[]{:S(2)}) collective-permute-start(bf16[512,1024]{1,0:T(8,128)(2,1)} %bitcast.39), channel_id=1, source_target_pairs={{0,0},{1,16},{16,1},{17,17},{2,2},{3,18},{18,3},{19,19},{4,4},{5,2... | collective-permute-start | bytes 3145736 | tf_op jit(solution)/shard_map/ppermute | solution.py:94
  1185.3 336.0 %collective-permute-start.64 = (bf16[512,1024]{1,0:T(8,128)(2,1)}, bf16[512,1024]{1,0:T(8,128)(2,1)}, u32[]{:S(2)}, u32[]{:S(2)}) collective-permute-start(bf16[512,1024]{1,0:T(8,128)(2,1)} %bitcast.38), channel_id=1, source_target_pairs={{0,0},{1,16},{16,1},{17,17},{2,2},{3,18},{18,3},{19,19},{4,4},{5,2... | collective-permute-start | bytes 3145736 | tf_op jit(solution)/shard_map/ppermute | solution.py:94
  1606.4 58.5 %collective-permute-start.69 = (f32[1,512,32]{1,2,0:T(8,128)S(1)}, f32[1,512,32]{1,2,0:T(8,128)S(1)}, u32[]{:S(2)}, u32[]{:S(2)}) collective-permute-start(f32[1,512,32]{1,2,0:T(8,128)S(1)} %copy-done.129), channel_id=1, source_target_pairs={{0,1},{1,0},{2,3},{3,2},{4,5},{5,4},{6,7},{7,6},{8,9},{9,8},{10,11... | collective-permute-start | bytes 196616 | tf_op jit(solution)/shard_map/ppermute | solution.py:79
  1607.0 74.7 %collective-permute-start.68 = (bf16[1,512,2048]{2,1,0:T(8,128)(2,1)}, bf16[1,512,2048]{2,1,0:T(8,128)(2,1)}, u32[]{:S(2)}, u32[]{:S(2)}) collective-permute-start(bf16[1,512,2048]{2,1,0:T(8,128)(2,1)} %maximum_bitcast_fusion.3), channel_id=1, source_target_pairs={{0,1},{1,0},{2,3},{3,2},{4,5},{5,4},{6,7},{7,6},{8,9},{9,8},{10,11... | collective-permute-start | bytes 6291464 | tf_op jit(solution)/shard_map/ppermute | solution.py:79
  1630.8 184.0 %collective-permute-start.95 = (bf16[1,2,4,2,128,1024]{5,4,3,2,1,0:T(8,128)(2,1)}, bf16[1,2,4,2,128,1024]{5,4,3,2,1,0:T(8,128)(2,1)}, u32[]{:S(2)}, u32[]{:S(2)}) collective-permute-start(bf16[1,2,4,2,128,1024]{5,4,3,2,1,0:T(8,128)(2,1)} %get-tuple-element.2252), channel_id=1, source_target_pairs={{0,1},{1,0},{2,3},{3,2},{4,5},{5,4},{6,7},{7,6},{8,9},{9,8},{10,11... | collective-permute-start | bytes 12582920 | tf_op jit(solution)/shard_map/ppermute | solution.py:79
  1645.2 178.5 %collective-permute-start.87 = (bf16[1,2,4,2,32,4096]{5,4,3,2,1,0:T(8,128)(2,1)}, bf16[1,2,4,2,32,4096]{5,4,3,2,1,0:T(8,128)(2,1)}, u32[]{:S(2)}, u32[]{:S(2)}) collective-permute-start(bf16[1,2,4,2,32,4096]{5,4,3,2,1,0:T(8,128)(2,1)} %get-tuple-element.2254), channel_id=1, source_target_pairs={{0,1},{1,0},{2,3},{3,2},{4,5},{5,4},{6,7},{7,6},{8,9},{9,8},{10,11... | collective-permute-start | bytes 12582920 | tf_op jit(solution)/shard_map/ppermute | solution.py:79
  1679.9 109.6 %collective-permute-start.84 = (bf16[32,1024]{1,0:T(8,128)(2,1)}, bf16[32,1024]{1,0:T(8,128)(2,1)}, u32[]{:S(2)}, u32[]{:S(2)}) collective-permute-start(bf16[32,1024]{1,0:T(8,128)(2,1)} %pad_maximum_fusion.21), channel_id=1, source_target_pairs={{0,4},{4,8},{8,12},{12,0},{1,5},{5,9},{9,13},{13,1},{2,6},{6,10},{... | collective-permute-start | bytes 196616 | tf_op jit(solution)/shard_map/ppermute | solution.py:91
  1680.5 109.0 %collective-permute-start.85 = (bf16[32,1024]{1,0:T(8,128)(2,1)}, bf16[32,1024]{1,0:T(8,128)(2,1)}, u32[]{:S(2)}, u32[]{:S(2)}) collective-permute-start(bf16[32,1024]{1,0:T(8,128)(2,1)} %pad_maximum_fusion.22), channel_id=1, source_target_pairs={{0,8},{4,12},{8,0},{12,4},{1,9},{5,13},{9,1},{13,5},{2,10},{6,14},... | collective-permute-start | bytes 196616 | tf_op jit(solution)/shard_map/ppermute | solution.py:91
  1681.7 107.8 %collective-permute-start.86 = (bf16[32,1024]{1,0:T(8,128)(2,1)}, bf16[32,1024]{1,0:T(8,128)(2,1)}, u32[]{:S(2)}, u32[]{:S(2)}) collective-permute-start(bf16[32,1024]{1,0:T(8,128)(2,1)} %pad_maximum_fusion.23), channel_id=1, source_target_pairs={{0,12},{4,0},{8,4},{12,8},{1,13},{5,1},{9,5},{13,9},{2,14},{6,2},{... | collective-permute-start | bytes 196616 | tf_op jit(solution)/shard_map/ppermute | solution.py:91
  1811.3 69.9 %collective-permute-start.71 = (bf16[1,2,4,2,32,3072]{5,4,3,2,1,0:T(8,128)(2,1)}, bf16[1,2,4,2,32,3072]{5,4,3,2,1,0:T(8,128)(2,1)}, u32[]{:S(2)}, u32[]{:S(2)}) collective-permute-start(bf16[1,2,4,2,32,3072]{5,4,3,2,1,0:T(8,128)(2,1)} %get-tuple-element.2256), channel_id=1, source_target_pairs={{0,1},{1,0},{2,3},{3,2},{4,5},{5,4},{6,7},{7,6},{8,9},{9,8},{10,11... | collective-permute-start | bytes 9437192 | tf_op jit(solution)/shard_map/ppermute | solution.py:79
  1827.7 51.0 %collective-permute-start.88 = (bf16[1,4,2,16,4096]{4,3,2,1,0:T(8,128)(2,1)}, bf16[1,4,2,16,4096]{4,3,2,1,0:T(8,128)(2,1)}, u32[]{:S(2)}, u32[]{:S(2)}) collective-permute-start(bf16[1,4,2,16,4096]{4,3,2,1,0:T(8,128)(2,1)} %fusion.100), channel_id=1, source_target_pairs={{0,16},{16,0},{1,17},{17,1},{2,18},{18,2},{3,19},{19,3},{4,20},{20... | collective-permute-start | bytes 3145736 | tf_op jit(solution)/shard_map/ppermute | solution.py:79
  1831.8 49.1 %collective-permute-start.90 = (bf16[1,2,4,16,4096]{4,3,2,1,0:T(8,128)(2,1)}, bf16[1,2,4,16,4096]{4,3,2,1,0:T(8,128)(2,1)S(1)}, u32[]{:S(2)}, u32[]{:S(2)}) collective-permute-start(bf16[1,2,4,16,4096]{4,3,2,1,0:T(8,128)(2,1)} %fusion.101), channel_id=1, source_target_pairs={{0,2},{2,0},{1,3},{3,1},{4,6},{6,4},{5,7},{7,5},{8,10},{10,8},{9,1... | collective-permute-start | bytes 3145736 | tf_op jit(solution)/shard_map/ppermute | solution.py:79
  1890.7 62.6 %collective-permute-start.100 = (bf16[128,1024]{1,0:T(8,128)(2,1)S(1)}, bf16[128,1024]{1,0:T(8,128)(2,1)S(1)}, u32[]{:S(2)}, u32[]{:S(2)}) collective-permute-start(bf16[128,1024]{1,0:T(8,128)(2,1)S(1)} %pad_maximum_fusion.13), channel_id=1, source_target_pairs={{0,4},{4,8},{8,12},{12,0},{1,5},{5,9},{9,13},{13,1},{2,6},{6,10},{... | collective-permute-start | bytes 786440 | tf_op jit(solution)/shard_map/ppermute | solution.py:91
  1894.9 58.4 %collective-permute-start.101 = (bf16[128,1024]{1,0:T(8,128)(2,1)S(1)}, bf16[128,1024]{1,0:T(8,128)(2,1)S(1)}, u32[]{:S(2)}, u32[]{:S(2)}) collective-permute-start(bf16[128,1024]{1,0:T(8,128)(2,1)S(1)} %pad_maximum_fusion.14), channel_id=1, source_target_pairs={{0,8},{4,12},{8,0},{12,4},{1,9},{5,13},{9,1},{13,5},{2,10},{6,14},... | collective-permute-start | bytes 786440 | tf_op jit(solution)/shard_map/ppermute | solution.py:91
  (267 other events, 9013.1 us)

commit v2 on v1

v2 whole, which is shorter than its diff:
```python
from functools import partial
import math

import jax
import jax.numpy as jnp
import numpy as np
from jax import lax
from jax.experimental import pallas as pl
from jax.experimental.pallas import tpu as pltpu
from jax.sharding import Mesh, PartitionSpec as P

HEAD = 64
PAIR = 2 * HEAD
SCALE = 0.125
EPSILON = 1e-06
NEGATIVE = -1e30
ACROSS = (((0,), (0,)), ((), ()))
WITHIN = (((1,), (1,)), ((), ()))
BF = jnp.bfloat16
F32 = jnp.float32


def layer_norm(tensor, gain_row, shift_row):
    average = jnp.mean(tensor, axis=-1, keepdims=True)
    centred = tensor - average
    variance = jnp.mean(centred * centred, axis=-1, keepdims=True)
    return centred * lax.rsqrt(variance + EPSILON) * gain_row + shift_row


def product(left_side, right_side):
    return jnp.dot(left_side, right_side, preferred_element_type=F32)


def outer_sum(left_side, right_side):
    return lax.dot_general(left_side, right_side, ACROSS, preferred_element_type=F32)


def back_product(left_side, right_side):
    return lax.dot_general(left_side, right_side, WITHIN, preferred_element_type=F32)


def fill_bias(bias_ref, query_seg, query_pos, key_seg, key_open, key_pos):
    allowed = (key_seg == query_seg) & ((key_open == 1) | (key_pos == query_pos))
    bias_ref[...] = jnp.where(allowed, 0.0, NEGATIVE)


def half_lanes(tensor, side):
    lane = lax.broadcasted_iota(jnp.int32, tensor.shape, 1)
    return jnp.where((lane < HEAD) == (side == 0), tensor, jnp.zeros((), tensor.dtype))


def attention_forward(query, keys, values, query_labels, key_labels):
    tokens, model = query.shape
    every = keys.shape[0]
    pairs = model // PAIR
    step = math.gcd(tokens, 256)

    def kernel(q_ref, k_ref, v_ref, ql_ref, kl_ref, attn_ref, lse_ref, bias_ref):
        @pl.when(pl.program_id(0) == 0)
        def _():
            fill_bias(
                bias_ref, ql_ref[:, 0:1], ql_ref[:, 1:2], kl_ref[0:1], kl_ref[1:2], kl_ref[2:3]
            )

        keys_pair, values_pair = k_ref[...], v_ref[...]
        for start in range(0, tokens, step):
            query_pair = q_ref[start : start + step, :]
            sides = []
            for side in range(2):
                logits = back_product(half_lanes(query_pair, side), keys_pair)
                logits = logits + bias_ref[start : start + step, :]
                highest = jnp.max(logits, axis=1, keepdims=True)
                weights = jnp.exp(logits - highest)
                denominator = jnp.sum(weights, axis=1, keepdims=True)
                across = jnp.broadcast_to(highest + jnp.log(denominator), (step, PAIR)).T
                lse_ref[0, side : side + 1, start : start + step] = across[0:1]
                sides.append(product(weights.astype(BF), values_pair) / denominator)
            lane = lax.broadcasted_iota(jnp.int32, (step, PAIR), 1)
            attn_ref[start : start + step, :] = jnp.where(lane < HEAD, sides[0], sides[1])

    work = 2 * tokens * every * model
    return pl.pallas_call(
        kernel,
        grid=(pairs,),
        in_specs=[
            pl.BlockSpec((tokens, PAIR), lambda i: (0, i)),
            pl.BlockSpec((every, PAIR), lambda i: (0, i)),
            pl.BlockSpec((every, PAIR), lambda i: (0, i)),
            pl.BlockSpec(query_labels.shape, lambda i: (0, 0)),
            pl.BlockSpec(key_labels.shape, lambda i: (0, 0)),
        ],
        out_specs=[
            pl.BlockSpec((tokens, PAIR), lambda i: (0, i)),
            pl.BlockSpec((1, 2, tokens), lambda i: (i, 0, 0)),
        ],
        out_shape=[
            jax.ShapeDtypeStruct((tokens, model), F32),
            jax.ShapeDtypeStruct((pairs, 2, tokens), F32),
        ],
        scratch_shapes=[pltpu.VMEM((tokens, every), F32)],
        compiler_params=pltpu.CompilerParams(
            dimension_semantics=("arbitrary",), vmem_limit_bytes=48 << 20
        ),
        cost_estimate=pl.CostEstimate(
            flops=2 * work, transcendentals=work // PAIR, bytes_accessed=10 * every * model
        ),
        name="attention_forward",
    )(query, keys, values, query_labels, key_labels)


def attention_backward(query, keys, values, grad, attn, lse, query_labels, key_labels, first, pairs):
    tokens = query.shape[0]
    every = keys.shape[0]
    model = pairs * PAIR
    step = math.gcd(every, 256)

    def kernel(q_ref, k_ref, v_ref, g_ref, a_ref, lse_ref, ql_ref, kl_ref, dq_ref, dk_ref, dv_ref, bias_ref):
        @pl.when(pl.program_id(0) == 0)
        def _():
            fill_bias(
                bias_ref, ql_ref[0:1], ql_ref[1:2], kl_ref[:, 0:1], kl_ref[:, 1:2], kl_ref[:, 2:3]
            )

        query_pair, grad_pair = q_ref[...], g_ref[...]
        overlap = (grad_pair.astype(F32) * a_ref[...].astype(F32)).T
        deltas = [
            jnp.sum(overlap[side * HEAD : (side + 1) * HEAD], axis=0, keepdims=True)
            for side in range(2)
        ]
        keys_across = k_ref[...].astype(F32).T.astype(BF)
        query_sides = [half_lanes(query_pair, side) for side in range(2)]
        grad_sides = [half_lanes(grad_pair, side) for side in range(2)]
        grad_query = [jnp.zeros((HEAD, tokens), F32), jnp.zeros((HEAD, tokens), F32)]
        for start in range(0, every, step):
            keys_pair, values_pair = k_ref[start : start + step, :], v_ref[start : start + step, :]
            grad_keys, grad_values = [], []
            for side in range(2):
                logits = back_product(keys_pair, query_sides[side])
                logits = logits + bias_ref[start : start + step, :]
                probs = jnp.exp(logits - lse_ref[0, side : side + 1, :])
                grad_probs = back_product(values_pair, grad_sides[side])
                grad_logits = (probs * (grad_probs - deltas[side])).astype(BF)
                grad_values.append(product(probs.astype(BF), grad_sides[side]))
                grad_keys.append(product(grad_logits, query_sides[side]))
                grad_query[side] = grad_query[side] + product(
                    keys_across[side * HEAD : (side + 1) * HEAD, start : start + step], grad_logits
                )
            dk_ref[start : start + step, :] = (grad_keys[0] + grad_keys[1]).astype(BF)
            dv_ref[start : start + step, :] = (grad_values[0] + grad_values[1]).astype(BF)
        dq_ref[...] = (jnp.concatenate(grad_query, axis=0).T * SCALE).astype(BF)

    work = 2 * tokens * every * model
    own, own_out = (
        pl.BlockSpec((tokens, PAIR), lambda i: (0, i + first)),
        pl.BlockSpec((tokens, PAIR), lambda i: (0, i)),
    )
    whole, whole_out = (
        pl.BlockSpec((every, PAIR), lambda i: (0, i + first)),
        pl.BlockSpec((every, PAIR), lambda i: (0, i)),
    )
    return pl.pallas_call(
        kernel,
        grid=(pairs,),
        in_specs=[
            own,
            whole,
            whole,
            own,
            own,
            pl.BlockSpec((1, 2, tokens), lambda i: (i + first, 0, 0)),
            pl.BlockSpec(query_labels.shape, lambda i: (0, 0)),
            pl.BlockSpec(key_labels.shape, lambda i: (0, 0)),
        ],
        out_specs=[own_out, whole_out, whole_out],
        out_shape=[
            jax.ShapeDtypeStruct((tokens, model), BF),
            jax.ShapeDtypeStruct((every, model), BF),
            jax.ShapeDtypeStruct((every, model), BF),
        ],
        scratch_shapes=[pltpu.VMEM((every, tokens), F32)],
        compiler_params=pltpu.CompilerParams(
            dimension_semantics=("arbitrary",), vmem_limit_bytes=48 << 20
        ),
        cost_estimate=pl.CostEstimate(
            flops=5 * work, transcendentals=work // PAIR, bytes_accessed=12 * every * model
        ),
        name="attention_backward",
    )(query, keys, values, grad, attn, lse, query_labels, key_labels)


class Grid:
    def __init__(self, sizes):
        self.size = dict(sizes)
        self.at = {name: lax.axis_index(name) for name in sizes}
        self.places = jnp.stack([self.at[name] for name in sizes]).astype(jnp.int32)
        self.shards = math.prod(sizes.values())
        index = 0
        for name in sizes:
            index = index * sizes[name] + self.at[name]
        self.shard = index

    def shift(self, tensor, axis, step):
        n = self.size[axis]
        return lax.ppermute(tensor, axis, [(i, (i + step) % n) for i in range(n)])

    def far_steps(self):
        return [(a, b) for a in range(self.size["h"]) for b in range(self.size["z"])]

    def far_shift(self, tensor, step):
        high, deep = self.size["h"], self.size["z"]
        pairs = [
            (a * deep + b, ((a + step[0]) % high) * deep + (b + step[1]) % deep)
            for a in range(high)
            for b in range(deep)
        ]
        return lax.ppermute(tensor, ("h", "z"), pairs)

    def swap(self, tensor):
        return lax.ppermute(tensor, ("x", "c"), [(0, 0), (1, 2), (2, 1), (3, 3)])

    def rows(self, tensor):
        if self.size["h"] > 1:
            tensor = lax.all_gather(tensor, "h", axis=0, tiled=False)
        else:
            tensor = tensor[None]
        other = self.shift(tensor, "c", 1)
        first = self.at["c"] == 0
        both = jnp.stack([jnp.where(first, tensor, other), jnp.where(first, other, tensor)], axis=1)
        return both.reshape((-1,) + tensor.shape[2:])


def place(places, pieces, out_shapes, moves):
    count = len(pieces)
    landed = [pltpu.VMEM(piece.shape, piece.dtype) for piece in pieces]

    def kernel(at_ref, *refs):
        ins, outs = refs[:count], refs[count : count + len(out_shapes)]
        held, load_sems, store_sems = refs[-2 - count : -2], refs[-2], refs[-1]
        loads = [
            pltpu.make_async_copy(source, target, load_sems.at[i])
            for i, (source, target) in enumerate(zip(ins, held))
        ]
        for load in loads:
            load.start()
        stores = []
        ready = -1
        for piece, source, target in moves(at_ref, held, outs):
            while ready < piece:
                ready += 1
                loads[ready].wait()
            store = pltpu.make_async_copy(source, target, store_sems.at[len(stores)])
            store.start()
            stores.append(store)
        for store in stores:
            store.wait()

    moved = sum(math.prod(s.shape) * 2 for s in out_shapes)
    return pl.pallas_call(
        kernel,
        out_shape=out_shapes,
        in_specs=[pl.BlockSpec(memory_space=pltpu.SMEM)]
        + [pl.BlockSpec(memory_space=pl.ANY)] * count,
        out_specs=[pl.BlockSpec(memory_space=pl.ANY)] * len(out_shapes),
        scratch_shapes=landed
        + [pltpu.SemaphoreType.DMA((count,)), pltpu.SemaphoreType.DMA((2 * count,))],
        compiler_params=pltpu.CompilerParams(vmem_limit_bytes=moved + (4 << 20)),
        cost_estimate=pl.CostEstimate(flops=0, transcendentals=0, bytes_accessed=2 * moved),
        name="place",
    )(places, *pieces)


def gather_weights(grid, shard, widths):
    high, wide, deep, tall = (grid.size[name] for name in "hxzy")
    rows, columns = shard.shape
    half = rows // 2
    steps = grid.far_steps()
    pieces = [shard if step == (0, 0) else grid.far_shift(shard, step) for step in steps]

    def far_moves(at, ins, outs):
        listed = []
        for i, (step, ref) in enumerate(zip(steps, ins)):
            a = lax.rem(at[0] - step[0] + high, high)
            b = lax.rem(at[2] - step[1] + deep, deep)
            for colour in range(2):
                listed.append((i, ref.at[pl.ds(colour * half, half)], outs[colour].at[a, b]))
        return listed

    lines = place(
        grid.places,
        pieces,
        [jax.ShapeDtypeStruct((high, deep, half, columns), shard.dtype)] * 2,
        far_moves,
    )
    tagged = []
    first_a = [grid.shift(lines[0], "x", k) for k in range(1, wide)]
    first_b = [grid.shift(lines[1], "y", k) for k in range(1, tall)]
    tagged.append((lines[0], 0, 0, 0))
    tagged.append((lines[1], 0, 0, 1))
    tagged += [(t, k + 1, 0, 0) for k, t in enumerate(first_a)]
    tagged += [(t, 0, k + 1, 1) for k, t in enumerate(first_b)]
    held_a = [(lines[0], 0)] + [(t, k + 1) for k, t in enumerate(first_a)]
    held_b = [(lines[1], 0)] + [(t, k + 1) for k, t in enumerate(first_b)]
    for (ta, ka), (tb, kb) in zip(held_a, held_b):
        tagged += [(grid.shift(ta, "y", k), ka, k, 0) for k in range(1, tall)]
        tagged += [(grid.shift(tb, "x", k), k, kb, 1) for k in range(1, wide)]
    if len(held_b) > len(held_a):
        for tb, kb in held_b[len(held_a) :]:
            tagged += [(grid.shift(tb, "x", k), k, kb, 1) for k in range(1, wide)]
    pairs = [t + (0,) for t in tagged] + [(grid.shift(t[0], "c", 1),) + t[1:] + (1,) for t in tagged]
    offsets = [sum(widths[:i]) for i in range(len(widths))]

    def last_moves(at, ins, outs):
        listed = []
        for i, (ref, (_, kx, ky, colour, kc)) in enumerate(zip(ins, pairs)):
            px = lax.rem(at[1] - kx + wide, wide)
            py = lax.rem(at[3] - ky + tall, tall)
            pc = lax.rem(at[4] - kc + 2, 2)
            for out, offset, width in zip(outs, offsets, widths):
                listed.append(
                    (
                        i,
                        ref.at[:, :, :, pl.ds(offset, width)],
                        out.at[:, px, :, py, pc, pl.ds(colour * half, half)],
                    )
                )
        return listed

    full = place(
        grid.places,
        [t[0] for t in pairs],
        [
            jax.ShapeDtypeStruct((high, wide, deep, tall, 2, rows, width), shard.dtype)
            for width in widths
        ],
        last_moves,
    )
    return [t.reshape(-1, width) for t, width in zip(full, widths)]


def pick(tensor, index, axis):
    return lax.dynamic_index_in_dim(tensor, index, axis, keepdims=False)


def total(parts):
    result = parts[0].astype(F32)
    for part in parts[1:]:
        result = result + part.astype(F32)
    return result


class Scatter:
    def __init__(self, grid, term):
        self.grid = grid
        sizes = [grid.size[name] for name in "hxzy"]
        rows, columns = term.shape[0] // grid.shards, term.shape[1]
        half = rows // 2
        self.cuts = (slice(0, half), slice(half, rows))
        view = term.reshape(*sizes, 2, rows, columns)
        self.held = [[pick(view, grid.at["c"], 4)[..., cut, :]] for cut in self.cuts]
        self.sends = [pick(view, 1 - grid.at["c"], 4)]
        self.axes = [list("hxzy"), list("hxzy")]
        self.stage = 0

    def go(self):
        if self.stage == 0:
            self.arrived = [self.grid.shift(self.sends[0], "c", 1)]
        elif self.stage < 3:
            self.arrived = [self.grid.shift(t, *route) for t, route in zip(self.sends, self.routes)]
        else:
            self.arrived = [self.grid.far_shift(t, route) for t, route in zip(self.sends, self.routes)]

    def prepare(self):
        grid = self.grid
        for i, cut in enumerate(self.cuts):
            if self.stage == 0:
                self.held[i].append(self.arrived[0][..., cut, :])
            else:
                self.held[i] += [t for t, owner in zip(self.arrived, self.owners) if owner == i]
        self.stage += 1
        if self.stage == 3:
            self.routes = [step for step in grid.far_steps() if step != (0, 0)]
            self.sends = [self.at_far(step).astype(BF) for step in self.routes]
            return
        self.sends, self.routes, self.owners = [], [], []
        for i, order in enumerate(("xy", "yx")):
            name = order[self.stage - 1]
            n, own, axis = grid.size[name], grid.at[name], self.axes[i].index(name)
            for k in range(1, n):
                parts = [pick(t, lax.rem(own + k, n), axis) for t in self.held[i]]
                self.sends.append(total(parts).astype(BF))
                self.routes.append((name, k))
                self.owners.append(i)
            self.held[i] = [pick(t, own, axis) for t in self.held[i]]
            self.axes[i].remove(name)

    def at_far(self, step):
        a = lax.rem(self.grid.at["h"] + step[0], self.grid.size["h"])
        b = lax.rem(self.grid.at["z"] + step[1], self.grid.size["z"])
        return jnp.concatenate(
            [total([pick(pick(t, a, 0), b, 0) for t in held]) for held in self.held], axis=0
        )

    def result(self):
        return total([self.at_far((0, 0))] + self.arrived)


def order(values, sent=(), got=()):
    values, sends, arrived = lax.optimization_barrier(
        (values, [s.sends for s in sent], [s.arrived for s in got])
    )
    for scatter, arrays in zip(sent, sends):
        scatter.sends = arrays
    for scatter, arrays in zip(got, arrived):
        scatter.arrived = arrays
    return values


def everywhere(grid, tensor):
    for name in "cxy":
        tensor = total([tensor] + [grid.shift(tensor, name, k) for k in range(1, grid.size[name])]).astype(
            tensor.dtype
        )
    return total(
        [tensor] + [grid.far_shift(tensor, s) for s in grid.far_steps() if s != (0, 0)]
    ).astype(tensor.dtype)


def body(
    sizes,
    inputs,
    segment_ids,
    key_mask,
    lead_index,
    cotangent_first,
    cotangent_second,
    w_qkv,
    w_out,
    w_up,
    w_down,
    biases,
    up_bias,
    norm_gains,
    norm_shifts,
    lead_table,
):
    grid = Grid(sizes)
    tokens, model = inputs.shape[1], inputs.shape[2]
    shards = grid.shards
    share = model // shards

    small = jnp.concatenate(
        [t.reshape(-1) for t in (biases, up_bias, norm_gains, norm_shifts, lead_table)]
    )
    mine = jnp.arange(shards, dtype=jnp.int32)[:, None] == grid.shard
    small = everywhere(grid, jnp.where(mine, small[None, :], jnp.zeros((), BF)))
    lengths = [t.shape[0] for t in (biases, norm_gains, norm_shifts, lead_table)]

    def unpack(start, count):
        block = small[:, start : start + count * share].reshape(shards, count, share)
        return block.transpose(1, 0, 2).reshape(count, model).astype(F32)

    own_up = up_bias.shape[0]
    bias_full = unpack(0, lengths[0])
    bias_up = small[:, lengths[0] * share : lengths[0] * share + own_up].reshape(-1).astype(F32)
    begin = lengths[0] * share + own_up
    gains = unpack(begin, lengths[1])
    shifts = unpack(begin + lengths[1] * share, lengths[2])
    lead_rows = unpack(begin + (lengths[1] + lengths[2]) * share, lengths[3])

    labels = grid.swap(
        jnp.concatenate([segment_ids, key_mask, jnp.broadcast_to(lead_index.reshape(2, 1), (2, tokens))])
    )
    own_seg, own_open = labels[0], labels[1]
    leads = (labels[2, 0], labels[3, 0])
    start_low = grid.swap(inputs[0])
    seed_first = grid.swap(cotangent_first[0])
    seed_second = grid.swap(cotangent_second[0])
    every = grid.rows(labels[:2].T)
    all_seg, all_open = every[:, 0], every[:, 1]
    own_pos = (grid.at["h"] * 2 + grid.at["c"]) * tokens + jnp.arange(tokens, dtype=jnp.int32)

    (weight_qkv,) = gather_weights(grid, w_qkv, [w_qkv.shape[1]])
    weight_up, weight_out = gather_weights(
        grid, jnp.concatenate([w_up, w_out], axis=1), [w_up.shape[1], w_out.shape[1]]
    )
    (weight_down,) = gather_weights(grid, w_down, [w_down.shape[1]])

    query_labels = jnp.stack([own_seg, own_pos])
    query_labels_across = query_labels.T
    all_pos = jnp.arange(all_seg.shape[0], dtype=jnp.int32)
    key_labels = jnp.stack([all_seg, all_open, all_pos])
    key_labels_across = key_labels.T
    high = grid.size["h"]

    def forward(start_in, lead_id):
        chooser = (jnp.arange(lead_rows.shape[0], dtype=jnp.int32) == lead_id).astype(F32)
        lead_vec = jnp.sum(chooser[:, None] * lead_rows, axis=0)
        hidden = start_in + lead_vec[None, :]
        normed = layer_norm(hidden, gains[0], shifts[0]).astype(BF)
        mixed = product(normed, weight_qkv)
        query = (mixed[:, :model] + bias_full[0]).astype(BF) * jnp.asarray(SCALE, BF)
        keys = mixed[:, model : 2 * model].astype(BF)
        values = (mixed[:, 2 * model :] + bias_full[1]).astype(BF)
        every_key, every_value = grid.rows(keys), grid.rows(values)
        attn, lse = attention_forward(query, every_key, every_value, query_labels_across, key_labels)
        attn_low = attn.astype(BF)
        middle = hidden + product(attn_low, weight_out) + bias_full[2]
        normed_mid = layer_norm(middle, gains[1], shifts[1]).astype(BF)
        gate_in = product(normed_mid, weight_up) + bias_up
        activated = jax.nn.gelu(gate_in, approximate=False).astype(BF)
        result = middle + product(activated, weight_down) + bias_full[3]
        saved = (
            hidden, normed, query, every_key, every_value, lse, attn, attn_low, middle,
            normed_mid, gate_in, activated, chooser,
        )
        return (result, saved)

    def backward(saved, grad_res, earlier):
        (
            hidden, normed, query, every_key, every_value, lse, attn, attn_low, middle,
            normed_mid, gate_in, activated, chooser,
        ) = saved
        last = earlier is not None
        kinds = ("down", "up", "out", "qkv0", "qkv1")
        sums = {}

        def join(name, left_side, right_side):
            term = outer_sum(left_side, right_side)
            if last:
                term = earlier[name].astype(F32) + term
            sums[name] = Scatter(grid, term.astype(BF)) if last else term.astype(BF)

        def then(values, sent=(), got=()):
            if not last:
                return values
            values = order(values, [sums[name] for name in sent], [sums[name] for name in got])
            for name in sent:
                sums[name].go()
            return values

        def prepare(*names):
            if last:
                for name in names:
                    sums[name].prepare()

        grad_low = grad_res.astype(BF)
        join("down", activated, grad_low)
        grad_low = then(grad_low, sent=["down"])
        bias_down = jnp.sum(grad_low.astype(F32), axis=0)
        gate_pull = jax.vjp(partial(jax.nn.gelu, approximate=False), gate_in)[1]
        grad_gate = gate_pull(back_product(grad_low, weight_down))[0].astype(BF)
        grad_gate = then(grad_gate, got=["down"])
        prepare("down")
        grad_gate = then(grad_gate, sent=["down"])
        join("up", normed_mid, grad_gate)
        grad_gate = then(grad_gate, sent=["up"])
        bias_gate = jnp.sum(grad_gate.astype(F32), axis=0)
        mid_pull = jax.vjp(layer_norm, middle, gains[1], shifts[1])[1]
        grad_mid_part, gain_mid, shift_mid = mid_pull(back_product(grad_gate, weight_up))
        grad_mid = grad_res + grad_mid_part
        grad_mid = then(grad_mid, got=["up", "down"])
        prepare("down", "up")
        grad_mid = then(grad_mid, sent=["down", "up"])
        grad_branch = grad_mid.astype(BF)
        grad_attn = back_product(grad_branch, weight_out).astype(BF)
        bias_attn = jnp.sum(grad_branch.astype(F32), axis=0)
        pairs = model // PAIR
        cuts = (0, pairs // 2, pairs)
        mixed_parts, back_parts = [], []
        for half in range(2):
            first, count = cuts[half], cuts[half + 1] - cuts[half]
            query_low, partial_keys, partial_values = attention_backward(
                query, every_key, every_value, grad_attn, attn, lse, query_labels, key_labels_across,
                first, count,
            )
            width = count * PAIR
            partial_both = jnp.stack([partial_keys, partial_values]).reshape(2, high, 2, tokens, width)
            sent = pick(partial_both, 1 - grid.at["c"], 2)
            if half == 0:
                sent = then(sent, got=["down", "up"])
                prepare("down", "up")
                sent = then(sent, sent=["down", "up"])
                join("out", attn_low, grad_branch)
                sent, grad_attn = then((sent, grad_attn), sent=["out"])
            else:
                sent = then(sent, got=["qkv0", "down", "up", "out"])
                prepare("qkv0", "up", "out")
                sent = then(sent, sent=["qkv0", "up", "out"])
            both = total([pick(partial_both, grid.at["c"], 2), grid.shift(sent, "c", 1)])
            if high > 1:
                both = lax.psum_scatter(both.astype(BF), "h", scatter_dimension=1, tiled=False)
            else:
                both = both[:, 0]
            both = both.astype(BF)
            query_low = (query_low.astype(F32)).astype(BF)
            mixed = jnp.concatenate([query_low, both[0], both[1]], axis=1)
            join(f"qkv{half}", normed, mixed)
            if half == 0:
                grad_attn, mixed = then((grad_attn, mixed), sent=["qkv0"])
            else:
                mixed = then(mixed, sent=["qkv1"])
            mixed_parts.append(mixed)
        if last:
            mixed_parts[1] = then(mixed_parts[1], got=["qkv1", "qkv0", "out"])
            prepare("qkv1", "qkv0", "out")
            mixed_parts[1] = then(mixed_parts[1], sent=["qkv1", "qkv0", "out"])
        grad_mixed = jnp.concatenate(
            [p[:, i * p.shape[1] // 3 : (i + 1) * p.shape[1] // 3] for i in range(3) for p in mixed_parts],
            axis=1,
        )
        bias_query = jnp.sum(grad_mixed[:, :model].astype(F32), axis=0)
        bias_value = jnp.sum(grad_mixed[:, 2 * model :].astype(F32), axis=0)
        in_pull = jax.vjp(layer_norm, hidden, gains[0], shifts[0])[1]
        grad_in_part, gain_in, shift_in = in_pull(back_product(grad_mixed, weight_qkv))
        grad_start = grad_mid + grad_in_part
        lead_sum = jnp.sum(grad_start, axis=0)
        term_lead = chooser[:, None] * lead_sum[None, :]
        vectors = (
            jnp.stack([bias_query, bias_value, bias_attn, bias_down]),
            bias_gate,
            jnp.stack([gain_in, gain_mid]),
            jnp.stack([shift_in, shift_mid]),
            term_lead,
        )
        return (grad_start, sums, vectors)

    result_first, saved_first = forward(start_low.astype(F32), leads[0])
    first_low = result_first.astype(BF)
    result_second, saved_second = forward(first_low.astype(F32), leads[1])
    second_low = result_second.astype(BF)
    grad_between, terms_second, vectors_second = backward(saved_second, seed_second.astype(F32), None)
    grad_first, sums, vectors_first = backward(
        saved_first, seed_first.astype(F32) + grad_between, terms_second
    )
    shares = {}
    for name, scatter in sums.items():
        while scatter.stage < 3:
            scatter.prepare()
            scatter.go()
        shares[name] = scatter.result()
    width = shares["qkv0"].shape[1] // 3
    shares["qkv"] = jnp.concatenate(
        [shares[f"qkv{half}"][:, i * width : (i + 1) * width] for i in range(3) for half in range(2)],
        axis=1,
    )
    vectors = [a + b for a, b in zip(vectors_second, vectors_first)]

    def pack(block):
        return block.reshape(-1, shards, share).transpose(1, 0, 2).reshape(shards, -1)

    packed = jnp.concatenate(
        [
            pack(vectors[0]),
            vectors[1].reshape(shards, -1),
            pack(vectors[2]),
            pack(vectors[3]),
            pack(vectors[4]),
        ],
        axis=1,
    )
    own_row = pick(everywhere(grid, packed), grid.shard, 0)
    cuts = np.cumsum([lengths[0] * share, own_up, lengths[1] * share, lengths[2] * share])
    small_out = jnp.split(own_row, [int(cut) for cut in cuts])
    return (
        grid.swap(first_low)[None],
        grid.swap(second_low)[None],
        grid.swap(grad_first.astype(BF)).astype(F32)[None],
        shares["qkv"],
        shares["out"],
        shares["up"],
        shares["down"],
        small_out[0].reshape(lengths[0], share),
        small_out[1],
        small_out[2].reshape(lengths[1], share),
        small_out[3].reshape(lengths[2], share),
        small_out[4].reshape(lengths[3], share),
    )


def solution(mesh):
    dp, fsdp = mesh.shape["dp"], mesh.shape["fsdp"]
    tall = fsdp // 8
    sizes = {"h": dp // 2, "x": 2, "z": 4, "y": tall, "c": 2}
    fine = Mesh(np.asarray(mesh.devices).reshape(tuple(sizes.values())), tuple(sizes))
    one, two, every = ("z", "y", "c"), ("h", "x"), ("h", "x", "z", "y", "c")
    placed = (
        P(one, two, None),
        P(one, two),
        P(one, two),
        P(one, None),
        P(one, two, None),
        P(one, two, None),
        P(every, None),
        P(every, None),
        P(every, None),
        P(every, None),
        P(None, every),
        P(every),
        P(None, every),
        P(None, every),
        P(None, every),
    )
    return jax.shard_map(
        partial(body, sizes),
        mesh=fine,
        in_specs=placed,
        out_specs=(
            P(one, two, None),
            P(one, two, None),
            P(one, two, None),
            P(every, None),
            P(every, None),
            P(every, None),
            P(every, None),
            P(None, every),
            P(every),
            P(None, every),
            P(None, every),
            P(None, every),
        ),
        check_vma=False,
    )
```

time: 1980 us -> 895 us (0.45)
  Pallas kernels: 870 us -> 123 us
  matrix products: 485 us -> 202 us
  waiting for transfers between devices: 187 us -> 147 us
  starting transfers between devices: 137 us -> 173 us
  local copies, waits for them, and re-layouts: 154 us -> 123 us
    pallas_call x6, Pallas kernels: 870 us -> 21.5 us  [place(): pl.pallas_call(kernel, out_shape=out_shapes, in_specs=[pl.BlockSpec(memor...]
    dot_general x28 -> x0, matrix products: 279 us -> none  [the longest x12 99 us: scores(): jnp.einsum('bhd,khd->hbk', query_heads, key_heads, preferred_element_type...]
    pallas_call x0 -> x6, Pallas kernels: none -> 101 us  [the longest x4 60.6 us: attention_backward(): pl.pallas_call(kernel, grid=(pairs,), in_specs=[own, whole, whole, own, o...]
    ppermute x75 -> x82, waiting for transfers between devices: 151 us -> 94.2 us  [shift(): return lax.ppermute(tensor, axis, [(i, (i + step) % n) for i in range(n)])]
    dynamic_slice x44 -> x0, local copies, waits for them, and re-layouts: 36.5 us -> none  [the longest x8 11.4 us: visitor(): key_block = by_heads(lax.dynamic_slice_in_dim(key_part, offset, stride, 0))]
    reduce_sum x10 -> x5, other arithmetic: 40.3 us -> 4.13 us  [the longest x2 1.56 us: backward(): bias_query = jnp.sum(grad_mixed[:, :model].astype(F32), axis=0)]
    ppermute x7, starting transfers between devices: 34.4 us -> 57.7 us  [swap(): return lax.ppermute(tensor, ('x', 'c'), [(0, 0), (1, 2), (2, 1), (3, 3)])]
    ppermute x27 -> x30, waiting for transfers between devices: 36.1 us -> 52.5 us  [far_shift(): return lax.ppermute(tensor, ('h', 'z'), pairs)]
  transfers between devices with their start and end apart: 109 -> 119, of which waited for: 31 -> 31; matrix products, arithmetic and copies ran while one was open for 28% -> 30% of each run, Pallas kernels for 44% -> 12%
where the time goes in v2:
time: 895 us; the launch traced here: 883 us
  matrix products  202 us (23%)
  starting transfers between devices  173 us (19%)
  waiting for transfers between devices  147 us (16%)
  local copies, waits for them, and re-layouts  123 us (14%)
  Pallas kernels  123 us (14%)
  other arithmetic  112 us (13%)
    ppermute x82, waiting for transfers between devices, shift(): return lax.ppermute(tensor, axis, [(i, (i + step) % n) for i in range(n)])  94.2 us
    dot_general x8, matrix products, product(): return jnp.dot(left_side, right_side, preferred_element_type=F32)  82.1 us
    dot_general x8, matrix products, back_product(): lax.dot_general(left_side, right_side, WITHIN, preferred_element_type=F32)  62.4 us
    pallas_call x4, Pallas kernels, attention_backward(): pl.pallas_call(kernel, grid=(pairs,), in_specs=[own, whole, whole, own, o...  60.6 us
    ppermute x7, starting transfers between devices, swap(): return lax.ppermute(tensor, ('x', 'c'), [(0, 0), (1, 2), (2, 1), (3, 3)])  57.7 us
    ppermute x82, starting transfers between devices, shift(): return lax.ppermute(tensor, axis, [(i, (i + step) % n) for i in range(n)])  57.6 us
    dot_general x10, matrix products, outer_sum(): lax.dot_general(left_side, right_side, ACROSS, preferred_element_type=F32)  57.4 us
    ppermute x30, starting transfers between devices, far_shift(): return lax.ppermute(tensor, ('h', 'z'), pairs)  57.3 us
  transfers between devices with their start and end apart: 119, of which 31 were waited for; matrix products, arithmetic and copies ran while one was open for 30% of the time, Pallas kernels for 12%

profile of v2, /device:TPU:0, one launch (start us, length us, event | category | flops | bytes accessed | tf_op | source)
XLA Modules:
  0.0 882.9 jit_solution(2032844748051670292)
XLA Ops:
  34.2 23.4 %collective-permute-done.10.refs_3_ = bf16[32,3072]{1,0:T(8,128)(2,1)S(1)} collective-permute-done((bf16[32,3072]{1,0:T(8,128)(2,1)}, bf16[32,3072]{1,0:T(8,128)(2,1)S(1)}, u32[]{:S(2)}, u32[]{:S(2)}) %collective-permute-start.10) | collective-permute-done | bytes 196640 | tf_op jit(solution)/shard_map/ppermute | solution.py:216
  66.7 8.5 collective-permute-start.11
  92.7 9.1 %collective-permute-done.14.refs_5_ = bf16[1,4,16,3072]{3,2,1,0:T(8,128)(2,1)S(1)} collective-permute-done((bf16[1,4,16,3072]{3,2,1,0:T(8,128)(2,1)S(1)}, bf16[1,4,16,3072]{3,2,1,0:T(8,128)(2,1)S(1)}, u32[]{:S(2)}, u32[]{:S(2)}) %collective-permute-start.14) | collective-permute-done | bytes 393248 | tf_op jit(solution)/shard_map/ppermute | solution.py:204
  121.2 10.4 %collective-permute-done.31.refs_2_ = bf16[1,4,16,5120]{3,2,1,0:T(8,128)(2,1)S(1)} collective-permute-done((bf16[1,4,16,5120]{3,2,1,0:T(8,128)(2,1)S(1)}, bf16[1,4,16,5120]{3,2,1,0:T(8,128)(2,1)S(1)}, u32[]{:S(2)}, u32[]{:S(2)}) %collective-permute-start.31) | collective-permute-done | bytes 655392 | tf_op jit(solution)/shard_map/ppermute | solution.py:204
  131.6 9.5 %collective-permute-start = (bf16[512,1024]{1,0:T(8,128)(2,1)}, bf16[512,1024]{1,0:T(8,128)(2,1)}, u32[]{:S(2)}, u32[]{:S(2)}) collective-permute-start(bf16[512,1024]{1,0:T(8,128)(2,1)} %bitcast.790), channel_id=1, source_target_pairs={{0,0},{1,16},{16,1},{17,17},{2,2},{3,18},{18,3},{19,19},{4,4},{5,2... | collective-permute-start | bytes 3145736 | tf_op jit(solution)/shard_map/ppermute | solution.py:219
  197.5 7.5 collective-permute-done.35.refs_6_
  249.9 20.3 %attention_forward.2 = (f32[512,1024]{1,0:T(8,128)S(1)}, f32[8,2,512]{2,1,0:T(2,128)S(1)}) custom-call(bf16[512,1024]{1,0:T(8,128)(2,1)S(1)} %get-tuple-element.240.q_ref, bf16[1024,1024]{1,0:T(8,128)(2,1)S(1)} %bitcast.755, bf16[1024,1024]{1,0:T(8,128)(2,1)} %bitcast.780, s32[512,2]{1,0:T(8,128)S(1)} %copy-done.64, s32[3,1024]{1,0:T(4,128)S(1)} %pad_add_fusion.kl_ref), custom_call_target="tpu_custom_call" | custom-call | flops 2147483648 | bytes 10485760 | tf_op jit(solution)/shard_map/attention_forward/pallas_call | solution.py:82
  275.5 27.8 %multiply_convert_fusion.1 = (bf16[512,4096]{1,0:T(8,128)(2,1)S(1)}, f32[512,4096]{1,0:T(8,128)}, f32[512,4096]{1,0:T(8,128)}) fusion(f32[4096]{0:T(1024)S(1)} %copy-done.185, bf16[1024,4096]{1,0:T(8,128)(2,1)} %bitcast.765, f32[512,1024]{1,0:T(8,128)S(1)} %get-tuple-element.346, f32[1024]{0:T(1024)S(1)} %copy-done.207, f32[1024]{0:T(1024)S(1)} %copy-done.172, ...), kind=kOutput, calls=%fused_computation.31 | convolution fusion | flops 4436000768 | bytes 31485952 | tf_op jit(solution)/shard_map/dot_general | solution.py:31
  319.4 9.5 %collective-permute-start.67 = (bf16[512,1024]{1,0:T(8,128)(2,1)}, bf16[512,1024]{1,0:T(8,128)(2,1)}, u32[]{:S(2)}, u32[]{:S(2)}) collective-permute-start(bf16[512,1024]{1,0:T(8,128)(2,1)} %bitcast.44), channel_id=1, source_target_pairs={{0,0},{1,16},{16,1},{17,17},{2,2},{3,18},{18,3},{19,19},{4,4},{5,2... | collective-permute-start | bytes 3145736 | tf_op jit(solution)/shard_map/ppermute | solution.py:219
  328.9 9.5 %collective-permute-start.66 = (bf16[512,1024]{1,0:T(8,128)(2,1)}, bf16[512,1024]{1,0:T(8,128)(2,1)}, u32[]{:S(2)}, u32[]{:S(2)}) collective-permute-start(bf16[512,1024]{1,0:T(8,128)(2,1)} %bitcast.43), channel_id=1, source_target_pairs={{0,0},{1,16},{16,1},{17,17},{2,2},{3,18},{18,3},{19,19},{4,4},{5,2... | collective-permute-start | bytes 3145736 | tf_op jit(solution)/shard_map/ppermute | solution.py:219
  344.8 20.4 %attention_forward.3 = (f32[512,1024]{1,0:T(8,128)S(1)}, f32[8,2,512]{2,1,0:T(2,128)S(1)}) custom-call(bf16[512,1024]{1,0:T(8,128)(2,1)S(1)} %get-tuple-element.238.q_ref, bf16[1024,1024]{1,0:T(8,128)(2,1)S(1)} %bitcast.758, bf16[1024,1024]{1,0:T(8,128)(2,1)} %bitcast.783, s32[512,2]{1,0:T(8,128)S(1)} %copy-done.64, s32[3,1024]{1,0:T(4,128)S(1)} %pad_add_fusion.kl_ref), custom_call_target="tpu_custom_call" | custom-call | flops 2147483648 | bytes 10485760 | tf_op jit(solution)/shard_map/attention_forward/pallas_call | solution.py:82
  369.7 25.7 %multiply_convert_fusion = (bf16[512,4096]{1,0:T(8,128)(2,1)}, f32[512,4096]{1,0:T(8,128)}, f32[512,4096]{1,0:T(8,128)}) fusion(f32[4096]{0:T(1024)S(1)} %copy-done.185, bf16[1024,4096]{1,0:T(8,128)(2,1)S(1)} %bitcast.769, f32[512,1024]{1,0:T(8,128)S(1)} %get-tuple-element.351, f32[512]{0:T(512)S(1)} %fusion.192, f32[512]{0:T(512)S(1)} %broadcast_multiply_fusion, ...), kind=kOutput, calls=%fused_computation.18 | convolution fusion | flops 4436000768 | bytes 31485952 | tf_op jit(solution)/shard_map/dot_general | solution.py:31
  395.4 13.5 %convert_reduce_fusion.1 = (f32[4096]{0:T(1024)}, bf16[512,4096]{1,0:T(8,128)(2,1)}) fusion(f32[512,4096]{1,0:T(8,128)} %get-tuple-element.230, bf16[4096,1024]{1,0:T(8,128)(2,1)S(1)} %bitcast.725, bf16[512,1024]{1,0:T(8,128)(2,1)} %collective-permute-done.67, f32[512,4096]{1,0:T(8,128)} %get-tuple-element.352, f32[4096]{0:T(1024)S(1)} %copy-done.185), kind=kOutput, calls=%fused_computation.16 | convolution fusion | flops 4330614784 | bytes 30441472 | tf_op jit(solution)/shard_map/dot_general | solution.py:39
  408.9 8.6 multiply_reduce_fusion.2
  422.2 15.3 %attention_backward.4 = (bf16[512,512]{1,0:T(8,128)(2,1)S(1)}, bf16[1024,512]{1,0:T(8,128)(2,1)S(1)}, bf16[1024,512]{1,0:T(8,128)(2,1)S(1)}) custom-call(bf16[512,1024]{1,0:T(8,128)(2,1)S(1)} %copy-done.11, bf16[1024,1024]{1,0:T(8,128)(2,1)} %bitcast.759, bf16[1024,1024]{1,0:T(8,128)(2,1)} %bitcast.784, ...), custom_call_target="tpu_custom_call" | custom-call | flops 2684354560 | bytes 6291456 | tf_op jit(solution)/shard_map/attention_backward/pallas_call | solution.py:161
  437.5 15.1 %attention_backward.5 = (bf16[512,512]{1,0:T(8,128)(2,1)S(1)}, bf16[1024,512]{1,0:T(8,128)(2,1)S(1)}, bf16[1024,512]{1,0:T(8,128)(2,1)S(1)}) custom-call(bf16[512,1024]{1,0:T(8,128)(2,1)S(1)} %copy-done.11, bf16[1024,1024]{1,0:T(8,128)(2,1)} %bitcast.760, bf16[1024,1024]{1,0:T(8,128)(2,1)} %bitcast.785, ...), custom_call_target="tpu_custom_call" | custom-call | flops 2684354560 | bytes 6291456 | tf_op jit(solution)/shard_map/attention_backward/pallas_call | solution.py:161
  453.5 10.7 %fusion.227 = bf16[4096,1024]{1,0:T(8,128)(2,1)} fusion(bf16[512,4096]{1,0:T(8,128)(2,1)} %get-tuple-element.229, bf16[512,1024]{1,0:T(8,128)(2,1)} %collective-permute-done.67), kind=kOutput, calls=%fused_computation.655 | convolution fusion | flops 4294967296 | bytes 13631488 | tf_op jit(solution)/shard_map/dot_general | solution.py:35
  479.4 9.4 %add_convert_fusion.1 = bf16[4096,1024]{1,0:T(8,128)(2,1)} fusion(bf16[4096,1024]{1,0:T(8,128)(2,1)} %fusion.227, bf16[512,4096]{1,0:T(8,128)(2,1)S(1)} %copy-done.214, bf16[512,1024]{1,0:T(8,128)(2,1)S(1)} %fusion.43), kind=kOutput, calls=%fused_computation.1 | convolution fusion | flops 4307550208 | bytes 22020096 | tf_op jit(solution)/shard_map/dot_general | solution.py:35
  488.8 8.4 dynamic-slice_bitcast_fusion.2
  497.2 10.9 %fusion.200 = bf16[1024,4096]{1,0:T(8,128)(2,1)} fusion(bf16[512,4096]{1,0:T(8,128)(2,1)} %get-tuple-element.358, f32[512,1024]{1,0:T(8,128)} %copy-done.87, f32[512]{0:T(512)S(1)} %fusion.192, f32[512]{0:T(512)S(1)} %broadcast_multiply_fusion, f32[1024]{0:T(1024)S(1)} %copy-done.207, f32[1024]{0:T(1024)S(1)} %copy-done.172), kind=kOutput, calls=%fused_computation.631 | convolution fusion | flops 4297588736 | bytes 14692352 | tf_op jit(solution)/shard_map/dot_general | solution.py:35
  508.6 16.3 %add_convert_fusion.2 = bf16[512,4096]{1,0:T(8,128)(2,1)} fusion(f32[512,4096]{1,0:T(8,128)} %get-tuple-element.232, f32[512,4096]{1,0:T(8,128)} %get-tuple-element.347, f32[4096]{0:T(1024)S(1)} %copy-done.185, bf16[512,1024]{1,0:T(8,128)(2,1)S(1)} %fusion.43, bf16[4096,1024]{1,0:T(8,128)(2,1)} %bitcast.722), kind=kOutput, calls=%fused_computation.17 | convolution fusion | flops 4326424576 | bytes 30425088 | tf_op jit(solution)/shard_map/dot_general | solution.py:39
  531.2 8.5 add_convert_fusion
  544.9 10.8 %multiply_reduce_fusion = (f32[1024]{0:T(1024)}, f32[512]{0:T(512)S(1)}, f32[1024]{0:T(1024)}, f32[512,1024]{1,0:T(8,128)S(1)}) fusion(f32[512,1024]{1,0:T(8,128)} %copy-done.90, f32[512]{0:T(512)S(1)} %copy-done.191, f32[512]{0:T(512)S(1)} %copy-done.180, f32[1024]{0:T(1024)S(1)} %copy-done.172, bf16[512,4096]{1,0:T(8,128)(2,1)} %add_convert_fusion.2, ...), kind=kOutput, calls=%fused_computation.99 | convolution fusion | flops 4299159040 | bytes 16795648 | tf_op jit(solution)/shard_map/dot_general | solution.py:39
  560.3 9.2 %collective-permute-done.72 = bf16[1,4,2,64,1024]{4,3,2,1,0:T(8,128)(2,1)S(1)} collective-permute-done((bf16[1,4,2,64,1024]{4,3,2,1,0:T(8,128)(2,1)}, bf16[1,4,2,64,1024]{4,3,2,1,0:T(8,128)(2,1)S(1)}, u32[]{:S(2)}, u32[]{:S(2)}) %collective-permute-start.72) | collective-permute-done | bytes 1048608 | tf_op jit(solution)/shard_map/ppermute | solution.py:204
  586.6 15.1 %attention_backward.6 = (bf16[512,512]{1,0:T(8,128)(2,1)S(1)}, bf16[1024,512]{1,0:T(8,128)(2,1)S(1)}, bf16[1024,512]{1,0:T(8,128)(2,1)S(1)}) custom-call(bf16[512,1024]{1,0:T(8,128)(2,1)S(1)} %copy-done.9, bf16[1024,1024]{1,0:T(8,128)(2,1)} %bitcast.756, bf16[1024,1024]{1,0:T(8,128)(2,1)} %bitcast.781, ...), custom_call_target="tpu_custom_call" | custom-call | flops 2684354560 | bytes 6291456 | tf_op jit(solution)/shard_map/attention_backward/pallas_call | solution.py:161
  607.9 10.6 %collective-permute-done.76 = bf16[1,4,2,16,4096]{4,3,2,1,0:T(8,128)(2,1)S(1)} collective-permute-done((bf16[1,4,2,16,4096]{4,3,2,1,0:T(8,128)(2,1)}, bf16[1,4,2,16,4096]{4,3,2,1,0:T(8,128)(2,1)S(1)}, u32[]{:S(2)}, u32[]{:S(2)}) %collective-permute-start.76) | collective-permute-done | bytes 1048608 | tf_op jit(solution)/shard_map/ppermute | solution.py:204
  659.7 9.5 %collective-permute-done.81 = bf16[128,1024]{1,0:T(8,128)(2,1)S(1)} collective-permute-done((bf16[128,1024]{1,0:T(8,128)(2,1)S(1)}, bf16[128,1024]{1,0:T(8,128)(2,1)S(1)}, u32[]{:S(2)}, u32[]{:S(2)}) %collective-permute-start.81) | collective-permute-done | bytes 262176 | tf_op jit(solution)/shard_map/ppermute | solution.py:216
  669.9 15.0 %attention_backward.7 = (bf16[512,512]{1,0:T(8,128)(2,1)S(1)}, bf16[1024,512]{1,0:T(8,128)(2,1)S(1)}, bf16[1024,512]{1,0:T(8,128)(2,1)S(1)}) custom-call(bf16[512,1024]{1,0:T(8,128)(2,1)S(1)} %copy-done.9, bf16[1024,1024]{1,0:T(8,128)(2,1)} %bitcast.757, bf16[1024,1024]{1,0:T(8,128)(2,1)} %bitcast.782, ...), custom_call_target="tpu_custom_call" | custom-call | flops 2684354560 | bytes 6291456 | tf_op jit(solution)/shard_map/attention_backward/pallas_call | solution.py:161
  686.1 9.5 %collective-permute-start.62 = (bf16[512,1024]{1,0:T(8,128)(2,1)}, bf16[512,1024]{1,0:T(8,128)(2,1)}, u32[]{:S(2)}, u32[]{:S(2)}) collective-permute-start(bf16[512,1024]{1,0:T(8,128)(2,1)} %get-tuple-element.349), channel_id=1, source_target_pairs={{0,0},{1,16},{16,1},{17,17},{2,2},{3,18},{18,3},{19,19},{4,4},{5,2... | collective-permute-start | bytes 3145736 | tf_op jit(solution)/shard_map/ppermute | solution.py:219
  695.6 9.5 %collective-permute-start.65 = (bf16[512,1024]{1,0:T(8,128)(2,1)}, bf16[512,1024]{1,0:T(8,128)(2,1)}, u32[]{:S(2)}, u32[]{:S(2)}) collective-permute-start(bf16[512,1024]{1,0:T(8,128)(2,1)} %add_convert_fusion.10), channel_id=1, source_target_pairs={{0,0},{1,16},{16,1},{17,17},{2,2},{3,18},{18,3},{19,19},{4,4},{5,2... | collective-permute-start | bytes 3145736 | tf_op jit(solution)/shard_map/ppermute | solution.py:219
  750.2 12.0 %collective-permute-done.90 = bf16[1,4,2,16,1024]{4,3,2,1,0:T(8,128)(2,1)S(1)} collective-permute-done((bf16[1,4,2,16,1024]{4,3,2,1,0:T(8,128)(2,1)S(1)}, bf16[1,4,2,16,1024]{4,3,2,1,0:T(8,128)(2,1)S(1)}, u32[]{:S(2)}, u32[]{:S(2)}) %collective-permute-start.90) | collective-permute-done | bytes 262176 | tf_op jit(solution)/shard_map/ppermute | solution.py:204
  800.8 9.6 %collective-permute-start.92 = (bf16[512,1024]{1,0:T(8,128)(2,1)}, bf16[512,1024]{1,0:T(8,128)(2,1)}, u32[]{:S(2)}, u32[]{:S(2)}) collective-permute-start(bf16[512,1024]{1,0:T(8,128)(2,1)} %get-tuple-element.257), channel_id=1, source_target_pairs={{0,0},{1,16},{16,1},{17,17},{2,2},{3,18},{18,3},{19,19},{4,4},{5,2... | collective-permute-start | bytes 3145736 | tf_op jit(solution)/shard_map/ppermute | solution.py:219
  (948 shorter events, 470.2 us)
Async XLA Ops:
  0.6 30.3 %collective-permute-start.8 = (bf16[32,3072]{1,0:T(8,128)(2,1)}, bf16[32,3072]{1,0:T(8,128)(2,1)S(1)}, u32[]{:S(2)}, u32[]{:S(2)}) collective-permute-start(bf16[32,3072]{1,0:T(8,128)(2,1)} %refs_0_.2), channel_id=1, source_target_pairs={{0,4},{4,8},{8,12},{12,0},{1,5},{5,9},{9,13},{13,1},{2,6},{6,10},{... | collective-permute-start | bytes 589832 | tf_op jit(solution)/shard_map/ppermute | solution.py:216
  3.7 29.5 %collective-permute-start.9 = (bf16[32,3072]{1,0:T(8,128)(2,1)}, bf16[32,3072]{1,0:T(8,128)(2,1)S(1)}, u32[]{:S(2)}, u32[]{:S(2)}) collective-permute-start(bf16[32,3072]{1,0:T(8,128)(2,1)} %refs_0_.2), channel_id=1, source_target_pairs={{0,8},{4,12},{8,0},{12,4},{1,9},{5,13},{9,1},{13,5},{2,10},{6,14},... | collective-permute-start | bytes 589832 | tf_op jit(solution)/shard_map/ppermute | solution.py:216
  26.3 51.0 %collective-permute-start.28 = (bf16[32,5120]{1,0:T(8,128)(2,1)S(1)}, bf16[32,5120]{1,0:T(8,128)(2,1)S(1)}, u32[]{:S(2)}, u32[]{:S(2)}) collective-permute-start(bf16[32,5120]{1,0:T(8,128)(2,1)S(1)} %constant_dynamic-update-slice_fusion.refs_0_), channel_id=1, source_target_pairs={{0,4},{4,8},{8,12},{12,0},{1,5},{5,9},{9,13},{13,1},{2,6},{6,10},{... | collective-permute-start | bytes 983048 | tf_op jit(solution)/shard_map/ppermute | solution.py:216
  28.9 37.7 %collective-permute-start.45 = (bf16[128,1024]{1,0:T(8,128)(2,1)}, bf16[128,1024]{1,0:T(8,128)(2,1)S(1)}, u32[]{:S(2)}, u32[]{:S(2)}) collective-permute-start(bf16[128,1024]{1,0:T(8,128)(2,1)} %refs_0_.3), channel_id=1, source_target_pairs={{0,4},{4,8},{8,12},{12,0},{1,5},{5,9},{9,13},{13,1},{2,6},{6,10},{... | collective-permute-start | bytes 786440 | tf_op jit(solution)/shard_map/ppermute | solution.py:216
  29.8 45.4 %collective-permute-start.46 = (bf16[128,1024]{1,0:T(8,128)(2,1)}, bf16[128,1024]{1,0:T(8,128)(2,1)S(1)}, u32[]{:S(2)}, u32[]{:S(2)}) collective-permute-start(bf16[128,1024]{1,0:T(8,128)(2,1)} %refs_0_.3), channel_id=1, source_target_pairs={{0,8},{4,12},{8,0},{12,4},{1,9},{5,13},{9,1},{13,5},{2,10},{6,14},... | collective-permute-start | bytes 786440 | tf_op jit(solution)/shard_map/ppermute | solution.py:216
  31.0 45.4 %collective-permute-start.47 = (bf16[128,1024]{1,0:T(8,128)(2,1)}, bf16[128,1024]{1,0:T(8,128)(2,1)S(1)}, u32[]{:S(2)}, u32[]{:S(2)}) collective-permute-start(bf16[128,1024]{1,0:T(8,128)(2,1)} %refs_0_.3), channel_id=1, source_target_pairs={{0,12},{4,0},{8,4},{12,8},{1,13},{5,1},{9,5},{13,9},{2,14},{6,2},{... | collective-permute-start | bytes 786440 | tf_op jit(solution)/shard_map/ppermute | solution.py:216
  57.6 26.7 %collective-permute-start.29 = (bf16[32,5120]{1,0:T(8,128)(2,1)S(1)}, bf16[32,5120]{1,0:T(8,128)(2,1)S(1)}, u32[]{:S(2)}, u32[]{:S(2)}) collective-permute-start(bf16[32,5120]{1,0:T(8,128)(2,1)S(1)} %constant_dynamic-update-slice_fusion.refs_0_), channel_id=1, source_target_pairs={{0,8},{4,12},{8,0},{12,4},{1,9},{5,13},{9,1},{13,5},{2,10},{6,14},... | collective-permute-start | bytes 983048 | tf_op jit(solution)/shard_map/ppermute | solution.py:216
  85.8 27.3 %collective-permute-start.49 = (bf16[1,4,64,1024]{3,2,1,0:T(8,128)(2,1)S(1)}, bf16[1,4,64,1024]{3,2,1,0:T(8,128)(2,1)S(1)}, u32[]{:S(2)}, u32[]{:S(2)}) collective-permute-start(bf16[1,4,64,1024]{3,2,1,0:T(8,128)(2,1)S(1)} %get-tuple-element.110.refs_1_), channel_id=1, source_target_pairs={{0,2},{2,0},{1,3},{3,1},{4,6},{6,4},{5,7},{7,5},{8,10},{10,8},{9,1... | collective-permute-start | bytes 1572872 | tf_op jit(solution)/shard_map/ppermute | solution.py:204
  114.8 31.1 %collective-permute-start.33 = (bf16[1,4,16,5120]{3,2,1,0:T(8,128)(2,1)S(1)}, bf16[1,4,16,5120]{3,2,1,0:T(8,128)(2,1)}, u32[]{:S(2)}, u32[]{:S(2)}) collective-permute-start(bf16[1,4,16,5120]{3,2,1,0:T(8,128)(2,1)S(1)} %get-tuple-element.105.refs_0_), channel_id=1, source_target_pairs={{0,2},{2,0},{1,3},{3,1},{4,6},{6,4},{5,7},{7,5},{8,10},{10,8},{9,1... | collective-permute-start | bytes 1966088 | tf_op jit(solution)/shard_map/ppermute | solution.py:204
  115.2 30.3 %collective-permute-start.32 = (bf16[1,4,16,5120]{3,2,1,0:T(8,128)(2,1)S(1)}, bf16[1,4,16,5120]{3,2,1,0:T(8,128)(2,1)}, u32[]{:S(2)}, u32[]{:S(2)}) collective-permute-start(bf16[1,4,16,5120]{3,2,1,0:T(8,128)(2,1)S(1)} %get-tuple-element.106.refs_1_), channel_id=1, source_target_pairs={{0,2},{2,0},{1,3},{3,1},{4,6},{6,4},{5,7},{7,5},{8,10},{10,8},{9,1... | collective-permute-start | bytes 1966088 | tf_op jit(solution)/shard_map/ppermute | solution.py:204
  116.9 29.1 %collective-permute-start.34 = (bf16[1,4,16,5120]{3,2,1,0:T(8,128)(2,1)S(1)}, bf16[1,4,16,5120]{3,2,1,0:T(8,128)(2,1)}, u32[]{:S(2)}, u32[]{:S(2)}) collective-permute-start(bf16[1,4,16,5120]{3,2,1,0:T(8,128)(2,1)S(1)} %get-tuple-element.106.refs_1_), channel_id=1, source_target_pairs={{0,16},{16,0},{1,17},{17,1},{2,18},{18,2},{3,19},{19,3},{4,20},{20... | collective-permute-start | bytes 1966088 | tf_op jit(solution)/shard_map/ppermute | solution.py:204
  118.7 29.0 %collective-permute-start.37 = (bf16[1,4,16,5120]{3,2,1,0:T(8,128)(2,1)S(1)}, bf16[1,4,16,5120]{3,2,1,0:T(8,128)(2,1)S(1)}, u32[]{:S(2)}, u32[]{:S(2)}) collective-permute-start(bf16[1,4,16,5120]{3,2,1,0:T(8,128)(2,1)S(1)} %get-tuple-element.105.refs_0_), channel_id=1, source_target_pairs={{0,1},{1,0},{2,3},{3,2},{4,5},{5,4},{6,7},{7,6},{8,9},{9,8},{10,11... | collective-permute-start | bytes 1966088 | tf_op jit(solution)/shard_map/ppermute | solution.py:204
  131.6 39.6 %collective-permute-start = (bf16[512,1024]{1,0:T(8,128)(2,1)}, bf16[512,1024]{1,0:T(8,128)(2,1)}, u32[]{:S(2)}, u32[]{:S(2)}) collective-permute-start(bf16[512,1024]{1,0:T(8,128)(2,1)} %bitcast.790), channel_id=1, source_target_pairs={{0,0},{1,16},{16,1},{17,17},{2,2},{3,18},{18,3},{19,19},{4,4},{5,2... | collective-permute-start | bytes 3145736 | tf_op jit(solution)/shard_map/ppermute | solution.py:219
  211.6 31.3 %collective-permute-start.25 = (bf16[1,512,1024]{2,1,0:T(8,128)(2,1)}, bf16[1,512,1024]{2,1,0:T(8,128)(2,1)}, u32[]{:S(2)}, u32[]{:S(2)}) collective-permute-start(bf16[1,512,1024]{2,1,0:T(8,128)(2,1)} %get-tuple-element.239), channel_id=1, source_target_pairs={{0,1},{1,0},{2,3},{3,2},{4,5},{5,4},{6,7},{7,6},{8,9},{9,8},{10,11... | collective-permute-start | bytes 3145736 | tf_op jit(solution)/shard_map/ppermute | solution.py:204
  216.5 29.0 %collective-permute-start.26 = (bf16[1,512,1024]{2,1,0:T(8,128)(2,1)}, bf16[1,512,1024]{2,1,0:T(8,128)(2,1)}, u32[]{:S(2)}, u32[]{:S(2)}) collective-permute-start(bf16[1,512,1024]{2,1,0:T(8,128)(2,1)} %fusion.51), channel_id=1, source_target_pairs={{0,1},{1,0},{2,3},{3,2},{4,5},{5,4},{6,7},{7,6},{8,9},{9,8},{10,11... | collective-permute-start | bytes 3145736 | tf_op jit(solution)/shard_map/ppermute | solution.py:204
  319.4 76.0 %collective-permute-start.67 = (bf16[512,1024]{1,0:T(8,128)(2,1)}, bf16[512,1024]{1,0:T(8,128)(2,1)}, u32[]{:S(2)}, u32[]{:S(2)}) collective-permute-start(bf16[512,1024]{1,0:T(8,128)(2,1)} %bitcast.44), channel_id=1, source_target_pairs={{0,0},{1,16},{16,1},{17,17},{2,2},{3,18},{18,3},{19,19},{4,4},{5,2... | collective-permute-start | bytes 3145736 | tf_op jit(solution)/shard_map/ppermute | solution.py:219
  328.9 147.3 %collective-permute-start.66 = (bf16[512,1024]{1,0:T(8,128)(2,1)}, bf16[512,1024]{1,0:T(8,128)(2,1)}, u32[]{:S(2)}, u32[]{:S(2)}) collective-permute-start(bf16[512,1024]{1,0:T(8,128)(2,1)} %bitcast.43), channel_id=1, source_target_pairs={{0,0},{1,16},{16,1},{17,17},{2,2},{3,18},{18,3},{19,19},{4,4},{5,2... | collective-permute-start | bytes 3145736 | tf_op jit(solution)/shard_map/ppermute | solution.py:219
  497.2 27.8 %collective-permute-start.70 = (bf16[1,2,4,2,128,1024]{5,4,3,2,1,0:T(8,128)(2,1)}, bf16[1,2,4,2,128,1024]{5,4,3,2,1,0:T(8,128)(2,1)}, u32[]{:S(2)}, u32[]{:S(2)}) collective-permute-start(bf16[1,2,4,2,128,1024]{5,4,3,2,1,0:T(8,128)(2,1)} %get-tuple-element.120), channel_id=1, source_target_pairs={{0,1},{1,0},{2,3},{3,2},{4,5},{5,4},{6,7},{7,6},{8,9},{9,8},{10,11... | collective-permute-start | bytes 12582920 | tf_op jit(solution)/shard_map/ppermute | solution.py:204
  543.6 26.0 %collective-permute-start.71 = (bf16[1,2,4,2,32,4096]{5,4,3,2,1,0:T(8,128)(2,1)}, bf16[1,2,4,2,32,4096]{5,4,3,2,1,0:T(8,128)(2,1)}, u32[]{:S(2)}, u32[]{:S(2)}) collective-permute-start(bf16[1,2,4,2,32,4096]{5,4,3,2,1,0:T(8,128)(2,1)} %get-tuple-element.125), channel_id=1, source_target_pairs={{0,1},{1,0},{2,3},{3,2},{4,5},{5,4},{6,7},{7,6},{8,9},{9,8},{10,11... | collective-permute-start | bytes 12582920 | tf_op jit(solution)/shard_map/ppermute | solution.py:204
  584.2 34.3 %collective-permute-start.76 = (bf16[1,4,2,16,4096]{4,3,2,1,0:T(8,128)(2,1)}, bf16[1,4,2,16,4096]{4,3,2,1,0:T(8,128)(2,1)S(1)}, u32[]{:S(2)}, u32[]{:S(2)}) collective-permute-start(bf16[1,4,2,16,4096]{4,3,2,1,0:T(8,128)(2,1)} %fusion.47), channel_id=1, source_target_pairs={{0,16},{16,0},{1,17},{17,1},{2,18},{18,2},{3,19},{19,3},{4,20},{20... | collective-permute-start | bytes 3145736 | tf_op jit(solution)/shard_map/ppermute | solution.py:204
  585.1 33.4 %collective-permute-start.77 = (bf16[1,2,4,16,4096]{4,3,2,1,0:T(8,128)(2,1)}, bf16[1,2,4,16,4096]{4,3,2,1,0:T(8,128)(2,1)}, u32[]{:S(2)}, u32[]{:S(2)}) collective-permute-start(bf16[1,2,4,16,4096]{4,3,2,1,0:T(8,128)(2,1)} %fusion.48), channel_id=1, source_target_pairs={{0,2},{2,0},{1,3},{3,1},{4,6},{6,4},{5,7},{7,5},{8,10},{10,8},{9,1... | collective-permute-start | bytes 3145736 | tf_op jit(solution)/shard_map/ppermute | solution.py:204
  638.8 66.3 %collective-permute-start.79 = (bf16[1,2,4,2,32,1536]{5,4,3,2,1,0:T(8,128)(2,1)}, bf16[1,2,4,2,32,1536]{5,4,3,2,1,0:T(8,128)(2,1)}, u32[]{:S(2)}, u32[]{:S(2)}) collective-permute-start(bf16[1,2,4,2,32,1536]{5,4,3,2,1,0:T(8,128)(2,1)} %get-tuple-element.154), channel_id=1, source_target_pairs={{0,1},{1,0},{2,3},{3,2},{4,5},{5,4},{6,7},{7,6},{8,9},{9,8},{10,11... | collective-permute-start | bytes 4718600 | tf_op jit(solution)/shard_map/ppermute | solution.py:204
  647.5 57.6 %collective-permute-start.85 = (bf16[1,2,4,2,32,1024]{5,4,3,2,1,0:T(8,128)(2,1)}, bf16[1,2,4,2,32,1024]{5,4,3,2,1,0:T(8,128)(2,1)S(1)}, u32[]{:S(2)}, u32[]{:S(2)}) collective-permute-start(bf16[1,2,4,2,32,1024]{5,4,3,2,1,0:T(8,128)(2,1)} %get-tuple-element.160), channel_id=1, source_target_pairs={{0,1},{1,0},{2,3},{3,2},{4,5},{5,4},{6,7},{7,6},{8,9},{9,8},{10,11... | collective-permute-start | bytes 3145736 | tf_op jit(solution)/shard_map/ppermute | solution.py:204
  652.0 43.6 %collective-permute-start.83 = (bf16[1,4,16,4096]{3,2,1,0:T(8,128)(2,1)}, bf16[1,4,16,4096]{3,2,1,0:T(8,128)(2,1)S(1)}, u32[]{:S(2)}, u32[]{:S(2)}) collective-permute-start(bf16[1,4,16,4096]{3,2,1,0:T(8,128)(2,1)} %fusion.72), channel_id=1, source_target_pairs={{0,2},{2,0},{1,3},{3,1},{4,6},{6,4},{5,7},{7,5},{8,10},{10,8},{9,1... | collective-permute-start | bytes 1572872 | tf_op jit(solution)/shard_map/ppermute | solution.py:204
  658.4 46.7 %collective-permute-start.84 = (bf16[1,4,16,4096]{3,2,1,0:T(8,128)(2,1)}, bf16[1,4,16,4096]{3,2,1,0:T(8,128)(2,1)S(1)}, u32[]{:S(2)}, u32[]{:S(2)}) collective-permute-start(bf16[1,4,16,4096]{3,2,1,0:T(8,128)(2,1)} %fusion.71), channel_id=1, source_target_pairs={{0,16},{16,0},{1,17},{17,1},{2,18},{18,2},{3,19},{19,3},{4,20},{20... | collective-permute-start | bytes 1572872 | tf_op jit(solution)/shard_map/ppermute | solution.py:204
  686.1 32.3 %collective-permute-start.62 = (bf16[512,1024]{1,0:T(8,128)(2,1)}, bf16[512,1024]{1,0:T(8,128)(2,1)}, u32[]{:S(2)}, u32[]{:S(2)}) collective-permute-start(bf16[512,1024]{1,0:T(8,128)(2,1)} %get-tuple-element.349), channel_id=1, source_target_pairs={{0,0},{1,16},{16,1},{17,17},{2,2},{3,18},{18,3},{19,19},{4,4},{5,2... | collective-permute-start | bytes 3145736 | tf_op jit(solution)/shard_map/ppermute | solution.py:219
  762.2 36.3 %collective-permute-start.112 = (bf16[32,4096]{1,0:T(8,128)(2,1)}, bf16[32,4096]{1,0:T(8,128)(2,1)}, u32[]{:S(2)}, u32[]{:S(2)}) collective-permute-start(bf16[32,4096]{1,0:T(8,128)(2,1)} %pad_maximum_fusion.11), channel_id=1, source_target_pairs={{0,12},{4,0},{8,4},{12,8},{1,13},{5,1},{9,5},{13,9},{2,14},{6,2},{... | collective-permute-start | bytes 786440 | tf_op jit(solution)/shard_map/ppermute | solution.py:216
  763.2 35.5 %collective-permute-start.111 = (bf16[32,4096]{1,0:T(8,128)(2,1)}, bf16[32,4096]{1,0:T(8,128)(2,1)}, u32[]{:S(2)}, u32[]{:S(2)}) collective-permute-start(bf16[32,4096]{1,0:T(8,128)(2,1)} %pad_maximum_fusion.10), channel_id=1, source_target_pairs={{0,8},{4,12},{8,0},{12,4},{1,9},{5,13},{9,1},{13,5},{2,10},{6,14},... | collective-permute-start | bytes 786440 | tf_op jit(solution)/shard_map/ppermute | solution.py:216
  765.7 33.0 %collective-permute-start.110 = (bf16[32,4096]{1,0:T(8,128)(2,1)}, bf16[32,4096]{1,0:T(8,128)(2,1)}, u32[]{:S(2)}, u32[]{:S(2)}) collective-permute-start(bf16[32,4096]{1,0:T(8,128)(2,1)} %pad_maximum_fusion.9), channel_id=1, source_target_pairs={{0,4},{4,8},{8,12},{12,0},{1,5},{5,9},{9,13},{13,1},{2,6},{6,10},{... | collective-permute-start | bytes 786440 | tf_op jit(solution)/shard_map/ppermute | solution.py:216
  781.9 29.0 %collective-permute-start.106 = (bf16[1,4,16,1024]{3,2,1,0:T(8,128)(2,1)}, bf16[1,4,16,1024]{3,2,1,0:T(8,128)(2,1)}, u32[]{:S(2)}, u32[]{:S(2)}) collective-permute-start(bf16[1,4,16,1024]{3,2,1,0:T(8,128)(2,1)} %fusion.96), channel_id=1, source_target_pairs={{0,16},{16,0},{1,17},{17,1},{2,18},{18,2},{3,19},{19,3},{4,20},{20... | collective-permute-start | bytes 393224 | tf_op jit(solution)/shard_map/ppermute | solution.py:204
  782.4 31.6 %collective-permute-start.105 = (bf16[1,4,16,1024]{3,2,1,0:T(8,128)(2,1)}, bf16[1,4,16,1024]{3,2,1,0:T(8,128)(2,1)}, u32[]{:S(2)}, u32[]{:S(2)}) collective-permute-start(bf16[1,4,16,1024]{3,2,1,0:T(8,128)(2,1)} %fusion.97), channel_id=1, source_target_pairs={{0,2},{2,0},{1,3},{3,1},{4,6},{6,4},{5,7},{7,5},{8,10},{10,8},{9,1... | collective-permute-start | bytes 393224 | tf_op jit(solution)/shard_map/ppermute | solution.py:204
  800.8 74.6 %collective-permute-start.92 = (bf16[512,1024]{1,0:T(8,128)(2,1)}, bf16[512,1024]{1,0:T(8,128)(2,1)}, u32[]{:S(2)}, u32[]{:S(2)}) collective-permute-start(bf16[512,1024]{1,0:T(8,128)(2,1)} %get-tuple-element.257), channel_id=1, source_target_pairs={{0,0},{1,16},{16,1},{17,17},{2,2},{3,18},{18,3},{19,19},{4,4},{5,2... | collective-permute-start | bytes 3145736 | tf_op jit(solution)/shard_map/ppermute | solution.py:219
  (315 other events, 4216.3 us)

commit v3 on v2

v3 whole, which is shorter than its diff:
```python
from functools import partial
import math

import jax
import jax.numpy as jnp
import numpy as np
from jax import lax
from jax.experimental import pallas as pl
from jax.experimental.pallas import tpu as pltpu
from jax.sharding import Mesh, PartitionSpec as P

HEAD = 64
PAIR = 2 * HEAD
SCALE = 0.125
EPSILON = 1e-06
NEGATIVE = -1e30
ACROSS = (((0,), (0,)), ((), ()))
WITHIN = (((1,), (1,)), ((), ()))
BF = jnp.bfloat16
F32 = jnp.float32


def layer_norm(tensor, gain_row, shift_row):
    average = jnp.mean(tensor, axis=-1, keepdims=True)
    centred = tensor - average
    variance = jnp.mean(centred * centred, axis=-1, keepdims=True)
    return centred * lax.rsqrt(variance + EPSILON) * gain_row + shift_row


def product(left_side, right_side):
    return jnp.dot(left_side, right_side, preferred_element_type=F32)


def outer_sum(left_side, right_side):
    return lax.dot_general(left_side, right_side, ACROSS, preferred_element_type=F32)


def back_product(left_side, right_side):
    return lax.dot_general(left_side, right_side, WITHIN, preferred_element_type=F32)


def fill_bias(bias_ref, query_labels, key_labels):
    query_seg, _, query_pos = query_labels
    key_seg, key_open, key_pos = key_labels
    allowed = (key_seg == query_seg) & ((key_open == 1) | (key_pos == query_pos))
    bias_ref[...] = jnp.where(allowed, 0.0, NEGATIVE)


def columns_of(ref):
    return tuple(ref[:, i : i + 1] for i in range(3))


def rows_of(ref):
    return tuple(ref[i : i + 1, :] for i in range(3))


def half_lanes(tensor, side):
    lane = lax.broadcasted_iota(jnp.int32, tensor.shape, 1)
    return jnp.where((lane < HEAD) == (side == 0), tensor, jnp.zeros((), tensor.dtype))


def attention_forward(query, mates, query_labels, key_labels):
    tokens, model = query.shape
    part = mates[0].shape[0]
    every = 2 * part
    pairs = model // PAIR
    step = math.gcd(tokens, 256)

    def kernel(q_ref, k0_ref, k1_ref, v0_ref, v1_ref, ql_ref, kl_ref, attn_ref, lse_ref, bias_ref):
        @pl.when(pl.program_id(0) == 0)
        def _():
            fill_bias(bias_ref, columns_of(ql_ref), rows_of(kl_ref))

        keys_pair = jnp.concatenate([k0_ref[...], k1_ref[...]], axis=0)
        values_pair = jnp.concatenate([v0_ref[...], v1_ref[...]], axis=0)
        for start in range(0, tokens, step):
            query_pair = q_ref[start : start + step, :]
            sides = []
            for side in range(2):
                logits = back_product(half_lanes(query_pair, side), keys_pair)
                logits = logits + bias_ref[start : start + step, :]
                highest = jnp.max(logits, axis=1, keepdims=True)
                weights = jnp.exp(logits - highest)
                denominator = jnp.sum(weights, axis=1, keepdims=True)
                across = jnp.broadcast_to(highest + jnp.log(denominator), (step, PAIR)).T
                lse_ref[0, side : side + 1, start : start + step] = across[0:1]
                sides.append(product(weights.astype(BF), values_pair) / denominator)
            lane = lax.broadcasted_iota(jnp.int32, (step, PAIR), 1)
            attn_ref[start : start + step, :] = jnp.where(lane < HEAD, sides[0], sides[1]).astype(BF)

    work = 2 * tokens * every * model
    keys_at = pl.BlockSpec((part, PAIR), lambda i: (0, i))
    values_at = pl.BlockSpec((part, PAIR), lambda i: (0, i + pairs))
    return pl.pallas_call(
        kernel,
        grid=(pairs,),
        in_specs=[
            pl.BlockSpec((tokens, PAIR), lambda i: (0, i)),
            keys_at,
            keys_at,
            values_at,
            values_at,
            pl.BlockSpec(query_labels.shape, lambda i: (0, 0)),
            pl.BlockSpec(key_labels.shape, lambda i: (0, 0)),
        ],
        out_specs=[
            pl.BlockSpec((tokens, PAIR), lambda i: (0, i)),
            pl.BlockSpec((1, 2, tokens), lambda i: (i, 0, 0)),
        ],
        out_shape=[
            jax.ShapeDtypeStruct((tokens, model), BF),
            jax.ShapeDtypeStruct((pairs, 2, tokens), F32),
        ],
        scratch_shapes=[pltpu.VMEM((tokens, every), F32)],
        compiler_params=pltpu.CompilerParams(
            dimension_semantics=("arbitrary",), vmem_limit_bytes=40 << 20
        ),
        cost_estimate=pl.CostEstimate(
            flops=2 * work, transcendentals=work // PAIR, bytes_accessed=10 * every * model
        ),
        name="attention_forward",
    )(query, *mates, *mates, query_labels, key_labels)


def attention_backward(query, mates, grad, attn, lse, query_labels, key_labels, first, pairs):
    tokens = query.shape[0]
    part = mates[0].shape[0]
    every, total_pairs = 2 * part, query.shape[1] // PAIR
    model = pairs * PAIR
    step = math.gcd(part, 256)

    def kernel(q_ref, k0_ref, k1_ref, v0_ref, v1_ref, g_ref, a_ref, lse_ref, ql_ref, kl_ref,
               dq_ref, d0_ref, d1_ref, bias_ref):
        @pl.when(pl.program_id(0) == 0)
        def _():
            fill_bias(bias_ref, rows_of(ql_ref), columns_of(kl_ref))

        query_pair, grad_pair = q_ref[...], g_ref[...]
        overlap = (grad_pair.astype(F32) * a_ref[...].astype(F32)).T
        deltas = [
            jnp.sum(overlap[side * HEAD : (side + 1) * HEAD], axis=0, keepdims=True)
            for side in range(2)
        ]
        query_sides = [half_lanes(query_pair, side) for side in range(2)]
        grad_sides = [half_lanes(grad_pair, side) for side in range(2)]
        grad_query = [jnp.zeros((HEAD, tokens), F32), jnp.zeros((HEAD, tokens), F32)]
        for mate, (k_ref, v_ref, d_ref) in enumerate(((k0_ref, v0_ref, d0_ref), (k1_ref, v1_ref, d1_ref))):
            keys_across = k_ref[...].astype(F32).T.astype(BF)
            for start in range(0, part, step):
                rows = slice(start, start + step)
                grad_keys, grad_values = [], []
                for side in range(2):
                    logits = back_product(k_ref[rows, :], query_sides[side])
                    logits = logits + bias_ref[mate * part + start : mate * part + start + step, :]
                    probs = jnp.exp(logits - lse_ref[0, side : side + 1, :])
                    grad_probs = back_product(v_ref[rows, :], grad_sides[side])
                    grad_logits = (probs * (grad_probs - deltas[side])).astype(BF)
                    grad_values.append(product(probs.astype(BF), grad_sides[side]))
                    grad_keys.append(product(grad_logits, query_sides[side]))
                    grad_query[side] = grad_query[side] + product(
                        keys_across[side * HEAD : (side + 1) * HEAD, rows], grad_logits
                    )
                d_ref[0, rows, :] = (grad_keys[0] + grad_keys[1]).astype(BF)
                d_ref[1, rows, :] = (grad_values[0] + grad_values[1]).astype(BF)
        dq_ref[...] = (jnp.concatenate(grad_query, axis=0).T * SCALE).astype(BF)

    work = 2 * tokens * every * model
    own = pl.BlockSpec((tokens, PAIR), lambda i: (0, i + first))
    keys_at = pl.BlockSpec((part, PAIR), lambda i: (0, i + first))
    values_at = pl.BlockSpec((part, PAIR), lambda i: (0, i + first + total_pairs))
    mate_out = pl.BlockSpec((2, part, PAIR), lambda i: (0, 0, i))
    return pl.pallas_call(
        kernel,
        grid=(pairs,),
        in_specs=[
            own,
            keys_at,
            keys_at,
            values_at,
            values_at,
            own,
            own,
            pl.BlockSpec((1, 2, tokens), lambda i: (i + first, 0, 0)),
            pl.BlockSpec(query_labels.shape, lambda i: (0, 0)),
            pl.BlockSpec(key_labels.shape, lambda i: (0, 0)),
        ],
        out_specs=[pl.BlockSpec((tokens, PAIR), lambda i: (0, i)), mate_out, mate_out],
        out_shape=[
            jax.ShapeDtypeStruct((tokens, model), BF),
            jax.ShapeDtypeStruct((2, part, model), BF),
            jax.ShapeDtypeStruct((2, part, model), BF),
        ],
        scratch_shapes=[pltpu.VMEM((every, tokens), F32)],
        compiler_params=pltpu.CompilerParams(
            dimension_semantics=("arbitrary",), vmem_limit_bytes=40 << 20
        ),
        cost_estimate=pl.CostEstimate(
            flops=5 * work, transcendentals=work // PAIR, bytes_accessed=12 * every * model
        ),
        name="attention_backward",
    )(query, *mates, *mates, grad, attn, lse, query_labels, key_labels)


def gated(normed, weight, bias_rows):
    tokens, model = normed.shape
    hidden_units = weight.shape[1]
    width = math.gcd(bias_rows.shape[1], 512)
    per_row = bias_rows.shape[1] // width
    rows = math.gcd(tokens, 128)
    bias = bias_rows.reshape(-1, 1, width)

    def kernel(x_ref, w_ref, b_ref, act_ref, slope_ref):
        for start in range(0, tokens, rows):
            gate = jnp.dot(
                x_ref[start : start + rows, :], w_ref[...], preferred_element_type=F32
            ) + b_ref[0]
            share = 0.5 + 0.5 * lax.erf(gate * math.sqrt(0.5))
            density = jnp.exp(gate * gate * -0.5) * (1.0 / math.sqrt(2.0 * math.pi))
            act_ref[start : start + rows, :] = (gate * share).astype(BF)
            slope_ref[start : start + rows, :] = (share + gate * density).astype(BF)

    block = pl.BlockSpec((tokens, width), lambda i: (0, i))
    return pl.pallas_call(
        kernel,
        grid=(hidden_units // width,),
        in_specs=[
            pl.BlockSpec((tokens, model), lambda i: (0, 0)),
            pl.BlockSpec((model, width), lambda i: (0, i)),
            pl.BlockSpec((1, 1, width), lambda i: (i, 0, 0)),
        ],
        out_specs=[block, block],
        out_shape=[jax.ShapeDtypeStruct((tokens, hidden_units), BF)] * 2,
        compiler_params=pltpu.CompilerParams(
            dimension_semantics=("arbitrary",), vmem_limit_bytes=40 << 20
        ),
        cost_estimate=pl.CostEstimate(
            flops=2 * tokens * model * hidden_units,
            transcendentals=2 * tokens * hidden_units,
            bytes_accessed=2 * (model + 2 * tokens) * hidden_units,
        ),
        name="gated",
    )(normed, weight, bias)


def gated_backward(grad_low, slope, weight_down, weight_up):
    tokens, model = grad_low.shape
    hidden_units = slope.shape[1]
    width = math.gcd(hidden_units, 512)
    steps = hidden_units // width
    rows = math.gcd(tokens, 256)

    def kernel(g_ref, s_ref, down_ref, up_ref, gate_ref, bias_ref, out_ref, acc_ref):
        @pl.when(pl.program_id(0) == 0)
        def _():
            acc_ref[...] = jnp.zeros_like(acc_ref)

        column = jnp.zeros((1, width), F32)
        for start in range(0, tokens, rows):
            cut = slice(start, start + rows)
            pulled = back_product(g_ref[cut, :], down_ref[...]) * s_ref[cut, :].astype(F32)
            low = pulled.astype(BF)
            gate_ref[cut, :] = low
            column = column + jnp.sum(low.astype(F32), axis=0, keepdims=True)
            acc_ref[cut, :] += back_product(low, up_ref[...])
        bias_ref[0] = column

        @pl.when(pl.program_id(0) == steps - 1)
        def _():
            out_ref[...] = acc_ref[...]

    return pl.pallas_call(
        kernel,
        grid=(steps,),
        in_specs=[
            pl.BlockSpec((tokens, model), lambda i: (0, 0)),
            pl.BlockSpec((tokens, width), lambda i: (0, i)),
            pl.BlockSpec((width, model), lambda i: (i, 0)),
            pl.BlockSpec((model, width), lambda i: (0, i)),
        ],
        out_specs=[
            pl.BlockSpec((tokens, width), lambda i: (0, i)),
            pl.BlockSpec((1, 1, width), lambda i: (i, 0, 0)),
            pl.BlockSpec((tokens, model), lambda i: (0, 0)),
        ],
        out_shape=[
            jax.ShapeDtypeStruct((tokens, hidden_units), BF),
            jax.ShapeDtypeStruct((steps, 1, width), F32),
            jax.ShapeDtypeStruct((tokens, model), F32),
        ],
        scratch_shapes=[pltpu.VMEM((tokens, model), F32)],
        compiler_params=pltpu.CompilerParams(
            dimension_semantics=("arbitrary",), vmem_limit_bytes=40 << 20
        ),
        cost_estimate=pl.CostEstimate(
            flops=4 * tokens * model * hidden_units,
            transcendentals=0,
            bytes_accessed=4 * (model + tokens) * hidden_units,
        ),
        name="gated_backward",
    )(grad_low, slope, weight_down, weight_up)


def weight_terms(grid, jobs):
    tokens, height = jobs[0][0][0].shape
    shards = grid.shards
    rows = height // shards
    widths = [rights[0].shape[1] for _, rights in jobs]
    columns = sum(widths)
    if rows % 16:
        acc = jnp.concatenate(
            [sum(outer_sum(left, right) for left, right in zip(*job)) for job in jobs], axis=1
        )
        acc = acc.astype(BF).reshape(shards // 2, 2, rows, columns)
        return tuple(pick(acc, lax.rem(grid.at["c"] + k, 2), 1) for k in range(2))
    lefts = [left for job in jobs for left in job[0]]
    rights = [right for job in jobs for right in job[1]]
    count, depth = len(lefts), len(jobs[0][0])
    block = 256
    pairs = block // (2 * rows)

    def kernel(at_ref, *refs):
        left_refs, right_refs = refs[:count], refs[count : 2 * count]
        kept_ref, sent_ref = refs[2 * count :]
        upper = at_ref[4] == 1
        begin = 0
        for job, width in enumerate(widths):
            chunk = math.gcd(width, 1024) if width % 1024 == 0 else math.gcd(width, 512)
            turn = slice(job * depth, (job + 1) * depth)
            for start in range(0, width, chunk):
                acc = None
                for left, right in zip(left_refs[turn], right_refs[turn]):
                    part = outer_sum(left[...], right[:, start : start + chunk])
                    acc = part if acc is None else acc + part
                acc = acc.reshape(pairs, 2, rows, chunk)
                at = slice(begin + start, begin + start + chunk)
                kept_ref[:, :, at] = jnp.where(upper, acc[:, 1], acc[:, 0]).astype(BF)
                sent_ref[:, :, at] = jnp.where(upper, acc[:, 0], acc[:, 1]).astype(BF)
            begin += width

    out = pl.BlockSpec((pairs, rows, columns), lambda i: (i, 0, 0))
    return pl.pallas_call(
        kernel,
        grid=(height // block,),
        in_specs=[pl.BlockSpec(memory_space=pltpu.SMEM)]
        + [pl.BlockSpec((tokens, block), lambda i: (0, i))] * count
        + [
            pl.BlockSpec((tokens, right.shape[1]), lambda i: (0, 0), pipeline_mode=pl.Buffered(1))
            for right in rights
        ],
        out_specs=[out, out],
        out_shape=[jax.ShapeDtypeStruct((shards // 2, rows, columns), BF)] * 2,
        compiler_params=pltpu.CompilerParams(
            dimension_semantics=("arbitrary",), vmem_limit_bytes=48 << 20
        ),
        cost_estimate=pl.CostEstimate(
            flops=2 * depth * tokens * height * columns,
            transcendentals=0,
            bytes_accessed=2 * height * columns + 2 * depth * tokens * (height + columns),
        ),
        name="weight_terms",
    )(grid.places, *lefts, *rights)


class Grid:
    def __init__(self, sizes):
        self.size = dict(sizes)
        self.at = {name: lax.axis_index(name) for name in sizes}
        self.places = jnp.stack([self.at[name] for name in sizes]).astype(jnp.int32)
        self.shards = math.prod(sizes.values())
        index = 0
        for name in sizes:
            index = index * sizes[name] + self.at[name]
        self.shard = index

    def shift(self, tensor, axis, step):
        n = self.size[axis]
        return lax.ppermute(tensor, axis, [(i, (i + step) % n) for i in range(n)])

    def far_steps(self):
        return [(a, b) for a in range(self.size["h"]) for b in range(self.size["z"])]

    def far_shift(self, tensor, step):
        high, deep = self.size["h"], self.size["z"]
        pairs = [
            (a * deep + b, ((a + step[0]) % high) * deep + (b + step[1]) % deep)
            for a in range(high)
            for b in range(deep)
        ]
        return lax.ppermute(tensor, ("h", "z"), pairs)

    def swapped(self, tensor):
        return lax.ppermute(tensor, ("x", "c"), [(1, 2), (2, 1)])

    def choose(self, tensor, moved):
        return jnp.where(self.at["x"] == self.at["c"], tensor, moved)

    def mates(self, tensor):
        if self.size["h"] > 1:
            tensor = lax.all_gather(tensor, "h", axis=0, tiled=True)
        return tensor, self.shift(tensor, "c", 1)


def place(places, pieces, out_shapes, moves):
    count = len(pieces)
    landed = [pltpu.VMEM(piece.shape, piece.dtype) for piece in pieces]

    def kernel(at_ref, *refs):
        ins, outs = refs[:count], refs[count : count + len(out_shapes)]
        held, load_sems, store_sems = refs[-2 - count : -2], refs[-2], refs[-1]
        loads = [
            pltpu.make_async_copy(source, target, load_sems.at[i])
            for i, (source, target) in enumerate(zip(ins, held))
        ]
        for load in loads:
            load.start()
        stores = []
        ready = -1
        for piece, source, target in moves(at_ref, held, outs):
            while ready < piece:
                ready += 1
                loads[ready].wait()
            store = pltpu.make_async_copy(source, target, store_sems.at[len(stores)])
            store.start()
            stores.append(store)
        for store in stores:
            store.wait()

    moved = sum(math.prod(s.shape) * 2 for s in out_shapes)
    return pl.pallas_call(
        kernel,
        out_shape=out_shapes,
        in_specs=[pl.BlockSpec(memory_space=pltpu.SMEM)]
        + [pl.BlockSpec(memory_space=pl.ANY)] * count,
        out_specs=[pl.BlockSpec(memory_space=pl.ANY)] * len(out_shapes),
        scratch_shapes=landed
        + [pltpu.SemaphoreType.DMA((count,)), pltpu.SemaphoreType.DMA((8 * count,))],
        compiler_params=pltpu.CompilerParams(vmem_limit_bytes=moved + (4 << 20)),
        cost_estimate=pl.CostEstimate(flops=0, transcendentals=0, bytes_accessed=2 * moved),
        name="place",
    )(places, *pieces)


class Gather:
    def __init__(self, grid, chunks, widths):
        self.grid, self.widths = grid, widths
        self.chunks = list(chunks)
        self.half = chunks[0].shape[0] // 2
        self.columns = sum(chunk.shape[1] for chunk in chunks)
        self.kind = chunks[0].dtype
        self.far = [None] * len(chunks)

    def new(self, *lead):
        return jax.ShapeDtypeStruct((*lead, self.half, self.columns), self.kind)

    def go_far(self, i):
        self.far[i] = [self.grid.far_shift(self.chunks[i], step) for step in self.grid.far_steps()[1:]]

    def make_lines(self):
        high, deep = self.grid.size["h"], self.grid.size["z"]
        steps, half = self.grid.far_steps(), self.half

        widths = [chunk.shape[1] for chunk in self.chunks]
        pieces = [
            (tensor, step, sum(widths[:i]), widths[i])
            for i, chunk in enumerate(self.chunks)
            for tensor, step in zip([chunk] + self.far[i], steps)
        ]

        def moves(at, ins, outs):
            listed = []
            for i, (ref, (_, step, offset, width)) in enumerate(zip(ins, pieces)):
                a = lax.rem(at[0] - step[0] + high, high)
                b = lax.rem(at[2] - step[1] + deep, deep)
                for colour in range(2):
                    listed.append(
                        (
                            i,
                            ref.at[pl.ds(colour * half, half)],
                            outs[colour].at[a, b, :, pl.ds(offset, width)],
                        )
                    )
            return listed

        self.sends = place(
            self.grid.places, [p[0] for p in pieces], [self.new(high, deep)] * 2, moves
        )

    def go_first(self):
        self.own = self.sends
        self.arrived = [
            self.grid.shift(t, name, k)
            for t, name in zip(self.sends, "xy")
            for k in range(1, self.grid.size[name])
        ]

    def make_planes(self):
        high, wide, deep, tall = (self.grid.size[name] for name in "hxzy")
        spots = [(0, 0), (1, 0)] + [(0, k) for k in range(1, wide)] + [(1, k) for k in range(1, tall)]

        def moves(at, ins, outs):
            return [(i, ref, outs[c].at[k]) for i, (ref, (c, k)) in enumerate(zip(ins, spots))]

        self.sends = place(
            self.grid.places,
            list(self.own) + self.arrived,
            [self.new(wide, high, deep), self.new(tall, high, deep)],
            moves,
        )

    def go_second(self):
        self.near = [(self.sends[0], 0, 0), (self.sends[1], 1, 0)]
        self.arrived = [
            self.grid.shift(t, name, k)
            for t, name in zip(self.sends, "yx")
            for k in range(1, self.grid.size[name])
        ]

    def go_pair_near(self):
        self.pairs = [(self.grid.shift(t, "c", 1), colour, k) for t, colour, k in self.near]

    def go_pair_far(self):
        counts = [(c, k) for c, name in enumerate("yx") for k in range(1, self.grid.size[name])]
        distant = [(t, c, k) for t, (c, k) in zip(self.arrived, counts)]
        self.near += distant
        self.pairs += [(self.grid.shift(t, "c", 1), colour, k) for t, colour, k in distant]

    def result(self):
        high, wide, deep, tall = (self.grid.size[name] for name in "hxzy")
        half, widths = self.half, self.widths
        pieces = [t + (0,) for t in self.near] + [t + (1,) for t in self.pairs]
        offsets = [sum(widths[:i]) for i in range(len(widths))]

        def moves(at, ins, outs):
            listed = []
            for i, (ref, (_, colour, far, kc)) in enumerate(zip(ins, pieces)):
                pc = lax.rem(at[4] + kc, 2)
                for k in range(wide if colour == 0 else tall):
                    kx, ky = (k, far) if colour == 0 else (far, k)
                    px = lax.rem(at[1] - kx + wide, wide)
                    py = lax.rem(at[3] - ky + tall, tall)
                    for out, offset, width in zip(outs, offsets, widths):
                        listed.append(
                            (
                                i,
                                ref.at[k, :, :, :, pl.ds(offset, width)],
                                out.at[:, px, :, py, pc, pl.ds(colour * half, half)],
                            )
                        )
            return listed

        full = place(
            self.grid.places,
            [t[0] for t in pieces],
            [
                jax.ShapeDtypeStruct((high, wide, deep, tall, 2, 2 * half, width), self.kind)
                for width in widths
            ],
            moves,
        )
        return [t.reshape(-1, width) for t, width in zip(full, widths)]


def pick(tensor, index, axis):
    return lax.dynamic_index_in_dim(tensor, index, axis, keepdims=False)


def total(parts):
    result = parts[0].astype(F32)
    for part in parts[1:]:
        result = result + part.astype(F32)
    return result


def tie(*groups):
    return lax.optimization_barrier(groups)


class Scatter:
    def __init__(self, grid, kept, sent):
        self.grid = grid
        sizes = [grid.size[name] for name in "hxzy"]
        self.rows, self.columns = kept.shape[1:]
        self.half = self.rows // 2
        kept = kept.reshape(*sizes, self.rows, self.columns)
        self.held = [[(kept, "hxzy", i * self.half)] for i in range(2)]
        self.picked = [{}, {}]
        self.sends = [sent.reshape(*sizes, self.rows, self.columns)]
        self.stage = 0

    def go(self):
        if self.stage == 0:
            self.arrived = [self.grid.shift(self.sends[0], "c", 1)]
        elif self.stage < 3:
            self.arrived = [self.grid.shift(t, *route) for t, route in zip(self.sends, self.routes)]
        else:
            self.arrived = [self.grid.far_shift(t, route) for t, route in zip(self.sends, self.routes)]

    def slices(self, i, extra):
        places = {**self.picked[i], **extra}
        parts = []
        for tensor, axes, row in self.held[i]:
            starts = [places.get(name, 0) for name in axes] + [row, 0]
            sizes = [1 if name in places else self.grid.size[name] for name in axes]
            part = lax.dynamic_slice(tensor, starts, sizes + [self.half, self.columns])
            left = [self.grid.size[name] for name in axes if name not in places]
            parts.append(part.reshape(*left, self.half, self.columns))
        return total(parts)

    def prepare(self):
        grid = self.grid
        if self.stage == 0:
            for i in range(2):
                self.held[i].append((self.arrived[0], "hxzy", i * self.half))
        else:
            for tensor, i in zip(self.arrived, self.owners):
                axes = "".join(name for name in "hxzy" if name not in self.picked[i])
                self.held[i].append((tensor, axes, 0))
        self.stage += 1
        if self.stage == 3:
            self.routes = [step for step in grid.far_steps() if step != (0, 0)]
            self.sends = [self.at_far(step).astype(BF) for step in self.routes]
            return
        self.sends, self.routes, self.owners = [], [], []
        for i, order in enumerate(("xy", "yx")):
            name = order[self.stage - 1]
            n, own = grid.size[name], grid.at[name]
            for k in range(1, n):
                self.sends.append(self.slices(i, {name: lax.rem(own + k, n)}).astype(BF))
                self.routes.append((name, k))
                self.owners.append(i)
            self.picked[i][name] = own

    def at_far(self, step):
        place = {
            name: lax.rem(self.grid.at[name] + k, self.grid.size[name]) for name, k in zip("hz", step)
        }
        return jnp.concatenate([self.slices(i, place) for i in range(2)], axis=0)

    def result(self):
        return total([self.at_far((0, 0))] + self.arrived)


def order(values, sent=(), got=()):
    values, sends, arrived = lax.optimization_barrier(
        (values, [s.sends for s in sent], [s.arrived for s in got])
    )
    for scatter, arrays in zip(sent, sends):
        scatter.sends = arrays
    for scatter, arrays in zip(got, arrived):
        scatter.arrived = arrays
    return values


def sum_far(grid, tensor):
    arrived = [grid.far_shift(tensor, s) for s in grid.far_steps() if s != (0, 0)]
    return total([tensor] + arrived).astype(tensor.dtype)


def sum_near(grid, tensor, name):
    arrived = [grid.shift(tensor, name, k) for k in range(1, grid.size[name])]
    return total([tensor] + arrived).astype(tensor.dtype)


def body(
    sizes,
    inputs,
    segment_ids,
    key_mask,
    lead_index,
    cotangent_first,
    cotangent_second,
    w_qkv,
    w_out,
    w_up,
    w_down,
    biases,
    up_bias,
    norm_gains,
    norm_shifts,
    lead_table,
):
    grid = Grid(sizes)
    tokens, model = inputs.shape[1], inputs.shape[2]
    shards = grid.shards
    share = model // shards
    tie = lax.optimization_barrier

    middle_up, middle_down = w_up.shape[1] // 2, w_down.shape[1] // 2
    one = Gather(grid, [w_qkv], [w_qkv.shape[1]])
    two = Gather(
        grid,
        [w_up[:, :middle_up], jnp.concatenate([w_up[:, middle_up:], w_out], axis=1)],
        [w_up.shape[1], w_out.shape[1]],
    )
    three = Gather(grid, [w_down[:, :middle_down], w_down[:, middle_down:]], [w_down.shape[1]])
    rows_small = jnp.concatenate([biases, norm_gains, norm_shifts, lead_table])
    lengths = [t.shape[0] for t in (biases, norm_gains, norm_shifts, lead_table)]
    cuts = [sum(lengths[:i]) for i in range(5)]
    lane = jnp.arange(model, dtype=jnp.int32)[None, :]
    to_lane = (lane == grid.shard * share + jnp.arange(share, dtype=jnp.int32)[:, None]).astype(BF)
    own_up = up_bias.shape[0]
    per_row = model // own_up
    up_rows = shards // per_row
    up_lane = (
        lane == (grid.shard % per_row) * own_up + jnp.arange(own_up, dtype=jnp.int32)[:, None]
    ).astype(BF)
    up_row = jnp.arange(up_rows, dtype=jnp.int32)[:, None] == grid.shard // per_row
    small = jnp.concatenate(
        [
            product(rows_small, to_lane),
            product(jnp.where(up_row, up_bias[None, :], jnp.zeros((), BF)), up_lane),
        ]
    )
    labels = jnp.concatenate(
        [segment_ids, key_mask, jnp.broadcast_to(lead_index.reshape(2, 1), (2, tokens))]
    )
    one.go_far(0)
    start_moved = grid.swapped(inputs[0])
    labels_moved = grid.swapped(labels)
    small = sum_near(grid, sum_near(grid, small.astype(BF), "c"), "y")
    one.far, labels_moved, start_moved, small = tie((one.far, labels_moved, start_moved, small))
    labels = grid.choose(labels, labels_moved)
    start_low = grid.choose(inputs[0], start_moved)
    one.make_lines()
    one.sends, two.chunks[0], small = tie((one.sends, two.chunks[0], small))
    one.go_first()
    two.go_far(0)
    small = sum_far(grid, sum_near(grid, small, "x"))
    one.arrived, two.far[0], small, labels = tie((one.arrived, two.far[0], small, labels))
    small = small.astype(F32)
    bias_full, gains, shifts, lead_rows = (small[cuts[i] : cuts[i + 1]] for i in range(4))
    bias_up = small[cuts[4] :]
    leads = (labels[2, 0], labels[3, 0])
    own_pos = (grid.at["h"] * 2 + grid.at["c"]) * tokens + jnp.arange(tokens, dtype=jnp.int32)
    own_labels = jnp.stack([labels[0], labels[1], own_pos], axis=1)
    key_labels = jnp.concatenate(grid.mates(own_labels))
    own_labels_across, key_labels_across = own_labels.T, key_labels.T
    high = grid.size["h"]

    one.make_planes()
    one.sends, two.chunks[1] = tie((one.sends, two.chunks[1]))
    one.go_second()
    two.go_far(1)
    one.arrived, two.far[1] = tie((one.arrived, two.far[1]))
    one.go_pair_near()
    one.go_pair_far()
    two.make_lines()
    crossed = [t[0] for t in one.pairs]
    crossed, two.sends, three.chunks[0] = tie((crossed, two.sends, three.chunks[0]))
    one.pairs = [(t,) + pair[1:] for t, pair in zip(crossed, one.pairs)]
    two.go_first()
    three.go_far(0)
    (weight_qkv,) = one.result()
    weights = {"qkv": weight_qkv}

    def before_exchange(values):
        values, two.arrived, three.far[0] = tie((values, two.arrived, three.far[0]))
        two.make_planes()
        values, two.sends, three.chunks[1] = tie((values, two.sends, three.chunks[1]))
        two.go_second()
        three.go_far(1)
        return values

    def after_attention(values):
        values, two.arrived, three.far[1] = tie((values, two.arrived, three.far[1]))
        two.go_pair_near()
        two.go_pair_far()
        three.make_lines()
        crossed = [t[0] for t in two.pairs]
        values, crossed, three.sends = tie((values, crossed, three.sends))
        two.pairs = [(t,) + pair[1:] for t, pair in zip(crossed, two.pairs)]
        three.go_first()
        weights["up"], weights["out"] = two.result()
        return values

    def before_gate(values):
        values, three.arrived = tie((values, three.arrived))
        three.make_planes()
        values, three.sends = tie((values, three.sends))
        three.go_second()
        three.go_pair_near()
        return values

    def after_gate(values):
        values, three.arrived = tie((values, three.arrived))
        three.go_pair_far()
        (weights["down"],) = three.result()
        return values

    def keep(values):
        return values

    def forward(start_in, lead_id, hooks):
        chooser = (jnp.arange(lead_rows.shape[0], dtype=jnp.int32) == lead_id).astype(F32)
        lead_vec = jnp.sum(chooser[:, None] * lead_rows, axis=0)
        hidden = start_in + lead_vec[None, :]
        normed = layer_norm(hidden, gains[0], shifts[0]).astype(BF)
        mixed = product(normed, weights["qkv"])
        query = (mixed[:, :model] + bias_full[0]).astype(BF) * jnp.asarray(SCALE, BF)
        both_bias = jnp.concatenate([jnp.zeros((model,), F32), bias_full[1]])
        keys_values = (mixed[:, model:] + both_bias).astype(BF)
        query, keys_values = hooks[0]((query, keys_values))
        mates = grid.mates(keys_values)
        attn_low, lse = attention_forward(query, mates, own_labels, key_labels_across)
        attn_low, lse = hooks[1]((attn_low, lse))
        middle = hidden + product(attn_low, weights["out"]) + bias_full[2]
        normed_mid = layer_norm(middle, gains[1], shifts[1]).astype(BF)
        normed_mid = hooks[2](normed_mid)
        activated, slope = gated(normed_mid, weights["up"], bias_up)
        activated, slope = hooks[3]((activated, slope))
        result = middle + product(activated, weights["down"]) + bias_full[3]
        saved = (
            hidden, normed, query, mates, lse, attn_low, middle, normed_mid, slope, activated, chooser,
        )
        return (result, saved)

    def backward(saved, grad_res, earlier, hooks):
        hidden, normed, query, mates, lse, attn_low, middle, normed_mid, slope, activated, chooser = saved
        last = earlier is not None
        operands, sums = {}, {}

        def start(name, **joined):
            operands.update(joined)
            if last:
                jobs = [tuple(zip(operands[part], earlier[part])) for part in joined]
                sums[name] = Scatter(grid, *weight_terms(grid, jobs))

        def then(values, sent=(), got=()):
            if not last:
                return values
            values = order(values, [sums[name] for name in sent], [sums[name] for name in got])
            for name in sent:
                sums[name].go()
            return values

        def step(values, names, begin=(), got=()):
            if not last:
                return values
            ready = [sums[name] for name in begin]
            values = order(values, ready, [sums[name] for name in (*names, *got)])
            for name in names:
                sums[name].prepare()
            return then(values, sent=[*names, *begin])

        grad_low = grad_res.astype(BF)
        start("down", down=(activated, grad_low))
        grad_low = then(grad_low, sent=["down"])
        bias_down = jnp.sum(grad_low.astype(F32), axis=0)
        grad_low = hooks[0](grad_low)
        grad_gate, bias_gate, grad_normed_mid = gated_backward(
            grad_low, slope, weights["down"], weights["up"]
        )
        grad_gate, grad_normed_mid = hooks[1]((grad_gate, grad_normed_mid))
        grad_gate, grad_normed_mid = step((grad_gate, grad_normed_mid), ["down"])
        start("up", up=(normed_mid, grad_gate))
        mid_pull = jax.vjp(layer_norm, middle, gains[1], shifts[1])[1]
        grad_mid_part, gain_mid, shift_mid = mid_pull(grad_normed_mid)
        grad_mid = grad_res + grad_mid_part
        grad_branch = grad_mid.astype(BF)
        grad_attn = back_product(grad_branch, weights["out"]).astype(BF)
        bias_attn = jnp.sum(grad_branch.astype(F32), axis=0)
        grad_attn = hooks[2](grad_attn)
        grad_attn = step(grad_attn, ["down"], begin=["up"])
        pairs = model // PAIR
        halves = (0, pairs // 2, pairs)

        def attend_back(half):
            first, count = halves[half], halves[half + 1] - halves[half]
            return attention_backward(
                query, mates, grad_attn, attn_low, lse, own_labels_across, key_labels, first, count
            )

        def mix(query_low, near, far):
            both = total([near, far])
            if high > 1:
                both = lax.psum_scatter(both.astype(BF), "h", scatter_dimension=1, tiled=True)
            both = both.astype(BF)
            return jnp.concatenate([query_low, both[0], both[1]], axis=1)

        query_low, near, sent = hooks[3](attend_back(0))
        query_low, near, sent, grad_attn = step((query_low, near, sent, grad_attn), ["down", "up"])
        far = grid.shift(sent, "c", 1)
        other_low, other_near, sent = attend_back(1)
        mixed_low = mix(query_low, near, far)
        start("mix", qkv0=(normed, mixed_low), out=(attn_low, grad_branch))
        other_low, other_near, sent, mixed_low = step(
            (other_low, other_near, sent, mixed_low), ["up"], begin=["mix"], got=["down"]
        )
        far = grid.shift(sent, "c", 1)
        mixed_high = mix(other_low, other_near, far)
        start("qkv1", qkv1=(normed, mixed_high))
        mixed_low, mixed_high = step((mixed_low, mixed_high), ["up", "mix"], begin=["qkv1"])
        grad_mixed = jnp.concatenate(
            [
                p[:, i * p.shape[1] // 3 : (i + 1) * p.shape[1] // 3]
                for i in range(3)
                for p in (mixed_low, mixed_high)
            ],
            axis=1,
        )
        grad_normed = back_product(grad_mixed, weights["qkv"])
        bias_query = jnp.sum(grad_mixed[:, :model].astype(F32), axis=0)
        bias_value = jnp.sum(grad_mixed[:, 2 * model :].astype(F32), axis=0)
        in_pull = jax.vjp(layer_norm, hidden, gains[0], shifts[0])[1]
        grad_in_part, gain_in, shift_in = in_pull(grad_normed)
        grad_start = grad_mid + grad_in_part
        grad_start = step(grad_start, ["mix", "qkv1"], got=["up"])
        lead_sum = jnp.sum(grad_start, axis=0)
        vectors = jnp.concatenate(
            [
                jnp.stack([bias_query, bias_value, bias_attn, bias_down, gain_in, gain_mid, shift_in, shift_mid]),
                chooser[:, None] * lead_sum[None, :],
                bias_gate.reshape(-1, model),
            ]
        )
        return (grad_start, operands, sums, vectors)

    result_first, saved_first = forward(
        start_low.astype(F32), leads[0], [before_exchange, after_attention, before_gate, after_gate]
    )
    first_low = result_first.astype(BF)
    first_low, seed_first, seed_second = tie((first_low, cotangent_first[0], cotangent_second[0]))
    moved = {"second": grid.swapped(seed_second)}

    def moves(begin, *names):
        def hook(values):
            values, taken = tie((values, {name: moved[name] for name in names}))
            moved.update(taken)
            if begin is None:
                return values
            values, sent = tie((values, begin[1]))
            moved[begin[0]] = grid.swapped(sent)
            return values

        return hook

    result_second, saved_second = forward(
        first_low.astype(F32),
        leads[1],
        [keep, moves(("first", seed_first), "second"), keep, moves(None, "first")],
    )
    second_low = result_second.astype(BF)
    seed_second = grid.choose(seed_second, moved["second"])
    seed_second, second_low = tie((seed_second, second_low))
    grad_between, operands, _, vectors_second = backward(
        saved_second,
        seed_second.astype(F32),
        None,
        [
            moves(("first_out", first_low)),
            moves(None, "first_out"),
            moves(("second_out", second_low)),
            moves(None, "second_out"),
        ],
    )
    seed_first = grid.choose(seed_first, moved["first"])
    first_low = grid.choose(first_low, moved["first_out"])
    second_low = grid.choose(second_low, moved["second_out"])
    grad_first, _, sums, vectors_first = backward(
        saved_first, seed_first.astype(F32) + grad_between, operands, [keep] * 4
    )
    vectors = vectors_second + vectors_first
    grad_low = grad_first.astype(BF)

    def step(values, names):
        scatters = [sums[name] for name in names]
        values = order(values, (), scatters)
        for scatter in scatters:
            scatter.prepare()
        values = order(values, scatters, ())
        for scatter in scatters:
            scatter.go()
        return values

    vectors = sum_near(grid, vectors, "c")
    vectors, grad_low = step((vectors, grad_low), ["mix", "qkv1"])
    grad_moved = grid.swapped(grad_low)
    vectors = sum_near(grid, vectors, "y")
    vectors, grad_moved = step((vectors, grad_moved), ["qkv1"])
    vectors = sum_far(grid, sum_near(grid, vectors, "x"))
    input_grad = grid.choose(grad_low, grad_moved).astype(F32)
    shares = {name: sums[name].result() for name in ("down", "up", "mix", "qkv1")}
    width = shares["qkv1"].shape[1] // 3
    parts = [shares["mix"], shares["qkv1"]]
    own_columns = lax.dynamic_slice_in_dim(vectors, grid.shard * share, share, 1)
    small_out = [own_columns[cuts[i] : cuts[i + 1]] for i in range(4)]
    up_out = lax.dynamic_slice(
        vectors, (cuts[4] + grid.shard // per_row, (grid.shard % per_row) * own_up), (1, own_up)
    )[0]
    return (
        first_low[None],
        second_low[None],
        input_grad[None],
        jnp.concatenate([p[:, i * width : (i + 1) * width] for i in range(3) for p in parts], axis=1),
        shares["mix"][:, 3 * width :],
        shares["up"],
        shares["down"],
        small_out[0],
        up_out,
        small_out[1],
        small_out[2],
        small_out[3],
    )


def solution(mesh):
    dp, fsdp = mesh.shape["dp"], mesh.shape["fsdp"]
    tall = fsdp // 8
    sizes = {"h": dp // 2, "x": 2, "z": 4, "y": tall, "c": 2}
    fine = Mesh(np.asarray(mesh.devices).reshape(tuple(sizes.values())), tuple(sizes))
    one, two, every = ("z", "y", "c"), ("h", "x"), ("h", "x", "z", "y", "c")
    placed = (
        P(one, two, None),
        P(one, two),
        P(one, two),
        P(one, None),
        P(one, two, None),
        P(one, two, None),
        P(every, None),
        P(every, None),
        P(every, None),
        P(every, None),
        P(None, every),
        P(every),
        P(None, every),
        P(None, every),
        P(None, every),
    )
    return jax.shard_map(
        partial(body, sizes),
        mesh=fine,
        in_specs=placed,
        out_specs=(
            P(one, two, None),
            P(one, two, None),
            P(one, two, None),
            P(every, None),
            P(every, None),
            P(every, None),
            P(every, None),
            P(None, every),
            P(every),
            P(None, every),
            P(None, every),
            P(None, every),
        ),
        check_vma=False,
    )
```

time: 895 us -> 636 us (0.71)
  matrix products: 202 us -> 35.3 us
  Pallas kernels: 123 us -> 229 us
  starting transfers between devices: 173 us -> 99.8 us
  local copies, waits for them, and re-layouts: 123 us -> 52.4 us
  other arithmetic: 112 us -> 82.5 us
  waiting for transfers between devices: 147 us -> 123 us
    pallas_call x4 -> x12, Pallas kernels: 60.6 us -> 161 us  [the longest x4 60.8 us: attention_backward(): pl.pallas_call(kernel, grid=(pairs,), in_specs=[own, keys_at, keys_at, va...]
    dot_general x8, matrix products: 82.1 us -> 23.4 us  [product(): return jnp.dot(left_side, right_side, preferred_element_type=F32)]
    dot_general x10 -> x0, matrix products: 57.4 us -> none  [outer_sum(): lax.dot_general(left_side, right_side, ACROSS, preferred_element_type=F32)]
    ppermute x7, starting transfers between devices: 57.7 us -> 7.03 us  [swapped(): return lax.ppermute(tensor, ('x', 'c'), [(1, 2), (2, 1)])]
    dot_general x8 -> x4, matrix products: 62.4 us -> 11.9 us  [back_product(): lax.dot_general(left_side, right_side, WITHIN, preferred_element_type=F32)]
    ppermute x82 -> x57, waiting for transfers between devices: 94.2 us -> 76.3 us  [shift(): return lax.ppermute(tensor, axis, [(i, (i + step) % n) for i in range(n)])]
    another operation x18 -> x0, other arithmetic: 16.7 us -> none  [the longest x10 12.7 us: rows(): jnp.stack([jnp.where(first, tensor, other), jnp.where(first, other, tenso...]
    squeeze x9 -> x5, local copies, waits for them, and re-layouts: 17.4 us -> 0.86 us  [the longest x1 0.58 us: body(): lax.dynamic_slice(vectors, (cuts[4] + grid.shard // per_row, grid.shard %...]
  transfers between devices with their start and end apart: 119 -> 97, of which waited for: 31 -> 43; matrix products, arithmetic and copies ran while one was open for 30% -> 9% of each run, Pallas kernels for 12% -> 31%
where the time goes in v3:
time: 636 us; the launch traced here: 625 us
  Pallas kernels  229 us (36%)
  waiting for transfers between devices  123 us (19%)
  starting transfers between devices  99.8 us (16%)
  other arithmetic  82.5 us (13%)
  local copies, waits for them, and re-layouts  52.4 us (8%)
  matrix products  35.3 us (6%)
    ppermute x57, waiting for transfers between devices, shift(): return lax.ppermute(tensor, axis, [(i, (i + step) % n) for i in range(n)])  76.3 us
    pallas_call x4, Pallas kernels, attention_backward(): pl.pallas_call(kernel, grid=(pairs,), in_specs=[own, keys_at, keys_at, va...  60.8 us
    pallas_call x4, Pallas kernels, weight_terms(): pl.pallas_call(kernel, grid=(height // block,), in_specs=[pl.BlockSpec(me...  49 us
    ppermute x57, starting transfers between devices, shift(): return lax.ppermute(tensor, axis, [(i, (i + step) % n) for i in range(n)])  48.7 us
    ppermute x33, waiting for transfers between devices, far_shift(): return lax.ppermute(tensor, ('h', 'z'), pairs)  47 us
    ppermute x33, starting transfers between devices, far_shift(): return lax.ppermute(tensor, ('h', 'z'), pairs)  44.1 us
    unnamed x329, local copies, waits for them, and re-layouts  40.6 us
    pallas_call x2, Pallas kernels, attention_forward(): pl.pallas_call(kernel, grid=(pairs,), in_specs=[pl.BlockSpec((tokens, PAI...  40 us
  transfers between devices with their start and end apart: 97, of which 43 were waited for; matrix products, arithmetic and copies ran while one was open for 9% of the time, Pallas kernels for 31%

profile of v3, /device:TPU:0, one launch (start us, length us, event | category | flops | bytes accessed | tf_op | source)
XLA Modules:
  0.0 625.4 jit_solution(7594423896564826156)
XLA Ops:
  0.7 4.1 collective-permute-start.1
  23.8 8.7 %collective-permute-start.12 = (bf16[20,1024]{1,0:T(8,128)(2,1)S(1)}, bf16[20,1024]{1,0:T(8,128)(2,1)S(1)}, u32[]{:S(2)}, u32[]{:S(2)}) collective-permute-start(bf16[20,1024]{1,0:T(8,128)(2,1)S(1)} %add_convert_fusion.20), channel_id=1, source_target_pairs={{0,16},{16,0},{1,17},{17,1},{2,18},{18,2},{3,19},{19,3},{4,20},{20... | collective-permute-start | bytes 122888 | tf_op jit(solution)/shard_map/ppermute | solution.py:377
  45.4 8.1 %collective-permute-done.10.refs_2_ = bf16[32,2048]{1,0:T(8,128)(2,1)S(1)} collective-permute-done((bf16[32,2048]{1,0:T(8,128)(2,1)S(1)}, bf16[32,2048]{1,0:T(8,128)(2,1)S(1)}, u32[]{:S(2)}, u32[]{:S(2)}) %collective-permute-start.10) | collective-permute-done | bytes 131104 | tf_op jit(solution)/shard_map/ppermute | solution.py:389
  65.9 9.1 %collective-permute-done.19.refs_6_ = bf16[32,3072]{1,0:T(8,128)(2,1)S(1)} collective-permute-done((bf16[32,3072]{1,0:T(8,128)(2,1)S(1)}, bf16[32,3072]{1,0:T(8,128)(2,1)S(1)}, u32[]{:S(2)}, u32[]{:S(2)}) %collective-permute-start.19) | collective-permute-done | bytes 196640 | tf_op jit(solution)/shard_map/ppermute | solution.py:389
  98.9 5.3 collective-permute-done.25.refs_2_
  117.5 20.1 %attention_forward.2 = (bf16[512,1024]{1,0:T(8,128)(2,1)S(1)}, f32[8,2,512]{2,1,0:T(2,128)S(1)}) custom-call(bf16[512,1024]{1,0:T(8,128)(2,1)S(1)} %fusion.16.q_ref, bf16[512,2048]{1,0:T(8,128)(2,1)S(1)} %fusion.1.k0_ref.v0_ref, bf16[512,2048]{1,0:T(8,128)(2,1)} %collective-permute-done.30.k1_ref.v1_ref, bf16[512,2048]{1,0:T(8,128)(2,1)S(1)} %fusion.1.k0_ref.v0_ref, ...), custom_call_target="tpu_custom_call" | custom-call | flops 2147483648 | bytes 10485760 | tf_op jit(solution)/shard_map/attention_forward/pallas_call | solution.py:94
  148.8 4.3 place.15
  167.2 10.7 %gated.2 = (bf16[512,4096]{1,0:T(8,128)(2,1)S(1)}, bf16[512,4096]{1,0:T(8,128)(2,1)S(1)}) custom-call(bf16[512,1024]{1,0:T(8,128)(2,1)S(1)} %copy-done.36, bf16[1024,4096]{1,0:T(8,128)(2,1)} %bitcast.439, f32[8,1,512]{2,1,0:T(1,128)S(1)} %reshape.1353.b_ref), custom_call_target="tpu_custom_call" | custom-call | flops 4294967296 | bytes 16777216 | tf_op jit(solution)/shard_map/gated/pallas_call | solution.py:223
  177.9 10.3 %collective-permute-done.43.refs_2_ = bf16[2,1,4,64,1024]{4,3,2,1,0:T(8,128)(2,1)} collective-permute-done((bf16[2,1,4,64,1024]{4,3,2,1,0:T(8,128)(2,1)S(1)}, bf16[2,1,4,64,1024]{4,3,2,1,0:T(8,128)(2,1)}, u32[]{:S(2)}, u32[]{:S(2)}) %collective-permute-start.43) | collective-permute-done | bytes 1048608 | tf_op jit(solution)/shard_map/ppermute | solution.py:377
  193.1 4.0 place.17
  197.1 4.5 add_convert_fusion.11
  203.0 5.4 fusion.97
  216.4 19.9 %attention_forward.3 = (bf16[512,1024]{1,0:T(8,128)(2,1)S(1)}, f32[8,2,512]{2,1,0:T(2,128)S(1)}) custom-call(bf16[512,1024]{1,0:T(8,128)(2,1)S(1)} %fusion.17.q_ref, bf16[512,2048]{1,0:T(8,128)(2,1)S(1)} %fusion.k0_ref.v0_ref, bf16[512,2048]{1,0:T(8,128)(2,1)S(1)} %collective-permute-done.49.k1_ref.v1_ref, bf16[512,2048]{1,0:T(8,128)(2,1)S(1)} %fusion.k0_ref.v0_ref, ...), custom_call_target="tpu_custom_call" | custom-call | flops 2147483648 | bytes 10485760 | tf_op jit(solution)/shard_map/attention_forward/pallas_call | solution.py:94
  243.3 11.1 %gated.3 = (bf16[512,4096]{1,0:T(8,128)(2,1)S(1)}, bf16[512,4096]{1,0:T(8,128)(2,1)S(1)}) custom-call(bf16[512,1024]{1,0:T(8,128)(2,1)S(1)} %add_convert_fusion.9.x_ref.refs_1_, bf16[1024,4096]{1,0:T(8,128)(2,1)} %bitcast.440, f32[8,1,512]{2,1,0:T(1,128)S(1)} %reshape.1353.b_ref), custom_call_target="tpu_custom_call" | custom-call | flops 4294967296 | bytes 16777216 | tf_op jit(solution)/shard_map/gated/pallas_call | solution.py:223
  254.5 5.5 add_convert_fusion.8
  262.9 14.4 %gated_backward.2 = (bf16[512,4096]{1,0:T(8,128)(2,1)S(1)}, f32[8,1,512]{2,1,0:T(1,128)S(1)}, f32[512,1024]{1,0:T(8,128)S(1)}) custom-call(bf16[512,1024]{1,0:T(8,128)(2,1)S(1)} %broadcast_select_fusion.1.g_ref.refs_3_, bf16[512,4096]{1,0:T(8,128)(2,1)S(1)} %copy-done.61, bf16[4096,1024]{1,0:T(8,128)(2,1)} %bitcast.423, bf16[1024,4096]{1,0:T(8,128)(2,1)} %bitcast.441), custom_call_target="tpu_custom_call" | custom-call | flops 8589934592 | bytes 25165824 | tf_op jit(solution)/shard_map/gated_backward/pallas_call | solution.py:271
  293.8 14.9 %attention_backward.5 = (bf16[512,512]{1,0:T(8,128)(2,1)S(1)}, bf16[2,512,512]{2,1,0:T(8,128)(2,1)S(1)}, bf16[2,512,512]{2,1,0:T(8,128)(2,1)S(1)}) custom-call(bf16[512,1024]{1,0:T(8,128)(2,1)S(1)} %copy-done.9, bf16[512,2048]{1,0:T(8,128)(2,1)S(1)} %copy-done.1, bf16[512,2048]{1,0:T(8,128)(2,1)S(1)} %copy-done.3, bf16[512,2048]{1,0:T(8,128)(2,1)S(1)} %copy-done.1, ...), custom_call_target="tpu_custom_call" | custom-call | flops 2684354560 | bytes 6291456 | tf_op jit(solution)/shard_map/attention_backward/pallas_call | solution.py:172
  308.7 5.3 collective-permute-start.55
  314.1 14.9 %attention_backward.4 = (bf16[512,512]{1,0:T(8,128)(2,1)S(1)}, bf16[2,512,512]{2,1,0:T(8,128)(2,1)S(1)}, bf16[2,512,512]{2,1,0:T(8,128)(2,1)S(1)}) custom-call(bf16[512,1024]{1,0:T(8,128)(2,1)S(1)} %copy-done.9, bf16[512,2048]{1,0:T(8,128)(2,1)S(1)} %copy-done.1, bf16[512,2048]{1,0:T(8,128)(2,1)S(1)} %copy-done.3, bf16[512,2048]{1,0:T(8,128)(2,1)S(1)} %copy-done.1, ...), custom_call_target="tpu_custom_call" | custom-call | flops 2684354560 | bytes 6291456 | tf_op jit(solution)/shard_map/attention_backward/pallas_call | solution.py:172
  342.9 18.0 %weight_terms.4 = (bf16[16,128,1024]{2,1,0:T(8,128)(2,1)}, bf16[16,128,1024]{2,1,0:T(8,128)(2,1)}) custom-call(s32[5]{0:T(128)S(1)} %stack.56.at_ref, bf16[512,4096]{1,0:T(8,128)(2,1)} %copy-done.58, bf16[512,4096]{1,0:T(8,128)(2,1)} %copy-done.59, bf16[512,1024]{1,0:T(8,128)(2,1)S(1)} %get-tuple-element.375.refs_2_.g_ref, bf16[512,1024]{1,0:T(8,128)(2,1)S(1)} %copy-done.7), custom_call_target="tpu_custom_call" | custom-call | flops 8589934592 | bytes 18874368 | tf_op jit(solution)/shard_map/weight_terms/pallas_call | solution.py:341
  364.4 14.8 %gated_backward.3 = (bf16[512,4096]{1,0:T(8,128)(2,1)S(1)}, f32[8,1,512]{2,1,0:T(1,128)S(1)}, f32[512,1024]{1,0:T(8,128)S(1)}) custom-call(bf16[512,1024]{1,0:T(8,128)(2,1)S(1)} %copy-done.24, bf16[512,4096]{1,0:T(8,128)(2,1)S(1)} %copy-done.57, bf16[4096,1024]{1,0:T(8,128)(2,1)} %bitcast.424, bf16[1024,4096]{1,0:T(8,128)(2,1)} %bitcast.442), custom_call_target="tpu_custom_call" | custom-call | flops 8589934592 | bytes 25165824 | tf_op jit(solution)/shard_map/gated_backward/pallas_call | solution.py:271
  387.9 3.9 convert_reduce_fusion.2
  395.1 14.6 %weight_terms.5 = (bf16[16,32,4096]{2,1,0:T(8,128)(2,1)}, bf16[16,32,4096]{2,1,0:T(8,128)(2,1)}) custom-call(s32[5]{0:T(128)S(1)} %stack.56.at_ref, bf16[512,1024]{1,0:T(8,128)(2,1)S(1)} %copy-done.37, bf16[512,1024]{1,0:T(8,128)(2,1)S(1)} %copy-done.39, bf16[512,4096]{1,0:T(8,128)(2,1)} %copy-done.63, bf16[512,4096]{1,0:T(8,128)(2,1)} %copy-done.62), custom_call_target="tpu_custom_call" | custom-call | flops 8589934592 | bytes 18874368 | tf_op jit(solution)/shard_map/weight_terms/pallas_call | solution.py:341
  421.6 15.4 %attention_backward.6 = (bf16[512,512]{1,0:T(8,128)(2,1)S(1)}, bf16[2,512,512]{2,1,0:T(8,128)(2,1)S(1)}, bf16[2,512,512]{2,1,0:T(8,128)(2,1)S(1)}) custom-call(bf16[512,1024]{1,0:T(8,128)(2,1)S(1)} %copy-done.5, bf16[512,2048]{1,0:T(8,128)(2,1)S(1)} %fusion.1.k0_ref.v0_ref, bf16[512,2048]{1,0:T(8,128)(2,1)} %collective-permute-done.30.k1_ref.v1_ref, ...), custom_call_target="tpu_custom_call" | custom-call | flops 2684354560 | bytes 6291456 | tf_op jit(solution)/shard_map/attention_backward/pallas_call | solution.py:172
  453.0 15.6 %attention_backward.7 = (bf16[512,512]{1,0:T(8,128)(2,1)S(1)}, bf16[2,512,512]{2,1,0:T(8,128)(2,1)S(1)}, bf16[2,512,512]{2,1,0:T(8,128)(2,1)}) custom-call(bf16[512,1024]{1,0:T(8,128)(2,1)S(1)} %copy-done.5, bf16[512,2048]{1,0:T(8,128)(2,1)S(1)} %fusion.1.k0_ref.v0_ref, bf16[512,2048]{1,0:T(8,128)(2,1)} %collective-permute-done.30.k1_ref.v1_ref, ...), custom_call_target="tpu_custom_call" | custom-call | flops 2684354560 | bytes 6291456 | tf_op jit(solution)/shard_map/attention_backward/pallas_call | solution.py:172
  472.7 10.0 %weight_terms.6 = (bf16[16,32,2560]{2,1,0:T(8,128)(2,1)}, bf16[16,32,2560]{2,1,0:T(8,128)(2,1)}) custom-call(s32[5]{0:T(128)S(1)} %stack.56.at_ref, bf16[512,1024]{1,0:T(8,128)(2,1)S(1)} %copy-done.31, bf16[512,1024]{1,0:T(8,128)(2,1)S(1)} %copy-done.34, bf16[512,1024]{1,0:T(8,128)(2,1)S(1)} %copy-done.17, bf16[512,1024]{1,0:T(8,128)(2,1)S(1)} %copy-done.20, ...), custom_call_target="tpu_custom_call" | custom-call | flops 5368709120 | bytes 12582912 | tf_op jit(solution)/shard_map/weight_terms/pallas_call | solution.py:341
  482.8 10.6 %collective-permute-done.64 = bf16[1,2,4,16,4096]{4,3,2,1,0:T(8,128)(2,1)S(1)} collective-permute-done((bf16[1,2,4,16,4096]{4,3,2,1,0:T(8,128)(2,1)S(1)}, bf16[1,2,4,16,4096]{4,3,2,1,0:T(8,128)(2,1)S(1)}, u32[]{:S(2)}, u32[]{:S(2)}) %collective-permute-start.64) | collective-permute-done | bytes 1048608 | tf_op jit(solution)/shard_map/ppermute | solution.py:377
  508.4 6.4 %weight_terms.7 = (bf16[16,32,1536]{2,1,0:T(8,128)(2,1)S(1)}, bf16[16,32,1536]{2,1,0:T(8,128)(2,1)S(1)}) custom-call(s32[5]{0:T(128)S(1)} %stack.56.at_ref, bf16[512,1024]{1,0:T(8,128)(2,1)S(1)} %copy-done.32, bf16[512,1024]{1,0:T(8,128)(2,1)S(1)} %copy-done.35, bf16[512,1536]{1,0:T(8,128)(2,1)} %pad_maximum_fusion.2.refs_2_, ...), custom_call_target="tpu_custom_call" | custom-call | flops 3221225472 | bytes 8388608 | tf_op jit(solution)/shard_map/weight_terms/pallas_call | solution.py:341
  539.2 4.8 collective-permute-done.76
  544.0 5.4 collective-permute-done.77
  566.2 7.3 %collective-permute-done.81 = bf16[1,4,2,16,1536]{4,3,2,1,0:T(8,128)(2,1)} collective-permute-done((bf16[1,4,2,16,1536]{4,3,2,1,0:T(8,128)(2,1)}, bf16[1,4,2,16,1536]{4,3,2,1,0:T(8,128)(2,1)}, u32[]{:S(2)}, u32[]{:S(2)}) %collective-permute-start.81) | collective-permute-done | bytes 393248 | tf_op jit(solution)/shard_map/ppermute | solution.py:377
  592.1 9.5 %collective-permute-done.86 = bf16[1,4,16,1536]{3,2,1,0:T(8,128)(2,1)S(1)} collective-permute-done((bf16[1,4,16,1536]{3,2,1,0:T(8,128)(2,1)S(1)}, bf16[1,4,16,1536]{3,2,1,0:T(8,128)(2,1)S(1)}, u32[]{:S(2)}, u32[]{:S(2)}) %collective-permute-start.86) | collective-permute-done | bytes 196640 | tf_op jit(solution)/shard_map/ppermute | solution.py:377
  (673 shorter events, 305.2 us)
Async XLA Ops:
  32.5 21.0 %collective-permute-start.7 = (bf16[1,4,16,3072]{3,2,1,0:T(8,128)(2,1)S(1)}, bf16[1,4,16,3072]{3,2,1,0:T(8,128)(2,1)S(1)}, u32[]{:S(2)}, u32[]{:S(2)}) collective-permute-start(bf16[1,4,16,3072]{3,2,1,0:T(8,128)(2,1)S(1)} %get-tuple-element.259.refs_0_), channel_id=1, source_target_pairs={{0,16},{16,0},{1,17},{17,1},{2,18},{18,2},{3,19},{19,3},{4,20},{20... | collective-permute-start | bytes 1179656 | tf_op jit(solution)/shard_map/ppermute | solution.py:377
  32.6 20.9 %collective-permute-start.8 = (bf16[1,4,16,3072]{3,2,1,0:T(8,128)(2,1)S(1)}, bf16[1,4,16,3072]{3,2,1,0:T(8,128)(2,1)S(1)}, u32[]{:S(2)}, u32[]{:S(2)}) collective-permute-start(bf16[1,4,16,3072]{3,2,1,0:T(8,128)(2,1)S(1)} %get-tuple-element.260.refs_1_), channel_id=1, source_target_pairs={{0,2},{2,0},{1,3},{3,1},{4,6},{6,4},{5,7},{7,5},{8,10},{10,8},{9,1... | collective-permute-start | bytes 1179656 | tf_op jit(solution)/shard_map/ppermute | solution.py:377
  65.9 19.2 %collective-permute-start.21 = (bf16[2,1,4,16,3072]{4,3,2,1,0:T(8,128)(2,1)S(1)}, bf16[2,1,4,16,3072]{4,3,2,1,0:T(8,128)(2,1)S(1)}, u32[]{:S(2)}, u32[]{:S(2)}) collective-permute-start(bf16[2,1,4,16,3072]{4,3,2,1,0:T(8,128)(2,1)S(1)} %get-tuple-element.270.refs_0_), channel_id=1, source_target_pairs={{0,1},{1,0},{2,3},{3,2},{4,5},{5,4},{6,7},{7,6},{8,9},{9,8},{10,11... | collective-permute-start | bytes 2359304 | tf_op jit(solution)/shard_map/ppermute | solution.py:377
  107.5 31.5 %collective-permute-start.32 = (bf16[2,1,4,16,5120]{4,3,2,1,0:T(8,128)(2,1)}, bf16[2,1,4,16,5120]{4,3,2,1,0:T(8,128)(2,1)}, u32[]{:S(2)}, u32[]{:S(2)}) collective-permute-start(bf16[2,1,4,16,5120]{4,3,2,1,0:T(8,128)(2,1)} %get-tuple-element.300.refs_0_), channel_id=1, source_target_pairs={{0,2},{2,0},{1,3},{3,1},{4,6},{6,4},{5,7},{7,5},{8,10},{10,8},{9,1... | collective-permute-start | bytes 3932168 | tf_op jit(solution)/shard_map/ppermute | solution.py:377
  108.1 31.2 %collective-permute-start.33 = (bf16[2,1,4,16,5120]{4,3,2,1,0:T(8,128)(2,1)}, bf16[2,1,4,16,5120]{4,3,2,1,0:T(8,128)(2,1)}, u32[]{:S(2)}, u32[]{:S(2)}) collective-permute-start(bf16[2,1,4,16,5120]{4,3,2,1,0:T(8,128)(2,1)} %get-tuple-element.301.refs_1_), channel_id=1, source_target_pairs={{0,16},{16,0},{1,17},{17,1},{2,18},{18,2},{3,19},{19,3},{4,20},{20... | collective-permute-start | bytes 3932168 | tf_op jit(solution)/shard_map/ppermute | solution.py:377
  112.3 25.3 %collective-permute-start.36 = (bf16[128,512]{1,0:T(8,128)(2,1)S(1)}, bf16[128,512]{1,0:T(8,128)(2,1)S(1)}, u32[]{:S(2)}, u32[]{:S(2)}) collective-permute-start(bf16[128,512]{1,0:T(8,128)(2,1)S(1)} %get-tuple-element.302.refs_4_), channel_id=1, source_target_pairs={{0,12},{4,0},{8,4},{12,8},{1,13},{5,1},{9,5},{13,9},{2,14},{6,2},{... | collective-permute-start | bytes 393224 | tf_op jit(solution)/shard_map/ppermute | solution.py:389
  115.3 22.4 %collective-permute-start.35 = (bf16[128,512]{1,0:T(8,128)(2,1)S(1)}, bf16[128,512]{1,0:T(8,128)(2,1)S(1)}, u32[]{:S(2)}, u32[]{:S(2)}) collective-permute-start(bf16[128,512]{1,0:T(8,128)(2,1)S(1)} %get-tuple-element.302.refs_4_), channel_id=1, source_target_pairs={{0,8},{4,12},{8,0},{12,4},{1,9},{5,13},{9,1},{13,5},{2,10},{6,14},... | collective-permute-start | bytes 393224 | tf_op jit(solution)/shard_map/ppermute | solution.py:389
  116.1 22.1 %collective-permute-start.34 = (bf16[128,512]{1,0:T(8,128)(2,1)S(1)}, bf16[128,512]{1,0:T(8,128)(2,1)S(1)}, u32[]{:S(2)}, u32[]{:S(2)}) collective-permute-start(bf16[128,512]{1,0:T(8,128)(2,1)S(1)} %get-tuple-element.302.refs_4_), channel_id=1, source_target_pairs={{0,4},{4,8},{8,12},{12,0},{1,5},{5,9},{9,13},{13,1},{2,6},{6,10},{... | collective-permute-start | bytes 393224 | tf_op jit(solution)/shard_map/ppermute | solution.py:389
  164.0 24.2 %collective-permute-start.43 = (bf16[2,1,4,64,1024]{4,3,2,1,0:T(8,128)(2,1)S(1)}, bf16[2,1,4,64,1024]{4,3,2,1,0:T(8,128)(2,1)}, u32[]{:S(2)}, u32[]{:S(2)}) collective-permute-start(bf16[2,1,4,64,1024]{4,3,2,1,0:T(8,128)(2,1)S(1)} %get-tuple-element.332.refs_0_), channel_id=1, source_target_pairs={{0,2},{2,0},{1,3},{3,1},{4,6},{6,4},{5,7},{7,5},{8,10},{10,8},{9,1... | collective-permute-start | bytes 3145736 | tf_op jit(solution)/shard_map/ppermute | solution.py:377
  164.6 24.1 %collective-permute-start.44 = (bf16[2,1,4,64,1024]{4,3,2,1,0:T(8,128)(2,1)}, bf16[2,1,4,64,1024]{4,3,2,1,0:T(8,128)(2,1)}, u32[]{:S(2)}, u32[]{:S(2)}) collective-permute-start(bf16[2,1,4,64,1024]{4,3,2,1,0:T(8,128)(2,1)} %get-tuple-element.333.refs_1_), channel_id=1, source_target_pairs={{0,16},{16,0},{1,17},{17,1},{2,18},{18,2},{3,19},{19,3},{4,20},{20... | collective-permute-start | bytes 3145736 | tf_op jit(solution)/shard_map/ppermute | solution.py:377
  165.4 23.8 %collective-permute-start.45 = (bf16[2,1,4,64,1024]{4,3,2,1,0:T(8,128)(2,1)S(1)}, bf16[2,1,4,64,1024]{4,3,2,1,0:T(8,128)(2,1)S(1)}, u32[]{:S(2)}, u32[]{:S(2)}) collective-permute-start(bf16[2,1,4,64,1024]{4,3,2,1,0:T(8,128)(2,1)S(1)} %get-tuple-element.332.refs_0_), channel_id=1, source_target_pairs={{0,1},{1,0},{2,3},{3,2},{4,5},{5,4},{6,7},{7,6},{8,9},{9,8},{10,11... | collective-permute-start | bytes 3145736 | tf_op jit(solution)/shard_map/ppermute | solution.py:377
  165.5 23.8 %collective-permute-start.46 = (bf16[2,1,4,64,1024]{4,3,2,1,0:T(8,128)(2,1)}, bf16[2,1,4,64,1024]{4,3,2,1,0:T(8,128)(2,1)S(1)}, u32[]{:S(2)}, u32[]{:S(2)}) collective-permute-start(bf16[2,1,4,64,1024]{4,3,2,1,0:T(8,128)(2,1)} %get-tuple-element.333.refs_1_), channel_id=1, source_target_pairs={{0,1},{1,0},{2,3},{3,2},{4,5},{5,4},{6,7},{7,6},{8,9},{9,8},{10,11... | collective-permute-start | bytes 3145736 | tf_op jit(solution)/shard_map/ppermute | solution.py:377
  212.4 24.0 %collective-permute-start.50 = (bf16[512,1024]{1,0:T(8,128)(2,1)S(1)}, bf16[512,1024]{1,0:T(8,128)(2,1)S(1)}, u32[]{:S(2)}, u32[]{:S(2)}) collective-permute-start(bf16[512,1024]{1,0:T(8,128)(2,1)S(1)} %bitcast.461), channel_id=1, source_target_pairs={{1,16},{16,1},{3,18},{18,3},{5,20},{20,5},{7,22},{22,7},{9,24},{24... | collective-permute-start | bytes 3145736 | tf_op jit(solution)/shard_map/ppermute | solution.py:392
  285.1 43.9 %collective-permute-start.53 = (bf16[512,1024]{1,0:T(8,128)(2,1)}, bf16[512,1024]{1,0:T(8,128)(2,1)}, u32[]{:S(2)}, u32[]{:S(2)}) collective-permute-start(bf16[512,1024]{1,0:T(8,128)(2,1)} %add_convert_fusion.8), channel_id=1, source_target_pairs={{1,16},{16,1},{3,18},{18,3},{5,20},{20,5},{7,22},{22,7},{9,24},{24... | collective-permute-start | bytes 3145736 | tf_op jit(solution)/shard_map/ppermute | solution.py:392
  308.7 20.5 %collective-permute-start.55 = (bf16[2,512,512]{2,1,0:T(8,128)(2,1)S(1)}, bf16[2,512,512]{2,1,0:T(8,128)(2,1)S(1)}, u32[]{:S(2)}, u32[]{:S(2)}) collective-permute-start(bf16[2,512,512]{2,1,0:T(8,128)(2,1)S(1)} %get-tuple-element.371), channel_id=1, source_target_pairs={{0,1},{1,0},{2,3},{3,2},{4,5},{5,4},{6,7},{7,6},{8,9},{9,8},{10,11... | collective-permute-start | bytes 3145736 | tf_op jit(solution)/shard_map/ppermute | solution.py:377
  385.6 25.5 %collective-permute-start.57 = (bf16[1,4,2,64,1024]{4,3,2,1,0:T(8,128)(2,1)S(1)}, bf16[1,4,2,64,1024]{4,3,2,1,0:T(8,128)(2,1)S(1)}, u32[]{:S(2)}, u32[]{:S(2)}) collective-permute-start(bf16[1,4,2,64,1024]{4,3,2,1,0:T(8,128)(2,1)S(1)} %fusion.12), channel_id=1, source_target_pairs={{0,16},{16,0},{1,17},{17,1},{2,18},{18,2},{3,19},{19,3},{4,20},{20... | collective-permute-start | bytes 3145736 | tf_op jit(solution)/shard_map/ppermute | solution.py:377
  386.6 24.9 %collective-permute-start.58 = (bf16[1,2,4,64,1024]{4,3,2,1,0:T(8,128)(2,1)S(1)}, bf16[1,2,4,64,1024]{4,3,2,1,0:T(8,128)(2,1)S(1)}, u32[]{:S(2)}, u32[]{:S(2)}) collective-permute-start(bf16[1,2,4,64,1024]{4,3,2,1,0:T(8,128)(2,1)S(1)} %fusion.13), channel_id=1, source_target_pairs={{0,2},{2,0},{1,3},{3,1},{4,6},{6,4},{5,7},{7,5},{8,10},{10,8},{9,1... | collective-permute-start | bytes 3145736 | tf_op jit(solution)/shard_map/ppermute | solution.py:377
  415.0 22.0 %collective-permute-start.61 = (bf16[1,2,4,2,32,4096]{5,4,3,2,1,0:T(8,128)(2,1)}, bf16[1,2,4,2,32,4096]{5,4,3,2,1,0:T(8,128)(2,1)}, u32[]{:S(2)}, u32[]{:S(2)}) collective-permute-start(bf16[1,2,4,2,32,4096]{5,4,3,2,1,0:T(8,128)(2,1)} %bitcast.44), channel_id=1, source_target_pairs={{0,1},{1,0},{2,3},{3,2},{4,5},{5,4},{6,7},{7,6},{8,9},{9,8},{10,11... | collective-permute-start | bytes 12582920 | tf_op jit(solution)/shard_map/ppermute | solution.py:377
  415.0 22.0 %collective-permute-start.59 = (bf16[1,4,64,1024]{3,2,1,0:T(8,128)(2,1)}, bf16[1,4,64,1024]{3,2,1,0:T(8,128)(2,1)}, u32[]{:S(2)}, u32[]{:S(2)}) collective-permute-start(bf16[1,4,64,1024]{3,2,1,0:T(8,128)(2,1)} %get-tuple-element.399), channel_id=1, source_target_pairs={{0,2},{2,0},{1,3},{3,1},{4,6},{6,4},{5,7},{7,5},{8,10},{10,8},{9,1... | collective-permute-start | bytes 1572872 | tf_op jit(solution)/shard_map/ppermute | solution.py:377
  416.6 20.5 %collective-permute-start.60 = (bf16[1,4,64,1024]{3,2,1,0:T(8,128)(2,1)}, bf16[1,4,64,1024]{3,2,1,0:T(8,128)(2,1)}, u32[]{:S(2)}, u32[]{:S(2)}) collective-permute-start(bf16[1,4,64,1024]{3,2,1,0:T(8,128)(2,1)} %get-tuple-element.400), channel_id=1, source_target_pairs={{0,16},{16,0},{1,17},{17,1},{2,18},{18,2},{3,19},{19,3},{4,20},{20... | collective-permute-start | bytes 1572872 | tf_op jit(solution)/shard_map/ppermute | solution.py:377
  446.2 22.4 %collective-permute-start.62 = (bf16[2,512,512]{2,1,0:T(8,128)(2,1)S(1)}, bf16[2,512,512]{2,1,0:T(8,128)(2,1)S(1)}, u32[]{:S(2)}, u32[]{:S(2)}) collective-permute-start(bf16[2,512,512]{2,1,0:T(8,128)(2,1)S(1)} %get-tuple-element.416), channel_id=1, source_target_pairs={{0,1},{1,0},{2,3},{3,2},{4,5},{5,4},{6,7},{7,6},{8,9},{9,8},{10,11... | collective-permute-start | bytes 3145736 | tf_op jit(solution)/shard_map/ppermute | solution.py:377
  447.6 35.1 %collective-permute-start.65 = (bf16[128,1024]{1,0:T(8,128)(2,1)}, bf16[128,1024]{1,0:T(8,128)(2,1)S(1)}, u32[]{:S(2)}, u32[]{:S(2)}) collective-permute-start(bf16[128,1024]{1,0:T(8,128)(2,1)} %pad_maximum_fusion.4), channel_id=1, source_target_pairs={{0,4},{4,8},{8,12},{12,0},{1,5},{5,9},{9,13},{13,1},{2,6},{6,10},{... | collective-permute-start | bytes 786440 | tf_op jit(solution)/shard_map/ppermute | solution.py:389
  450.0 32.8 %collective-permute-start.66 = (bf16[128,1024]{1,0:T(8,128)(2,1)}, bf16[128,1024]{1,0:T(8,128)(2,1)S(1)}, u32[]{:S(2)}, u32[]{:S(2)}) collective-permute-start(bf16[128,1024]{1,0:T(8,128)(2,1)} %pad_maximum_fusion.5), channel_id=1, source_target_pairs={{0,8},{4,12},{8,0},{12,4},{1,9},{5,13},{9,1},{13,5},{2,10},{6,14},... | collective-permute-start | bytes 786440 | tf_op jit(solution)/shard_map/ppermute | solution.py:389
  451.7 31.0 %collective-permute-start.67 = (bf16[128,1024]{1,0:T(8,128)(2,1)}, bf16[128,1024]{1,0:T(8,128)(2,1)}, u32[]{:S(2)}, u32[]{:S(2)}) collective-permute-start(bf16[128,1024]{1,0:T(8,128)(2,1)} %pad_maximum_fusion.6), channel_id=1, source_target_pairs={{0,12},{4,0},{8,4},{12,8},{1,13},{5,1},{9,5},{13,9},{2,14},{6,2},{... | collective-permute-start | bytes 786440 | tf_op jit(solution)/shard_map/ppermute | solution.py:389
  452.4 30.4 %collective-permute-start.63 = (bf16[1,4,2,16,4096]{4,3,2,1,0:T(8,128)(2,1)S(1)}, bf16[1,4,2,16,4096]{4,3,2,1,0:T(8,128)(2,1)S(1)}, u32[]{:S(2)}, u32[]{:S(2)}) collective-permute-start(bf16[1,4,2,16,4096]{4,3,2,1,0:T(8,128)(2,1)S(1)} %fusion.14), channel_id=1, source_target_pairs={{0,16},{16,0},{1,17},{17,1},{2,18},{18,2},{3,19},{19,3},{4,20},{20... | collective-permute-start | bytes 3145736 | tf_op jit(solution)/shard_map/ppermute | solution.py:377
  468.6 24.8 %collective-permute-start.64 = (bf16[1,2,4,16,4096]{4,3,2,1,0:T(8,128)(2,1)S(1)}, bf16[1,2,4,16,4096]{4,3,2,1,0:T(8,128)(2,1)S(1)}, u32[]{:S(2)}, u32[]{:S(2)}) collective-permute-start(bf16[1,2,4,16,4096]{4,3,2,1,0:T(8,128)(2,1)S(1)} %fusion.15), channel_id=1, source_target_pairs={{0,2},{2,0},{1,3},{3,1},{4,6},{6,4},{5,7},{7,5},{8,10},{10,8},{9,1... | collective-permute-start | bytes 3145736 | tf_op jit(solution)/shard_map/ppermute | solution.py:377
  496.6 20.8 %collective-permute-start.71 = (bf16[1,2,4,2,32,2560]{5,4,3,2,1,0:T(8,128)(2,1)}, bf16[1,2,4,2,32,2560]{5,4,3,2,1,0:T(8,128)(2,1)}, u32[]{:S(2)}, u32[]{:S(2)}) collective-permute-start(bf16[1,2,4,2,32,2560]{5,4,3,2,1,0:T(8,128)(2,1)} %bitcast.72), channel_id=1, source_target_pairs={{0,1},{1,0},{2,3},{3,2},{4,5},{5,4},{6,7},{7,6},{8,9},{9,8},{10,11... | collective-permute-start | bytes 7864328 | tf_op jit(solution)/shard_map/ppermute | solution.py:377
  524.5 19.5 %collective-permute-start.76 = (bf16[32,4096]{1,0:T(8,128)(2,1)S(1)}, bf16[32,4096]{1,0:T(8,128)(2,1)S(1)}, u32[]{:S(2)}, u32[]{:S(2)}) collective-permute-start(bf16[32,4096]{1,0:T(8,128)(2,1)S(1)} %pad_maximum_fusion.8), channel_id=1, source_target_pairs={{0,8},{4,12},{8,0},{12,4},{1,9},{5,13},{9,1},{13,5},{2,10},{6,14},... | collective-permute-start | bytes 786440 | tf_op jit(solution)/shard_map/ppermute | solution.py:389
  525.7 23.7 %collective-permute-start.72 = (bf16[1,4,2,16,2560]{4,3,2,1,0:T(8,128)(2,1)S(1)}, bf16[1,4,2,16,2560]{4,3,2,1,0:T(8,128)(2,1)S(1)}, u32[]{:S(2)}, u32[]{:S(2)}) collective-permute-start(bf16[1,4,2,16,2560]{4,3,2,1,0:T(8,128)(2,1)S(1)} %fusion.22), channel_id=1, source_target_pairs={{0,16},{16,0},{1,17},{17,1},{2,18},{18,2},{3,19},{19,3},{4,20},{20... | collective-permute-start | bytes 1966088 | tf_op jit(solution)/shard_map/ppermute | solution.py:377
  527.0 22.4 %collective-permute-start.73 = (bf16[1,2,4,16,2560]{4,3,2,1,0:T(8,128)(2,1)S(1)}, bf16[1,2,4,16,2560]{4,3,2,1,0:T(8,128)(2,1)S(1)}, u32[]{:S(2)}, u32[]{:S(2)}) collective-permute-start(bf16[1,2,4,16,2560]{4,3,2,1,0:T(8,128)(2,1)S(1)} %fusion.23), channel_id=1, source_target_pairs={{0,2},{2,0},{1,3},{3,1},{4,6},{6,4},{5,7},{7,5},{8,10},{10,8},{9,1... | collective-permute-start | bytes 1966088 | tf_op jit(solution)/shard_map/ppermute | solution.py:377
  528.6 20.9 %collective-permute-start.74 = (bf16[1,2,4,2,32,1536]{5,4,3,2,1,0:T(8,128)(2,1)S(1)}, bf16[1,2,4,2,32,1536]{5,4,3,2,1,0:T(8,128)(2,1)S(1)}, u32[]{:S(2)}, u32[]{:S(2)}) collective-permute-start(bf16[1,2,4,2,32,1536]{5,4,3,2,1,0:T(8,128)(2,1)S(1)} %bitcast.447), channel_id=1, source_target_pairs={{0,1},{1,0},{2,3},{3,2},{4,5},{5,4},{6,7},{7,6},{8,9},{9,8},{10,11... | collective-permute-start | bytes 4718600 | tf_op jit(solution)/shard_map/ppermute | solution.py:377
  581.4 20.2 %collective-permute-start.84 = (bf16[512,1024]{1,0:T(8,128)(2,1)S(1)}, bf16[512,1024]{1,0:T(8,128)(2,1)S(1)}, u32[]{:S(2)}, u32[]{:S(2)}) collective-permute-start(bf16[512,1024]{1,0:T(8,128)(2,1)S(1)} %get-tuple-element.470), channel_id=1, source_target_pairs={{1,16},{16,1},{3,18},{18,3},{5,20},{20,5},{7,22},{22,7},{9,24},{24... | collective-permute-start | bytes 3145736 | tf_op jit(solution)/shard_map/ppermute | solution.py:392
  (222 other events, 2040.0 us)

commit v4 on v3

--- a/solution.py
+++ b/solution.py
@@ -11,6 +11,7 @@
 
 HEAD = 64
 PAIR = 2 * HEAD
+LANES = 128
 SCALE = 0.125
 EPSILON = 1e-06
 NEGATIVE = -1e30
@@ -64,9 +65,9 @@
     part = mates[0].shape[0]
     every = 2 * part
     pairs = model // PAIR
-    step = math.gcd(tokens, 256)
-
-    def kernel(q_ref, k0_ref, k1_ref, v0_ref, v1_ref, ql_ref, kl_ref, attn_ref, lse_ref, bias_ref):
+    step = math.gcd(tokens, 512)
+
+    def kernel(q_ref, k0_ref, k1_ref, v0_ref, v1_ref, ql_ref, kl_ref, attn_ref, low_ref, lse_ref, bias_ref):
         @pl.when(pl.program_id(0) == 0)
         def _():
             fill_bias(bias_ref, columns_of(ql_ref), rows_of(kl_ref))
@@ -86,7 +87,9 @@
                 lse_ref[0, side : side + 1, start : start + step] = across[0:1]
                 sides.append(product(weights.astype(BF), values_pair) / denominator)
             lane = lax.broadcasted_iota(jnp.int32, (step, PAIR), 1)
-            attn_ref[start : start + step, :] = jnp.where(lane < HEAD, sides[0], sides[1]).astype(BF)
+            both = jnp.where(lane < HEAD, sides[0], sides[1])
+            attn_ref[start : start + step, :] = both
+            low_ref[start : start + step, :] = both.astype(BF)
 
     work = 2 * tokens * every * model
     keys_at = pl.BlockSpec((part, PAIR), lambda i: (0, i))
@@ -105,15 +108,17 @@
         ],
         out_specs=[
             pl.BlockSpec((tokens, PAIR), lambda i: (0, i)),
+            pl.BlockSpec((tokens, PAIR), lambda i: (0, i)),
             pl.BlockSpec((1, 2, tokens), lambda i: (i, 0, 0)),
         ],
         out_shape=[
+            jax.ShapeDtypeStruct((tokens, model), F32),
             jax.ShapeDtypeStruct((tokens, model), BF),
             jax.ShapeDtypeStruct((pairs, 2, tokens), F32),
         ],
         scratch_shapes=[pltpu.VMEM((tokens, every), F32)],
         compiler_params=pltpu.CompilerParams(
-            dimension_semantics=("arbitrary",), vmem_limit_bytes=40 << 20
+            dimension_semantics=("arbitrary",), vmem_limit_bytes=60 << 20
         ),
         cost_estimate=pl.CostEstimate(
             flops=2 * work, transcendentals=work // PAIR, bytes_accessed=10 * every * model
@@ -127,7 +132,7 @@
     part = mates[0].shape[0]
     every, total_pairs = 2 * part, query.shape[1] // PAIR
     model = pairs * PAIR
-    step = math.gcd(part, 256)
+    step = math.gcd(part, 512)
 
     def kernel(q_ref, k0_ref, k1_ref, v0_ref, v1_ref, g_ref, a_ref, lse_ref, ql_ref, kl_ref,
                dq_ref, d0_ref, d1_ref, bias_ref):
@@ -136,7 +141,7 @@
             fill_bias(bias_ref, rows_of(ql_ref), columns_of(kl_ref))
 
         query_pair, grad_pair = q_ref[...], g_ref[...]
-        overlap = (grad_pair.astype(F32) * a_ref[...].astype(F32)).T
+        overlap = (grad_pair.astype(F32) * a_ref[...]).T
         deltas = [
             jnp.sum(overlap[side * HEAD : (side + 1) * HEAD], axis=0, keepdims=True)
             for side in range(2)
@@ -192,7 +197,7 @@
         ],
         scratch_shapes=[pltpu.VMEM((every, tokens), F32)],
         compiler_params=pltpu.CompilerParams(
-            dimension_semantics=("arbitrary",), vmem_limit_bytes=40 << 20
+            dimension_semantics=("arbitrary",), vmem_limit_bytes=60 << 20
         ),
         cost_estimate=pl.CostEstimate(
             flops=5 * work, transcendentals=work // PAIR, bytes_accessed=12 * every * model
@@ -245,7 +250,7 @@
 def gated_backward(grad_low, slope, weight_down, weight_up):
     tokens, model = grad_low.shape
     hidden_units = slope.shape[1]
-    width = math.gcd(hidden_units, 512)
+    width = math.gcd(hidden_units, 1024)
     steps = hidden_units // width
     rows = math.gcd(tokens, 256)
 
@@ -304,49 +309,65 @@
     tokens, height = jobs[0][0][0].shape
     shards = grid.shards
     rows = height // shards
-    widths = [rights[0].shape[1] for _, rights in jobs]
+    widths = [part[0][0].shape[-1] for _, parts in jobs for part in parts]
     columns = sum(widths)
     if rows % 16:
         acc = jnp.concatenate(
-            [sum(outer_sum(left, right) for left, right in zip(*job)) for job in jobs], axis=1
+            [
+                sum(
+                    outer_sum(left, right if at is None else right[at])
+                    for left, (right, at) in zip(lefts, part)
+                )
+                for lefts, parts in jobs
+                for part in parts
+            ],
+            axis=1,
         )
         acc = acc.astype(BF).reshape(shards // 2, 2, rows, columns)
         return tuple(pick(acc, lax.rem(grid.at["c"] + k, 2), 1) for k in range(2))
     lefts = [left for job in jobs for left in job[0]]
-    rights = [right for job in jobs for right in job[1]]
-    count, depth = len(lefts), len(jobs[0][0])
+    rights = [right for _, parts in jobs for part in parts for right in part]
+    depth = len(jobs[0][0])
+    left_of = [job for job, (_, parts) in enumerate(jobs) for _ in parts]
     block = 256
     pairs = block // (2 * rows)
 
     def kernel(at_ref, *refs):
-        left_refs, right_refs = refs[:count], refs[count : 2 * count]
-        kept_ref, sent_ref = refs[2 * count :]
+        left_refs, right_refs = refs[: len(lefts)], refs[len(lefts) : len(lefts) + len(rights)]
+        kept_ref, sent_ref = refs[len(lefts) + len(rights) :]
         upper = at_ref[4] == 1
         begin = 0
-        for job, width in enumerate(widths):
-            chunk = math.gcd(width, 1024) if width % 1024 == 0 else math.gcd(width, 512)
-            turn = slice(job * depth, (job + 1) * depth)
+        for part, width in enumerate(widths):
+            chunk = math.gcd(width, 1024)
+            job = left_of[part]
             for start in range(0, width, chunk):
                 acc = None
-                for left, right in zip(left_refs[turn], right_refs[turn]):
-                    part = outer_sum(left[...], right[:, start : start + chunk])
-                    acc = part if acc is None else acc + part
+                for k in range(depth):
+                    more = outer_sum(
+                        left_refs[job * depth + k][...],
+                        right_refs[part * depth + k][:, start : start + chunk],
+                    )
+                    acc = more if acc is None else acc + more
                 acc = acc.reshape(pairs, 2, rows, chunk)
                 at = slice(begin + start, begin + start + chunk)
                 kept_ref[:, :, at] = jnp.where(upper, acc[:, 1], acc[:, 0]).astype(BF)
                 sent_ref[:, :, at] = jnp.where(upper, acc[:, 0], acc[:, 1]).astype(BF)
             begin += width
 
+    def whole(right, at):
+        if at is None:
+            return pl.BlockSpec(right.shape, lambda i: (0, 0), pipeline_mode=pl.Buffered(1))
+        return pl.BlockSpec(
+            (None,) + right.shape[1:], lambda i: (at, 0, 0), pipeline_mode=pl.Buffered(1)
+        )
+
     out = pl.BlockSpec((pairs, rows, columns), lambda i: (i, 0, 0))
     return pl.pallas_call(
         kernel,
         grid=(height // block,),
         in_specs=[pl.BlockSpec(memory_space=pltpu.SMEM)]
-        + [pl.BlockSpec((tokens, block), lambda i: (0, i))] * count
-        + [
-            pl.BlockSpec((tokens, right.shape[1]), lambda i: (0, 0), pipeline_mode=pl.Buffered(1))
-            for right in rights
-        ],
+        + [pl.BlockSpec((tokens, block), lambda i: (0, i))] * len(lefts)
+        + [whole(*right) for right in rights],
         out_specs=[out, out],
         out_shape=[jax.ShapeDtypeStruct((shards // 2, rows, columns), BF)] * 2,
         compiler_params=pltpu.CompilerParams(
@@ -358,7 +379,7 @@
             bytes_accessed=2 * height * columns + 2 * depth * tokens * (height + columns),
         ),
         name="weight_terms",
-    )(grid.places, *lefts, *rights)
+    )(grid.places, *lefts, *(right for right, _ in rights))
 
 
 class Grid:
@@ -400,7 +421,7 @@
         return tensor, self.shift(tensor, "c", 1)
 
 
-def place(places, pieces, out_shapes, moves):
+def place(places, pieces, out_shapes, moves, room=None):
     count = len(pieces)
     landed = [pltpu.VMEM(piece.shape, piece.dtype) for piece in pieces]
 
@@ -434,7 +455,7 @@
         out_specs=[pl.BlockSpec(memory_space=pl.ANY)] * len(out_shapes),
         scratch_shapes=landed
         + [pltpu.SemaphoreType.DMA((count,)), pltpu.SemaphoreType.DMA((8 * count,))],
-        compiler_params=pltpu.CompilerParams(vmem_limit_bytes=moved + (4 << 20)),
+        compiler_params=pltpu.CompilerParams(vmem_limit_bytes=room or moved + (4 << 20)),
         cost_estimate=pl.CostEstimate(flops=0, transcendentals=0, bytes_accessed=2 * moved),
         name="place",
     )(places, *pieces)
@@ -482,7 +503,11 @@
             return listed
 
         self.sends = place(
-            self.grid.places, [p[0] for p in pieces], [self.new(high, deep)] * 2, moves
+            self.grid.places,
+            [p[0] for p in pieces],
+            [self.new(high, deep)] * 2,
+            moves,
+            (60 << 20) if len(self.chunks) > 1 else None,
         )
 
     def go_first(self):
@@ -587,13 +612,15 @@
         self.sends = [sent.reshape(*sizes, self.rows, self.columns)]
         self.stage = 0
 
-    def go(self):
+    def go(self, part=0):
         if self.stage == 0:
             self.arrived = [self.grid.shift(self.sends[0], "c", 1)]
         elif self.stage < 3:
             self.arrived = [self.grid.shift(t, *route) for t, route in zip(self.sends, self.routes)]
         else:
-            self.arrived = [self.grid.far_shift(t, route) for t, route in zip(self.sends, self.routes)]
+            now = list(zip(self.sends, self.routes))[part::2]
+            held = self.arrived if part else []
+            self.arrived = held + [self.grid.far_shift(t, route) for t, route in now]
 
     def slices(self, i, extra):
         places = {**self.picked[i], **extra}
@@ -651,6 +678,18 @@
     return values
 
 
+def advance(values, scatters, begin=(), got=(), rest=()):
+    values = order(values, [*begin, *rest], [*scatters, *got])
+    for scatter in scatters:
+        scatter.prepare()
+    values = order(values, [*scatters, *begin, *rest])
+    for scatter in (*begin, *scatters):
+        scatter.go()
+    for scatter in rest:
+        scatter.go(1)
+    return values
+
+
 def sum_far(grid, tensor):
     arrived = [grid.far_shift(tensor, s) for s in grid.far_steps() if s != (0, 0)]
     return total([tensor] + arrived).astype(tensor.dtype)
@@ -685,58 +724,58 @@
     share = model // shards
     tie = lax.optimization_barrier
 
+    rows_small = jnp.concatenate([biases, norm_gains, norm_shifts, lead_table])
+    lengths = [t.shape[0] for t in (biases, norm_gains, norm_shifts, lead_table)]
+    cuts = [sum(lengths[:i]) for i in range(5)]
+    own_up = up_bias.shape[0]
+    per_row = model // own_up
+    shard_rows = w_qkv.shape[0]
+    tiles = -(-(cuts[4] + 1) // shard_rows)
+
+    def to_lanes(rows, width):
+        lane = jnp.arange(LANES, dtype=jnp.int32)[None, :]
+        begin = (grid.shard % (LANES // width)) * width
+        spread = lane == begin + jnp.arange(width, dtype=jnp.int32)[:, None]
+        return product(rows, spread.astype(BF)).astype(BF)
+
+    def from_lanes(tensor, width):
+        groups = tensor.reshape(-1, LANES // width, *tensor.shape[1:])
+        return jnp.sum(groups.astype(F32), axis=1)
+
+    block = jnp.concatenate([to_lanes(rows_small, share), to_lanes(up_bias[None, :], own_up)])
+    block = jnp.pad(block, ((0, tiles * shard_rows - block.shape[0]), (0, 0)))
+    block = block.reshape(tiles, shard_rows, LANES).transpose(1, 0, 2).reshape(shard_rows, -1)
+
     middle_up, middle_down = w_up.shape[1] // 2, w_down.shape[1] // 2
-    one = Gather(grid, [w_qkv], [w_qkv.shape[1]])
+    one = Gather(
+        grid, [jnp.concatenate([w_qkv, block], axis=1)], [w_qkv.shape[1], tiles * LANES]
+    )
     two = Gather(
         grid,
         [w_up[:, :middle_up], jnp.concatenate([w_up[:, middle_up:], w_out], axis=1)],
         [w_up.shape[1], w_out.shape[1]],
     )
     three = Gather(grid, [w_down[:, :middle_down], w_down[:, middle_down:]], [w_down.shape[1]])
-    rows_small = jnp.concatenate([biases, norm_gains, norm_shifts, lead_table])
-    lengths = [t.shape[0] for t in (biases, norm_gains, norm_shifts, lead_table)]
-    cuts = [sum(lengths[:i]) for i in range(5)]
-    lane = jnp.arange(model, dtype=jnp.int32)[None, :]
-    to_lane = (lane == grid.shard * share + jnp.arange(share, dtype=jnp.int32)[:, None]).astype(BF)
-    own_up = up_bias.shape[0]
-    per_row = model // own_up
-    up_rows = shards // per_row
-    up_lane = (
-        lane == (grid.shard % per_row) * own_up + jnp.arange(own_up, dtype=jnp.int32)[:, None]
-    ).astype(BF)
-    up_row = jnp.arange(up_rows, dtype=jnp.int32)[:, None] == grid.shard // per_row
-    small = jnp.concatenate(
-        [
-            product(rows_small, to_lane),
-            product(jnp.where(up_row, up_bias[None, :], jnp.zeros((), BF)), up_lane),
-        ]
-    )
     labels = jnp.concatenate(
         [segment_ids, key_mask, jnp.broadcast_to(lead_index.reshape(2, 1), (2, tokens))]
     )
     one.go_far(0)
-    start_moved = grid.swapped(inputs[0])
-    labels_moved = grid.swapped(labels)
-    small = sum_near(grid, sum_near(grid, small.astype(BF), "c"), "y")
-    one.far, labels_moved, start_moved, small = tie((one.far, labels_moved, start_moved, small))
+    start_moved, labels_moved = grid.swapped(inputs[0]), grid.swapped(labels)
+    one.far, labels_moved, start_moved = tie((one.far, labels_moved, start_moved))
     labels = grid.choose(labels, labels_moved)
+    leads = (labels[2, 0], labels[3, 0])
     start_low = grid.choose(inputs[0], start_moved)
-    one.make_lines()
-    one.sends, two.chunks[0], small = tie((one.sends, two.chunks[0], small))
-    one.go_first()
-    two.go_far(0)
-    small = sum_far(grid, sum_near(grid, small, "x"))
-    one.arrived, two.far[0], small, labels = tie((one.arrived, two.far[0], small, labels))
-    small = small.astype(F32)
-    bias_full, gains, shifts, lead_rows = (small[cuts[i] : cuts[i + 1]] for i in range(4))
-    bias_up = small[cuts[4] :]
-    leads = (labels[2, 0], labels[3, 0])
     own_pos = (grid.at["h"] * 2 + grid.at["c"]) * tokens + jnp.arange(tokens, dtype=jnp.int32)
     own_labels = jnp.stack([labels[0], labels[1], own_pos], axis=1)
     key_labels = jnp.concatenate(grid.mates(own_labels))
     own_labels_across, key_labels_across = own_labels.T, key_labels.T
     high = grid.size["h"]
 
+    one.make_lines()
+    one.sends, two.chunks[0] = tie((one.sends, two.chunks[0]))
+    one.go_first()
+    two.go_far(0)
+    one.arrived, two.far[0] = tie((one.arrived, two.far[0]))
     one.make_planes()
     one.sends, two.chunks[1] = tie((one.sends, two.chunks[1]))
     one.go_second()
@@ -750,8 +789,15 @@
     one.pairs = [(t,) + pair[1:] for t, pair in zip(crossed, one.pairs)]
     two.go_first()
     three.go_far(0)
-    (weight_qkv,) = one.result()
+    weight_qkv, small = one.result()
     weights = {"qkv": weight_qkv}
+    small = small.reshape(shards, shard_rows, -1)
+    up_row, up_lanes = cuts[4] % shard_rows, cuts[4] // shard_rows * LANES
+    bias_up = from_lanes(small[:, up_row, up_lanes : up_lanes + LANES][:, None], own_up)
+    bias_up = bias_up.reshape(-1, model)
+    small = from_lanes(small, share).reshape(-1, shard_rows, tiles, LANES)
+    small = small.transpose(2, 1, 0, 3).reshape(tiles * shard_rows, model)
+    bias_full, gains, shifts, lead_rows = (small[cuts[i] : cuts[i + 1]] for i in range(4))
 
     def before_exchange(values):
         values, two.arrived, three.far[0] = tie((values, two.arrived, three.far[0]))
@@ -801,7 +847,7 @@
         keys_values = (mixed[:, model:] + both_bias).astype(BF)
         query, keys_values = hooks[0]((query, keys_values))
         mates = grid.mates(keys_values)
-        attn_low, lse = attention_forward(query, mates, own_labels, key_labels_across)
+        attn, attn_low, lse = attention_forward(query, mates, own_labels, key_labels_across)
         attn_low, lse = hooks[1]((attn_low, lse))
         middle = hidden + product(attn_low, weights["out"]) + bias_full[2]
         normed_mid = layer_norm(middle, gains[1], shifts[1]).astype(BF)
@@ -810,19 +856,29 @@
         activated, slope = hooks[3]((activated, slope))
         result = middle + product(activated, weights["down"]) + bias_full[3]
         saved = (
-            hidden, normed, query, mates, lse, attn_low, middle, normed_mid, slope, activated, chooser,
+            hidden, normed, query, mates, lse, attn, attn_low, middle, normed_mid, slope, activated,
+            chooser,
         )
         return (result, saved)
 
     def backward(saved, grad_res, earlier, hooks):
-        hidden, normed, query, mates, lse, attn_low, middle, normed_mid, slope, activated, chooser = saved
+        (
+            hidden, normed, query, mates, lse, attn, attn_low, middle, normed_mid, slope, activated,
+            chooser,
+        ) = saved
         last = earlier is not None
         operands, sums = {}, {}
 
         def start(name, **joined):
             operands.update(joined)
             if last:
-                jobs = [tuple(zip(operands[part], earlier[part])) for part in joined]
+                jobs = [
+                    (
+                        (joined[part][0], earlier[part][0]),
+                        list(zip(joined[part][1], earlier[part][1])),
+                    )
+                    for part in joined
+                ]
                 sums[name] = Scatter(grid, *weight_terms(grid, jobs))
 
         def then(values, sent=(), got=()):
@@ -833,17 +889,15 @@
                 sums[name].go()
             return values
 
-        def step(values, names, begin=(), got=()):
+        def step(values, names, begin=(), got=(), rest=()):
             if not last:
                 return values
-            ready = [sums[name] for name in begin]
-            values = order(values, ready, [sums[name] for name in (*names, *got)])
-            for name in names:
-                sums[name].prepare()
-            return then(values, sent=[*names, *begin])
+            return advance(
+                values, *([sums[name] for name in group] for group in (names, begin, got, rest))
+            )
 
         grad_low = grad_res.astype(BF)
-        start("down", down=(activated, grad_low))
+        start("down", down=(activated, [(grad_low, None)]))
         grad_low = then(grad_low, sent=["down"])
         bias_down = jnp.sum(grad_low.astype(F32), axis=0)
         grad_low = hooks[0](grad_low)
@@ -852,13 +906,13 @@
         )
         grad_gate, grad_normed_mid = hooks[1]((grad_gate, grad_normed_mid))
         grad_gate, grad_normed_mid = step((grad_gate, grad_normed_mid), ["down"])
-        start("up", up=(normed_mid, grad_gate))
         mid_pull = jax.vjp(layer_norm, middle, gains[1], shifts[1])[1]
         grad_mid_part, gain_mid, shift_mid = mid_pull(grad_normed_mid)
         grad_mid = grad_res + grad_mid_part
         grad_branch = grad_mid.astype(BF)
         grad_attn = back_product(grad_branch, weights["out"]).astype(BF)
         bias_attn = jnp.sum(grad_branch.astype(F32), axis=0)
+        start("up", up=(normed_mid, [(grad_gate, None)]), out=(attn_low, [(grad_branch, None)]))
         grad_attn = hooks[2](grad_attn)
         grad_attn = step(grad_attn, ["down"], begin=["up"])
         pairs = model // PAIR
@@ -867,36 +921,39 @@
         def attend_back(half):
             first, count = halves[half], halves[half + 1] - halves[half]
             return attention_backward(
-                query, mates, grad_attn, attn_low, lse, own_labels_across, key_labels, first, count
+                query, mates, grad_attn, attn, lse, own_labels_across, key_labels, first, count
             )
 
-        def mix(query_low, near, far):
+        def add(near, far):
             both = total([near, far])
             if high > 1:
                 both = lax.psum_scatter(both.astype(BF), "h", scatter_dimension=1, tiled=True)
-            both = both.astype(BF)
-            return jnp.concatenate([query_low, both[0], both[1]], axis=1)
+            return both.astype(BF)
+
+        def parts(query_low, both):
+            return (normed, [(query_low, None), (both, 0), (both, 1)])
 
         query_low, near, sent = hooks[3](attend_back(0))
         query_low, near, sent, grad_attn = step((query_low, near, sent, grad_attn), ["down", "up"])
         far = grid.shift(sent, "c", 1)
         other_low, other_near, sent = attend_back(1)
-        mixed_low = mix(query_low, near, far)
-        start("mix", qkv0=(normed, mixed_low), out=(attn_low, grad_branch))
-        other_low, other_near, sent, mixed_low = step(
-            (other_low, other_near, sent, mixed_low), ["up"], begin=["mix"], got=["down"]
+        both = add(near, far)
+        start("mix", qkv0=parts(query_low, both))
+        other_low, other_near, sent, query_low, both = step(
+            (other_low, other_near, sent, query_low, both),
+            ["up"],
+            begin=["mix"],
+            got=["down"],
+            rest=["down"],
         )
         far = grid.shift(sent, "c", 1)
-        mixed_high = mix(other_low, other_near, far)
-        start("qkv1", qkv1=(normed, mixed_high))
-        mixed_low, mixed_high = step((mixed_low, mixed_high), ["up", "mix"], begin=["qkv1"])
+        other_both = add(other_near, far)
+        start("qkv1", qkv1=parts(other_low, other_both))
+        query_low, both, other_low, other_both = step(
+            (query_low, both, other_low, other_both), ["up", "mix"], begin=["qkv1"], got=["down"]
+        )
         grad_mixed = jnp.concatenate(
-            [
-                p[:, i * p.shape[1] // 3 : (i + 1) * p.shape[1] // 3]
-                for i in range(3)
-                for p in (mixed_low, mixed_high)
-            ],
-            axis=1,
+            [query_low, other_low, both[0], other_both[0], both[1], other_both[1]], axis=1
         )
         grad_normed = back_product(grad_mixed, weights["qkv"])
         bias_query = jnp.sum(grad_mixed[:, :model].astype(F32), axis=0)
@@ -904,7 +961,7 @@
         in_pull = jax.vjp(layer_norm, hidden, gains[0], shifts[0])[1]
         grad_in_part, gain_in, shift_in = in_pull(grad_normed)
         grad_start = grad_mid + grad_in_part
-        grad_start = step(grad_start, ["mix", "qkv1"], got=["up"])
+        grad_start = step(grad_start, ["mix", "qkv1"], got=["up"], rest=["up"])
         lead_sum = jnp.sum(grad_start, axis=0)
         vectors = jnp.concatenate(
             [
@@ -962,26 +1019,18 @@
     vectors = vectors_second + vectors_first
     grad_low = grad_first.astype(BF)
 
-    def step(values, names):
-        scatters = [sums[name] for name in names]
-        values = order(values, (), scatters)
-        for scatter in scatters:
-            scatter.prepare()
-        values = order(values, scatters, ())
-        for scatter in scatters:
-            scatter.go()
-        return values
-
-    vectors = sum_near(grid, vectors, "c")
-    vectors, grad_low = step((vectors, grad_low), ["mix", "qkv1"])
+    mix, qkv1, up = (sums[name] for name in ("mix", "qkv1", "up"))
+    vectors, grad_low = advance((vectors, grad_low), [mix, qkv1], got=[up])
+    mix.go(1)
+    vectors = sum_near(grid, sum_near(grid, vectors, "c"), "y")
+    vectors, grad_low = advance((vectors, grad_low), [qkv1])
+    qkv1.go(1)
     grad_moved = grid.swapped(grad_low)
-    vectors = sum_near(grid, vectors, "y")
-    vectors, grad_moved = step((vectors, grad_moved), ["qkv1"])
     vectors = sum_far(grid, sum_near(grid, vectors, "x"))
     input_grad = grid.choose(grad_low, grad_moved).astype(F32)
     shares = {name: sums[name].result() for name in ("down", "up", "mix", "qkv1")}
     width = shares["qkv1"].shape[1] // 3
-    parts = [shares["mix"], shares["qkv1"]]
+    sides = [shares["mix"], shares["qkv1"]]
     own_columns = lax.dynamic_slice_in_dim(vectors, grid.shard * share, share, 1)
     small_out = [own_columns[cuts[i] : cuts[i + 1]] for i in range(4)]
     up_out = lax.dynamic_slice(
@@ -991,9 +1040,9 @@
         first_low[None],
         second_low[None],
         input_grad[None],
-        jnp.concatenate([p[:, i * width : (i + 1) * width] for i in range(3) for p in parts], axis=1),
-        shares["mix"][:, 3 * width :],
-        shares["up"],
+        jnp.concatenate([p[:, i * width : (i + 1) * width] for i in range(3) for p in sides], axis=1),
+        shares["up"][:, w_up.shape[1] :],
+        shares["up"][:, : w_up.shape[1]],
         shares["down"],
         small_out[0],
         up_out,

time: 636 us -> 602 us (0.947)
  local copies, waits for them, and re-layouts: 52.4 us -> 34.4 us
  waiting for transfers between devices: 123 us -> 112 us
  Pallas kernels: 229 us -> 222 us
    unnamed x329 -> x299, local copies, waits for them, and re-layouts: 40.6 us -> 20.4 us
    ppermute x57 -> x54, waiting for transfers between devices: 76.3 us -> 59.1 us  [shift(): return lax.ppermute(tensor, axis, [(i, (i + step) % n) for i in range(n)])]
    ppermute x33 -> x30, starting transfers between devices: 44.1 us -> 53.6 us  [far_shift(): return lax.ppermute(tensor, ('h', 'z'), pairs)]
    ppermute x57 -> x54, starting transfers between devices: 48.7 us -> 42.3 us  [shift(): return lax.ppermute(tensor, axis, [(i, (i + step) % n) for i in range(n)])]
    ppermute x33 -> x30, waiting for transfers between devices: 47 us -> 53.1 us  [far_shift(): return lax.ppermute(tensor, ('h', 'z'), pairs)]
  transfers between devices with their start and end apart: 97 -> 91, of which waited for: 43 -> 37; matrix products, arithmetic and copies ran while one was open for 9% -> 9% of each run, Pallas kernels for 31% -> 32%
where the time goes in v4:
time: 602 us; the launch traced here: 592 us
  Pallas kernels  222 us (37%)
  waiting for transfers between devices  112 us (19%)
  starting transfers between devices  103 us (17%)
  other arithmetic  80.5 us (13%)
  matrix products  36.4 us (6%)
  local copies, waits for them, and re-layouts  34.4 us (6%)
    pallas_call x4, Pallas kernels, attention_backward(): pl.pallas_call(kernel, grid=(pairs,), in_specs=[own, keys_at, keys_at, va...  60.3 us
    ppermute x54, waiting for transfers between devices, shift(): return lax.ppermute(tensor, axis, [(i, (i + step) % n) for i in range(n)])  59.1 us
    ppermute x30, starting transfers between devices, far_shift(): return lax.ppermute(tensor, ('h', 'z'), pairs)  53.6 us
    ppermute x30, waiting for transfers between devices, far_shift(): return lax.ppermute(tensor, ('h', 'z'), pairs)  53.1 us
    pallas_call x4, Pallas kernels, weight_terms(): pl.pallas_call(kernel, grid=(height // block,), in_specs=[pl.BlockSpec(me...  47.2 us
    ppermute x54, starting transfers between devices, shift(): return lax.ppermute(tensor, axis, [(i, (i + step) % n) for i in range(n)])  42.3 us
    pallas_call x2, Pallas kernels, attention_forward(): pl.pallas_call(kernel, grid=(pairs,), in_specs=[pl.BlockSpec((tokens, PAI...  39.8 us
    pallas_call x9, Pallas kernels, place(): pl.pallas_call(kernel, out_shape=out_shapes, in_specs=[pl.BlockSpec(memor...  26.7 us
  transfers between devices with their start and end apart: 91, of which 37 were waited for; matrix products, arithmetic and copies ran while one was open for 9% of the time, Pallas kernels for 32%

profile of v4, /device:TPU:0, one launch (start us, length us, event | category | flops | bytes accessed | tf_op | source)
XLA Modules:
  0.0 592.5 jit_solution(9809077082484468656)
XLA Ops:
  13.8 9.5 %collective-permute-done.1.refs_2_ = bf16[32,3200]{1,0:T(8,128)(2,1)S(1)} collective-permute-done((bf16[32,3200]{1,0:T(8,128)(2,1)S(1)}, bf16[32,3200]{1,0:T(8,128)(2,1)S(1)}, u32[]{:S(2)}, u32[]{:S(2)}) %collective-permute-start.1) | collective-permute-done | bytes 204832 | tf_op jit(solution)/shard_map/ppermute | solution.py:410
  28.6 4.9 collective-permute-start.7
  39.0 4.2 collective-permute-done.8.refs_2_
  54.1 4.4 collective-permute-done.12.refs_5_
  58.6 6.4 %collective-permute-done.13.refs_6_ = bf16[32,3072]{1,0:T(8,128)(2,1)S(1)} collective-permute-done((bf16[32,3072]{1,0:T(8,128)(2,1)S(1)}, bf16[32,3072]{1,0:T(8,128)(2,1)S(1)}, u32[]{:S(2)}, u32[]{:S(2)}) %collective-permute-start.13) | collective-permute-done | bytes 196640 | tf_op jit(solution)/shard_map/ppermute | solution.py:410
  97.1 6.1 %collective-permute-done.19.refs_2_ = bf16[1,4,16,5120]{3,2,1,0:T(8,128)(2,1)S(1)} collective-permute-done((bf16[1,4,16,5120]{3,2,1,0:T(8,128)(2,1)S(1)}, bf16[1,4,16,5120]{3,2,1,0:T(8,128)(2,1)S(1)}, u32[]{:S(2)}, u32[]{:S(2)}) %collective-permute-start.19) | collective-permute-done | bytes 655392 | tf_op jit(solution)/shard_map/ppermute | solution.py:398
  116.3 19.9 %attention_forward.2 = (f32[512,1024]{1,0:T(8,128)}, bf16[512,1024]{1,0:T(8,128)(2,1)}, f32[8,2,512]{2,1,0:T(2,128)}) custom-call(bf16[512,1024]{1,0:T(8,128)(2,1)} %fusion.20.q_ref, bf16[512,2048]{1,0:T(8,128)(2,1)} %fusion.1.k0_ref.v0_ref, bf16[512,2048]{1,0:T(8,128)(2,1)} %collective-permute-done.24.k1_ref.v1_ref, bf16[512,2048]{1,0:T(8,128)(2,1)} %fusion.1.k0_ref.v0_ref, ...), custom_call_target="tpu_custom_call" | custom-call | flops 2147483648 | bytes 10485760 | tf_op jit(solution)/shard_map/attention_forward/pallas_call | solution.py:97
  145.2 4.8 place.15
  156.5 10.9 %collective-permute-done.35.refs_2_ = bf16[1,4,64,1024]{3,2,1,0:T(8,128)(2,1)S(1)} collective-permute-done((bf16[1,4,64,1024]{3,2,1,0:T(8,128)(2,1)S(1)}, bf16[1,4,64,1024]{3,2,1,0:T(8,128)(2,1)S(1)}, u32[]{:S(2)}, u32[]{:S(2)}) %collective-permute-start.35) | collective-permute-done | bytes 524320 | tf_op jit(solution)/shard_map/ppermute | solution.py:398
  172.2 10.9 %gated.2 = (bf16[512,4096]{1,0:T(8,128)(2,1)S(1)}, bf16[512,4096]{1,0:T(8,128)(2,1)S(1)}) custom-call(bf16[512,1024]{1,0:T(8,128)(2,1)S(1)} %add_convert_fusion.12.x_ref.refs_0_, bf16[1024,4096]{1,0:T(8,128)(2,1)} %bitcast.458, f32[8,1,512]{2,1,0:T(1,128)S(1)} %bitcast.456), custom_call_target="tpu_custom_call" | custom-call | flops 4294967296 | bytes 16777216 | tf_op jit(solution)/shard_map/gated/pallas_call | solution.py:228
  183.1 10.2 %collective-permute-done.37.refs_2_ = bf16[2,1,4,64,1024]{4,3,2,1,0:T(8,128)(2,1)S(1)} collective-permute-done((bf16[2,1,4,64,1024]{4,3,2,1,0:T(8,128)(2,1)S(1)}, bf16[2,1,4,64,1024]{4,3,2,1,0:T(8,128)(2,1)S(1)}, u32[]{:S(2)}, u32[]{:S(2)}) %collective-permute-start.37) | collective-permute-done | bytes 1048608 | tf_op jit(solution)/shard_map/ppermute | solution.py:398
  201.2 4.6 add_convert_fusion.11
  216.4 19.9 %attention_forward.3 = (f32[512,1024]{1,0:T(8,128)}, bf16[512,1024]{1,0:T(8,128)(2,1)}, f32[8,2,512]{2,1,0:T(2,128)}) custom-call(bf16[512,1024]{1,0:T(8,128)(2,1)} %fusion.21.q_ref, bf16[512,2048]{1,0:T(8,128)(2,1)} %copy-done.46, bf16[512,2048]{1,0:T(8,128)(2,1)} %collective-permute-done.43.k1_ref.v1_ref, bf16[512,2048]{1,0:T(8,128)(2,1)} %copy-done.46, ...), custom_call_target="tpu_custom_call" | custom-call | flops 2147483648 | bytes 10485760 | tf_op jit(solution)/shard_map/attention_forward/pallas_call | solution.py:97
  242.2 11.5 %gated.3 = (bf16[512,4096]{1,0:T(8,128)(2,1)S(1)}, bf16[512,4096]{1,0:T(8,128)(2,1)S(1)}) custom-call(bf16[512,1024]{1,0:T(8,128)(2,1)S(1)} %add_convert_fusion.9.x_ref.refs_1_, bf16[1024,4096]{1,0:T(8,128)(2,1)} %bitcast.459, f32[8,1,512]{2,1,0:T(1,128)S(1)} %bitcast.457), custom_call_target="tpu_custom_call" | custom-call | flops 4294967296 | bytes 16777216 | tf_op jit(solution)/shard_map/gated/pallas_call | solution.py:228
  253.8 5.5 add_convert_fusion.8
  260.2 12.7 %gated_backward.2 = (bf16[512,4096]{1,0:T(8,128)(2,1)S(1)}, f32[4,1,1024]{2,1,0:T(1,128)S(1)}, f32[512,1024]{1,0:T(8,128)S(1)}) custom-call(bf16[512,1024]{1,0:T(8,128)(2,1)S(1)} %broadcast_select_fusion.1.g_ref.refs_3_, bf16[512,4096]{1,0:T(8,128)(2,1)S(1)} %get-tuple-element.364.s_ref, bf16[4096,1024]{1,0:T(8,128)(2,1)} %bitcast.450, ...), custom_call_target="tpu_custom_call" | custom-call | flops 8589934592 | bytes 25165824 | tf_op jit(solution)/shard_map/gated_backward/pallas_call | solution.py:276
  283.5 15.0 %attention_backward.5 = (bf16[512,512]{1,0:T(8,128)(2,1)}, bf16[2,512,512]{2,1,0:T(8,128)(2,1)}, bf16[2,512,512]{2,1,0:T(8,128)(2,1)}) custom-call(bf16[512,1024]{1,0:T(8,128)(2,1)} %fusion.21.q_ref, bf16[512,2048]{1,0:T(8,128)(2,1)} %copy-done.46, bf16[512,2048]{1,0:T(8,128)(2,1)} %collective-permute-done.43.k1_ref.v1_ref, bf16[512,2048]{1,0:T(8,128)(2,1)} %copy-done.46, ...), custom_call_target="tpu_custom_call" | custom-call | flops 2684354560 | bytes 6291456 | tf_op jit(solution)/shard_map/attention_backward/pallas_call | solution.py:177
  298.5 5.7 collective-permute-start.49
  304.2 15.1 %attention_backward.4 = (bf16[512,512]{1,0:T(8,128)(2,1)}, bf16[2,512,512]{2,1,0:T(8,128)(2,1)}, bf16[2,512,512]{2,1,0:T(8,128)(2,1)}) custom-call(bf16[512,1024]{1,0:T(8,128)(2,1)} %fusion.21.q_ref, bf16[512,2048]{1,0:T(8,128)(2,1)} %copy-done.46, bf16[512,2048]{1,0:T(8,128)(2,1)} %collective-permute-done.43.k1_ref.v1_ref, bf16[512,2048]{1,0:T(8,128)(2,1)} %copy-done.46, ...), custom_call_target="tpu_custom_call" | custom-call | flops 2684354560 | bytes 6291456 | tf_op jit(solution)/shard_map/attention_backward/pallas_call | solution.py:177
  324.7 5.9 multiply_reduce_fusion.4
  335.0 17.9 %weight_terms.4 = (bf16[16,128,1024]{2,1,0:T(8,128)(2,1)}, bf16[16,128,1024]{2,1,0:T(8,128)(2,1)}) custom-call(s32[5]{0:T(128)S(1)} %copy-done.30, bf16[512,4096]{1,0:T(8,128)(2,1)} %copy-done.39, bf16[512,4096]{1,0:T(8,128)(2,1)} %copy-done.40, bf16[512,1024]{1,0:T(8,128)(2,1)S(1)} %get-tuple-element.388.refs_2_.g_ref, ...), custom_call_target="tpu_custom_call" | custom-call | flops 8589934592 | bytes 18874368 | tf_op jit(solution)/shard_map/weight_terms/pallas_call | solution.py:365
  356.7 13.0 %gated_backward.3 = (bf16[512,4096]{1,0:T(8,128)(2,1)S(1)}, f32[4,1,1024]{2,1,0:T(1,128)S(1)}, f32[512,1024]{1,0:T(8,128)S(1)}) custom-call(bf16[512,1024]{1,0:T(8,128)(2,1)S(1)} %copy-done.4, bf16[512,4096]{1,0:T(8,128)(2,1)S(1)} %copy-done.38, bf16[4096,1024]{1,0:T(8,128)(2,1)} %bitcast.451, bf16[1024,4096]{1,0:T(8,128)(2,1)} %bitcast.461), custom_call_target="tpu_custom_call" | custom-call | flops 8589934592 | bytes 25165824 | tf_op jit(solution)/shard_map/gated_backward/pallas_call | solution.py:276
  381.6 17.4 %weight_terms.5 = (bf16[16,32,5120]{2,1,0:T(8,128)(2,1)}, bf16[16,32,5120]{2,1,0:T(8,128)(2,1)}) custom-call(s32[5]{0:T(128)S(1)} %copy-done.30, bf16[512,1024]{1,0:T(8,128)(2,1)S(1)} %copy-done.20, bf16[512,1024]{1,0:T(8,128)(2,1)S(1)} %copy-done.22, bf16[512,1024]{1,0:T(8,128)(2,1)S(1)} %copy-done.42, bf16[512,1024]{1,0:T(8,128)(2,1)S(1)} %copy-done.43, ...), custom_call_target="tpu_custom_call" | custom-call | flops 10737418240 | bytes 23068672 | tf_op jit(solution)/shard_map/weight_terms/pallas_call | solution.py:365
  406.7 15.2 %attention_backward.6 = (bf16[512,512]{1,0:T(8,128)(2,1)}, bf16[2,512,512]{2,1,0:T(8,128)(2,1)}, bf16[2,512,512]{2,1,0:T(8,128)(2,1)}) custom-call(bf16[512,1024]{1,0:T(8,128)(2,1)} %fusion.20.q_ref, bf16[512,2048]{1,0:T(8,128)(2,1)} %fusion.1.k0_ref.v0_ref, bf16[512,2048]{1,0:T(8,128)(2,1)} %collective-permute-done.24.k1_ref.v1_ref, ...), custom_call_target="tpu_custom_call" | custom-call | flops 2684354560 | bytes 6291456 | tf_op jit(solution)/shard_map/attention_backward/pallas_call | solution.py:177
  440.5 15.0 %attention_backward.7 = (bf16[512,512]{1,0:T(8,128)(2,1)}, bf16[2,512,512]{2,1,0:T(8,128)(2,1)}, bf16[2,512,512]{2,1,0:T(8,128)(2,1)}) custom-call(bf16[512,1024]{1,0:T(8,128)(2,1)} %fusion.20.q_ref, bf16[512,2048]{1,0:T(8,128)(2,1)} %fusion.1.k0_ref.v0_ref, bf16[512,2048]{1,0:T(8,128)(2,1)} %collective-permute-done.24.k1_ref.v1_ref, ...), custom_call_target="tpu_custom_call" | custom-call | flops 2684354560 | bytes 6291456 | tf_op jit(solution)/shard_map/attention_backward/pallas_call | solution.py:177
  458.0 5.8 weight_terms.6
  481.2 6.0 %weight_terms.7 = (bf16[16,32,1536]{2,1,0:T(8,128)(2,1)}, bf16[16,32,1536]{2,1,0:T(8,128)(2,1)}) custom-call(s32[5]{0:T(128)S(1)} %copy-done.30, bf16[512,1024]{1,0:T(8,128)(2,1)S(1)} %copy-done.15, bf16[512,1024]{1,0:T(8,128)(2,1)S(1)} %copy-done.18, bf16[512,512]{1,0:T(8,128)(2,1)S(1)} %copy-done.12, bf16[512,512]{1,0:T(8,128)(2,1)S(1)} %copy-done.8, ...), custom_call_target="tpu_custom_call" | custom-call | flops 3221225472 | bytes 8388608 | tf_op jit(solution)/shard_map/weight_terms/pallas_call | solution.py:365
  487.3 4.7 collective-permute-done.65
  494.4 4.3 convert_add_fusion.14
  519.5 4.8 collective-permute-done.70
  538.3 6.0 %collective-permute-done.71 = bf16[1,4,16,1536]{3,2,1,0:T(8,128)(2,1)} collective-permute-done((bf16[1,4,16,1536]{3,2,1,0:T(8,128)(2,1)}, bf16[1,4,16,1536]{3,2,1,0:T(8,128)(2,1)}, u32[]{:S(2)}, u32[]{:S(2)}) %collective-permute-start.71) | collective-permute-done | bytes 196640 | tf_op jit(solution)/shard_map/ppermute | solution.py:398
  582.9 5.0 collective-permute-done.89
  (619 shorter events, 285.7 us)
Async XLA Ops:
  0.7 22.6 %collective-permute-start.4 = (bf16[512,1024]{1,0:T(8,128)(2,1)}, bf16[512,1024]{1,0:T(8,128)(2,1)S(1)}, u32[]{:S(2)}, u32[]{:S(2)}) collective-permute-start(bf16[512,1024]{1,0:T(8,128)(2,1)} %bitcast.493), channel_id=1, source_target_pairs={{1,16},{16,1},{3,18},{18,3},{5,20},{20,5},{7,22},{22,7},{9,24},{24... | collective-permute-start | bytes 3145736 | tf_op jit(solution)/shard_map/ppermute | solution.py:413
  46.5 20.1 %collective-permute-start.10 = (bf16[2,1,4,16,3200]{4,3,2,1,0:T(8,128)(2,1)S(1)}, bf16[2,1,4,16,3200]{4,3,2,1,0:T(8,128)(2,1)S(1)}, u32[]{:S(2)}, u32[]{:S(2)}) collective-permute-start(bf16[2,1,4,16,3200]{4,3,2,1,0:T(8,128)(2,1)S(1)} %get-tuple-element.280.refs_0_), channel_id=1, source_target_pairs={{0,2},{2,0},{1,3},{3,1},{4,6},{6,4},{5,7},{7,5},{8,10},{10,8},{9,1... | collective-permute-start | bytes 2457608 | tf_op jit(solution)/shard_map/ppermute | solution.py:398
  47.1 19.7 %collective-permute-start.11 = (bf16[2,1,4,16,3200]{4,3,2,1,0:T(8,128)(2,1)S(1)}, bf16[2,1,4,16,3200]{4,3,2,1,0:T(8,128)(2,1)S(1)}, u32[]{:S(2)}, u32[]{:S(2)}) collective-permute-start(bf16[2,1,4,16,3200]{4,3,2,1,0:T(8,128)(2,1)S(1)} %get-tuple-element.281.refs_1_), channel_id=1, source_target_pairs={{0,16},{16,0},{1,17},{17,1},{2,18},{18,2},{3,19},{19,3},{4,20},{20... | collective-permute-start | bytes 2457608 | tf_op jit(solution)/shard_map/ppermute | solution.py:398
  75.0 22.1 %collective-permute-start.21 = (bf16[128,512]{1,0:T(8,128)(2,1)S(1)}, bf16[128,512]{1,0:T(8,128)(2,1)S(1)}, u32[]{:S(2)}, u32[]{:S(2)}) collective-permute-start(bf16[128,512]{1,0:T(8,128)(2,1)S(1)} %get-tuple-element.301.refs_0_), channel_id=1, source_target_pairs={{0,4},{4,8},{8,12},{12,0},{1,5},{5,9},{9,13},{13,1},{2,6},{6,10},{... | collective-permute-start | bytes 393224 | tf_op jit(solution)/shard_map/ppermute | solution.py:410
  78.4 18.7 %collective-permute-start.22 = (bf16[128,512]{1,0:T(8,128)(2,1)S(1)}, bf16[128,512]{1,0:T(8,128)(2,1)S(1)}, u32[]{:S(2)}, u32[]{:S(2)}) collective-permute-start(bf16[128,512]{1,0:T(8,128)(2,1)S(1)} %get-tuple-element.301.refs_0_), channel_id=1, source_target_pairs={{0,8},{4,12},{8,0},{12,4},{1,9},{5,13},{9,1},{13,5},{2,10},{6,14},... | collective-permute-start | bytes 393224 | tf_op jit(solution)/shard_map/ppermute | solution.py:410
  106.9 31.3 %collective-permute-start.26 = (bf16[2,1,4,16,5120]{4,3,2,1,0:T(8,128)(2,1)S(1)}, bf16[2,1,4,16,5120]{4,3,2,1,0:T(8,128)(2,1)}, u32[]{:S(2)}, u32[]{:S(2)}) collective-permute-start(bf16[2,1,4,16,5120]{4,3,2,1,0:T(8,128)(2,1)S(1)} %get-tuple-element.312.refs_0_), channel_id=1, source_target_pairs={{0,2},{2,0},{1,3},{3,1},{4,6},{6,4},{5,7},{7,5},{8,10},{10,8},{9,1... | collective-permute-start | bytes 3932168 | tf_op jit(solution)/shard_map/ppermute | solution.py:398
  108.5 30.9 %collective-permute-start.27 = (bf16[2,1,4,16,5120]{4,3,2,1,0:T(8,128)(2,1)S(1)}, bf16[2,1,4,16,5120]{4,3,2,1,0:T(8,128)(2,1)}, u32[]{:S(2)}, u32[]{:S(2)}) collective-permute-start(bf16[2,1,4,16,5120]{4,3,2,1,0:T(8,128)(2,1)S(1)} %get-tuple-element.313.refs_1_), channel_id=1, source_target_pairs={{0,16},{16,0},{1,17},{17,1},{2,18},{18,2},{3,19},{19,3},{4,20},{20... | collective-permute-start | bytes 3932168 | tf_op jit(solution)/shard_map/ppermute | solution.py:398
  111.9 24.3 %collective-permute-start.28 = (bf16[128,512]{1,0:T(8,128)(2,1)S(1)}, bf16[128,512]{1,0:T(8,128)(2,1)S(1)}, u32[]{:S(2)}, u32[]{:S(2)}) collective-permute-start(bf16[128,512]{1,0:T(8,128)(2,1)S(1)} %copy-done.88), channel_id=1, source_target_pairs={{0,4},{4,8},{8,12},{12,0},{1,5},{5,9},{9,13},{13,1},{2,6},{6,10},{... | collective-permute-start | bytes 393224 | tf_op jit(solution)/shard_map/ppermute | solution.py:410
  113.1 23.1 %collective-permute-start.29 = (bf16[128,512]{1,0:T(8,128)(2,1)S(1)}, bf16[128,512]{1,0:T(8,128)(2,1)S(1)}, u32[]{:S(2)}, u32[]{:S(2)}) collective-permute-start(bf16[128,512]{1,0:T(8,128)(2,1)S(1)} %copy-done.88), channel_id=1, source_target_pairs={{0,8},{4,12},{8,0},{12,4},{1,9},{5,13},{9,1},{13,5},{2,10},{6,14},... | collective-permute-start | bytes 393224 | tf_op jit(solution)/shard_map/ppermute | solution.py:410
  114.1 22.7 %collective-permute-start.30 = (bf16[128,512]{1,0:T(8,128)(2,1)S(1)}, bf16[128,512]{1,0:T(8,128)(2,1)S(1)}, u32[]{:S(2)}, u32[]{:S(2)}) collective-permute-start(bf16[128,512]{1,0:T(8,128)(2,1)S(1)} %copy-done.88), channel_id=1, source_target_pairs={{0,12},{4,0},{8,4},{12,8},{1,13},{5,1},{9,5},{13,9},{2,14},{6,2},{... | collective-permute-start | bytes 393224 | tf_op jit(solution)/shard_map/ppermute | solution.py:410
  169.3 24.1 %collective-permute-start.37 = (bf16[2,1,4,64,1024]{4,3,2,1,0:T(8,128)(2,1)S(1)}, bf16[2,1,4,64,1024]{4,3,2,1,0:T(8,128)(2,1)S(1)}, u32[]{:S(2)}, u32[]{:S(2)}) collective-permute-start(bf16[2,1,4,64,1024]{4,3,2,1,0:T(8,128)(2,1)S(1)} %get-tuple-element.344.refs_0_), channel_id=1, source_target_pairs={{0,2},{2,0},{1,3},{3,1},{4,6},{6,4},{5,7},{7,5},{8,10},{10,8},{9,1... | collective-permute-start | bytes 3145736 | tf_op jit(solution)/shard_map/ppermute | solution.py:398
  170.7 23.8 %collective-permute-start.38 = (bf16[2,1,4,64,1024]{4,3,2,1,0:T(8,128)(2,1)S(1)}, bf16[2,1,4,64,1024]{4,3,2,1,0:T(8,128)(2,1)S(1)}, u32[]{:S(2)}, u32[]{:S(2)}) collective-permute-start(bf16[2,1,4,64,1024]{4,3,2,1,0:T(8,128)(2,1)S(1)} %get-tuple-element.345.refs_1_), channel_id=1, source_target_pairs={{0,16},{16,0},{1,17},{17,1},{2,18},{18,2},{3,19},{19,3},{4,20},{20... | collective-permute-start | bytes 3145736 | tf_op jit(solution)/shard_map/ppermute | solution.py:398
  171.6 23.3 %collective-permute-start.39 = (bf16[2,1,4,64,1024]{4,3,2,1,0:T(8,128)(2,1)S(1)}, bf16[2,1,4,64,1024]{4,3,2,1,0:T(8,128)(2,1)S(1)}, u32[]{:S(2)}, u32[]{:S(2)}) collective-permute-start(bf16[2,1,4,64,1024]{4,3,2,1,0:T(8,128)(2,1)S(1)} %get-tuple-element.344.refs_0_), channel_id=1, source_target_pairs={{0,1},{1,0},{2,3},{3,2},{4,5},{5,4},{6,7},{7,6},{8,9},{9,8},{10,11... | collective-permute-start | bytes 3145736 | tf_op jit(solution)/shard_map/ppermute | solution.py:398
  171.7 23.2 %collective-permute-start.40 = (bf16[2,1,4,64,1024]{4,3,2,1,0:T(8,128)(2,1)S(1)}, bf16[2,1,4,64,1024]{4,3,2,1,0:T(8,128)(2,1)S(1)}, u32[]{:S(2)}, u32[]{:S(2)}) collective-permute-start(bf16[2,1,4,64,1024]{4,3,2,1,0:T(8,128)(2,1)S(1)} %get-tuple-element.345.refs_1_), channel_id=1, source_target_pairs={{0,1},{1,0},{2,3},{3,2},{4,5},{5,4},{6,7},{7,6},{8,9},{9,8},{10,11... | collective-permute-start | bytes 3145736 | tf_op jit(solution)/shard_map/ppermute | solution.py:398
  212.3 24.0 %collective-permute-start.44 = (bf16[512,1024]{1,0:T(8,128)(2,1)}, bf16[512,1024]{1,0:T(8,128)(2,1)}, u32[]{:S(2)}, u32[]{:S(2)}) collective-permute-start(bf16[512,1024]{1,0:T(8,128)(2,1)} %bitcast.32), channel_id=1, source_target_pairs={{1,16},{16,1},{3,18},{18,3},{5,20},{20,5},{7,22},{22,7},{9,24},{24... | collective-permute-start | bytes 3145736 | tf_op jit(solution)/shard_map/ppermute | solution.py:413
  280.4 38.9 %collective-permute-start.47 = (bf16[512,1024]{1,0:T(8,128)(2,1)}, bf16[512,1024]{1,0:T(8,128)(2,1)}, u32[]{:S(2)}, u32[]{:S(2)}) collective-permute-start(bf16[512,1024]{1,0:T(8,128)(2,1)} %add_convert_fusion.8), channel_id=1, source_target_pairs={{1,16},{16,1},{3,18},{18,3},{5,20},{20,5},{7,22},{22,7},{9,24},{24... | collective-permute-start | bytes 3145736 | tf_op jit(solution)/shard_map/ppermute | solution.py:413
  298.5 22.2 %collective-permute-start.49 = (bf16[2,512,512]{2,1,0:T(8,128)(2,1)}, bf16[2,512,512]{2,1,0:T(8,128)(2,1)S(1)}, u32[]{:S(2)}, u32[]{:S(2)}) collective-permute-start(bf16[2,512,512]{2,1,0:T(8,128)(2,1)} %get-tuple-element.384), channel_id=1, source_target_pairs={{0,1},{1,0},{2,3},{3,2},{4,5},{5,4},{6,7},{7,6},{8,9},{9,8},{10,11... | collective-permute-start | bytes 3145736 | tf_op jit(solution)/shard_map/ppermute | solution.py:398
  375.7 25.3 %collective-permute-start.51 = (bf16[1,4,2,64,1024]{4,3,2,1,0:T(8,128)(2,1)S(1)}, bf16[1,4,2,64,1024]{4,3,2,1,0:T(8,128)(2,1)}, u32[]{:S(2)}, u32[]{:S(2)}) collective-permute-start(bf16[1,4,2,64,1024]{4,3,2,1,0:T(8,128)(2,1)S(1)} %fusion.18), channel_id=1, source_target_pairs={{0,16},{16,0},{1,17},{17,1},{2,18},{18,2},{3,19},{19,3},{4,20},{20... | collective-permute-start | bytes 3145736 | tf_op jit(solution)/shard_map/ppermute | solution.py:398
  376.5 25.3 %collective-permute-start.52 = (bf16[1,2,4,64,1024]{4,3,2,1,0:T(8,128)(2,1)S(1)}, bf16[1,2,4,64,1024]{4,3,2,1,0:T(8,128)(2,1)}, u32[]{:S(2)}, u32[]{:S(2)}) collective-permute-start(bf16[1,2,4,64,1024]{4,3,2,1,0:T(8,128)(2,1)S(1)} %fusion.19), channel_id=1, source_target_pairs={{0,2},{2,0},{1,3},{3,1},{4,6},{6,4},{5,7},{7,5},{8,10},{10,8},{9,1... | collective-permute-start | bytes 3145736 | tf_op jit(solution)/shard_map/ppermute | solution.py:398
  433.2 22.3 %collective-permute-start.56 = (bf16[2,512,512]{2,1,0:T(8,128)(2,1)}, bf16[2,512,512]{2,1,0:T(8,128)(2,1)}, u32[]{:S(2)}, u32[]{:S(2)}) collective-permute-start(bf16[2,512,512]{2,1,0:T(8,128)(2,1)} %get-tuple-element.430), channel_id=1, source_target_pairs={{0,1},{1,0},{2,3},{3,2},{4,5},{5,4},{6,7},{7,6},{8,9},{9,8},{10,11... | collective-permute-start | bytes 3145736 | tf_op jit(solution)/shard_map/ppermute | solution.py:398
  433.2 31.5 %collective-permute-start.57 = (bf16[1,4,2,16,5120]{4,3,2,1,0:T(8,128)(2,1)}, bf16[1,4,2,16,5120]{4,3,2,1,0:T(8,128)(2,1)}, u32[]{:S(2)}, u32[]{:S(2)}) collective-permute-start(bf16[1,4,2,16,5120]{4,3,2,1,0:T(8,128)(2,1)} %fusion.12), channel_id=1, source_target_pairs={{0,16},{16,0},{1,17},{17,1},{2,18},{18,2},{3,19},{19,3},{4,20},{20... | collective-permute-start | bytes 3932168 | tf_op jit(solution)/shard_map/ppermute | solution.py:398
  434.3 31.2 %collective-permute-start.58 = (bf16[1,2,4,16,5120]{4,3,2,1,0:T(8,128)(2,1)}, bf16[1,2,4,16,5120]{4,3,2,1,0:T(8,128)(2,1)}, u32[]{:S(2)}, u32[]{:S(2)}) collective-permute-start(bf16[1,2,4,16,5120]{4,3,2,1,0:T(8,128)(2,1)} %fusion.13), channel_id=1, source_target_pairs={{0,2},{2,0},{1,3},{3,1},{4,6},{6,4},{5,7},{7,5},{8,10},{10,8},{9,1... | collective-permute-start | bytes 3932168 | tf_op jit(solution)/shard_map/ppermute | solution.py:398
  436.7 27.1 %collective-permute-start.59 = (bf16[128,1024]{1,0:T(8,128)(2,1)}, bf16[128,1024]{1,0:T(8,128)(2,1)S(1)}, u32[]{:S(2)}, u32[]{:S(2)}) collective-permute-start(bf16[128,1024]{1,0:T(8,128)(2,1)} %pad_maximum_fusion.3), channel_id=1, source_target_pairs={{0,4},{4,8},{8,12},{12,0},{1,5},{5,9},{9,13},{13,1},{2,6},{6,10},{... | collective-permute-start | bytes 786440 | tf_op jit(solution)/shard_map/ppermute | solution.py:410
  437.2 26.6 %collective-permute-start.60 = (bf16[128,1024]{1,0:T(8,128)(2,1)}, bf16[128,1024]{1,0:T(8,128)(2,1)S(1)}, u32[]{:S(2)}, u32[]{:S(2)}) collective-permute-start(bf16[128,1024]{1,0:T(8,128)(2,1)} %pad_maximum_fusion.5), channel_id=1, source_target_pairs={{0,12},{4,0},{8,4},{12,8},{1,13},{5,1},{9,5},{13,9},{2,14},{6,2},{... | collective-permute-start | bytes 786440 | tf_op jit(solution)/shard_map/ppermute | solution.py:410
  471.8 20.2 %collective-permute-start.64 = (bf16[1,2,4,2,32,1536]{5,4,3,2,1,0:T(8,128)(2,1)}, bf16[1,2,4,2,32,1536]{5,4,3,2,1,0:T(8,128)(2,1)}, u32[]{:S(2)}, u32[]{:S(2)}) collective-permute-start(bf16[1,2,4,2,32,1536]{5,4,3,2,1,0:T(8,128)(2,1)} %bitcast.80), channel_id=1, source_target_pairs={{0,1},{1,0},{2,3},{3,2},{4,5},{5,4},{6,7},{7,6},{8,9},{9,8},{10,11... | collective-permute-start | bytes 4718600 | tf_op jit(solution)/shard_map/ppermute | solution.py:398
  473.2 18.8 %collective-permute-start.62 = (bf16[1,4,16,5120]{3,2,1,0:T(8,128)(2,1)}, bf16[1,4,16,5120]{3,2,1,0:T(8,128)(2,1)}, u32[]{:S(2)}, u32[]{:S(2)}) collective-permute-start(bf16[1,4,16,5120]{3,2,1,0:T(8,128)(2,1)} %get-tuple-element.452), channel_id=1, source_target_pairs={{0,2},{2,0},{1,3},{3,1},{4,6},{6,4},{5,7},{7,5},{8,10},{10,8},{9,1... | collective-permute-start | bytes 1966088 | tf_op jit(solution)/shard_map/ppermute | solution.py:398
  474.4 17.5 %collective-permute-start.63 = (bf16[1,4,16,5120]{3,2,1,0:T(8,128)(2,1)}, bf16[1,4,16,5120]{3,2,1,0:T(8,128)(2,1)}, u32[]{:S(2)}, u32[]{:S(2)}) collective-permute-start(bf16[1,4,16,5120]{3,2,1,0:T(8,128)(2,1)} %get-tuple-element.453), channel_id=1, source_target_pairs={{0,16},{16,0},{1,17},{17,1},{2,18},{18,2},{3,19},{19,3},{4,20},{20... | collective-permute-start | bytes 1966088 | tf_op jit(solution)/shard_map/ppermute | solution.py:398
  505.2 19.2 %collective-permute-start.66 = (bf16[1,4,2,16,1536]{4,3,2,1,0:T(8,128)(2,1)S(1)}, bf16[1,4,2,16,1536]{4,3,2,1,0:T(8,128)(2,1)S(1)}, u32[]{:S(2)}, u32[]{:S(2)}) collective-permute-start(bf16[1,4,2,16,1536]{4,3,2,1,0:T(8,128)(2,1)S(1)} %fusion.30), channel_id=1, source_target_pairs={{0,16},{16,0},{1,17},{17,1},{2,18},{18,2},{3,19},{19,3},{4,20},{20... | collective-permute-start | bytes 1179656 | tf_op jit(solution)/shard_map/ppermute | solution.py:398
  506.3 18.0 %collective-permute-start.67 = (bf16[1,2,4,16,1536]{4,3,2,1,0:T(8,128)(2,1)S(1)}, bf16[1,2,4,16,1536]{4,3,2,1,0:T(8,128)(2,1)S(1)}, u32[]{:S(2)}, u32[]{:S(2)}) collective-permute-start(bf16[1,2,4,16,1536]{4,3,2,1,0:T(8,128)(2,1)S(1)} %fusion.31), channel_id=1, source_target_pairs={{0,2},{2,0},{1,3},{3,1},{4,6},{6,4},{5,7},{7,5},{8,10},{10,8},{9,1... | collective-permute-start | bytes 1179656 | tf_op jit(solution)/shard_map/ppermute | solution.py:398
  528.4 19.1 %collective-permute-start.73 = (bf16[1,4,2,16,1536]{4,3,2,1,0:T(8,128)(2,1)}, bf16[1,4,2,16,1536]{4,3,2,1,0:T(8,128)(2,1)S(1)}, u32[]{:S(2)}, u32[]{:S(2)}) collective-permute-start(bf16[1,4,2,16,1536]{4,3,2,1,0:T(8,128)(2,1)} %fusion.32), channel_id=1, source_target_pairs={{0,16},{16,0},{1,17},{17,1},{2,18},{18,2},{3,19},{19,3},{4,20},{20... | collective-permute-start | bytes 1179656 | tf_op jit(solution)/shard_map/ppermute | solution.py:398
  529.4 18.2 %collective-permute-start.74 = (bf16[1,2,4,16,1536]{4,3,2,1,0:T(8,128)(2,1)}, bf16[1,2,4,16,1536]{4,3,2,1,0:T(8,128)(2,1)}, u32[]{:S(2)}, u32[]{:S(2)}) collective-permute-start(bf16[1,2,4,16,1536]{4,3,2,1,0:T(8,128)(2,1)} %fusion.33), channel_id=1, source_target_pairs={{0,2},{2,0},{1,3},{3,1},{4,6},{6,4},{5,7},{7,5},{8,10},{10,8},{9,1... | collective-permute-start | bytes 1179656 | tf_op jit(solution)/shard_map/ppermute | solution.py:398
  572.3 18.2 %collective-permute-start.80 = (bf16[512,1024]{1,0:T(8,128)(2,1)S(1)}, bf16[512,1024]{1,0:T(8,128)(2,1)S(1)}, u32[]{:S(2)}, u32[]{:S(2)}) collective-permute-start(bf16[512,1024]{1,0:T(8,128)(2,1)S(1)} %get-tuple-element.506), channel_id=1, source_target_pairs={{1,16},{16,1},{3,18},{18,3},{5,20},{20,5},{7,22},{22,7},{9,24},{24... | collective-permute-start | bytes 3145736 | tf_op jit(solution)/shard_map/ppermute | solution.py:413
  (200 other events, 1791.0 us)

commit v5 on v4

--- a/solution.py
+++ b/solution.py
@@ -211,7 +211,7 @@
     hidden_units = weight.shape[1]
     width = math.gcd(bias_rows.shape[1], 512)
     per_row = bias_rows.shape[1] // width
-    rows = math.gcd(tokens, 128)
+    rows = math.gcd(tokens, 256)
     bias = bias_rows.reshape(-1, 1, width)
 
     def kernel(x_ref, w_ref, b_ref, act_ref, slope_ref):
@@ -329,7 +329,7 @@
     rights = [right for _, parts in jobs for part in parts for right in part]
     depth = len(jobs[0][0])
     left_of = [job for job, (_, parts) in enumerate(jobs) for _ in parts]
-    block = 256
+    block = 1024 if height > 1024 else 256
     pairs = block // (2 * rows)
 
     def kernel(at_ref, *refs):
@@ -371,7 +371,7 @@
         out_specs=[out, out],
         out_shape=[jax.ShapeDtypeStruct((shards // 2, rows, columns), BF)] * 2,
         compiler_params=pltpu.CompilerParams(
-            dimension_semantics=("arbitrary",), vmem_limit_bytes=48 << 20
+            dimension_semantics=("arbitrary",), vmem_limit_bytes=(60 if height > 1024 else 48) << 20
         ),
         cost_estimate=pl.CostEstimate(
             flops=2 * depth * tokens * height * columns,
@@ -469,6 +469,7 @@
         self.columns = sum(chunk.shape[1] for chunk in chunks)
         self.kind = chunks[0].dtype
         self.far = [None] * len(chunks)
+        self.roomy = len(widths) > 1 or len(chunks) > 1
 
     def new(self, *lead):
         return jax.ShapeDtypeStruct((*lead, self.half, self.columns), self.kind)
@@ -507,7 +508,7 @@
             [p[0] for p in pieces],
             [self.new(high, deep)] * 2,
             moves,
-            (60 << 20) if len(self.chunks) > 1 else None,
+            (60 << 20) if self.roomy else None,
         )
 
     def go_first(self):
@@ -746,7 +747,7 @@
     block = jnp.pad(block, ((0, tiles * shard_rows - block.shape[0]), (0, 0)))
     block = block.reshape(tiles, shard_rows, LANES).transpose(1, 0, 2).reshape(shard_rows, -1)
 
-    middle_up, middle_down = w_up.shape[1] // 2, w_down.shape[1] // 2
+    middle_up = w_up.shape[1] // 2
     one = Gather(
         grid, [jnp.concatenate([w_qkv, block], axis=1)], [w_qkv.shape[1], tiles * LANES]
     )
@@ -755,7 +756,7 @@
         [w_up[:, :middle_up], jnp.concatenate([w_up[:, middle_up:], w_out], axis=1)],
         [w_up.shape[1], w_out.shape[1]],
     )
-    three = Gather(grid, [w_down[:, :middle_down], w_down[:, middle_down:]], [w_down.shape[1]])
+    three = Gather(grid, [w_down], [w_down.shape[1]])
     labels = jnp.concatenate(
         [segment_ids, key_mask, jnp.broadcast_to(lead_index.reshape(2, 1), (2, tokens))]
     )
@@ -770,6 +771,7 @@
     key_labels = jnp.concatenate(grid.mates(own_labels))
     own_labels_across, key_labels_across = own_labels.T, key_labels.T
     high = grid.size["h"]
+    blocks = high * grid.size["x"] * grid.size["z"]
 
     one.make_lines()
     one.sends, two.chunks[0] = tie((one.sends, two.chunks[0]))
@@ -785,10 +787,9 @@
     one.go_pair_far()
     two.make_lines()
     crossed = [t[0] for t in one.pairs]
-    crossed, two.sends, three.chunks[0] = tie((crossed, two.sends, three.chunks[0]))
+    crossed, two.sends = tie((crossed, two.sends))
     one.pairs = [(t,) + pair[1:] for t, pair in zip(crossed, one.pairs)]
     two.go_first()
-    three.go_far(0)
     weight_qkv, small = one.result()
     weights = {"qkv": weight_qkv}
     small = small.reshape(shards, shard_rows, -1)
@@ -800,15 +801,15 @@
     bias_full, gains, shifts, lead_rows = (small[cuts[i] : cuts[i + 1]] for i in range(4))
 
     def before_exchange(values):
+        values, two.arrived, three.chunks[0] = tie((values, two.arrived, three.chunks[0]))
+        two.make_planes()
+        values, two.sends, three.chunks[0] = tie((values, two.sends, three.chunks[0]))
+        two.go_second()
+        three.go_far(0)
+        return values
+
+    def after_attention(values):
         values, two.arrived, three.far[0] = tie((values, two.arrived, three.far[0]))
-        two.make_planes()
-        values, two.sends, three.chunks[1] = tie((values, two.sends, three.chunks[1]))
-        two.go_second()
-        three.go_far(1)
-        return values
-
-    def after_attention(values):
-        values, two.arrived, three.far[1] = tie((values, two.arrived, three.far[1]))
         two.go_pair_near()
         two.go_pair_far()
         three.make_lines()
@@ -816,13 +817,11 @@
         values, crossed, three.sends = tie((values, crossed, three.sends))
         two.pairs = [(t,) + pair[1:] for t, pair in zip(crossed, two.pairs)]
         three.go_first()
-        weights["up"], weights["out"] = two.result()
-        return values
-
-    def before_gate(values):
-        values, three.arrived = tie((values, three.arrived))
+        placed = two.result()
+        values, three.arrived, placed = tie((values, three.arrived, placed))
         three.make_planes()
-        values, three.sends = tie((values, three.sends))
+        values, three.sends, placed = tie((values, three.sends, placed))
+        weights["up"], weights["out"] = placed
         three.go_second()
         three.go_pair_near()
         return values
@@ -967,13 +966,13 @@
             [
                 jnp.stack([bias_query, bias_value, bias_attn, bias_down, gain_in, gain_mid, shift_in, shift_mid]),
                 chooser[:, None] * lead_sum[None, :],
-                bias_gate.reshape(-1, model),
+                bias_gate.reshape(blocks, -1, model // blocks).transpose(1, 0, 2).reshape(-1, model),
             ]
         )
         return (grad_start, operands, sums, vectors)
 
     result_first, saved_first = forward(
-        start_low.astype(F32), leads[0], [before_exchange, after_attention, before_gate, after_gate]
+        start_low.astype(F32), leads[0], [before_exchange, after_attention, keep, after_gate]
     )
     first_low = result_first.astype(BF)
     first_low, seed_first, seed_second = tie((first_low, cotangent_first[0], cotangent_second[0]))
@@ -1026,15 +1025,30 @@
     vectors, grad_low = advance((vectors, grad_low), [qkv1])
     qkv1.go(1)
     grad_moved = grid.swapped(grad_low)
-    vectors = sum_far(grid, sum_near(grid, vectors, "x"))
+    vectors = sum_near(grid, vectors, "x")
+
+    def block_at(step):
+        place = {
+            name: lax.rem(grid.at[name] + k, grid.size[name]) for name, k in zip("hz", step)
+        }
+        at = (place["h"] * grid.size["x"] + grid.at["x"]) * grid.size["z"] + place["z"]
+        return lax.dynamic_slice_in_dim(vectors, at * (model // blocks), model // blocks, 1)
+
+    vectors = total(
+        [block_at((0, 0))]
+        + [grid.far_shift(block_at(step), step) for step in grid.far_steps() if step != (0, 0)]
+    )
     input_grad = grid.choose(grad_low, grad_moved).astype(F32)
     shares = {name: sums[name].result() for name in ("down", "up", "mix", "qkv1")}
     width = shares["qkv1"].shape[1] // 3
     sides = [shares["mix"], shares["qkv1"]]
-    own_columns = lax.dynamic_slice_in_dim(vectors, grid.shard * share, share, 1)
+    within = grid.at["y"] * 2 + grid.at["c"]
+    own_columns = lax.dynamic_slice_in_dim(vectors, within * share, share, 1)
     small_out = [own_columns[cuts[i] : cuts[i + 1]] for i in range(4)]
+    up_at = within * own_up
+    up_width = model // blocks
     up_out = lax.dynamic_slice(
-        vectors, (cuts[4] + grid.shard // per_row, (grid.shard % per_row) * own_up), (1, own_up)
+        vectors, (cuts[4] + up_at // up_width, up_at % up_width), (1, own_up)
     )[0]
     return (
         first_low[None],

time: 602 us -> 584 us (0.970)
  starting transfers between devices: 103 us -> 96.6 us
    ppermute x54, waiting for transfers between devices: 59.1 us -> 49.5 us  [shift(): return lax.ppermute(tensor, axis, [(i, (i + step) % n) for i in range(n)])]
    ppermute x30 -> x27, starting transfers between devices: 53.6 us -> 47.4 us  [far_shift(): return lax.ppermute(tensor, ('h', 'z'), pairs)]
    ppermute x30 -> x27, waiting for transfers between devices: 53.1 us -> 56.3 us  [far_shift(): return lax.ppermute(tensor, ('h', 'z'), pairs)]
    unnamed x299 -> x273, local copies, waits for them, and re-layouts: 20.4 us -> 20.1 us
  transfers between devices with their start and end apart: 91 -> 88, of which waited for: 37 -> 36; matrix products, arithmetic and copies ran while one was open for 9% -> 10% of each run, Pallas kernels for 32% -> 33%
where the time goes in v5:
time: 584 us; the launch traced here: 573 us
  Pallas kernels  216 us (37%)
  waiting for transfers between devices  106 us (18%)
  starting transfers between devices  96.6 us (17%)
  other arithmetic  82.4 us (14%)
  matrix products  36 us (6%)
  local copies, waits for them, and re-layouts  32.9 us (6%)
    pallas_call x4, Pallas kernels, attention_backward(): pl.pallas_call(kernel, grid=(pairs,), in_specs=[own, keys_at, keys_at, va...  60 us
    ppermute x27, waiting for transfers between devices, far_shift(): return lax.ppermute(tensor, ('h', 'z'), pairs)  56.3 us
    ppermute x54, waiting for transfers between devices, shift(): return lax.ppermute(tensor, axis, [(i, (i + step) % n) for i in range(n)])  49.5 us
    ppermute x27, starting transfers between devices, far_shift(): return lax.ppermute(tensor, ('h', 'z'), pairs)  47.4 us
    pallas_call x4, Pallas kernels, weight_terms(): pl.pallas_call(kernel, grid=(height // block,), in_specs=[pl.BlockSpec(me...  43.5 us
    ppermute x54, starting transfers between devices, shift(): return lax.ppermute(tensor, axis, [(i, (i + step) % n) for i in range(n)])  40.7 us
    pallas_call x2, Pallas kernels, attention_forward(): pl.pallas_call(kernel, grid=(pairs,), in_specs=[pl.BlockSpec((tokens, PAI...  39.8 us
    pallas_call x2, Pallas kernels, gated_backward(): pl.pallas_call(kernel, grid=(steps,), in_specs=[pl.BlockSpec((tokens, mod...  25.6 us
  transfers between devices with their start and end apart: 88, of which 36 were waited for; matrix products, arithmetic and copies ran while one was open for 10% of the time, Pallas kernels for 33%

profile of v5, /device:TPU:0, one launch (start us, length us, event | category | flops | bytes accessed | tf_op | source)
XLA Modules:
  0.0 573.2 jit_solution(4587653460401608191)
XLA Ops:
  14.4 9.0 %collective-permute-done.1.refs_2_ = bf16[32,3200]{1,0:T(8,128)(2,1)S(1)} collective-permute-done((bf16[32,3200]{1,0:T(8,128)(2,1)S(1)}, bf16[32,3200]{1,0:T(8,128)(2,1)S(1)}, u32[]{:S(2)}, u32[]{:S(2)}) %collective-permute-start.1) | collective-permute-done | bytes 204832 | tf_op jit(solution)/shard_map/ppermute | solution.py:410
  29.4 4.8 collective-permute-start.7
  39.8 4.2 collective-permute-done.8.refs_2_
  56.9 4.9 collective-permute-done.12.refs_5_
  61.8 6.5 %collective-permute-done.13.refs_6_ = bf16[32,3072]{1,0:T(8,128)(2,1)S(1)} collective-permute-done((bf16[32,3072]{1,0:T(8,128)(2,1)S(1)}, bf16[32,3072]{1,0:T(8,128)(2,1)S(1)}, u32[]{:S(2)}, u32[]{:S(2)}) %collective-permute-start.13) | collective-permute-done | bytes 196640 | tf_op jit(solution)/shard_map/ppermute | solution.py:410
  91.5 6.6 %collective-permute-done.19.refs_2_ = bf16[1,4,16,5120]{3,2,1,0:T(8,128)(2,1)S(1)} collective-permute-done((bf16[1,4,16,5120]{3,2,1,0:T(8,128)(2,1)S(1)}, bf16[1,4,16,5120]{3,2,1,0:T(8,128)(2,1)S(1)}, u32[]{:S(2)}, u32[]{:S(2)}) %collective-permute-start.19) | collective-permute-done | bytes 655392 | tf_op jit(solution)/shard_map/ppermute | solution.py:398
  112.5 19.9 %attention_forward.2 = (f32[512,1024]{1,0:T(8,128)}, bf16[512,1024]{1,0:T(8,128)(2,1)}, f32[8,2,512]{2,1,0:T(2,128)}) custom-call(bf16[512,1024]{1,0:T(8,128)(2,1)} %fusion.20.q_ref, bf16[512,2048]{1,0:T(8,128)(2,1)} %fusion.1.k0_ref.v0_ref, bf16[512,2048]{1,0:T(8,128)(2,1)} %collective-permute-done.21.k1_ref.v1_ref, bf16[512,2048]{1,0:T(8,128)(2,1)} %fusion.1.k0_ref.v0_ref, ...), custom_call_target="tpu_custom_call" | custom-call | flops 2147483648 | bytes 10485760 | tf_op jit(solution)/shard_map/attention_forward/pallas_call | solution.py:97
  147.4 7.9 %collective-permute-done.32.refs_2_ = bf16[1,4,64,1024]{3,2,1,0:T(8,128)(2,1)S(1)} collective-permute-done((bf16[1,4,64,1024]{3,2,1,0:T(8,128)(2,1)S(1)}, bf16[1,4,64,1024]{3,2,1,0:T(8,128)(2,1)S(1)}, u32[]{:S(2)}, u32[]{:S(2)}) %collective-permute-start.32) | collective-permute-done | bytes 524320 | tf_op jit(solution)/shard_map/ppermute | solution.py:398
  161.9 11.1 %gated.2 = (bf16[512,4096]{1,0:T(8,128)(2,1)S(1)}, bf16[512,4096]{1,0:T(8,128)(2,1)S(1)}) custom-call(bf16[512,1024]{1,0:T(8,128)(2,1)S(1)} %add_convert_fusion.12.x_ref.refs_0_, bf16[1024,4096]{1,0:T(8,128)(2,1)} %bitcast.464, f32[8,1,512]{2,1,0:T(1,128)S(1)} %bitcast.460), custom_call_target="tpu_custom_call" | custom-call | flops 4294967296 | bytes 16777216 | tf_op jit(solution)/shard_map/gated/pallas_call | solution.py:228
  173.0 8.2 %collective-permute-done.34.refs_2_ = bf16[2,1,4,64,1024]{4,3,2,1,0:T(8,128)(2,1)S(1)} collective-permute-done((bf16[2,1,4,64,1024]{4,3,2,1,0:T(8,128)(2,1)S(1)}, bf16[2,1,4,64,1024]{4,3,2,1,0:T(8,128)(2,1)S(1)}, u32[]{:S(2)}, u32[]{:S(2)}) %collective-permute-start.34) | collective-permute-done | bytes 1048608 | tf_op jit(solution)/shard_map/ppermute | solution.py:398
  190.9 4.6 add_convert_fusion.11
  206.1 19.9 %attention_forward.3 = (f32[512,1024]{1,0:T(8,128)}, bf16[512,1024]{1,0:T(8,128)(2,1)}, f32[8,2,512]{2,1,0:T(2,128)}) custom-call(bf16[512,1024]{1,0:T(8,128)(2,1)} %fusion.21.q_ref, bf16[512,2048]{1,0:T(8,128)(2,1)} %copy-done.47, bf16[512,2048]{1,0:T(8,128)(2,1)} %collective-permute-done.40.k1_ref.v1_ref, bf16[512,2048]{1,0:T(8,128)(2,1)} %copy-done.47, ...), custom_call_target="tpu_custom_call" | custom-call | flops 2147483648 | bytes 10485760 | tf_op jit(solution)/shard_map/attention_forward/pallas_call | solution.py:97
  233.0 11.7 %gated.3 = (bf16[512,4096]{1,0:T(8,128)(2,1)S(1)}, bf16[512,4096]{1,0:T(8,128)(2,1)S(1)}) custom-call(bf16[512,1024]{1,0:T(8,128)(2,1)S(1)} %add_convert_fusion.9.x_ref.refs_1_, bf16[1024,4096]{1,0:T(8,128)(2,1)} %bitcast.465, f32[8,1,512]{2,1,0:T(1,128)S(1)} %bitcast.461), custom_call_target="tpu_custom_call" | custom-call | flops 4294967296 | bytes 16777216 | tf_op jit(solution)/shard_map/gated/pallas_call | solution.py:228
  244.8 5.5 add_convert_fusion.8
  253.2 12.8 %gated_backward.2 = (bf16[512,4096]{1,0:T(8,128)(2,1)S(1)}, f32[4,1,1024]{2,1,0:T(1,128)S(1)}, f32[512,1024]{1,0:T(8,128)S(1)}) custom-call(bf16[512,1024]{1,0:T(8,128)(2,1)S(1)} %broadcast_select_fusion.1.g_ref.refs_3_, bf16[512,4096]{1,0:T(8,128)(2,1)S(1)} %copy-done.41, bf16[4096,1024]{1,0:T(8,128)(2,1)} %bitcast.454, bf16[1024,4096]{1,0:T(8,128)(2,1)} %bitcast.466), custom_call_target="tpu_custom_call" | custom-call | flops 8589934592 | bytes 25165824 | tf_op jit(solution)/shard_map/gated_backward/pallas_call | solution.py:276
  275.5 15.0 %attention_backward.5 = (bf16[512,512]{1,0:T(8,128)(2,1)}, bf16[2,512,512]{2,1,0:T(8,128)(2,1)}, bf16[2,512,512]{2,1,0:T(8,128)(2,1)}) custom-call(bf16[512,1024]{1,0:T(8,128)(2,1)} %fusion.21.q_ref, bf16[512,2048]{1,0:T(8,128)(2,1)} %copy-done.47, bf16[512,2048]{1,0:T(8,128)(2,1)} %collective-permute-done.40.k1_ref.v1_ref, bf16[512,2048]{1,0:T(8,128)(2,1)} %copy-done.47, ...), custom_call_target="tpu_custom_call" | custom-call | flops 2684354560 | bytes 6291456 | tf_op jit(solution)/shard_map/attention_backward/pallas_call | solution.py:177
  290.5 4.8 collective-permute-start.46
  295.3 15.0 %attention_backward.4 = (bf16[512,512]{1,0:T(8,128)(2,1)}, bf16[2,512,512]{2,1,0:T(8,128)(2,1)}, bf16[2,512,512]{2,1,0:T(8,128)(2,1)}) custom-call(bf16[512,1024]{1,0:T(8,128)(2,1)} %fusion.21.q_ref, bf16[512,2048]{1,0:T(8,128)(2,1)} %copy-done.47, bf16[512,2048]{1,0:T(8,128)(2,1)} %collective-permute-done.40.k1_ref.v1_ref, bf16[512,2048]{1,0:T(8,128)(2,1)} %copy-done.47, ...), custom_call_target="tpu_custom_call" | custom-call | flops 2684354560 | bytes 6291456 | tf_op jit(solution)/shard_map/attention_backward/pallas_call | solution.py:177
  315.8 5.8 %multiply_reduce_fusion.4 = (f32[512]{0:T(512)S(1)}, f32[512,1024]{1,0:T(8,128)S(1)}) fusion(bf16[512,1024]{1,0:T(8,128)(2,1)S(1)} %copy-done.50, f32[512]{0:T(512)S(1)} %broadcast_multiply_fusion.3, f32[1024]{0:T(1024)S(1)} %bitcast.524, f32[1024]{0:T(1024)S(1)} %bitcast.501, bf16[512,3072]{1,0:T(8,128)(2,1)S(1)} %constant_dynamic-update-slice_fusion, ...), kind=kOutput, calls=%fused_computation.32 | convolution fusion | flops 3224370688 | bytes 12595200 | tf_op jit(solution)/shard_map/dot_general | solution.py:40
  326.9 14.1 %weight_terms.4 = (bf16[16,128,1024]{2,1,0:T(8,128)(2,1)}, bf16[16,128,1024]{2,1,0:T(8,128)(2,1)}) custom-call(s32[5]{0:T(128)} %stack.56.at_ref, bf16[512,4096]{1,0:T(8,128)(2,1)} %copy-done.38, bf16[512,4096]{1,0:T(8,128)(2,1)} %copy-done.39, bf16[512,1024]{1,0:T(8,128)(2,1)} %get-tuple-element.394.refs_2_.g_ref, bf16[512,1024]{1,0:T(8,128)(2,1)} %copy-done.2), custom_call_target="tpu_custom_call" | custom-call | flops 8589934592 | bytes 18874368 | tf_op jit(solution)/shard_map/weight_terms/pallas_call | solution.py:365
  343.6 12.8 %gated_backward.3 = (bf16[512,4096]{1,0:T(8,128)(2,1)S(1)}, f32[4,1,1024]{2,1,0:T(1,128)S(1)}, f32[512,1024]{1,0:T(8,128)S(1)}) custom-call(bf16[512,1024]{1,0:T(8,128)(2,1)S(1)} %copy-done.4, bf16[512,4096]{1,0:T(8,128)(2,1)S(1)} %copy-done.37, bf16[4096,1024]{1,0:T(8,128)(2,1)} %bitcast.455, bf16[1024,4096]{1,0:T(8,128)(2,1)} %bitcast.467), custom_call_target="tpu_custom_call" | custom-call | flops 8589934592 | bytes 25165824 | tf_op jit(solution)/shard_map/gated_backward/pallas_call | solution.py:276
  369.6 17.6 %weight_terms.5 = (bf16[16,32,5120]{2,1,0:T(8,128)(2,1)}, bf16[16,32,5120]{2,1,0:T(8,128)(2,1)}) custom-call(s32[5]{0:T(128)S(1)} %copy-done.30, bf16[512,1024]{1,0:T(8,128)(2,1)S(1)} %copy-done.20, bf16[512,1024]{1,0:T(8,128)(2,1)S(1)} %copy-done.22, bf16[512,1024]{1,0:T(8,128)(2,1)S(1)} %copy-done.43, bf16[512,1024]{1,0:T(8,128)(2,1)S(1)} %copy-done.44, ...), custom_call_target="tpu_custom_call" | custom-call | flops 10737418240 | bytes 23068672 | tf_op jit(solution)/shard_map/weight_terms/pallas_call | solution.py:365
  393.5 15.0 %attention_backward.6 = (bf16[512,512]{1,0:T(8,128)(2,1)}, bf16[2,512,512]{2,1,0:T(8,128)(2,1)}, bf16[2,512,512]{2,1,0:T(8,128)(2,1)}) custom-call(bf16[512,1024]{1,0:T(8,128)(2,1)} %fusion.20.q_ref, bf16[512,2048]{1,0:T(8,128)(2,1)} %fusion.1.k0_ref.v0_ref, bf16[512,2048]{1,0:T(8,128)(2,1)} %collective-permute-done.21.k1_ref.v1_ref, ...), custom_call_target="tpu_custom_call" | custom-call | flops 2684354560 | bytes 6291456 | tf_op jit(solution)/shard_map/attention_backward/pallas_call | solution.py:177
  427.1 15.0 %attention_backward.7 = (bf16[512,512]{1,0:T(8,128)(2,1)}, bf16[2,512,512]{2,1,0:T(8,128)(2,1)}, bf16[2,512,512]{2,1,0:T(8,128)(2,1)}) custom-call(bf16[512,1024]{1,0:T(8,128)(2,1)} %fusion.20.q_ref, bf16[512,2048]{1,0:T(8,128)(2,1)} %fusion.1.k0_ref.v0_ref, bf16[512,2048]{1,0:T(8,128)(2,1)} %collective-permute-done.21.k1_ref.v1_ref, ...), custom_call_target="tpu_custom_call" | custom-call | flops 2684354560 | bytes 6291456 | tf_op jit(solution)/shard_map/attention_backward/pallas_call | solution.py:177
  444.6 5.8 %weight_terms.6 = (bf16[16,32,1536]{2,1,0:T(8,128)(2,1)}, bf16[16,32,1536]{2,1,0:T(8,128)(2,1)}) custom-call(s32[5]{0:T(128)S(1)} %copy-done.30, bf16[512,1024]{1,0:T(8,128)(2,1)S(1)} %copy-done.14, bf16[512,1024]{1,0:T(8,128)(2,1)S(1)} %copy-done.17, bf16[512,512]{1,0:T(8,128)(2,1)S(1)} %copy-done.10, bf16[512,512]{1,0:T(8,128)(2,1)S(1)} %copy-done.9, ...), custom_call_target="tpu_custom_call" | custom-call | flops 3221225472 | bytes 8388608 | tf_op jit(solution)/shard_map/weight_terms/pallas_call | solution.py:365
  466.8 6.0 %weight_terms.7 = (bf16[16,32,1536]{2,1,0:T(8,128)(2,1)}, bf16[16,32,1536]{2,1,0:T(8,128)(2,1)}) custom-call(s32[5]{0:T(128)S(1)} %copy-done.30, bf16[512,1024]{1,0:T(8,128)(2,1)S(1)} %copy-done.15, bf16[512,1024]{1,0:T(8,128)(2,1)S(1)} %copy-done.18, bf16[512,512]{1,0:T(8,128)(2,1)S(1)} %copy-done.12, bf16[512,512]{1,0:T(8,128)(2,1)S(1)} %copy-done.8, ...), custom_call_target="tpu_custom_call" | custom-call | flops 3221225472 | bytes 8388608 | tf_op jit(solution)/shard_map/weight_terms/pallas_call | solution.py:365
  472.8 5.9 %collective-permute-done.62 = bf16[128,1024]{1,0:T(8,128)(2,1)S(1)} collective-permute-done((bf16[128,1024]{1,0:T(8,128)(2,1)S(1)}, bf16[128,1024]{1,0:T(8,128)(2,1)S(1)}, u32[]{:S(2)}, u32[]{:S(2)}) %collective-permute-start.62) | collective-permute-done | bytes 262176 | tf_op jit(solution)/shard_map/ppermute | solution.py:410
  481.1 4.3 convert_add_fusion.14
  500.1 6.0 %collective-permute-done.66 = bf16[32,5120]{1,0:T(8,128)(2,1)S(1)} collective-permute-done((bf16[32,5120]{1,0:T(8,128)(2,1)S(1)}, bf16[32,5120]{1,0:T(8,128)(2,1)S(1)}, u32[]{:S(2)}, u32[]{:S(2)}) %collective-permute-start.66) | collective-permute-done | bytes 327712 | tf_op jit(solution)/shard_map/ppermute | solution.py:410
  506.1 4.6 collective-permute-done.67
  524.1 5.6 collective-permute-done.68
  567.1 4.2 collective-permute-done.81
  (587 shorter events, 274.9 us)
Async XLA Ops:
  0.7 22.8 %collective-permute-start.4 = (bf16[512,1024]{1,0:T(8,128)(2,1)}, bf16[512,1024]{1,0:T(8,128)(2,1)S(1)}, u32[]{:S(2)}, u32[]{:S(2)}) collective-permute-start(bf16[512,1024]{1,0:T(8,128)(2,1)} %bitcast.496), channel_id=1, source_target_pairs={{1,16},{16,1},{3,18},{18,3},{5,20},{20,5},{7,22},{22,7},{9,24},{24... | collective-permute-start | bytes 3145736 | tf_op jit(solution)/shard_map/ppermute | solution.py:413
  27.1 17.0 %collective-permute-start.5 = (bf16[1,4,16,3200]{3,2,1,0:T(8,128)(2,1)}, bf16[1,4,16,3200]{3,2,1,0:T(8,128)(2,1)S(1)}, u32[]{:S(2)}, u32[]{:S(2)}) collective-permute-start(bf16[1,4,16,3200]{3,2,1,0:T(8,128)(2,1)} %get-tuple-element.276.refs_0_), channel_id=1, source_target_pairs={{0,16},{16,0},{1,17},{17,1},{2,18},{18,2},{3,19},{19,3},{4,20},{20... | collective-permute-start | bytes 1228808 | tf_op jit(solution)/shard_map/ppermute | solution.py:398
  49.8 20.1 %collective-permute-start.10 = (bf16[2,1,4,16,3200]{4,3,2,1,0:T(8,128)(2,1)S(1)}, bf16[2,1,4,16,3200]{4,3,2,1,0:T(8,128)(2,1)S(1)}, u32[]{:S(2)}, u32[]{:S(2)}) collective-permute-start(bf16[2,1,4,16,3200]{4,3,2,1,0:T(8,128)(2,1)S(1)} %get-tuple-element.283.refs_0_), channel_id=1, source_target_pairs={{0,2},{2,0},{1,3},{3,1},{4,6},{6,4},{5,7},{7,5},{8,10},{10,8},{9,1... | collective-permute-start | bytes 2457608 | tf_op jit(solution)/shard_map/ppermute | solution.py:398
  50.3 19.8 %collective-permute-start.11 = (bf16[2,1,4,16,3200]{4,3,2,1,0:T(8,128)(2,1)S(1)}, bf16[2,1,4,16,3200]{4,3,2,1,0:T(8,128)(2,1)S(1)}, u32[]{:S(2)}, u32[]{:S(2)}) collective-permute-start(bf16[2,1,4,16,3200]{4,3,2,1,0:T(8,128)(2,1)S(1)} %get-tuple-element.284.refs_1_), channel_id=1, source_target_pairs={{0,16},{16,0},{1,17},{17,1},{2,18},{18,2},{3,19},{19,3},{4,20},{20... | collective-permute-start | bytes 2457608 | tf_op jit(solution)/shard_map/ppermute | solution.py:398
  101.9 31.3 %collective-permute-start.23 = (bf16[2,1,4,16,5120]{4,3,2,1,0:T(8,128)(2,1)S(1)}, bf16[2,1,4,16,5120]{4,3,2,1,0:T(8,128)(2,1)}, u32[]{:S(2)}, u32[]{:S(2)}) collective-permute-start(bf16[2,1,4,16,5120]{4,3,2,1,0:T(8,128)(2,1)S(1)} %get-tuple-element.315.refs_0_), channel_id=1, source_target_pairs={{0,2},{2,0},{1,3},{3,1},{4,6},{6,4},{5,7},{7,5},{8,10},{10,8},{9,1... | collective-permute-start | bytes 3932168 | tf_op jit(solution)/shard_map/ppermute | solution.py:398
  103.5 31.0 %collective-permute-start.24 = (bf16[2,1,4,16,5120]{4,3,2,1,0:T(8,128)(2,1)S(1)}, bf16[2,1,4,16,5120]{4,3,2,1,0:T(8,128)(2,1)}, u32[]{:S(2)}, u32[]{:S(2)}) collective-permute-start(bf16[2,1,4,16,5120]{4,3,2,1,0:T(8,128)(2,1)S(1)} %get-tuple-element.316.refs_1_), channel_id=1, source_target_pairs={{0,16},{16,0},{1,17},{17,1},{2,18},{18,2},{3,19},{19,3},{4,20},{20... | collective-permute-start | bytes 3932168 | tf_op jit(solution)/shard_map/ppermute | solution.py:398
  106.0 26.4 %collective-permute-start.25 = (bf16[128,1024]{1,0:T(8,128)(2,1)S(1)}, bf16[128,1024]{1,0:T(8,128)(2,1)S(1)}, u32[]{:S(2)}, u32[]{:S(2)}) collective-permute-start(bf16[128,1024]{1,0:T(8,128)(2,1)S(1)} %copy-done.27), channel_id=1, source_target_pairs={{0,4},{4,8},{8,12},{12,0},{1,5},{5,9},{9,13},{13,1},{2,6},{6,10},{... | collective-permute-start | bytes 786440 | tf_op jit(solution)/shard_map/ppermute | solution.py:410
  109.0 23.4 %collective-permute-start.26 = (bf16[128,1024]{1,0:T(8,128)(2,1)S(1)}, bf16[128,1024]{1,0:T(8,128)(2,1)S(1)}, u32[]{:S(2)}, u32[]{:S(2)}) collective-permute-start(bf16[128,1024]{1,0:T(8,128)(2,1)S(1)} %copy-done.27), channel_id=1, source_target_pairs={{0,8},{4,12},{8,0},{12,4},{1,9},{5,13},{9,1},{13,5},{2,10},{6,14},... | collective-permute-start | bytes 786440 | tf_op jit(solution)/shard_map/ppermute | solution.py:410
  110.7 22.2 %collective-permute-start.27 = (bf16[128,1024]{1,0:T(8,128)(2,1)S(1)}, bf16[128,1024]{1,0:T(8,128)(2,1)S(1)}, u32[]{:S(2)}, u32[]{:S(2)}) collective-permute-start(bf16[128,1024]{1,0:T(8,128)(2,1)S(1)} %copy-done.27), channel_id=1, source_target_pairs={{0,12},{4,0},{8,4},{12,8},{1,13},{5,1},{9,5},{13,9},{2,14},{6,2},{... | collective-permute-start | bytes 786440 | tf_op jit(solution)/shard_map/ppermute | solution.py:410
  157.1 24.1 %collective-permute-start.34 = (bf16[2,1,4,64,1024]{4,3,2,1,0:T(8,128)(2,1)S(1)}, bf16[2,1,4,64,1024]{4,3,2,1,0:T(8,128)(2,1)S(1)}, u32[]{:S(2)}, u32[]{:S(2)}) collective-permute-start(bf16[2,1,4,64,1024]{4,3,2,1,0:T(8,128)(2,1)S(1)} %get-tuple-element.350.refs_0_), channel_id=1, source_target_pairs={{0,2},{2,0},{1,3},{3,1},{4,6},{6,4},{5,7},{7,5},{8,10},{10,8},{9,1... | collective-permute-start | bytes 3145736 | tf_op jit(solution)/shard_map/ppermute | solution.py:398
  158.5 26.1 %collective-permute-start.36 = (bf16[2,1,4,64,1024]{4,3,2,1,0:T(8,128)(2,1)S(1)}, bf16[2,1,4,64,1024]{4,3,2,1,0:T(8,128)(2,1)S(1)}, u32[]{:S(2)}, u32[]{:S(2)}) collective-permute-start(bf16[2,1,4,64,1024]{4,3,2,1,0:T(8,128)(2,1)S(1)} %get-tuple-element.350.refs_0_), channel_id=1, source_target_pairs={{0,1},{1,0},{2,3},{3,2},{4,5},{5,4},{6,7},{7,6},{8,9},{9,8},{10,11... | collective-permute-start | bytes 3145736 | tf_op jit(solution)/shard_map/ppermute | solution.py:398
  158.5 25.6 %collective-permute-start.35 = (bf16[2,1,4,64,1024]{4,3,2,1,0:T(8,128)(2,1)S(1)}, bf16[2,1,4,64,1024]{4,3,2,1,0:T(8,128)(2,1)S(1)}, u32[]{:S(2)}, u32[]{:S(2)}) collective-permute-start(bf16[2,1,4,64,1024]{4,3,2,1,0:T(8,128)(2,1)S(1)} %get-tuple-element.351.refs_1_), channel_id=1, source_target_pairs={{0,16},{16,0},{1,17},{17,1},{2,18},{18,2},{3,19},{19,3},{4,20},{20... | collective-permute-start | bytes 3145736 | tf_op jit(solution)/shard_map/ppermute | solution.py:398
  159.4 25.1 %collective-permute-start.37 = (bf16[2,1,4,64,1024]{4,3,2,1,0:T(8,128)(2,1)S(1)}, bf16[2,1,4,64,1024]{4,3,2,1,0:T(8,128)(2,1)S(1)}, u32[]{:S(2)}, u32[]{:S(2)}) collective-permute-start(bf16[2,1,4,64,1024]{4,3,2,1,0:T(8,128)(2,1)S(1)} %get-tuple-element.351.refs_1_), channel_id=1, source_target_pairs={{0,1},{1,0},{2,3},{3,2},{4,5},{5,4},{6,7},{7,6},{8,9},{9,8},{10,11... | collective-permute-start | bytes 3145736 | tf_op jit(solution)/shard_map/ppermute | solution.py:398
  202.0 24.1 %collective-permute-start.41 = (bf16[512,1024]{1,0:T(8,128)(2,1)}, bf16[512,1024]{1,0:T(8,128)(2,1)}, u32[]{:S(2)}, u32[]{:S(2)}) collective-permute-start(bf16[512,1024]{1,0:T(8,128)(2,1)} %bitcast.32), channel_id=1, source_target_pairs={{1,16},{16,1},{3,18},{18,3},{5,20},{20,5},{7,22},{22,7},{9,24},{24... | collective-permute-start | bytes 3145736 | tf_op jit(solution)/shard_map/ppermute | solution.py:413
  272.7 37.6 %collective-permute-start.44 = (bf16[512,1024]{1,0:T(8,128)(2,1)}, bf16[512,1024]{1,0:T(8,128)(2,1)}, u32[]{:S(2)}, u32[]{:S(2)}) collective-permute-start(bf16[512,1024]{1,0:T(8,128)(2,1)} %add_convert_fusion.8), channel_id=1, source_target_pairs={{1,16},{16,1},{3,18},{18,3},{5,20},{20,5},{7,22},{22,7},{9,24},{24... | collective-permute-start | bytes 3145736 | tf_op jit(solution)/shard_map/ppermute | solution.py:413
  290.5 21.2 %collective-permute-start.46 = (bf16[2,512,512]{2,1,0:T(8,128)(2,1)}, bf16[2,512,512]{2,1,0:T(8,128)(2,1)S(1)}, u32[]{:S(2)}, u32[]{:S(2)}) collective-permute-start(bf16[2,512,512]{2,1,0:T(8,128)(2,1)} %get-tuple-element.390), channel_id=1, source_target_pairs={{0,1},{1,0},{2,3},{3,2},{4,5},{5,4},{6,7},{7,6},{8,9},{9,8},{10,11... | collective-permute-start | bytes 3145736 | tf_op jit(solution)/shard_map/ppermute | solution.py:398
  362.2 25.4 %collective-permute-start.48 = (bf16[1,4,2,64,1024]{4,3,2,1,0:T(8,128)(2,1)S(1)}, bf16[1,4,2,64,1024]{4,3,2,1,0:T(8,128)(2,1)}, u32[]{:S(2)}, u32[]{:S(2)}) collective-permute-start(bf16[1,4,2,64,1024]{4,3,2,1,0:T(8,128)(2,1)S(1)} %fusion.18), channel_id=1, source_target_pairs={{0,16},{16,0},{1,17},{17,1},{2,18},{18,2},{3,19},{19,3},{4,20},{20... | collective-permute-start | bytes 3145736 | tf_op jit(solution)/shard_map/ppermute | solution.py:398
  363.1 25.3 %collective-permute-start.49 = (bf16[1,2,4,64,1024]{4,3,2,1,0:T(8,128)(2,1)S(1)}, bf16[1,2,4,64,1024]{4,3,2,1,0:T(8,128)(2,1)}, u32[]{:S(2)}, u32[]{:S(2)}) collective-permute-start(bf16[1,2,4,64,1024]{4,3,2,1,0:T(8,128)(2,1)S(1)} %fusion.19), channel_id=1, source_target_pairs={{0,2},{2,0},{1,3},{3,1},{4,6},{6,4},{5,7},{7,5},{8,10},{10,8},{9,1... | collective-permute-start | bytes 3145736 | tf_op jit(solution)/shard_map/ppermute | solution.py:398
  391.8 16.8 %collective-permute-start.52 = (bf16[1,2,4,2,32,5120]{5,4,3,2,1,0:T(8,128)(2,1)}, bf16[1,2,4,2,32,5120]{5,4,3,2,1,0:T(8,128)(2,1)}, u32[]{:S(2)}, u32[]{:S(2)}) collective-permute-start(bf16[1,2,4,2,32,5120]{5,4,3,2,1,0:T(8,128)(2,1)} %bitcast.554), channel_id=1, source_target_pairs={{0,1},{1,0},{2,3},{3,2},{4,5},{5,4},{6,7},{7,6},{8,9},{9,8},{10,11... | collective-permute-start | bytes 15728648 | tf_op jit(solution)/shard_map/ppermute | solution.py:398
  419.9 22.3 %collective-permute-start.53 = (bf16[2,512,512]{2,1,0:T(8,128)(2,1)}, bf16[2,512,512]{2,1,0:T(8,128)(2,1)}, u32[]{:S(2)}, u32[]{:S(2)}) collective-permute-start(bf16[2,512,512]{2,1,0:T(8,128)(2,1)} %get-tuple-element.436), channel_id=1, source_target_pairs={{0,1},{1,0},{2,3},{3,2},{4,5},{5,4},{6,7},{7,6},{8,9},{9,8},{10,11... | collective-permute-start | bytes 3145736 | tf_op jit(solution)/shard_map/ppermute | solution.py:398
  419.9 31.5 %collective-permute-start.54 = (bf16[1,4,2,16,5120]{4,3,2,1,0:T(8,128)(2,1)}, bf16[1,4,2,16,5120]{4,3,2,1,0:T(8,128)(2,1)}, u32[]{:S(2)}, u32[]{:S(2)}) collective-permute-start(bf16[1,4,2,16,5120]{4,3,2,1,0:T(8,128)(2,1)} %fusion.12), channel_id=1, source_target_pairs={{0,16},{16,0},{1,17},{17,1},{2,18},{18,2},{3,19},{19,3},{4,20},{20... | collective-permute-start | bytes 3932168 | tf_op jit(solution)/shard_map/ppermute | solution.py:398
  420.9 31.2 %collective-permute-start.55 = (bf16[1,2,4,16,5120]{4,3,2,1,0:T(8,128)(2,1)}, bf16[1,2,4,16,5120]{4,3,2,1,0:T(8,128)(2,1)}, u32[]{:S(2)}, u32[]{:S(2)}) collective-permute-start(bf16[1,2,4,16,5120]{4,3,2,1,0:T(8,128)(2,1)} %fusion.13), channel_id=1, source_target_pairs={{0,2},{2,0},{1,3},{3,1},{4,6},{6,4},{5,7},{7,5},{8,10},{10,8},{9,1... | collective-permute-start | bytes 3932168 | tf_op jit(solution)/shard_map/ppermute | solution.py:398
  423.3 27.1 %collective-permute-start.56 = (bf16[128,1024]{1,0:T(8,128)(2,1)}, bf16[128,1024]{1,0:T(8,128)(2,1)S(1)}, u32[]{:S(2)}, u32[]{:S(2)}) collective-permute-start(bf16[128,1024]{1,0:T(8,128)(2,1)} %pad_maximum_fusion.3), channel_id=1, source_target_pairs={{0,4},{4,8},{8,12},{12,0},{1,5},{5,9},{9,13},{13,1},{2,6},{6,10},{... | collective-permute-start | bytes 786440 | tf_op jit(solution)/shard_map/ppermute | solution.py:410
  423.8 26.6 %collective-permute-start.57 = (bf16[128,1024]{1,0:T(8,128)(2,1)}, bf16[128,1024]{1,0:T(8,128)(2,1)S(1)}, u32[]{:S(2)}, u32[]{:S(2)}) collective-permute-start(bf16[128,1024]{1,0:T(8,128)(2,1)} %pad_maximum_fusion.5), channel_id=1, source_target_pairs={{0,12},{4,0},{8,4},{12,8},{1,13},{5,1},{9,5},{13,9},{2,14},{6,2},{... | collective-permute-start | bytes 786440 | tf_op jit(solution)/shard_map/ppermute | solution.py:410
  458.4 20.4 %collective-permute-start.61 = (bf16[1,2,4,2,32,1536]{5,4,3,2,1,0:T(8,128)(2,1)}, bf16[1,2,4,2,32,1536]{5,4,3,2,1,0:T(8,128)(2,1)}, u32[]{:S(2)}, u32[]{:S(2)}) collective-permute-start(bf16[1,2,4,2,32,1536]{5,4,3,2,1,0:T(8,128)(2,1)} %bitcast.83), channel_id=1, source_target_pairs={{0,1},{1,0},{2,3},{3,2},{4,5},{5,4},{6,7},{7,6},{8,9},{9,8},{10,11... | collective-permute-start | bytes 4718600 | tf_op jit(solution)/shard_map/ppermute | solution.py:398
  459.8 19.0 %collective-permute-start.59 = (bf16[1,4,16,5120]{3,2,1,0:T(8,128)(2,1)}, bf16[1,4,16,5120]{3,2,1,0:T(8,128)(2,1)}, u32[]{:S(2)}, u32[]{:S(2)}) collective-permute-start(bf16[1,4,16,5120]{3,2,1,0:T(8,128)(2,1)} %get-tuple-element.458), channel_id=1, source_target_pairs={{0,2},{2,0},{1,3},{3,1},{4,6},{6,4},{5,7},{7,5},{8,10},{10,8},{9,1... | collective-permute-start | bytes 1966088 | tf_op jit(solution)/shard_map/ppermute | solution.py:398
  461.1 17.7 %collective-permute-start.60 = (bf16[1,4,16,5120]{3,2,1,0:T(8,128)(2,1)}, bf16[1,4,16,5120]{3,2,1,0:T(8,128)(2,1)}, u32[]{:S(2)}, u32[]{:S(2)}) collective-permute-start(bf16[1,4,16,5120]{3,2,1,0:T(8,128)(2,1)} %get-tuple-element.459), channel_id=1, source_target_pairs={{0,16},{16,0},{1,17},{17,1},{2,18},{18,2},{3,19},{19,3},{4,20},{20... | collective-permute-start | bytes 1966088 | tf_op jit(solution)/shard_map/ppermute | solution.py:398
  491.8 19.0 %collective-permute-start.65 = (bf16[1,2,4,2,32,1536]{5,4,3,2,1,0:T(8,128)(2,1)S(1)}, bf16[1,2,4,2,32,1536]{5,4,3,2,1,0:T(8,128)(2,1)S(1)}, u32[]{:S(2)}, u32[]{:S(2)}) collective-permute-start(bf16[1,2,4,2,32,1536]{5,4,3,2,1,0:T(8,128)(2,1)S(1)} %bitcast.556), channel_id=1, source_target_pairs={{0,1},{1,0},{2,3},{3,2},{4,5},{5,4},{6,7},{7,6},{8,9},{9,8},{10,11... | collective-permute-start | bytes 4718600 | tf_op jit(solution)/shard_map/ppermute | solution.py:398
  491.9 18.8 %collective-permute-start.63 = (bf16[1,4,2,16,1536]{4,3,2,1,0:T(8,128)(2,1)S(1)}, bf16[1,4,2,16,1536]{4,3,2,1,0:T(8,128)(2,1)S(1)}, u32[]{:S(2)}, u32[]{:S(2)}) collective-permute-start(bf16[1,4,2,16,1536]{4,3,2,1,0:T(8,128)(2,1)S(1)} %fusion.30), channel_id=1, source_target_pairs={{0,16},{16,0},{1,17},{17,1},{2,18},{18,2},{3,19},{19,3},{4,20},{20... | collective-permute-start | bytes 1179656 | tf_op jit(solution)/shard_map/ppermute | solution.py:398
  492.9 17.8 %collective-permute-start.64 = (bf16[1,2,4,16,1536]{4,3,2,1,0:T(8,128)(2,1)S(1)}, bf16[1,2,4,16,1536]{4,3,2,1,0:T(8,128)(2,1)S(1)}, u32[]{:S(2)}, u32[]{:S(2)}) collective-permute-start(bf16[1,2,4,16,1536]{4,3,2,1,0:T(8,128)(2,1)S(1)} %fusion.31), channel_id=1, source_target_pairs={{0,2},{2,0},{1,3},{3,1},{4,6},{6,4},{5,7},{7,5},{8,10},{10,8},{9,1... | collective-permute-start | bytes 1179656 | tf_op jit(solution)/shard_map/ppermute | solution.py:398
  514.8 18.2 %collective-permute-start.70 = (bf16[1,4,2,16,1536]{4,3,2,1,0:T(8,128)(2,1)}, bf16[1,4,2,16,1536]{4,3,2,1,0:T(8,128)(2,1)S(1)}, u32[]{:S(2)}, u32[]{:S(2)}) collective-permute-start(bf16[1,4,2,16,1536]{4,3,2,1,0:T(8,128)(2,1)} %fusion.32), channel_id=1, source_target_pairs={{0,16},{16,0},{1,17},{17,1},{2,18},{18,2},{3,19},{19,3},{4,20},{20... | collective-permute-start | bytes 1179656 | tf_op jit(solution)/shard_map/ppermute | solution.py:398
  515.7 17.3 %collective-permute-start.71 = (bf16[1,2,4,16,1536]{4,3,2,1,0:T(8,128)(2,1)}, bf16[1,2,4,16,1536]{4,3,2,1,0:T(8,128)(2,1)}, u32[]{:S(2)}, u32[]{:S(2)}) collective-permute-start(bf16[1,2,4,16,1536]{4,3,2,1,0:T(8,128)(2,1)} %fusion.33), channel_id=1, source_target_pairs={{0,2},{2,0},{1,3},{3,1},{4,6},{6,4},{5,7},{7,5},{8,10},{10,8},{9,1... | collective-permute-start | bytes 1179656 | tf_op jit(solution)/shard_map/ppermute | solution.py:398
  (185 other events, 1768.4 us)

commit v6 on v5

--- a/solution.py
+++ b/solution.py
@@ -813,9 +813,7 @@
         two.go_pair_near()
         two.go_pair_far()
         three.make_lines()
-        crossed = [t[0] for t in two.pairs]
-        values, crossed, three.sends = tie((values, crossed, three.sends))
-        two.pairs = [(t,) + pair[1:] for t, pair in zip(crossed, two.pairs)]
+        values, three.sends = tie((values, three.sends))
         three.go_first()
         placed = two.result()
         values, three.arrived, placed = tie((values, three.arrived, placed))

time: 584 us -> 583 us (level)
  transfers between devices with their start and end apart: 88 -> 88, of which waited for: 36 -> 37; matrix products, arithmetic and copies ran while one was open for 10% -> 10% of each run, Pallas kernels for 33% -> 33%
where the time goes in v6:
time: 583 us; the launch traced here: 573 us
  Pallas kernels  217 us (37%)
  waiting for transfers between devices  105 us (18%)
  starting transfers between devices  96.6 us (17%)
  other arithmetic  82.3 us (14%)
  matrix products  36 us (6%)
  local copies, waits for them, and re-layouts  32.9 us (6%)
    pallas_call x4, Pallas kernels, attention_backward(): pl.pallas_call(kernel, grid=(pairs,), in_specs=[own, keys_at, keys_at, va...  60 us
    ppermute x27, waiting for transfers between devices, far_shift(): return lax.ppermute(tensor, ('h', 'z'), pairs)  58.5 us
    ppermute x27, starting transfers between devices, far_shift(): return lax.ppermute(tensor, ('h', 'z'), pairs)  47.8 us
    ppermute x54, waiting for transfers between devices, shift(): return lax.ppermute(tensor, axis, [(i, (i + step) % n) for i in range(n)])  46.5 us
    pallas_call x4, Pallas kernels, weight_terms(): pl.pallas_call(kernel, grid=(height // block,), in_specs=[pl.BlockSpec(me...  43.5 us
    ppermute x54, starting transfers between devices, shift(): return lax.ppermute(tensor, axis, [(i, (i + step) % n) for i in range(n)])  40.3 us
    pallas_call x2, Pallas kernels, attention_forward(): pl.pallas_call(kernel, grid=(pairs,), in_specs=[pl.BlockSpec((tokens, PAI...  39.8 us
    pallas_call x2, Pallas kernels, gated_backward(): pl.pallas_call(kernel, grid=(steps,), in_specs=[pl.BlockSpec((tokens, mod...  25.6 us
  transfers between devices with their start and end apart: 88, of which 37 were waited for; matrix products, arithmetic and copies ran while one was open for 10% of the time, Pallas kernels for 33%

profile of v6, /device:TPU:0, one launch (start us, length us, event | category | flops | bytes accessed | tf_op | source)
XLA Modules:
  0.0 572.7 jit_solution(5325391577922803097)
XLA Ops:
  14.4 9.0 %collective-permute-done.1.refs_2_ = bf16[32,3200]{1,0:T(8,128)(2,1)S(1)} collective-permute-done((bf16[32,3200]{1,0:T(8,128)(2,1)S(1)}, bf16[32,3200]{1,0:T(8,128)(2,1)S(1)}, u32[]{:S(2)}, u32[]{:S(2)}) %collective-permute-start.1) | collective-permute-done | bytes 204832 | tf_op jit(solution)/shard_map/ppermute | solution.py:410
  29.4 4.8 collective-permute-start.7
  56.9 4.9 collective-permute-done.12.refs_5_
  61.8 6.5 %collective-permute-done.13.refs_6_ = bf16[32,3072]{1,0:T(8,128)(2,1)S(1)} collective-permute-done((bf16[32,3072]{1,0:T(8,128)(2,1)S(1)}, bf16[32,3072]{1,0:T(8,128)(2,1)S(1)}, u32[]{:S(2)}, u32[]{:S(2)}) %collective-permute-start.13) | collective-permute-done | bytes 196640 | tf_op jit(solution)/shard_map/ppermute | solution.py:410
  91.5 6.6 %collective-permute-done.19.refs_2_ = bf16[1,4,16,5120]{3,2,1,0:T(8,128)(2,1)S(1)} collective-permute-done((bf16[1,4,16,5120]{3,2,1,0:T(8,128)(2,1)S(1)}, bf16[1,4,16,5120]{3,2,1,0:T(8,128)(2,1)S(1)}, u32[]{:S(2)}, u32[]{:S(2)}) %collective-permute-start.19) | collective-permute-done | bytes 655392 | tf_op jit(solution)/shard_map/ppermute | solution.py:398
  110.4 4.7 collective-permute-done.25.refs_1_
  118.8 19.9 %attention_forward.2 = (f32[512,1024]{1,0:T(8,128)}, bf16[512,1024]{1,0:T(8,128)(2,1)}, f32[8,2,512]{2,1,0:T(2,128)}) custom-call(bf16[512,1024]{1,0:T(8,128)(2,1)} %fusion.20.q_ref, bf16[512,2048]{1,0:T(8,128)(2,1)} %fusion.1.k0_ref.v0_ref, bf16[512,2048]{1,0:T(8,128)(2,1)} %collective-permute-done.21.k1_ref.v1_ref, bf16[512,2048]{1,0:T(8,128)(2,1)} %fusion.1.k0_ref.v0_ref, ...), custom_call_target="tpu_custom_call" | custom-call | flops 2147483648 | bytes 10485760 | tf_op jit(solution)/shard_map/attention_forward/pallas_call | solution.py:97
  149.8 6.3 %collective-permute-done.28.refs_2_ = bf16[1,4,64,1024]{3,2,1,0:T(8,128)(2,1)S(1)} collective-permute-done((bf16[1,4,64,1024]{3,2,1,0:T(8,128)(2,1)S(1)}, bf16[1,4,64,1024]{3,2,1,0:T(8,128)(2,1)S(1)}, u32[]{:S(2)}, u32[]{:S(2)}) %collective-permute-start.28) | collective-permute-done | bytes 524320 | tf_op jit(solution)/shard_map/ppermute | solution.py:398
  162.0 11.1 %gated.2 = (bf16[512,4096]{1,0:T(8,128)(2,1)S(1)}, bf16[512,4096]{1,0:T(8,128)(2,1)S(1)}) custom-call(bf16[512,1024]{1,0:T(8,128)(2,1)S(1)} %add_convert_fusion.12.x_ref.refs_0_, bf16[1024,4096]{1,0:T(8,128)(2,1)} %bitcast.464, f32[8,1,512]{2,1,0:T(1,128)S(1)} %bitcast.460), custom_call_target="tpu_custom_call" | custom-call | flops 4294967296 | bytes 16777216 | tf_op jit(solution)/shard_map/gated/pallas_call | solution.py:228
  173.2 9.2 %collective-permute-done.34.refs_2_ = bf16[2,1,4,64,1024]{4,3,2,1,0:T(8,128)(2,1)S(1)} collective-permute-done((bf16[2,1,4,64,1024]{4,3,2,1,0:T(8,128)(2,1)S(1)}, bf16[2,1,4,64,1024]{4,3,2,1,0:T(8,128)(2,1)S(1)}, u32[]{:S(2)}, u32[]{:S(2)}) %collective-permute-start.34) | collective-permute-done | bytes 1048608 | tf_op jit(solution)/shard_map/ppermute | solution.py:398
  190.9 4.6 add_convert_fusion.11
  206.2 19.9 %attention_forward.3 = (f32[512,1024]{1,0:T(8,128)}, bf16[512,1024]{1,0:T(8,128)(2,1)}, f32[8,2,512]{2,1,0:T(2,128)}) custom-call(bf16[512,1024]{1,0:T(8,128)(2,1)} %fusion.21.q_ref, bf16[512,2048]{1,0:T(8,128)(2,1)} %copy-done.47, bf16[512,2048]{1,0:T(8,128)(2,1)} %collective-permute-done.40.k1_ref.v1_ref, bf16[512,2048]{1,0:T(8,128)(2,1)} %copy-done.47, ...), custom_call_target="tpu_custom_call" | custom-call | flops 2147483648 | bytes 10485760 | tf_op jit(solution)/shard_map/attention_forward/pallas_call | solution.py:97
  233.0 11.7 %gated.3 = (bf16[512,4096]{1,0:T(8,128)(2,1)S(1)}, bf16[512,4096]{1,0:T(8,128)(2,1)S(1)}) custom-call(bf16[512,1024]{1,0:T(8,128)(2,1)S(1)} %add_convert_fusion.9.x_ref.refs_1_, bf16[1024,4096]{1,0:T(8,128)(2,1)} %bitcast.465, f32[8,1,512]{2,1,0:T(1,128)S(1)} %bitcast.461), custom_call_target="tpu_custom_call" | custom-call | flops 4294967296 | bytes 16777216 | tf_op jit(solution)/shard_map/gated/pallas_call | solution.py:228
  244.8 5.5 add_convert_fusion.8
  253.2 12.8 %gated_backward.2 = (bf16[512,4096]{1,0:T(8,128)(2,1)S(1)}, f32[4,1,1024]{2,1,0:T(1,128)S(1)}, f32[512,1024]{1,0:T(8,128)S(1)}) custom-call(bf16[512,1024]{1,0:T(8,128)(2,1)S(1)} %broadcast_select_fusion.1.g_ref.refs_3_, bf16[512,4096]{1,0:T(8,128)(2,1)S(1)} %copy-done.41, bf16[4096,1024]{1,0:T(8,128)(2,1)} %bitcast.454, bf16[1024,4096]{1,0:T(8,128)(2,1)} %bitcast.466), custom_call_target="tpu_custom_call" | custom-call | flops 8589934592 | bytes 25165824 | tf_op jit(solution)/shard_map/gated_backward/pallas_call | solution.py:276
  275.5 15.0 %attention_backward.5 = (bf16[512,512]{1,0:T(8,128)(2,1)}, bf16[2,512,512]{2,1,0:T(8,128)(2,1)}, bf16[2,512,512]{2,1,0:T(8,128)(2,1)}) custom-call(bf16[512,1024]{1,0:T(8,128)(2,1)} %fusion.21.q_ref, bf16[512,2048]{1,0:T(8,128)(2,1)} %copy-done.47, bf16[512,2048]{1,0:T(8,128)(2,1)} %collective-permute-done.40.k1_ref.v1_ref, bf16[512,2048]{1,0:T(8,128)(2,1)} %copy-done.47, ...), custom_call_target="tpu_custom_call" | custom-call | flops 2684354560 | bytes 6291456 | tf_op jit(solution)/shard_map/attention_backward/pallas_call | solution.py:177
  290.5 4.8 collective-permute-start.46
  295.3 15.0 %attention_backward.4 = (bf16[512,512]{1,0:T(8,128)(2,1)}, bf16[2,512,512]{2,1,0:T(8,128)(2,1)}, bf16[2,512,512]{2,1,0:T(8,128)(2,1)}) custom-call(bf16[512,1024]{1,0:T(8,128)(2,1)} %fusion.21.q_ref, bf16[512,2048]{1,0:T(8,128)(2,1)} %copy-done.47, bf16[512,2048]{1,0:T(8,128)(2,1)} %collective-permute-done.40.k1_ref.v1_ref, bf16[512,2048]{1,0:T(8,128)(2,1)} %copy-done.47, ...), custom_call_target="tpu_custom_call" | custom-call | flops 2684354560 | bytes 6291456 | tf_op jit(solution)/shard_map/attention_backward/pallas_call | solution.py:177
  315.8 5.8 %multiply_reduce_fusion.4 = (f32[512]{0:T(512)S(1)}, f32[512,1024]{1,0:T(8,128)S(1)}) fusion(bf16[512,1024]{1,0:T(8,128)(2,1)S(1)} %copy-done.50, f32[512]{0:T(512)S(1)} %broadcast_multiply_fusion.3, f32[1024]{0:T(1024)S(1)} %bitcast.524, f32[1024]{0:T(1024)S(1)} %bitcast.501, bf16[512,3072]{1,0:T(8,128)(2,1)S(1)} %constant_dynamic-update-slice_fusion, ...), kind=kOutput, calls=%fused_computation.32 | convolution fusion | flops 3224370688 | bytes 12595200 | tf_op jit(solution)/shard_map/dot_general | solution.py:40
  327.0 14.1 %weight_terms.4 = (bf16[16,128,1024]{2,1,0:T(8,128)(2,1)}, bf16[16,128,1024]{2,1,0:T(8,128)(2,1)}) custom-call(s32[5]{0:T(128)} %stack.56.at_ref, bf16[512,4096]{1,0:T(8,128)(2,1)} %copy-done.38, bf16[512,4096]{1,0:T(8,128)(2,1)} %copy-done.39, bf16[512,1024]{1,0:T(8,128)(2,1)} %get-tuple-element.386.refs_2_.g_ref, bf16[512,1024]{1,0:T(8,128)(2,1)} %copy-done.2), custom_call_target="tpu_custom_call" | custom-call | flops 8589934592 | bytes 18874368 | tf_op jit(solution)/shard_map/weight_terms/pallas_call | solution.py:365
  343.7 12.8 %gated_backward.3 = (bf16[512,4096]{1,0:T(8,128)(2,1)S(1)}, f32[4,1,1024]{2,1,0:T(1,128)S(1)}, f32[512,1024]{1,0:T(8,128)S(1)}) custom-call(bf16[512,1024]{1,0:T(8,128)(2,1)S(1)} %copy-done.4, bf16[512,4096]{1,0:T(8,128)(2,1)S(1)} %copy-done.37, bf16[4096,1024]{1,0:T(8,128)(2,1)} %bitcast.455, bf16[1024,4096]{1,0:T(8,128)(2,1)} %bitcast.467), custom_call_target="tpu_custom_call" | custom-call | flops 8589934592 | bytes 25165824 | tf_op jit(solution)/shard_map/gated_backward/pallas_call | solution.py:276
  370.5 17.6 %weight_terms.5 = (bf16[16,32,5120]{2,1,0:T(8,128)(2,1)}, bf16[16,32,5120]{2,1,0:T(8,128)(2,1)}) custom-call(s32[5]{0:T(128)S(1)} %copy-done.30, bf16[512,1024]{1,0:T(8,128)(2,1)S(1)} %copy-done.20, bf16[512,1024]{1,0:T(8,128)(2,1)S(1)} %copy-done.22, bf16[512,1024]{1,0:T(8,128)(2,1)S(1)} %copy-done.43, bf16[512,1024]{1,0:T(8,128)(2,1)S(1)} %copy-done.44, ...), custom_call_target="tpu_custom_call" | custom-call | flops 10737418240 | bytes 23068672 | tf_op jit(solution)/shard_map/weight_terms/pallas_call | solution.py:365
  394.4 15.0 %attention_backward.6 = (bf16[512,512]{1,0:T(8,128)(2,1)}, bf16[2,512,512]{2,1,0:T(8,128)(2,1)}, bf16[2,512,512]{2,1,0:T(8,128)(2,1)}) custom-call(bf16[512,1024]{1,0:T(8,128)(2,1)} %fusion.20.q_ref, bf16[512,2048]{1,0:T(8,128)(2,1)} %fusion.1.k0_ref.v0_ref, bf16[512,2048]{1,0:T(8,128)(2,1)} %collective-permute-done.21.k1_ref.v1_ref, ...), custom_call_target="tpu_custom_call" | custom-call | flops 2684354560 | bytes 6291456 | tf_op jit(solution)/shard_map/attention_backward/pallas_call | solution.py:177
  427.2 15.0 %attention_backward.7 = (bf16[512,512]{1,0:T(8,128)(2,1)}, bf16[2,512,512]{2,1,0:T(8,128)(2,1)}, bf16[2,512,512]{2,1,0:T(8,128)(2,1)}) custom-call(bf16[512,1024]{1,0:T(8,128)(2,1)} %fusion.20.q_ref, bf16[512,2048]{1,0:T(8,128)(2,1)} %fusion.1.k0_ref.v0_ref, bf16[512,2048]{1,0:T(8,128)(2,1)} %collective-permute-done.21.k1_ref.v1_ref, ...), custom_call_target="tpu_custom_call" | custom-call | flops 2684354560 | bytes 6291456 | tf_op jit(solution)/shard_map/attention_backward/pallas_call | solution.py:177
  444.8 5.8 %weight_terms.6 = (bf16[16,32,1536]{2,1,0:T(8,128)(2,1)}, bf16[16,32,1536]{2,1,0:T(8,128)(2,1)}) custom-call(s32[5]{0:T(128)S(1)} %copy-done.30, bf16[512,1024]{1,0:T(8,128)(2,1)S(1)} %copy-done.14, bf16[512,1024]{1,0:T(8,128)(2,1)S(1)} %copy-done.17, bf16[512,512]{1,0:T(8,128)(2,1)S(1)} %copy-done.10, bf16[512,512]{1,0:T(8,128)(2,1)S(1)} %copy-done.9, ...), custom_call_target="tpu_custom_call" | custom-call | flops 3221225472 | bytes 8388608 | tf_op jit(solution)/shard_map/weight_terms/pallas_call | solution.py:365
  466.8 6.0 %weight_terms.7 = (bf16[16,32,1536]{2,1,0:T(8,128)(2,1)}, bf16[16,32,1536]{2,1,0:T(8,128)(2,1)}) custom-call(s32[5]{0:T(128)S(1)} %copy-done.30, bf16[512,1024]{1,0:T(8,128)(2,1)S(1)} %copy-done.15, bf16[512,1024]{1,0:T(8,128)(2,1)S(1)} %copy-done.18, bf16[512,512]{1,0:T(8,128)(2,1)S(1)} %copy-done.12, bf16[512,512]{1,0:T(8,128)(2,1)S(1)} %copy-done.8, ...), custom_call_target="tpu_custom_call" | custom-call | flops 3221225472 | bytes 8388608 | tf_op jit(solution)/shard_map/weight_terms/pallas_call | solution.py:365
  472.9 4.8 collective-permute-done.62
  480.6 4.3 convert_add_fusion.14
  500.3 6.0 %collective-permute-done.66 = bf16[32,5120]{1,0:T(8,128)(2,1)S(1)} collective-permute-done((bf16[32,5120]{1,0:T(8,128)(2,1)S(1)}, bf16[32,5120]{1,0:T(8,128)(2,1)S(1)}, u32[]{:S(2)}, u32[]{:S(2)}) %collective-permute-start.66) | collective-permute-done | bytes 327712 | tf_op jit(solution)/shard_map/ppermute | solution.py:410
  506.3 4.2 collective-permute-done.67
  524.3 5.6 collective-permute-done.68
  566.5 4.3 collective-permute-done.81
  (587 shorter events, 275.9 us)
Async XLA Ops:
  0.7 22.8 %collective-permute-start.4 = (bf16[512,1024]{1,0:T(8,128)(2,1)}, bf16[512,1024]{1,0:T(8,128)(2,1)S(1)}, u32[]{:S(2)}, u32[]{:S(2)}) collective-permute-start(bf16[512,1024]{1,0:T(8,128)(2,1)} %bitcast.496), channel_id=1, source_target_pairs={{1,16},{16,1},{3,18},{18,3},{5,20},{20,5},{7,22},{22,7},{9,24},{24... | collective-permute-start | bytes 3145736 | tf_op jit(solution)/shard_map/ppermute | solution.py:413
  27.1 17.0 %collective-permute-start.5 = (bf16[1,4,16,3200]{3,2,1,0:T(8,128)(2,1)}, bf16[1,4,16,3200]{3,2,1,0:T(8,128)(2,1)S(1)}, u32[]{:S(2)}, u32[]{:S(2)}) collective-permute-start(bf16[1,4,16,3200]{3,2,1,0:T(8,128)(2,1)} %get-tuple-element.272.refs_0_), channel_id=1, source_target_pairs={{0,16},{16,0},{1,17},{17,1},{2,18},{18,2},{3,19},{19,3},{4,20},{20... | collective-permute-start | bytes 1228808 | tf_op jit(solution)/shard_map/ppermute | solution.py:398
  49.8 20.1 %collective-permute-start.10 = (bf16[2,1,4,16,3200]{4,3,2,1,0:T(8,128)(2,1)S(1)}, bf16[2,1,4,16,3200]{4,3,2,1,0:T(8,128)(2,1)S(1)}, u32[]{:S(2)}, u32[]{:S(2)}) collective-permute-start(bf16[2,1,4,16,3200]{4,3,2,1,0:T(8,128)(2,1)S(1)} %get-tuple-element.279.refs_0_), channel_id=1, source_target_pairs={{0,2},{2,0},{1,3},{3,1},{4,6},{6,4},{5,7},{7,5},{8,10},{10,8},{9,1... | collective-permute-start | bytes 2457608 | tf_op jit(solution)/shard_map/ppermute | solution.py:398
  50.3 19.8 %collective-permute-start.11 = (bf16[2,1,4,16,3200]{4,3,2,1,0:T(8,128)(2,1)S(1)}, bf16[2,1,4,16,3200]{4,3,2,1,0:T(8,128)(2,1)S(1)}, u32[]{:S(2)}, u32[]{:S(2)}) collective-permute-start(bf16[2,1,4,16,3200]{4,3,2,1,0:T(8,128)(2,1)S(1)} %get-tuple-element.280.refs_1_), channel_id=1, source_target_pairs={{0,16},{16,0},{1,17},{17,1},{2,18},{18,2},{3,19},{19,3},{4,20},{20... | collective-permute-start | bytes 2457608 | tf_op jit(solution)/shard_map/ppermute | solution.py:398
  101.9 36.9 %collective-permute-start.23 = (bf16[2,1,4,16,5120]{4,3,2,1,0:T(8,128)(2,1)S(1)}, bf16[2,1,4,16,5120]{4,3,2,1,0:T(8,128)(2,1)}, u32[]{:S(2)}, u32[]{:S(2)}) collective-permute-start(bf16[2,1,4,16,5120]{4,3,2,1,0:T(8,128)(2,1)S(1)} %get-tuple-element.311.refs_0_), channel_id=1, source_target_pairs={{0,2},{2,0},{1,3},{3,1},{4,6},{6,4},{5,7},{7,5},{8,10},{10,8},{9,1... | collective-permute-start | bytes 3932168 | tf_op jit(solution)/shard_map/ppermute | solution.py:398
  103.5 35.3 %collective-permute-start.24 = (bf16[2,1,4,16,5120]{4,3,2,1,0:T(8,128)(2,1)S(1)}, bf16[2,1,4,16,5120]{4,3,2,1,0:T(8,128)(2,1)}, u32[]{:S(2)}, u32[]{:S(2)}) collective-permute-start(bf16[2,1,4,16,5120]{4,3,2,1,0:T(8,128)(2,1)S(1)} %get-tuple-element.312.refs_1_), channel_id=1, source_target_pairs={{0,16},{16,0},{1,17},{17,1},{2,18},{18,2},{3,19},{19,3},{4,20},{20... | collective-permute-start | bytes 3932168 | tf_op jit(solution)/shard_map/ppermute | solution.py:398
  109.4 33.4 %collective-permute-start.30 = (bf16[2,1,4,16,5120]{4,3,2,1,0:T(8,128)(2,1)S(1)}, bf16[2,1,4,16,5120]{4,3,2,1,0:T(8,128)(2,1)}, u32[]{:S(2)}, u32[]{:S(2)}) collective-permute-start(bf16[2,1,4,16,5120]{4,3,2,1,0:T(8,128)(2,1)S(1)} %get-tuple-element.311.refs_0_), channel_id=1, source_target_pairs={{0,1},{1,0},{2,3},{3,2},{4,5},{5,4},{6,7},{7,6},{8,9},{9,8},{10,11... | collective-permute-start | bytes 3932168 | tf_op jit(solution)/shard_map/ppermute | solution.py:398
  115.1 23.6 %collective-permute-start.26 = (bf16[128,1024]{1,0:T(8,128)(2,1)S(1)}, bf16[128,1024]{1,0:T(8,128)(2,1)S(1)}, u32[]{:S(2)}, u32[]{:S(2)}) collective-permute-start(bf16[128,1024]{1,0:T(8,128)(2,1)S(1)} %copy-done.27), channel_id=1, source_target_pairs={{0,8},{4,12},{8,0},{12,4},{1,9},{5,13},{9,1},{13,5},{2,10},{6,14},... | collective-permute-start | bytes 786440 | tf_op jit(solution)/shard_map/ppermute | solution.py:410
  115.4 23.4 %collective-permute-start.27 = (bf16[128,1024]{1,0:T(8,128)(2,1)S(1)}, bf16[128,1024]{1,0:T(8,128)(2,1)S(1)}, u32[]{:S(2)}, u32[]{:S(2)}) collective-permute-start(bf16[128,1024]{1,0:T(8,128)(2,1)S(1)} %copy-done.27), channel_id=1, source_target_pairs={{0,12},{4,0},{8,4},{12,8},{1,13},{5,1},{9,5},{13,9},{2,14},{6,2},{... | collective-permute-start | bytes 786440 | tf_op jit(solution)/shard_map/ppermute | solution.py:410
  157.9 24.5 %collective-permute-start.34 = (bf16[2,1,4,64,1024]{4,3,2,1,0:T(8,128)(2,1)S(1)}, bf16[2,1,4,64,1024]{4,3,2,1,0:T(8,128)(2,1)S(1)}, u32[]{:S(2)}, u32[]{:S(2)}) collective-permute-start(bf16[2,1,4,64,1024]{4,3,2,1,0:T(8,128)(2,1)S(1)} %get-tuple-element.342.refs_0_), channel_id=1, source_target_pairs={{0,2},{2,0},{1,3},{3,1},{4,6},{6,4},{5,7},{7,5},{8,10},{10,8},{9,1... | collective-permute-start | bytes 3145736 | tf_op jit(solution)/shard_map/ppermute | solution.py:398
  158.5 26.1 %collective-permute-start.36 = (bf16[2,1,4,64,1024]{4,3,2,1,0:T(8,128)(2,1)S(1)}, bf16[2,1,4,64,1024]{4,3,2,1,0:T(8,128)(2,1)S(1)}, u32[]{:S(2)}, u32[]{:S(2)}) collective-permute-start(bf16[2,1,4,64,1024]{4,3,2,1,0:T(8,128)(2,1)S(1)} %get-tuple-element.342.refs_0_), channel_id=1, source_target_pairs={{0,1},{1,0},{2,3},{3,2},{4,5},{5,4},{6,7},{7,6},{8,9},{9,8},{10,11... | collective-permute-start | bytes 3145736 | tf_op jit(solution)/shard_map/ppermute | solution.py:398
  158.5 25.6 %collective-permute-start.35 = (bf16[2,1,4,64,1024]{4,3,2,1,0:T(8,128)(2,1)S(1)}, bf16[2,1,4,64,1024]{4,3,2,1,0:T(8,128)(2,1)S(1)}, u32[]{:S(2)}, u32[]{:S(2)}) collective-permute-start(bf16[2,1,4,64,1024]{4,3,2,1,0:T(8,128)(2,1)S(1)} %get-tuple-element.343.refs_1_), channel_id=1, source_target_pairs={{0,16},{16,0},{1,17},{17,1},{2,18},{18,2},{3,19},{19,3},{4,20},{20... | collective-permute-start | bytes 3145736 | tf_op jit(solution)/shard_map/ppermute | solution.py:398
  159.6 25.0 %collective-permute-start.37 = (bf16[2,1,4,64,1024]{4,3,2,1,0:T(8,128)(2,1)S(1)}, bf16[2,1,4,64,1024]{4,3,2,1,0:T(8,128)(2,1)S(1)}, u32[]{:S(2)}, u32[]{:S(2)}) collective-permute-start(bf16[2,1,4,64,1024]{4,3,2,1,0:T(8,128)(2,1)S(1)} %get-tuple-element.343.refs_1_), channel_id=1, source_target_pairs={{0,1},{1,0},{2,3},{3,2},{4,5},{5,4},{6,7},{7,6},{8,9},{9,8},{10,11... | collective-permute-start | bytes 3145736 | tf_op jit(solution)/shard_map/ppermute | solution.py:398
  202.0 24.1 %collective-permute-start.41 = (bf16[512,1024]{1,0:T(8,128)(2,1)}, bf16[512,1024]{1,0:T(8,128)(2,1)}, u32[]{:S(2)}, u32[]{:S(2)}) collective-permute-start(bf16[512,1024]{1,0:T(8,128)(2,1)} %bitcast.32), channel_id=1, source_target_pairs={{1,16},{16,1},{3,18},{18,3},{5,20},{20,5},{7,22},{22,7},{9,24},{24... | collective-permute-start | bytes 3145736 | tf_op jit(solution)/shard_map/ppermute | solution.py:413
  272.7 37.6 %collective-permute-start.44 = (bf16[512,1024]{1,0:T(8,128)(2,1)}, bf16[512,1024]{1,0:T(8,128)(2,1)}, u32[]{:S(2)}, u32[]{:S(2)}) collective-permute-start(bf16[512,1024]{1,0:T(8,128)(2,1)} %add_convert_fusion.8), channel_id=1, source_target_pairs={{1,16},{16,1},{3,18},{18,3},{5,20},{20,5},{7,22},{22,7},{9,24},{24... | collective-permute-start | bytes 3145736 | tf_op jit(solution)/shard_map/ppermute | solution.py:413
  290.5 21.2 %collective-permute-start.46 = (bf16[2,512,512]{2,1,0:T(8,128)(2,1)}, bf16[2,512,512]{2,1,0:T(8,128)(2,1)S(1)}, u32[]{:S(2)}, u32[]{:S(2)}) collective-permute-start(bf16[2,512,512]{2,1,0:T(8,128)(2,1)} %get-tuple-element.382), channel_id=1, source_target_pairs={{0,1},{1,0},{2,3},{3,2},{4,5},{5,4},{6,7},{7,6},{8,9},{9,8},{10,11... | collective-permute-start | bytes 3145736 | tf_op jit(solution)/shard_map/ppermute | solution.py:398
  362.3 25.8 %collective-permute-start.48 = (bf16[1,4,2,64,1024]{4,3,2,1,0:T(8,128)(2,1)S(1)}, bf16[1,4,2,64,1024]{4,3,2,1,0:T(8,128)(2,1)}, u32[]{:S(2)}, u32[]{:S(2)}) collective-permute-start(bf16[1,4,2,64,1024]{4,3,2,1,0:T(8,128)(2,1)S(1)} %fusion.18), channel_id=1, source_target_pairs={{0,16},{16,0},{1,17},{17,1},{2,18},{18,2},{3,19},{19,3},{4,20},{20... | collective-permute-start | bytes 3145736 | tf_op jit(solution)/shard_map/ppermute | solution.py:398
  363.2 25.3 %collective-permute-start.49 = (bf16[1,2,4,64,1024]{4,3,2,1,0:T(8,128)(2,1)S(1)}, bf16[1,2,4,64,1024]{4,3,2,1,0:T(8,128)(2,1)}, u32[]{:S(2)}, u32[]{:S(2)}) collective-permute-start(bf16[1,2,4,64,1024]{4,3,2,1,0:T(8,128)(2,1)S(1)} %fusion.19), channel_id=1, source_target_pairs={{0,2},{2,0},{1,3},{3,1},{4,6},{6,4},{5,7},{7,5},{8,10},{10,8},{9,1... | collective-permute-start | bytes 3145736 | tf_op jit(solution)/shard_map/ppermute | solution.py:398
  391.9 17.5 %collective-permute-start.52 = (bf16[1,2,4,2,32,5120]{5,4,3,2,1,0:T(8,128)(2,1)}, bf16[1,2,4,2,32,5120]{5,4,3,2,1,0:T(8,128)(2,1)}, u32[]{:S(2)}, u32[]{:S(2)}) collective-permute-start(bf16[1,2,4,2,32,5120]{5,4,3,2,1,0:T(8,128)(2,1)} %bitcast.554), channel_id=1, source_target_pairs={{0,1},{1,0},{2,3},{3,2},{4,5},{5,4},{6,7},{7,6},{8,9},{9,8},{10,11... | collective-permute-start | bytes 15728648 | tf_op jit(solution)/shard_map/ppermute | solution.py:398
  391.9 17.5 %collective-permute-start.50 = (bf16[1,4,64,1024]{3,2,1,0:T(8,128)(2,1)}, bf16[1,4,64,1024]{3,2,1,0:T(8,128)(2,1)S(1)}, u32[]{:S(2)}, u32[]{:S(2)}) collective-permute-start(bf16[1,4,64,1024]{3,2,1,0:T(8,128)(2,1)} %get-tuple-element.411), channel_id=1, source_target_pairs={{0,2},{2,0},{1,3},{3,1},{4,6},{6,4},{5,7},{7,5},{8,10},{10,8},{9,1... | collective-permute-start | bytes 1572872 | tf_op jit(solution)/shard_map/ppermute | solution.py:398
  420.8 21.6 %collective-permute-start.53 = (bf16[2,512,512]{2,1,0:T(8,128)(2,1)}, bf16[2,512,512]{2,1,0:T(8,128)(2,1)}, u32[]{:S(2)}, u32[]{:S(2)}) collective-permute-start(bf16[2,512,512]{2,1,0:T(8,128)(2,1)} %get-tuple-element.428), channel_id=1, source_target_pairs={{0,1},{1,0},{2,3},{3,2},{4,5},{5,4},{6,7},{7,6},{8,9},{9,8},{10,11... | collective-permute-start | bytes 3145736 | tf_op jit(solution)/shard_map/ppermute | solution.py:398
  420.8 31.5 %collective-permute-start.54 = (bf16[1,4,2,16,5120]{4,3,2,1,0:T(8,128)(2,1)}, bf16[1,4,2,16,5120]{4,3,2,1,0:T(8,128)(2,1)}, u32[]{:S(2)}, u32[]{:S(2)}) collective-permute-start(bf16[1,4,2,16,5120]{4,3,2,1,0:T(8,128)(2,1)} %fusion.12), channel_id=1, source_target_pairs={{0,16},{16,0},{1,17},{17,1},{2,18},{18,2},{3,19},{19,3},{4,20},{20... | collective-permute-start | bytes 3932168 | tf_op jit(solution)/shard_map/ppermute | solution.py:398
  421.8 31.2 %collective-permute-start.55 = (bf16[1,2,4,16,5120]{4,3,2,1,0:T(8,128)(2,1)}, bf16[1,2,4,16,5120]{4,3,2,1,0:T(8,128)(2,1)}, u32[]{:S(2)}, u32[]{:S(2)}) collective-permute-start(bf16[1,2,4,16,5120]{4,3,2,1,0:T(8,128)(2,1)} %fusion.13), channel_id=1, source_target_pairs={{0,2},{2,0},{1,3},{3,1},{4,6},{6,4},{5,7},{7,5},{8,10},{10,8},{9,1... | collective-permute-start | bytes 3932168 | tf_op jit(solution)/shard_map/ppermute | solution.py:398
  423.4 27.1 %collective-permute-start.56 = (bf16[128,1024]{1,0:T(8,128)(2,1)}, bf16[128,1024]{1,0:T(8,128)(2,1)S(1)}, u32[]{:S(2)}, u32[]{:S(2)}) collective-permute-start(bf16[128,1024]{1,0:T(8,128)(2,1)} %pad_maximum_fusion.3), channel_id=1, source_target_pairs={{0,4},{4,8},{8,12},{12,0},{1,5},{5,9},{9,13},{13,1},{2,6},{6,10},{... | collective-permute-start | bytes 786440 | tf_op jit(solution)/shard_map/ppermute | solution.py:410
  423.4 27.1 %collective-permute-start.57 = (bf16[128,1024]{1,0:T(8,128)(2,1)}, bf16[128,1024]{1,0:T(8,128)(2,1)S(1)}, u32[]{:S(2)}, u32[]{:S(2)}) collective-permute-start(bf16[128,1024]{1,0:T(8,128)(2,1)} %pad_maximum_fusion.5), channel_id=1, source_target_pairs={{0,12},{4,0},{8,4},{12,8},{1,13},{5,1},{9,5},{13,9},{2,14},{6,2},{... | collective-permute-start | bytes 786440 | tf_op jit(solution)/shard_map/ppermute | solution.py:410
  459.2 19.1 %collective-permute-start.61 = (bf16[1,2,4,2,32,1536]{5,4,3,2,1,0:T(8,128)(2,1)}, bf16[1,2,4,2,32,1536]{5,4,3,2,1,0:T(8,128)(2,1)}, u32[]{:S(2)}, u32[]{:S(2)}) collective-permute-start(bf16[1,2,4,2,32,1536]{5,4,3,2,1,0:T(8,128)(2,1)} %bitcast.83), channel_id=1, source_target_pairs={{0,1},{1,0},{2,3},{3,2},{4,5},{5,4},{6,7},{7,6},{8,9},{9,8},{10,11... | collective-permute-start | bytes 4718600 | tf_op jit(solution)/shard_map/ppermute | solution.py:398
  460.7 17.5 %collective-permute-start.59 = (bf16[1,4,16,5120]{3,2,1,0:T(8,128)(2,1)}, bf16[1,4,16,5120]{3,2,1,0:T(8,128)(2,1)}, u32[]{:S(2)}, u32[]{:S(2)}) collective-permute-start(bf16[1,4,16,5120]{3,2,1,0:T(8,128)(2,1)} %get-tuple-element.450), channel_id=1, source_target_pairs={{0,2},{2,0},{1,3},{3,1},{4,6},{6,4},{5,7},{7,5},{8,10},{10,8},{9,1... | collective-permute-start | bytes 1966088 | tf_op jit(solution)/shard_map/ppermute | solution.py:398
  461.2 17.1 %collective-permute-start.60 = (bf16[1,4,16,5120]{3,2,1,0:T(8,128)(2,1)}, bf16[1,4,16,5120]{3,2,1,0:T(8,128)(2,1)}, u32[]{:S(2)}, u32[]{:S(2)}) collective-permute-start(bf16[1,4,16,5120]{3,2,1,0:T(8,128)(2,1)} %get-tuple-element.451), channel_id=1, source_target_pairs={{0,16},{16,0},{1,17},{17,1},{2,18},{18,2},{3,19},{19,3},{4,20},{20... | collective-permute-start | bytes 1966088 | tf_op jit(solution)/shard_map/ppermute | solution.py:398
  491.2 19.3 %collective-permute-start.65 = (bf16[1,2,4,2,32,1536]{5,4,3,2,1,0:T(8,128)(2,1)S(1)}, bf16[1,2,4,2,32,1536]{5,4,3,2,1,0:T(8,128)(2,1)S(1)}, u32[]{:S(2)}, u32[]{:S(2)}) collective-permute-start(bf16[1,2,4,2,32,1536]{5,4,3,2,1,0:T(8,128)(2,1)S(1)} %bitcast.556), channel_id=1, source_target_pairs={{0,1},{1,0},{2,3},{3,2},{4,5},{5,4},{6,7},{7,6},{8,9},{9,8},{10,11... | collective-permute-start | bytes 4718600 | tf_op jit(solution)/shard_map/ppermute | solution.py:398
  491.4 19.1 %collective-permute-start.63 = (bf16[1,4,2,16,1536]{4,3,2,1,0:T(8,128)(2,1)S(1)}, bf16[1,4,2,16,1536]{4,3,2,1,0:T(8,128)(2,1)S(1)}, u32[]{:S(2)}, u32[]{:S(2)}) collective-permute-start(bf16[1,4,2,16,1536]{4,3,2,1,0:T(8,128)(2,1)S(1)} %fusion.30), channel_id=1, source_target_pairs={{0,16},{16,0},{1,17},{17,1},{2,18},{18,2},{3,19},{19,3},{4,20},{20... | collective-permute-start | bytes 1179656 | tf_op jit(solution)/shard_map/ppermute | solution.py:398
  492.4 18.1 %collective-permute-start.64 = (bf16[1,2,4,16,1536]{4,3,2,1,0:T(8,128)(2,1)S(1)}, bf16[1,2,4,16,1536]{4,3,2,1,0:T(8,128)(2,1)S(1)}, u32[]{:S(2)}, u32[]{:S(2)}) collective-permute-start(bf16[1,2,4,16,1536]{4,3,2,1,0:T(8,128)(2,1)S(1)} %fusion.31), channel_id=1, source_target_pairs={{0,2},{2,0},{1,3},{3,1},{4,6},{6,4},{5,7},{7,5},{8,10},{10,8},{9,1... | collective-permute-start | bytes 1179656 | tf_op jit(solution)/shard_map/ppermute | solution.py:398
  514.5 17.9 %collective-permute-start.70 = (bf16[1,4,2,16,1536]{4,3,2,1,0:T(8,128)(2,1)}, bf16[1,4,2,16,1536]{4,3,2,1,0:T(8,128)(2,1)S(1)}, u32[]{:S(2)}, u32[]{:S(2)}) collective-permute-start(bf16[1,4,2,16,1536]{4,3,2,1,0:T(8,128)(2,1)} %fusion.32), channel_id=1, source_target_pairs={{0,16},{16,0},{1,17},{17,1},{2,18},{18,2},{3,19},{19,3},{4,20},{20... | collective-permute-start | bytes 1179656 | tf_op jit(solution)/shard_map/ppermute | solution.py:398
  (185 other events, 1762.1 us)
